TPU v7x, 32 devices: a whole 2x2x4 slice. The times are simulated.
32 devices in a mesh: dp: 4 (over y, x), expert: 8 (over z, core).
Axes of the slice: x: 2, y: 2, z: 4, core: 2. Of those that a mesh axis runs over, the one named last changes fastest.
Arguments:
- tokens: bfloat16 [4096, 2048], P(('dp', 'expert')), may hold values from -6 to 6
- out_grad: bfloat16 [4096, 2048], P(('dp', 'expert')), may hold values from -6 to 6
- routes: int32 [4096, 4], P(('dp', 'expert')), may hold values from 0 to 7, all different within a row; in each aligned block of 128 rows (0 to 127, 128 to 255, ...) at most 72 rows name the same one
- gate_values: float32 [4096, 4], P(('dp', 'expert')), may hold values from 0.05 to 1
- w_gate: bfloat16 [8, 2048, 768], P('expert', 'dp'), may hold values from -0.125 to 0.125
- w_up: bfloat16 [8, 2048, 768], P('expert', 'dp'), may hold values from -0.125 to 0.125
- w_down: bfloat16 [8, 768, 2048], P('expert', None, 'dp'), may hold values from -0.21875 to 0.21875
Outputs:
- input_grad: bfloat16 [4096, 2048], P(('dp', 'expert'))
- gate_grad: bfloat16 [8, 2048, 768], P('expert', 'dp')
- up_grad: bfloat16 [8, 2048, 768], P('expert', 'dp')
- down_grad: bfloat16 [8, 768, 2048], P('expert', None, 'dp')
Inputs may be any that keep to these rules, and one draw needn't show every extreme that they name: `routes`: each token names 4 different experts. Among the 128 tokens of one device (aligned blocks of 128 tokens) no expert is named by more than 72 tokens, and in every draw some device names some expert exactly 72 times.
All inputs are finite; a program needn't handle non-finite values.
Results may differ from a plain program's by a relative error of at most 0.0095.
Values may be sent and summed in bfloat16 or wider, within the bound.
No kernel may reach another device: no remote copies, remote signals or barrier semaphores. Data moves between devices by JAX's collectives and lax.ppermute only.
A program may use at most 128 MiB of HBM per device.

v0:
```python
import functools

import jax
import jax.numpy as jnp
from jax import lax
from jax.experimental import pallas as pl
from jax.experimental.pallas import tpu as pltpu
from jax.sharding import PartitionSpec as P


F32 = jnp.float32
BF16 = jnp.bfloat16
ANY = pl.BlockSpec(memory_space=pl.ANY)
VMEM = pl.BlockSpec(memory_space=pltpu.VMEM)
SMEM = pl.BlockSpec(memory_space=pltpu.SMEM)
LIMIT = 24 * 1024 * 1024
LANES = 128
NN = (((1,), (0,)), ((), ()))
NT = (((1,), (1,)), ((), ()))
TN = (((0,), (0,)), ((), ()))


def mm(a, b, dims):
    return lax.dot_general(a, b, dims, preferred_element_type=F32)


def slots_of(tok_rows, top_count, expert_count):
    return min(tok_rows, max(2, 9 * tok_rows * top_count // (8 * expert_count)))


def call(body, outs, ins, scratch, flops, moved):
    return pl.pallas_call(
        body,
        out_shape=[jax.ShapeDtypeStruct(s, d) for s, d, _ in outs],
        in_specs=[s for _, s in ins],
        out_specs=[s for _, _, s in outs],
        scratch_shapes=scratch,
        compiler_params=pltpu.CompilerParams(vmem_limit_bytes=LIMIT),
        cost_estimate=pl.CostEstimate(flops=flops, bytes_accessed=moved, transcendentals=0),
    )(*[a for a, _ in ins])


def prep_body(experts, routes, gates, rows, out):
    tok, width = rows.shape
    line = lax.broadcasted_iota(jnp.int32, (LANES, tok), 0)
    term, named = line // experts, line % experts
    value = jnp.zeros((LANES, tok), F32)
    for k in range(routes.shape[0]):
        value += jnp.where(routes[k : k + 1, :] == named, gates[k : k + 1, :], 0.0)
    high = value.astype(BF16).astype(F32)
    mid = (value - high).astype(BF16).astype(F32)
    low = value - high - mid
    value = jnp.where(term == 0, high, jnp.where(term == 1, mid, jnp.where(term == 2, low, 0.0)))
    out[:, :width] = rows[...]
    out[:, width:] = jnp.transpose(value).astype(BF16)


class Copies:
    def __init__(self, sems):
        self.sems, self.used = sems, 0

    def start(self, src, dst):
        copy = pltpu.make_async_copy(src, dst, self.sems.at[self.used])
        self.used += 1
        copy.start()
        return copy

    def pick(self, first, src, other, dst):
        sem = self.sems.at[self.used]
        self.used += 1

        @pl.when(first)
        def _():
            pltpu.make_async_copy(src, dst, sem).start()

        @pl.when(jnp.logical_not(first))
        def _():
            pltpu.make_async_copy(other, dst, sem).start()

        return pltpu.make_async_copy(other, dst, sem)


def load_rows(copies, chip, pieces, dst):
    tok = pieces[0].shape[0]
    started = []
    for core in (0, 1):
        own, two, right, left, far = pieces[5 * core : 5 * core + 5]
        at = [dst.at[pl.ds((4 * core + s) * tok, tok)] for s in range(4)]
        started.append(copies.start(own, at[0]))
        started.append(copies.pick(chip == 0, far, right, at[1]))
        started.append(copies.start(two, at[2]))
        started.append(copies.pick(chip == 3, far, left, at[3]))
    return started


def pre_body(place, *refs):
    pieces, w_gate, w_up = refs[:10], refs[10:14], refs[14:18]
    act, active_out, slope_out, x_out, x, wg, wu, sems = refs[18:]
    me, chip = place[0], place[1]
    copies = Copies(sems)
    rows = load_rows(copies, chip, pieces, x)
    share, hidden = w_gate[0].shape
    weights = []
    for k in range(4):
        at = pl.ds((me ^ k) * share, share)
        weights += [copies.start(w_gate[k], wg.at[at]), copies.start(w_up[k], wu.at[at])]
    for c in rows:
        c.wait()
    out = copies.start(x, x_out)
    for c in weights:
        c.wait()
    tm, tn = x.shape[0] // 2, 256

    def step(i, _):
        r = pl.ds(pl.multiple_of(i // (hidden // tn) * tm, tm), tm)
        c = pl.ds(pl.multiple_of(i % (hidden // tn) * tn, tn), tn)
        lhs = x[r, :]
        gate = mm(lhs, wg[:, c], NN)
        up = mm(lhs, wu[:, c], NN)
        sigma = jax.nn.sigmoid(gate)
        active = gate * sigma
        act[r, c] = (active * up).astype(BF16)
        active_out[r, c] = active
        slope_out[r, c] = up * sigma * (1.0 + gate * (1.0 - sigma))
        return 0

    lax.fori_loop(0, 2 * (hidden // tn), step, 0)
    out.wait()


def down_body(experts, place, *refs):
    pieces, act = refs[:10], refs[10]
    send_a, keep_a, send_b, keep_b, y_out, raw, y, sems = refs[11:]
    me, chip, expert = place[0], place[1], place[2]
    copies = Copies(sems)
    for c in load_rows(copies, chip, pieces, raw):
        c.wait()
    rows, width = y.shape
    tok = rows // 8
    lane = lax.broadcasted_iota(jnp.int32, (tok, LANES), 1)
    mine = jnp.logical_and(lane % experts == expert, lane < 3 * experts)

    def scale(i, _):
        r = pl.ds(pl.multiple_of(i * tok, tok), tok)
        gate = jnp.sum(jnp.where(mine, raw[r, width:].astype(F32), 0.0), axis=1, keepdims=True)
        y[r, :] = (raw[r, :width].astype(F32) * gate).astype(BF16)
        return 0

    lax.fori_loop(0, 8, scale, 0)
    out = copies.start(y, y_out)
    share = width // 4
    half = act.shape[1] // 2
    for dst, h, pair in ((send_a, 0, (1, 3)), (send_b, 1, (2, 3)), (keep_a, 0, (0, 2)), (keep_b, 1, (0, 1))):
        for slot, k in enumerate(pair):
            cols = pl.ds(pl.multiple_of((me ^ k) * share, share), share)
            dst[slot] = mm(act[:, h * half : (h + 1) * half], y[:, cols], TN).astype(BF16)
    out.wait()


def back_body(place, y, active, slope, own, from_x, from_y, diag_a, diag_b, gate_delta, up_delta, w, sems):
    me = place[0]
    copies = Copies(sems)
    hidden, share = own.shape
    half = hidden // 2
    started = []
    for k, src in ((0, own), (1, from_x), (2, from_y)):
        started.append(copies.start(src, w.at[me ^ k]))
    started.append(copies.start(diag_a, w.at[me ^ 3, pl.ds(0, half)]))
    started.append(copies.start(diag_b, w.at[me ^ 3, pl.ds(half, half)]))
    for c in started:
        c.wait()
    rows = y.shape[0]
    tm, tn = rows // 2, 256

    def step(i, _):
        r = pl.ds(pl.multiple_of(i // (hidden // tn) * tm, tm), tm)
        c = pl.ds(pl.multiple_of(i % (hidden // tn) * tn, tn), tn)
        back = mm(y[r, 0:share], w[0, c, :], NT)
        for j in range(1, 4):
            back += mm(y[r, j * share : (j + 1) * share], w[j, c, :], NT)
        up_delta[r, c] = (back * active[r, c]).astype(BF16)
        gate_delta[r, c] = (back * slope[r, c]).astype(BF16)
        return 0

    lax.fori_loop(0, 2 * (hidden // tn), step, 0)


def grad_body(send_pair, keep_pair, place, x, delta, send, keep):
    me = place[0]
    share = x.shape[1] // 4
    tm = share // 2
    for dst, pair in ((send, send_pair), (keep, keep_pair)):
        for slot, k in enumerate(pair):

            def step(i, _, dst=dst, slot=slot, k=k):
                cols = pl.ds(pl.multiple_of((me ^ k) * share + i * tm, tm), tm)
                dst[slot, pl.ds(pl.multiple_of(i * tm, tm), tm), :] = mm(x[:, cols], delta[...], TN).astype(BF16)
                return 0

            lax.fori_loop(0, 2, step, 0)


def pair_body(place, gate_delta, up_delta, *refs):
    w_gate, w_up = refs[:4], refs[4:8]
    send, keep, wg, wu, sems = refs[8:]
    me = place[0]
    copies = Copies(sems)
    started = []
    for k in range(4):
        started.append((copies.start(w_gate[k], wg.at[k]), copies.start(w_up[k], wu.at[k])))
    share = wg.shape[1]
    tn = share // 2
    rows = keep.shape[0]
    for k in range(4):
        for c in started[k]:
            c.wait()
    for dst, first in ((send, rows), (keep, 0)):

        def step(i, _, dst=dst, first=first):
            k, part = i // 2, pl.ds(pl.multiple_of(i % 2 * tn, tn), tn)
            total = mm(gate_delta[first : first + rows, :], wg[k, part, :], NT)
            total += mm(up_delta[first : first + rows, :], wu[k, part, :], NT)
            cols = pl.ds(pl.multiple_of((me ^ k) * share + i % 2 * tn, tn), tn)
            dst[:, cols] = total.astype(BF16)
            return 0

        lax.fori_loop(0, 8, step, 0)


def add(*terms):
    total = terms[0].astype(F32)
    for term in terms[1:]:
        total = total + term.astype(F32)
    return total.astype(BF16)


def dense(tokens, out_grad, routes, gate_values, w_gate, w_up, w_down):
    tok, width = tokens.shape
    experts = lax.axis_size("expert")
    chips = experts // 2
    hidden = w_gate.shape[2]
    share = width // 4
    half = hidden // 2
    rows = experts * tok
    expert = lax.axis_index("expert")
    chip = expert // 2
    place = jnp.stack([lax.axis_index("dp"), chip, expert]).astype(jnp.int32)

    def to_x(block):
        return lax.ppermute(block, "dp", [(i, i ^ 1) for i in range(4)])

    def to_y(block):
        return lax.ppermute(block, "dp", [(i, i ^ 2) for i in range(4)])

    def hop(block, moves):
        return lax.ppermute(block, "expert", [(2 * a + c, 2 * b + c) for a, b in moves for c in (0, 1)])

    def swap(block, at=range(chips)):
        return lax.ppermute(block, "expert", [(2 * z + c, 2 * z + 1 - c) for z in at for c in (0, 1)])

    def line(own):
        two = hop(own, [(z, (z + 2) % 4) for z in range(4)])
        right = hop(own, [(0, 1), (1, 2), (2, 3)])
        left = hop(own, [(1, 0), (2, 1), (3, 2)])
        far = hop(two, [(2, 3), (1, 0)])
        return [own, two, right, left, far] + [
            swap(own), swap(two), swap(right, (1, 2, 3)), swap(left, (0, 1, 2)), swap(far, (0, 3))
        ]

    x_pieces = line(tokens)
    (y_own,) = call(
        functools.partial(prep_body, experts),
        [((tok, width + LANES), BF16, VMEM)],
        [(routes.T, VMEM), (gate_values.T, VMEM), (out_grad, VMEM)],
        [],
        1000,
        4 * tok * width,
    )
    y_pieces = line(y_own)

    wg0, wu0, wd0 = w_gate[0], w_up[0], w_down[0]
    wg1, wu1 = to_x(wg0), to_y(wu0)
    wg2, wu2 = to_y(wg0), to_x(wu0)
    wg3, wu3 = to_y(wg1), to_x(wu1)
    w_g, w_u = (wg0, wg1, wg2, wg3), (wu0, wu2, wu1, wu3)
    wd1, wd2 = to_x(wd0), to_y(wd0)
    wd3a, wd3b = to_x(wd2[:half]), to_y(wd1[half:])

    def dma(n):
        return pltpu.SemaphoreType.DMA((n,))

    weight = pltpu.VMEM((width, hidden), BF16)
    act, active, slope, x = call(
        pre_body,
        [
            ((rows, hidden), BF16, VMEM),
            ((rows, hidden), F32, VMEM),
            ((rows, hidden), F32, VMEM),
            ((rows, width), BF16, ANY),
        ],
        [(place, SMEM)] + [(a, ANY) for a in x_pieces] + [(a, ANY) for a in w_g + w_u],
        [pltpu.VMEM((rows, width), BF16), weight, weight, dma(17)],
        4 * rows * width * hidden,
        2 * (2 * rows * width + 2 * width * hidden) + 10 * rows * hidden,
    )
    piece = (2, half, share)
    send_a, keep_a, send_b, keep_b, y = call(
        functools.partial(down_body, experts),
        [(piece, BF16, VMEM)] * 4 + [((rows, width), BF16, ANY)],
        [(place, SMEM)] + [(a, ANY) for a in y_pieces] + [(act, VMEM)],
        [pltpu.VMEM((rows, width + LANES), BF16), pltpu.VMEM((rows, width), BF16), dma(9)],
        2 * rows * width * hidden,
        2 * (2 * rows * width + rows * hidden + width * hidden),
    )
    got_a, got_b = to_x(send_a), to_y(send_b)
    gate_delta, up_delta = call(
        back_body,
        [((rows, hidden), BF16, VMEM)] * 2,
        [(place, SMEM), (y, VMEM), (active, VMEM), (slope, VMEM)] + [(a, ANY) for a in (wd0, wd1, wd2, wd3a, wd3b)],
        [pltpu.VMEM((4, hidden, share), BF16), dma(5)],
        2 * rows * width * hidden,
        2 * (rows * width + width * hidden) + 12 * rows * hidden,
    )
    piece = (2, share, hidden)

    def grad(delta, send_pair, keep_pair):
        return call(
            functools.partial(grad_body, send_pair, keep_pair),
            [(piece, BF16, VMEM)] * 2,
            [(place, SMEM), (x, VMEM), (delta, VMEM)],
            [],
            2 * rows * width * hidden,
            2 * (rows * width + rows * hidden + width * hidden),
        )

    gate_send, gate_keep = grad(gate_delta, (1, 3), (0, 2))
    gate_got = to_x(gate_send)
    up_send, up_keep = grad(up_delta, (2, 3), (0, 1))
    up_got = to_y(up_send)
    weight = pltpu.VMEM((4, share, hidden), BF16)
    pair_send, pair_keep = call(
        pair_body,
        [((rows // 2, width), BF16, VMEM)] * 2,
        [(place, SMEM), (gate_delta, VMEM), (up_delta, VMEM)] + [(a, ANY) for a in w_g + w_u],
        [weight, weight, dma(8)],
        4 * rows * width * hidden,
        2 * (rows * width + 2 * rows * hidden + 2 * width * hidden),
    )
    down_a = add(keep_a[0], got_a[0]), to_y(add(keep_a[1], got_a[1]))
    down_b = add(keep_b[0], got_b[0]), to_x(add(keep_b[1], got_b[1]))
    down_grad = jnp.concatenate([add(*down_a), add(*down_b)], axis=0)
    gate_grad = add(add(gate_keep[0], gate_got[0]), to_y(add(gate_keep[1], gate_got[1])))
    up_grad = add(add(up_keep[0], up_got[0]), to_x(add(up_keep[1], up_got[1])))

    total = add(pair_keep, swap(pair_send)).reshape(chips, tok, width)
    far = hop(jnp.where(chip == 0, total[1], total[3]), [(3, 2), (0, 1)])
    right = hop(total[3], [(0, 1), (1, 2), (2, 3)])
    left = hop(total[1], [(1, 0), (2, 1), (3, 2)])
    two = hop(add(total[2], far), [(z, (z + 2) % 4) for z in range(4)])
    input_grad = add(total[0], right, left, two)
    return input_grad, gate_grad[None], up_grad[None], down_grad[None]


def routed(tokens, out_grad, routes, gate_values, w_gate, w_up, w_down):
    tok_rows, model_width = tokens.shape
    top_count = routes.shape[1]
    group_count = lax.axis_size("expert")
    local_count = w_gate.shape[0]
    expert_count = group_count * local_count
    hidden_units = w_gate.shape[2]
    capacity = slots_of(tok_rows, top_count, expert_count)
    pair_count = tok_rows * top_count
    slot_count = group_count * capacity
    expert_of = routes.reshape(-1)
    onehot = (expert_of[:, None] == jnp.arange(expert_count, dtype=jnp.int32)[None, :]).astype(
        jnp.int32
    )
    before = jnp.cumsum(onehot, axis=0) - onehot
    placed = jnp.sum(before * onehot, axis=1)
    slot_of = expert_of * capacity + placed
    slot_table = jnp.full((expert_count * capacity,), pair_count, jnp.int32)
    slot_table = slot_table.at[slot_of].set(jnp.arange(pair_count, dtype=jnp.int32))
    filled = slot_table < pair_count
    source = jnp.where(filled, slot_table, 0)
    owner_row = source // top_count
    send_x = jnp.where(filled[:, None], tokens[owner_row], jnp.zeros((), jnp.bfloat16))
    scaled = gate_values.reshape(-1)[source][:, None] * out_grad[owner_row].astype(jnp.float32)
    send_dy = jnp.where(filled[:, None], scaled, 0.0).astype(jnp.bfloat16)
    send_x = send_x.reshape(expert_count, capacity, model_width)
    send_dy = send_dy.reshape(expert_count, capacity, model_width)
    recv_x, recv_dy = (
        lax.all_to_all(send_x, "expert", split_axis=0, concat_axis=0, tiled=True),
        lax.all_to_all(send_dy, "expert", split_axis=0, concat_axis=0, tiled=True),
    )

    def to_local(stacked):
        shaped = stacked.reshape(group_count, local_count, capacity, model_width)
        return shaped.transpose(1, 0, 2, 3).reshape(local_count, slot_count, model_width)

    slot_x = to_local(recv_x)
    slot_dy = to_local(recv_dy)
    part_x = slot_x
    gate_term = jnp.einsum(
        "asd,adf->asf",
        part_x,
        lax.all_gather(w_gate, "dp", axis=1, tiled=True),
        preferred_element_type=jnp.float32,
    )
    up_term = jnp.einsum(
        "asd,adf->asf",
        part_x,
        lax.all_gather(w_up, "dp", axis=1, tiled=True),
        preferred_element_type=jnp.float32,
    )
    full_gate, full_up, full_down = (
        lax.all_gather(w_gate, "dp", axis=1, tiled=True),
        lax.all_gather(w_up, "dp", axis=1, tiled=True),
        lax.all_gather(w_down, "dp", axis=2, tiled=True),
    )
    sigma = jax.nn.sigmoid(gate_term)
    active = gate_term * sigma
    activated = (active * up_term).astype(jnp.bfloat16)
    back_hidden = jnp.einsum("asd,afd->asf", slot_dy, full_down, preferred_element_type=jnp.float32)
    up_delta = (back_hidden * active).astype(jnp.bfloat16)
    gate_delta = (back_hidden * up_term * sigma * (1.0 + gate_term * (1.0 - sigma))).astype(
        jnp.bfloat16
    )
    pair_grad = (
        jnp.einsum("asf,adf->asd", gate_delta, full_gate, preferred_element_type=jnp.float32)
        + jnp.einsum("asf,adf->asd", up_delta, full_up, preferred_element_type=jnp.float32)
    ).astype(jnp.bfloat16)
    send_back = pair_grad.reshape(local_count, group_count, capacity, model_width).transpose(
        1, 0, 2, 3
    )
    send_back = send_back.reshape(expert_count, capacity, model_width)
    returned = lax.all_to_all(send_back, "expert", split_axis=0, concat_axis=0, tiled=True)
    per_pair = returned.reshape(expert_count * capacity, model_width)[slot_of].astype(jnp.float32)
    input_grad = jnp.sum(per_pair.reshape(tok_rows, top_count, model_width), axis=1).astype(
        jnp.bfloat16
    )
    block_width = local_count * hidden_units
    share_width = model_width // lax.axis_size("dp")
    part_x = slot_x
    term_gate = jnp.einsum("asd,asf->daf", part_x, gate_delta, preferred_element_type=jnp.float32)
    term_up = jnp.einsum("asd,asf->daf", part_x, up_delta, preferred_element_type=jnp.float32)
    term_down = jnp.einsum("asd,asf->daf", slot_dy, activated, preferred_element_type=jnp.float32)
    shares = lax.psum_scatter(
        jnp.concatenate(
            [
                term_gate.reshape(lax.axis_size("dp") * share_width, block_width),
                term_up.reshape(lax.axis_size("dp") * share_width, block_width),
                term_down.reshape(lax.axis_size("dp") * share_width, block_width),
            ],
            axis=1,
        ).astype(jnp.bfloat16),
        "dp",
        scatter_dimension=0,
        tiled=True,
    ).astype(jnp.float32)
    share_rows = shares.shape[0]

    def unpack(which):
        return shares[:, which * block_width : (which + 1) * block_width].reshape(
            share_rows, local_count, hidden_units
        )

    gate_grad = unpack(0).transpose(1, 0, 2).astype(jnp.bfloat16)
    up_grad = unpack(1).transpose(1, 0, 2).astype(jnp.bfloat16)
    down_grad = unpack(2).transpose(1, 2, 0).astype(jnp.bfloat16)
    return (input_grad, gate_grad, up_grad, down_grad)


def lined(dp, expert):
    return dp == 4 and expert == 8


def local(tokens, out_grad, routes, gate_values, w_gate, w_up, w_down):
    experts = lax.axis_size("expert") * w_gate.shape[0]
    capacity = slots_of(tokens.shape[0], routes.shape[1], experts)
    fits = w_gate.shape[0] == 1 and tokens.shape[0] <= 2 * capacity
    if not (fits and lined(lax.axis_size("dp"), lax.axis_size("expert"))):
        return routed(tokens, out_grad, routes, gate_values, w_gate, w_up, w_down)
    return dense(tokens, out_grad, routes, gate_values, w_gate, w_up, w_down)


def solution(mesh):
    return jax.shard_map(
        local,
        mesh=mesh,
        in_specs=(
            P(("dp", "expert"), None),
            P(("dp", "expert"), None),
            P(("dp", "expert"), None),
            P(("dp", "expert"), None),
            P("expert", "dp", None),
            P("expert", "dp", None),
            P("expert", None, "dp"),
        ),
        out_specs=(
            P(("dp", "expert"), None),
            P("expert", "dp", None),
            P("expert", "dp", None),
            P("expert", None, "dp"),
        ),
        check_vma=False,
    )
```

profile of v0, /device:TPU:0, one launch (start us, length us, event | category | flops | bytes accessed | tf_op | source)
XLA Modules:
  0.0 303.8 jit_solution(9635159536032364120)
XLA Ops:
  0.6 4.1 %collective-permute-start.9 = (bf16[128,2048]{1,0:T(8,128)(2,1)}, bf16[128,2048]{1,0:T(8,128)(2,1)S(1)}, u32[]{:S(2)}, u32[]{:S(2)}) collective-permute-start(bf16[128,2048]{1,0:T(8,128)(2,1)} %refs_0_.1), channel_id=1, source_target_pairs={{0,4},{1,5},{2,6},{3,7},{4,0},{5,1},{6,2},{7,3},{8,12},{9,13},{10,... | collective-permute-start | bytes 1572872 | tf_op jit(solution)/shard_map/ppermute | solution.py:256
  4.8 3.5 %collective-permute-start.10 = (bf16[128,2048]{1,0:T(8,128)(2,1)}, bf16[128,2048]{1,0:T(8,128)(2,1)S(1)}, u32[]{:S(2)}, u32[]{:S(2)}) collective-permute-start(bf16[128,2048]{1,0:T(8,128)(2,1)} %refs_0_.1), channel_id=1, source_target_pairs={{0,2},{1,3},{2,4},{3,5},{4,6},{5,7},{8,10},{9,11},{10,12},{11,13},... | collective-permute-start | bytes 1572872 | tf_op jit(solution)/shard_map/ppermute | solution.py:256
  8.3 1.3 collective-permute-start.11
  12.2 2.1 collective-permute-start
  14.3 15.6 %collective-permute-done.9.refs_1_ = bf16[128,2048]{1,0:T(8,128)(2,1)S(1)} collective-permute-done((bf16[128,2048]{1,0:T(8,128)(2,1)}, bf16[128,2048]{1,0:T(8,128)(2,1)S(1)}, u32[]{:S(2)}, u32[]{:S(2)}) %collective-permute-start.9) | collective-permute-done | bytes 524320 | tf_op jit(solution)/shard_map/ppermute | solution.py:256
  29.9 2.8 collective-permute-start.1
  32.7 1.3 collective-permute-start.2
  34.9 1.5 collective-permute-start.18
  36.4 27.9 %collective-permute-done.refs_1_ = bf16[128,2176]{1,0:T(8,128)(2,1)} collective-permute-done((bf16[128,2176]{1,0:T(8,128)(2,1)S(1)}, bf16[128,2176]{1,0:T(8,128)(2,1)}, u32[]{:S(2)}, u32[]{:S(2)}) %collective-permute-start) | collective-permute-done | bytes 557088 | tf_op jit(solution)/shard_map/ppermute | solution.py:256
  64.3 1.8 collective-permute-start.22
  66.3 9.0 %collective-permute-done.2.refs_3_ = bf16[128,2176]{1,0:T(8,128)(2,1)} collective-permute-done((bf16[128,2176]{1,0:T(8,128)(2,1)S(1)}, bf16[128,2176]{1,0:T(8,128)(2,1)}, u32[]{:S(2)}, u32[]{:S(2)}) %collective-permute-start.2) | collective-permute-done | bytes 557088 | tf_op jit(solution)/shard_map/ppermute | solution.py:256
  75.3 1.5 collective-permute-start.21
  77.7 1.5 collective-permute-start.25
  79.7 5.3 %collective-permute-done.22.refs_16_.refs_6_ = bf16[512,768]{1,0:T(8,128)(2,1)} collective-permute-done((bf16[512,768]{1,0:T(8,128)(2,1)}, bf16[512,768]{1,0:T(8,128)(2,1)}, u32[]{:S(2)}, u32[]{:S(2)}) %collective-permute-start.22) | collective-permute-done | bytes 786464 | tf_op jit(solution)/shard_map/ppermute | solution.py:253
  85.0 1.3 collective-permute-start.12
  86.3 15.5 %collective-permute-done.19.refs_12_.refs_2_ = bf16[512,768]{1,0:T(8,128)(2,1)S(1)} collective-permute-done((bf16[512,768]{1,0:T(8,128)(2,1)}, bf16[512,768]{1,0:T(8,128)(2,1)S(1)}, u32[]{:S(2)}, u32[]{:S(2)}) %collective-permute-start.19) | collective-permute-done | bytes 786464 | tf_op jit(solution)/shard_map/ppermute | solution.py:253
  105.9 10.2 %collective-permute-done.25.from_y = bf16[768,512]{1,0:T(8,128)(2,1)S(1)} collective-permute-done((bf16[768,512]{1,0:T(8,128)(2,1)}, bf16[768,512]{1,0:T(8,128)(2,1)S(1)}, u32[]{:S(2)}, u32[]{:S(2)}) %collective-permute-start.25) | collective-permute-done | bytes 786464 | tf_op jit(solution)/shard_map/ppermute | solution.py:253
  116.1 1.9 collective-permute-start.16
  118.9 1.3 collective-permute-start.20
  120.2 1.5 collective-permute-start.23
  122.5 1.3 collective-permute-start.3
  125.4 2.4 collective-permute-start.17
  128.0 11.2 %collective-permute-done.3.refs_4_ = bf16[128,2176]{1,0:T(8,128)(2,1)} collective-permute-done((bf16[128,2176]{1,0:T(8,128)(2,1)}, bf16[128,2176]{1,0:T(8,128)(2,1)}, u32[]{:S(2)}, u32[]{:S(2)}) %collective-permute-start.3) | collective-permute-done | bytes 557088 | tf_op jit(solution)/shard_map/ppermute | solution.py:256
  139.8 1.9 collective-permute-start.7
  143.1 1.9 collective-permute-start.8
  145.0 1.1 copy-done.16
  147.2 1.0 copy-done.22
  148.3 1.0 copy-done.24
  149.3 1.0 copy-done.26
  151.4 1.0 copy-done.30
  152.4 1.0 copy-done.32
  153.5 1.0 copy-done.34
  154.5 10.9 %shard_map.103 = (bf16[1024,768]{1,0:T(8,128)(2,1)S(1)}, f32[1024,768]{1,0:T(8,128)S(1)}, f32[1024,768]{1,0:T(8,128)S(1)}, bf16[1024,2048]{1,0:T(8,128)(2,1)S(1)}) custom-call(s32[3]{0:T(128)S(1)} %pad_add_fusion.place, bf16[128,2048]{1,0:T(8,128)(2,1)S(1)} %copy-done.20, bf16[128,2048]{1,0:T(8,128)(2,1)S(1)} %copy-done.22, ...), custom_call_target="tpu_custom_call" | custom-call | flops 6442450944 | bytes 22544384 | tf_op jit(solution)/shard_map/pallas_call | solution.py:32
  165.4 2.0 copy-done.35
  167.5 8.4 %shard_map.104 = (bf16[2,384,512]{2,1,0:T(8,128)(2,1)}, bf16[2,384,512]{2,1,0:T(8,128)(2,1)S(1)}, bf16[2,384,512]{2,1,0:T(8,128)(2,1)}, bf16[2,384,512]{2,1,0:T(8,128)(2,1)S(1)}, bf16[1024,2048]{1,0:T(8,128)(2,1)S(1)}) custom-call(s32[3]{0:T(128)S(1)} %pad_add_fusion.place, bf16[128,2176]{1,0:T(8,128)(2,1)S(1)} %shard_map.102.refs_0_, ...), custom_call_target="tpu_custom_call" | custom-call | flops 3221225472 | bytes 13107200 | tf_op jit(solution)/shard_map/pallas_call | solution.py:32
  175.9 1.3 collective-permute-start.37
  177.3 5.7 %shard_map.105 = (bf16[1024,768]{1,0:T(8,128)(2,1)S(1)}, bf16[1024,768]{1,0:T(8,128)(2,1)S(1)}) custom-call(s32[3]{0:T(128)S(1)} %pad_add_fusion.place, bf16[1024,2048]{1,0:T(8,128)(2,1)S(1)} %get-tuple-element.22.y, f32[1024,768]{1,0:T(8,128)S(1)} %get-tuple-element.23.active, f32[1024,768]{1,0:T(8,128)S(1)} %get-tuple-element.24.slope, ...), custom_call_target="tpu_custom_call" | custom-call | flops 3221225472 | bytes 16777216 | tf_op jit(solution)/shard_map/pallas_call | solution.py:32
  183.0 13.8 %shard_map.106 = (bf16[512,2048]{1,0:T(8,128)(2,1)}, bf16[512,2048]{1,0:T(8,128)(2,1)S(1)}) custom-call(s32[3]{0:T(128)S(1)} %pad_add_fusion.place, bf16[1024,768]{1,0:T(8,128)(2,1)S(1)} %get-tuple-element.25.gate_delta.delta, bf16[1024,768]{1,0:T(8,128)(2,1)S(1)} %get-tuple-element.26.up_delta.delta, bf16[512,768]{1,0:T(8,128)(2,1)S(1)} %bitcast.54, ...), custom_call_target="tpu_custom_call" | custom-call | flops 6442450944 | bytes 13631488 | tf_op jit(solution)/shard_map/pallas_call | solution.py:32
  197.2 1.5 collective-permute-start.39
  198.7 1.4 copy-done.9
  200.1 2.2 copy-done.36
  202.3 5.9 %shard_map.108 = (bf16[2,512,768]{2,1,0:T(8,128)(2,1)S(1)}, bf16[2,512,768]{2,1,0:T(8,128)(2,1)S(1)}) custom-call(s32[3]{0:T(128)S(1)} %pad_add_fusion.place, bf16[1024,2048]{1,0:T(8,128)(2,1)S(1)} %copy-done.36, bf16[1024,768]{1,0:T(8,128)(2,1)S(1)} %copy-done.9), custom_call_target="tpu_custom_call" | custom-call | flops 3221225472 | bytes 8912896 | tf_op jit(solution)/shard_map/pallas_call | solution.py:32
  208.2 1.2 fusion.11
  210.0 7.9 %collective-permute-done.39 = bf16[2,384,512]{2,1,0:T(8,128)(2,1)} collective-permute-done((bf16[2,384,512]{2,1,0:T(8,128)(2,1)}, bf16[2,384,512]{2,1,0:T(8,128)(2,1)}, u32[]{:S(2)}, u32[]{:S(2)}) %collective-permute-start.39) | collective-permute-done | bytes 786464 | tf_op jit(solution)/shard_map/ppermute | solution.py:253
  217.9 1.1 fusion.13
  219.8 5.9 %shard_map.107 = (bf16[2,512,768]{2,1,0:T(8,128)(2,1)S(1)}, bf16[2,512,768]{2,1,0:T(8,128)(2,1)S(1)}) custom-call(s32[3]{0:T(128)S(1)} %pad_add_fusion.place, bf16[1024,2048]{1,0:T(8,128)(2,1)S(1)} %copy-done.36, bf16[1024,768]{1,0:T(8,128)(2,1)S(1)} %copy-done.7), custom_call_target="tpu_custom_call" | custom-call | flops 3221225472 | bytes 8912896 | tf_op jit(solution)/shard_map/pallas_call | solution.py:32
  225.7 1.4 collective-permute-start.35
  227.1 1.5 collective-permute-start.33
  228.6 1.1 fusion.9
  229.9 1.1 fusion.8
  231.0 2.4 add_convert_fusion
  233.5 2.1 collective-permute-start.31
  235.6 24.9 %collective-permute-done.35 = bf16[2,512,768]{2,1,0:T(8,128)(2,1)S(1)} collective-permute-done((bf16[2,512,768]{2,1,0:T(8,128)(2,1)S(1)}, bf16[2,512,768]{2,1,0:T(8,128)(2,1)S(1)}, u32[]{:S(2)}, u32[]{:S(2)}) %collective-permute-start.35) | collective-permute-done | bytes 1572896 | tf_op jit(solution)/shard_map/ppermute | solution.py:253
  260.7 1.4 collective-permute-start.36
  263.0 1.1 collective-permute-done.33
  264.3 1.7 collective-permute-start.34
  266.1 1.9 collective-permute-start.29
  267.9 1.3 collective-permute-start.30
  269.4 3.2 %collective-permute-start.32 = (bf16[128,2048]{1,0:T(8,128)(2,1)S(1)}, bf16[128,2048]{1,0:T(8,128)(2,1)S(1)}, u32[]{:S(2)}, u32[]{:S(2)}) collective-permute-start(bf16[128,2048]{1,0:T(8,128)(2,1)S(1)} %add_convert_fusion.6), channel_id=1, source_target_pairs={{0,4},{1,5},{2,6},{3,7},{4,0},{5,1},{6,2},{7,3},{8,12},{9,13},{10,... | collective-permute-start | bytes 1572872 | tf_op jit(solution)/shard_map/ppermute | solution.py:256
  272.5 6.9 %collective-permute-done.36 = bf16[512,768]{1,0:T(8,128)(2,1)S(1)} collective-permute-done((bf16[512,768]{1,0:T(8,128)(2,1)S(1)}, bf16[512,768]{1,0:T(8,128)(2,1)S(1)}, u32[]{:S(2)}, u32[]{:S(2)}) %collective-permute-start.36) | collective-permute-done | bytes 786464 | tf_op jit(solution)/shard_map/ppermute | solution.py:250
  279.4 1.2 fusion.7
  280.6 1.2 fusion.6
  281.8 20.9 %collective-permute-done.32 = bf16[128,2048]{1,0:T(8,128)(2,1)S(1)} collective-permute-done((bf16[128,2048]{1,0:T(8,128)(2,1)S(1)}, bf16[128,2048]{1,0:T(8,128)(2,1)S(1)}, u32[]{:S(2)}, u32[]{:S(2)}) %collective-permute-start.32) | collective-permute-done | bytes 524320 | tf_op jit(solution)/shard_map/ppermute | solution.py:256
  302.7 1.1 add_convert_fusion.5
  (115 shorter events, 20.1 us)
Async XLA Ops:
  0.6 29.3 %collective-permute-start.9 = (bf16[128,2048]{1,0:T(8,128)(2,1)}, bf16[128,2048]{1,0:T(8,128)(2,1)S(1)}, u32[]{:S(2)}, u32[]{:S(2)}) collective-permute-start(bf16[128,2048]{1,0:T(8,128)(2,1)} %refs_0_.1), channel_id=1, source_target_pairs={{0,4},{1,5},{2,6},{3,7},{4,0},{5,1},{6,2},{7,3},{8,12},{9,13},{10,... | collective-permute-start | bytes 1572872 | tf_op jit(solution)/shard_map/ppermute | solution.py:256
  4.8 28.0 %collective-permute-start.10 = (bf16[128,2048]{1,0:T(8,128)(2,1)}, bf16[128,2048]{1,0:T(8,128)(2,1)S(1)}, u32[]{:S(2)}, u32[]{:S(2)}) collective-permute-start(bf16[128,2048]{1,0:T(8,128)(2,1)} %refs_0_.1), channel_id=1, source_target_pairs={{0,2},{1,3},{2,4},{3,5},{4,6},{5,7},{8,10},{9,11},{10,12},{11,13},... | collective-permute-start | bytes 1572872 | tf_op jit(solution)/shard_map/ppermute | solution.py:256
  8.3 25.7 %collective-permute-start.11 = (bf16[128,2048]{1,0:T(8,128)(2,1)}, bf16[128,2048]{1,0:T(8,128)(2,1)S(1)}, u32[]{:S(2)}, u32[]{:S(2)}) collective-permute-start(bf16[128,2048]{1,0:T(8,128)(2,1)} %refs_0_.1), channel_id=1, source_target_pairs={{2,0},{3,1},{4,2},{5,3},{6,4},{7,5},{10,8},{11,9},{12,10},{13,11},... | collective-permute-start | bytes 1572872 | tf_op jit(solution)/shard_map/ppermute | solution.py:256
  9.6 24.5 %collective-permute-start.13 = (bf16[128,2048]{1,0:T(8,128)(2,1)}, bf16[128,2048]{1,0:T(8,128)(2,1)S(1)}, u32[]{:S(2)}, u32[]{:S(2)}) collective-permute-start(bf16[128,2048]{1,0:T(8,128)(2,1)} %refs_0_.1), channel_id=1, source_target_pairs={{0,1},{1,0},{2,3},{3,2},{4,5},{5,4},{6,7},{7,6},{8,9},{9,8},{10,11... | collective-permute-start | bytes 1572872 | tf_op jit(solution)/shard_map/ppermute | solution.py:259
  9.7 1.0 copy-start.3
  12.1 132.9 %copy-start.10 = (bf16[1,512,768]{2,1,0:T(8,128)(2,1)S(1)}, bf16[1,512,768]{2,1,0:T(8,128)(2,1)}, u32[]{:S(2)}) copy-start(bf16[1,512,768]{2,1,0:T(8,128)(2,1)} %param.11) | copy-start | bytes 2359300
  12.2 52.1 %collective-permute-start = (bf16[128,2176]{1,0:T(8,128)(2,1)S(1)}, bf16[128,2176]{1,0:T(8,128)(2,1)}, u32[]{:S(2)}, u32[]{:S(2)}) collective-permute-start(bf16[128,2176]{1,0:T(8,128)(2,1)S(1)} %shard_map.102.refs_0_), channel_id=1, source_target_pairs={{0,4},{1,5},{2,6},{3,7},{4,0},{5,1},{6,2},{7,3},{8,12},{9,13},{10,... | collective-permute-start | bytes 1671176 | tf_op jit(solution)/shard_map/ppermute | solution.py:256
  29.9 36.2 %collective-permute-start.1 = (bf16[128,2176]{1,0:T(8,128)(2,1)S(1)}, bf16[128,2176]{1,0:T(8,128)(2,1)}, u32[]{:S(2)}, u32[]{:S(2)}) collective-permute-start(bf16[128,2176]{1,0:T(8,128)(2,1)S(1)} %shard_map.102.refs_0_), channel_id=1, source_target_pairs={{0,2},{1,3},{2,4},{3,5},{4,6},{5,7},{8,10},{9,11},{10,12},{11,13},... | collective-permute-start | bytes 1671176 | tf_op jit(solution)/shard_map/ppermute | solution.py:256
  32.7 42.6 %collective-permute-start.2 = (bf16[128,2176]{1,0:T(8,128)(2,1)S(1)}, bf16[128,2176]{1,0:T(8,128)(2,1)}, u32[]{:S(2)}, u32[]{:S(2)}) collective-permute-start(bf16[128,2176]{1,0:T(8,128)(2,1)S(1)} %shard_map.102.refs_0_), channel_id=1, source_target_pairs={{2,0},{3,1},{4,2},{5,3},{6,4},{7,5},{10,8},{11,9},{12,10},{13,11},... | collective-permute-start | bytes 1671176 | tf_op jit(solution)/shard_map/ppermute | solution.py:256
  34.0 42.9 %collective-permute-start.4 = (bf16[128,2176]{1,0:T(8,128)(2,1)S(1)}, bf16[128,2176]{1,0:T(8,128)(2,1)S(1)}, u32[]{:S(2)}, u32[]{:S(2)}) collective-permute-start(bf16[128,2176]{1,0:T(8,128)(2,1)S(1)} %shard_map.102.refs_0_), channel_id=1, source_target_pairs={{0,1},{1,0},{2,3},{3,2},{4,5},{5,4},{6,7},{7,6},{8,9},{9,8},{10,11... | collective-permute-start | bytes 1671176 | tf_op jit(solution)/shard_map/ppermute | solution.py:259
  34.9 44.3 %collective-permute-start.18 = (bf16[512,768]{1,0:T(8,128)(2,1)}, bf16[512,768]{1,0:T(8,128)(2,1)}, u32[]{:S(2)}, u32[]{:S(2)}) collective-permute-start(bf16[512,768]{1,0:T(8,128)(2,1)} %bitcast.51), channel_id=1, source_target_pairs={{0,8},{8,0},{16,24},{24,16},{1,9},{9,1},{17,25},{25,17},{2,10},{10... | collective-permute-start | bytes 2359304 | tf_op jit(solution)/shard_map/ppermute | solution.py:250
  64.3 20.7 %collective-permute-start.22 = (bf16[512,768]{1,0:T(8,128)(2,1)}, bf16[512,768]{1,0:T(8,128)(2,1)}, u32[]{:S(2)}, u32[]{:S(2)}) collective-permute-start(bf16[512,768]{1,0:T(8,128)(2,1)} %bitcast.55), channel_id=1, source_target_pairs={{0,16},{8,24},{16,0},{24,8},{1,17},{9,25},{17,1},{25,9},{2,18},{10... | collective-permute-start | bytes 2359304 | tf_op jit(solution)/shard_map/ppermute | solution.py:253
  66.1 35.6 %collective-permute-start.19 = (bf16[512,768]{1,0:T(8,128)(2,1)}, bf16[512,768]{1,0:T(8,128)(2,1)S(1)}, u32[]{:S(2)}, u32[]{:S(2)}) collective-permute-start(bf16[512,768]{1,0:T(8,128)(2,1)} %bitcast.52), channel_id=1, source_target_pairs={{0,16},{8,24},{16,0},{24,8},{1,17},{9,25},{17,1},{25,9},{2,18},{10... | collective-permute-start | bytes 2359304 | tf_op jit(solution)/shard_map/ppermute | solution.py:253
  75.3 28.1 %collective-permute-start.21 = (bf16[512,768]{1,0:T(8,128)(2,1)}, bf16[512,768]{1,0:T(8,128)(2,1)S(1)}, u32[]{:S(2)}, u32[]{:S(2)}) collective-permute-start(bf16[512,768]{1,0:T(8,128)(2,1)} %bitcast.56), channel_id=1, source_target_pairs={{0,8},{8,0},{16,24},{24,16},{1,9},{9,1},{17,25},{25,17},{2,10},{10... | collective-permute-start | bytes 2359304 | tf_op jit(solution)/shard_map/ppermute | solution.py:250
  77.7 38.4 %collective-permute-start.25 = (bf16[768,512]{1,0:T(8,128)(2,1)}, bf16[768,512]{1,0:T(8,128)(2,1)S(1)}, u32[]{:S(2)}, u32[]{:S(2)}) collective-permute-start(bf16[768,512]{1,0:T(8,128)(2,1)} %bitcast.46), channel_id=1, source_target_pairs={{0,16},{8,24},{16,0},{24,8},{1,17},{9,25},{17,1},{25,9},{2,18},{10... | collective-permute-start | bytes 2359304 | tf_op jit(solution)/shard_map/ppermute | solution.py:253
  79.2 39.6 %collective-permute-start.24 = (bf16[768,512]{1,0:T(8,128)(2,1)}, bf16[768,512]{1,0:T(8,128)(2,1)S(1)}, u32[]{:S(2)}, u32[]{:S(2)}) collective-permute-start(bf16[768,512]{1,0:T(8,128)(2,1)} %bitcast.47), channel_id=1, source_target_pairs={{0,8},{8,0},{16,24},{24,16},{1,9},{9,1},{17,25},{25,17},{2,10},{10... | collective-permute-start | bytes 2359304 | tf_op jit(solution)/shard_map/ppermute | solution.py:250
  85.0 35.1 %collective-permute-start.12 = (bf16[128,2048]{1,0:T(8,128)(2,1)S(1)}, bf16[128,2048]{1,0:T(8,128)(2,1)}, u32[]{:S(2)}, u32[]{:S(2)}) collective-permute-start(bf16[128,2048]{1,0:T(8,128)(2,1)S(1)} %collective-permute-done.9.refs_1_), channel_id=1, source_target_pairs={{4,6},{5,7},{2,0},{3,1},{12,14},{13,15},{10,8},{11,9},{20,22},{21,... | collective-permute-start | bytes 1572872 | tf_op jit(solution)/shard_map/ppermute | solution.py:256
  102.6 19.0 %collective-permute-start.14 = (bf16[128,2048]{1,0:T(8,128)(2,1)S(1)}, bf16[128,2048]{1,0:T(8,128)(2,1)S(1)}, u32[]{:S(2)}, u32[]{:S(2)}) collective-permute-start(bf16[128,2048]{1,0:T(8,128)(2,1)S(1)} %collective-permute-done.9.refs_1_), channel_id=1, source_target_pairs={{0,1},{1,0},{2,3},{3,2},{4,5},{5,4},{6,7},{7,6},{8,9},{9,8},{10,11... | collective-permute-start | bytes 1572872 | tf_op jit(solution)/shard_map/ppermute | solution.py:259
  104.3 19.4 %collective-permute-start.15 = (bf16[128,2048]{1,0:T(8,128)(2,1)S(1)}, bf16[128,2048]{1,0:T(8,128)(2,1)S(1)}, u32[]{:S(2)}, u32[]{:S(2)}) collective-permute-start(bf16[128,2048]{1,0:T(8,128)(2,1)S(1)} %collective-permute-done.10.refs_2_), channel_id=1, source_target_pairs={{2,3},{3,2},{4,5},{5,4},{6,7},{7,6},{10,11},{11,10},{12,13},{13,12... | collective-permute-start | bytes 1572872 | tf_op jit(solution)/shard_map/ppermute | solution.py:259
  116.1 8.5 %collective-permute-start.16 = (bf16[128,2048]{1,0:T(8,128)(2,1)S(1)}, bf16[128,2048]{1,0:T(8,128)(2,1)S(1)}, u32[]{:S(2)}, u32[]{:S(2)}) collective-permute-start(bf16[128,2048]{1,0:T(8,128)(2,1)S(1)} %collective-permute-done.11.refs_3_), channel_id=1, source_target_pairs={{0,1},{1,0},{2,3},{3,2},{4,5},{5,4},{8,9},{9,8},{10,11},{11,10},{1... | collective-permute-start | bytes 1572872 | tf_op jit(solution)/shard_map/ppermute | solution.py:259
  118.9 23.5 %collective-permute-start.20 = (bf16[512,768]{1,0:T(8,128)(2,1)}, bf16[512,768]{1,0:T(8,128)(2,1)}, u32[]{:S(2)}, u32[]{:S(2)}) collective-permute-start(bf16[512,768]{1,0:T(8,128)(2,1)} %collective-permute-done.18.refs_11_.refs_1_), channel_id=1, source_target_pairs={{0,16},{8,24},{16,0},{24,8},{1,17},{9,25},{17,1},{25,9},{2,18},{10... | collective-permute-start | bytes 2359304 | tf_op jit(solution)/shard_map/ppermute | solution.py:253
  120.2 22.9 %collective-permute-start.23 = (bf16[512,768]{1,0:T(8,128)(2,1)}, bf16[512,768]{1,0:T(8,128)(2,1)}, u32[]{:S(2)}, u32[]{:S(2)}) collective-permute-start(bf16[512,768]{1,0:T(8,128)(2,1)} %collective-permute-done.22.refs_16_.refs_6_), channel_id=1, source_target_pairs={{0,8},{8,0},{16,24},{24,16},{1,9},{9,1},{17,25},{25,17},{2,10},{10... | collective-permute-start | bytes 2359304 | tf_op jit(solution)/shard_map/ppermute | solution.py:250
  122.5 16.7 %collective-permute-start.3 = (bf16[128,2176]{1,0:T(8,128)(2,1)}, bf16[128,2176]{1,0:T(8,128)(2,1)}, u32[]{:S(2)}, u32[]{:S(2)}) collective-permute-start(bf16[128,2176]{1,0:T(8,128)(2,1)} %collective-permute-done.refs_1_), channel_id=1, source_target_pairs={{4,6},{5,7},{2,0},{3,1},{12,14},{13,15},{10,8},{11,9},{20,22},{21,... | collective-permute-start | bytes 1671176 | tf_op jit(solution)/shard_map/ppermute | solution.py:256
  124.5 15.3 %collective-permute-start.5 = (bf16[128,2176]{1,0:T(8,128)(2,1)}, bf16[128,2176]{1,0:T(8,128)(2,1)}, u32[]{:S(2)}, u32[]{:S(2)}) collective-permute-start(bf16[128,2176]{1,0:T(8,128)(2,1)} %collective-permute-done.refs_1_), channel_id=1, source_target_pairs={{0,1},{1,0},{2,3},{3,2},{4,5},{5,4},{6,7},{7,6},{8,9},{9,8},{10,11... | collective-permute-start | bytes 1671176 | tf_op jit(solution)/shard_map/ppermute | solution.py:259
  125.4 16.4 %collective-permute-start.17 = (bf16[128,2048]{1,0:T(8,128)(2,1)}, bf16[128,2048]{1,0:T(8,128)(2,1)}, u32[]{:S(2)}, u32[]{:S(2)}) collective-permute-start(bf16[128,2048]{1,0:T(8,128)(2,1)} %collective-permute-done.12.refs_4_), channel_id=1, source_target_pairs={{0,1},{1,0},{6,7},{7,6},{8,9},{9,8},{14,15},{15,14},{16,17},{17,16... | collective-permute-start | bytes 1572872 | tf_op jit(solution)/shard_map/ppermute | solution.py:259
  127.8 17.2 %copy-start.12 = (bf16[1,512,768]{2,1,0:T(8,128)(2,1)S(1)}, bf16[1,512,768]{2,1,0:T(8,128)(2,1)}, u32[]{:S(2)}) copy-start(bf16[1,512,768]{2,1,0:T(8,128)(2,1)} %param.12) | copy-start | bytes 2359300
  127.8 17.2 %copy-start.14 = (bf16[512,768]{1,0:T(8,128)(2,1)S(1)}, bf16[512,768]{1,0:T(8,128)(2,1)}, u32[]{:S(2)}) copy-start(bf16[512,768]{1,0:T(8,128)(2,1)} %copy-done.13) | copy-start | bytes 2359300
  139.1 28.4 %collective-permute-start.6 = (bf16[128,2176]{1,0:T(8,128)(2,1)}, bf16[128,2176]{1,0:T(8,128)(2,1)S(1)}, u32[]{:S(2)}, u32[]{:S(2)}) collective-permute-start(bf16[128,2176]{1,0:T(8,128)(2,1)} %collective-permute-done.1.refs_2_), channel_id=1, source_target_pairs={{2,3},{3,2},{4,5},{5,4},{6,7},{7,6},{10,11},{11,10},{12,13},{13,12... | collective-permute-start | bytes 1671176 | tf_op jit(solution)/shard_map/ppermute | solution.py:259
  139.8 27.7 %collective-permute-start.7 = (bf16[128,2176]{1,0:T(8,128)(2,1)}, bf16[128,2176]{1,0:T(8,128)(2,1)S(1)}, u32[]{:S(2)}, u32[]{:S(2)}) collective-permute-start(bf16[128,2176]{1,0:T(8,128)(2,1)} %collective-permute-done.2.refs_3_), channel_id=1, source_target_pairs={{0,1},{1,0},{2,3},{3,2},{4,5},{5,4},{8,9},{9,8},{10,11},{11,10},{1... | collective-permute-start | bytes 1671176 | tf_op jit(solution)/shard_map/ppermute | solution.py:259
  141.8 35.5 %collective-permute-start.26 = (bf16[384,512]{1,0:T(8,128)(2,1)S(1)}, bf16[384,512]{1,0:T(8,128)(2,1)S(1)}, u32[]{:S(2)}, u32[]{:S(2)}) collective-permute-start(bf16[384,512]{1,0:T(8,128)(2,1)S(1)} %slice.94), channel_id=1, source_target_pairs={{0,8},{8,0},{16,24},{24,16},{1,9},{9,1},{17,25},{25,17},{2,10},{10... | collective-permute-start | bytes 1179656 | tf_op jit(solution)/shard_map/ppermute | solution.py:250
  142.4 34.9 %collective-permute-start.27 = (bf16[384,512]{1,0:T(8,128)(2,1)S(1)}, bf16[384,512]{1,0:T(8,128)(2,1)S(1)}, u32[]{:S(2)}, u32[]{:S(2)}) collective-permute-start(bf16[384,512]{1,0:T(8,128)(2,1)S(1)} %slice.95), channel_id=1, source_target_pairs={{0,16},{8,24},{16,0},{24,8},{1,17},{9,25},{17,1},{25,9},{2,18},{10... | collective-permute-start | bytes 1179656 | tf_op jit(solution)/shard_map/ppermute | solution.py:253
  143.1 24.4 %collective-permute-start.8 = (bf16[128,2176]{1,0:T(8,128)(2,1)}, bf16[128,2176]{1,0:T(8,128)(2,1)S(1)}, u32[]{:S(2)}, u32[]{:S(2)}) collective-permute-start(bf16[128,2176]{1,0:T(8,128)(2,1)} %collective-permute-done.3.refs_4_), channel_id=1, source_target_pairs={{0,1},{1,0},{6,7},{7,6},{8,9},{9,8},{14,15},{15,14},{16,17},{17,16... | collective-permute-start | bytes 1671176 | tf_op jit(solution)/shard_map/ppermute | solution.py:259
  145.0 1.1 copy-start.16
  146.2 1.0 copy-start.20
  147.2 1.0 copy-start.22
  148.3 1.0 copy-start.24
  149.3 1.0 copy-start.26
  150.3 1.0 copy-start.28
  151.4 1.0 copy-start.30
  154.5 13.0 %copy-start.19 = (bf16[128,2176]{1,0:T(8,128)(2,1)S(1)}, bf16[128,2176]{1,0:T(8,128)(2,1)}, u32[]{:S(2)}) copy-start(bf16[128,2176]{1,0:T(8,128)(2,1)} %copy-done.18) | copy-start | bytes 1671172
  165.4 2.0 copy-start.35
  167.5 9.8 %copy-start.2 = (bf16[1,768,512]{2,1,0:T(8,128)(2,1)S(1)}, bf16[1,768,512]{2,1,0:T(8,128)(2,1)}, u32[]{:S(2)}) copy-start(bf16[1,768,512]{2,1,0:T(8,128)(2,1)} %param.13) | copy-start | bytes 2359300
  175.9 7.1 %copy-start = (bf16[2,384,512]{2,1,0:T(8,128)(2,1)}, bf16[2,384,512]{2,1,0:T(8,128)(2,1)S(1)}, u32[]{:S(2)}) copy-start(bf16[2,384,512]{2,1,0:T(8,128)(2,1)S(1)} %get-tuple-element.34) | copy-start | bytes 2359300
  175.9 32.3 %collective-permute-start.37 = (bf16[2,384,512]{2,1,0:T(8,128)(2,1)}, bf16[2,384,512]{2,1,0:T(8,128)(2,1)}, u32[]{:S(2)}, u32[]{:S(2)}) collective-permute-start(bf16[2,384,512]{2,1,0:T(8,128)(2,1)} %get-tuple-element.35), channel_id=1, source_target_pairs={{0,8},{8,0},{16,24},{24,16},{1,9},{9,1},{17,25},{25,17},{2,10},{10... | collective-permute-start | bytes 2359304 | tf_op jit(solution)/shard_map/ppermute | solution.py:250
  177.3 5.7 %copy-start.11 = (bf16[1,512,768]{2,1,0:T(8,128)(2,1)S(1)}, bf16[1,512,768]{2,1,0:T(8,128)(2,1)}, u32[]{:S(2)}) copy-start(bf16[1,512,768]{2,1,0:T(8,128)(2,1)} %param.11) | copy-start | bytes 2359300
  177.3 5.7 %copy-start.17 = (bf16[512,768]{1,0:T(8,128)(2,1)S(1)}, bf16[512,768]{1,0:T(8,128)(2,1)}, u32[]{:S(2)}) copy-start(bf16[512,768]{1,0:T(8,128)(2,1)} %copy-done.15) | copy-start | bytes 2359300
  183.0 13.9 %copy-start.6 = (bf16[1024,768]{1,0:T(8,128)(2,1)}, bf16[1024,768]{1,0:T(8,128)(2,1)S(1)}, u32[]{:S(2)}) copy-start(bf16[1024,768]{1,0:T(8,128)(2,1)S(1)} %get-tuple-element.25.gate_delta.delta) | copy-start | bytes 4718596
  183.0 13.9 %copy-start.8 = (bf16[1024,768]{1,0:T(8,128)(2,1)}, bf16[1024,768]{1,0:T(8,128)(2,1)S(1)}, u32[]{:S(2)}) copy-start(bf16[1024,768]{1,0:T(8,128)(2,1)S(1)} %get-tuple-element.26.up_delta.delta) | copy-start | bytes 4718596
  196.9 34.1 %collective-permute-start.28 = (bf16[512,2048]{1,0:T(8,128)(2,1)}, bf16[512,2048]{1,0:T(8,128)(2,1)}, u32[]{:S(2)}, u32[]{:S(2)}) collective-permute-start(bf16[512,2048]{1,0:T(8,128)(2,1)} %get-tuple-element.28), channel_id=1, source_target_pairs={{0,1},{1,0},{2,3},{3,2},{4,5},{5,4},{6,7},{7,6},{8,9},{9,8},{10,11... | collective-permute-start | bytes 6291464 | tf_op jit(solution)/shard_map/ppermute | solution.py:259
  197.2 20.7 %collective-permute-start.39 = (bf16[2,384,512]{2,1,0:T(8,128)(2,1)}, bf16[2,384,512]{2,1,0:T(8,128)(2,1)}, u32[]{:S(2)}, u32[]{:S(2)}) collective-permute-start(bf16[2,384,512]{2,1,0:T(8,128)(2,1)} %get-tuple-element.37), channel_id=1, source_target_pairs={{0,16},{8,24},{16,0},{24,8},{1,17},{9,25},{17,1},{25,9},{2,18},{10... | collective-permute-start | bytes 2359304 | tf_op jit(solution)/shard_map/ppermute | solution.py:253
  198.7 1.4 copy-start.9
  200.1 2.2 copy-start.36
  202.3 5.9 %copy-start.1 = (bf16[2,384,512]{2,1,0:T(8,128)(2,1)S(1)}, bf16[2,384,512]{2,1,0:T(8,128)(2,1)}, u32[]{:S(2)}) copy-start(bf16[2,384,512]{2,1,0:T(8,128)(2,1)} %copy-done) | copy-start | bytes 2359300
  208.2 11.6 %copy-start.7 = (bf16[1024,768]{1,0:T(8,128)(2,1)S(1)}, bf16[1024,768]{1,0:T(8,128)(2,1)}, u32[]{:S(2)}) copy-start(bf16[1024,768]{1,0:T(8,128)(2,1)} %copy-done.6) | copy-start | bytes 4718596
  209.4 19.1 %collective-permute-start.38 = (bf16[384,512]{1,0:T(8,128)(2,1)S(1)}, bf16[384,512]{1,0:T(8,128)(2,1)S(1)}, u32[]{:S(2)}, u32[]{:S(2)}) collective-permute-start(bf16[384,512]{1,0:T(8,128)(2,1)S(1)} %fusion.11), channel_id=1, source_target_pairs={{0,16},{8,24},{16,0},{24,8},{1,17},{9,25},{17,1},{25,9},{2,18},{10... | collective-permute-start | bytes 1179656 | tf_op jit(solution)/shard_map/ppermute | solution.py:253
  219.0 10.9 %collective-permute-start.40 = (bf16[384,512]{1,0:T(8,128)(2,1)S(1)}, bf16[384,512]{1,0:T(8,128)(2,1)S(1)}, u32[]{:S(2)}, u32[]{:S(2)}) collective-permute-start(bf16[384,512]{1,0:T(8,128)(2,1)S(1)} %fusion.13), channel_id=1, source_target_pairs={{0,8},{8,0},{16,24},{24,16},{1,9},{9,1},{17,25},{25,17},{2,10},{10... | collective-permute-start | bytes 1179656 | tf_op jit(solution)/shard_map/ppermute | solution.py:250
  225.7 34.8 %collective-permute-start.35 = (bf16[2,512,768]{2,1,0:T(8,128)(2,1)S(1)}, bf16[2,512,768]{2,1,0:T(8,128)(2,1)S(1)}, u32[]{:S(2)}, u32[]{:S(2)}) collective-permute-start(bf16[2,512,768]{2,1,0:T(8,128)(2,1)S(1)} %get-tuple-element.33), channel_id=1, source_target_pairs={{0,16},{8,24},{16,0},{24,8},{1,17},{9,25},{17,1},{25,9},{2,18},{10... | collective-permute-start | bytes 4718600 | tf_op jit(solution)/shard_map/ppermute | solution.py:253
  227.1 37.0 %collective-permute-start.33 = (bf16[2,512,768]{2,1,0:T(8,128)(2,1)S(1)}, bf16[2,512,768]{2,1,0:T(8,128)(2,1)S(1)}, u32[]{:S(2)}, u32[]{:S(2)}) collective-permute-start(bf16[2,512,768]{2,1,0:T(8,128)(2,1)S(1)} %get-tuple-element.31), channel_id=1, source_target_pairs={{0,8},{8,0},{16,24},{24,16},{1,9},{9,1},{17,25},{25,17},{2,10},{10... | collective-permute-start | bytes 4718600 | tf_op jit(solution)/shard_map/ppermute | solution.py:250
  233.5 35.7 %collective-permute-start.31 = (bf16[128,2048]{1,0:T(8,128)(2,1)S(1)}, bf16[128,2048]{1,0:T(8,128)(2,1)S(1)}, u32[]{:S(2)}, u32[]{:S(2)}) collective-permute-start(bf16[128,2048]{1,0:T(8,128)(2,1)S(1)} %get-tuple-element.39), channel_id=1, source_target_pairs={{6,4},{7,5},{0,2},{1,3},{14,12},{15,13},{8,10},{9,11},{22,20},{23,... | collective-permute-start | bytes 1572872 | tf_op jit(solution)/shard_map/ppermute | solution.py:256
  260.7 18.7 %collective-permute-start.36 = (bf16[512,768]{1,0:T(8,128)(2,1)S(1)}, bf16[512,768]{1,0:T(8,128)(2,1)S(1)}, u32[]{:S(2)}, u32[]{:S(2)}) collective-permute-start(bf16[512,768]{1,0:T(8,128)(2,1)S(1)} %fusion.5), channel_id=1, source_target_pairs={{0,8},{8,0},{16,24},{24,16},{1,9},{9,1},{17,25},{25,17},{2,10},{10... | collective-permute-start | bytes 2359304 | tf_op jit(solution)/shard_map/ppermute | solution.py:250
  264.3 16.3 %collective-permute-start.34 = (bf16[512,768]{1,0:T(8,128)(2,1)S(1)}, bf16[512,768]{1,0:T(8,128)(2,1)S(1)}, u32[]{:S(2)}, u32[]{:S(2)}) collective-permute-start(bf16[512,768]{1,0:T(8,128)(2,1)S(1)} %fusion.3), channel_id=1, source_target_pairs={{0,16},{8,24},{16,0},{24,8},{1,17},{9,25},{17,1},{25,9},{2,18},{10... | collective-permute-start | bytes 2359304 | tf_op jit(solution)/shard_map/ppermute | solution.py:253
  266.1 15.8 %collective-permute-start.29 = (bf16[128,2048]{1,0:T(8,128)(2,1)S(1)}, bf16[128,2048]{1,0:T(8,128)(2,1)S(1)}, u32[]{:S(2)}, u32[]{:S(2)}) collective-permute-start(bf16[128,2048]{1,0:T(8,128)(2,1)S(1)} %get-tuple-element.38), channel_id=1, source_target_pairs={{0,2},{1,3},{2,4},{3,5},{4,6},{5,7},{8,10},{9,11},{10,12},{11,13},... | collective-permute-start | bytes 1572872 | tf_op jit(solution)/shard_map/ppermute | solution.py:256
  267.9 13.9 %collective-permute-start.30 = (bf16[128,2048]{1,0:T(8,128)(2,1)S(1)}, bf16[128,2048]{1,0:T(8,128)(2,1)S(1)}, u32[]{:S(2)}, u32[]{:S(2)}) collective-permute-start(bf16[128,2048]{1,0:T(8,128)(2,1)S(1)} %get-tuple-element.40), channel_id=1, source_target_pairs={{2,0},{3,1},{4,2},{5,3},{6,4},{7,5},{10,8},{11,9},{12,10},{13,11},... | collective-permute-start | bytes 1572872 | tf_op jit(solution)/shard_map/ppermute | solution.py:256
  269.4 33.3 %collective-permute-start.32 = (bf16[128,2048]{1,0:T(8,128)(2,1)S(1)}, bf16[128,2048]{1,0:T(8,128)(2,1)S(1)}, u32[]{:S(2)}, u32[]{:S(2)}) collective-permute-start(bf16[128,2048]{1,0:T(8,128)(2,1)S(1)} %add_convert_fusion.6), channel_id=1, source_target_pairs={{0,4},{1,5},{2,6},{3,7},{4,0},{5,1},{6,2},{7,3},{8,12},{9,13},{10,... | collective-permute-start | bytes 1572872 | tf_op jit(solution)/shard_map/ppermute | solution.py:256
  (14 other events, 11.7 us)
where the time goes:
time: 305 us; the launch traced here: 304 us
  waiting for transfers between devices  156 us (51%)
  starting transfers between devices  57.5 us (19%)
  Pallas kernels  50.7 us (17%)
  local copies, waits for them, and re-layouts  25.8 us (8%)
  other arithmetic  12.1 us (4%)
    ppermute x12, waiting for transfers between devices, hop(): lax.ppermute(block, 'expert', [(2 * a + c, 2 * b + c) for a, b in moves f...  84.5 us
    ppermute x9, waiting for transfers between devices, to_y(): return lax.ppermute(block, 'dp', [(i, i ^ 2) for i in range(4)])  63.8 us
    pallas_call x7, Pallas kernels, call(): pl.pallas_call(body, out_shape=[jax.ShapeDtypeStruct(s, d) for s, d, _ in...  50.7 us
    ppermute x12, starting transfers between devices, hop(): lax.ppermute(block, 'expert', [(2 * a + c, 2 * b + c) for a, b in moves f...  26.1 us
    unnamed x74, local copies, waits for them, and re-layouts  25.8 us
    ppermute x9, starting transfers between devices, to_y(): return lax.ppermute(block, 'dp', [(i, i ^ 2) for i in range(4)])  10.8 us
    ppermute x9, starting transfers between devices, to_x(): return lax.ppermute(block, 'dp', [(i, i ^ 1) for i in range(4)])  10.7 us
    ppermute x11, starting transfers between devices, swap(): lax.ppermute(block, 'expert', [(2 * z + c, 2 * z + 1 - c) for z in at for...  9.93 us
  transfers between devices with their start and end apart: 41, of which 13 were waited for; matrix products, arithmetic and copies ran while one was open for 4% of the time, Pallas kernels for 17%

commit v1 on v0

--- a/solution.py
+++ b/solution.py
@@ -17,7 +17,6 @@
 LANES = 128
 NN = (((1,), (0,)), ((), ()))
 NT = (((1,), (1,)), ((), ()))
-TN = (((0,), (0,)), ((), ()))
 
 
 def mm(a, b, dims):
@@ -128,10 +127,10 @@
     out.wait()
 
 
-def down_body(experts, place, *refs):
+def down_send_body(experts, place, *refs):
     pieces, act = refs[:10], refs[10]
-    send_a, keep_a, send_b, keep_b, y_out, raw, y, sems = refs[11:]
-    me, chip, expert = place[0], place[1], place[2]
+    send_a, send_b, y, raw, sems = refs[11:]
+    chip, expert = place[1], place[2]
     copies = Copies(sems)
     for c in load_rows(copies, chip, pieces, raw):
         c.wait()
@@ -147,14 +146,26 @@
         return 0
 
     lax.fori_loop(0, 8, scale, 0)
-    out = copies.start(y, y_out)
-    share = width // 4
+    down_blocks(place, act, y, ((0, 1, send_a, 0), (0, 3, send_a, 1), (1, 2, send_b, 0), (1, 3, send_b, 1)))
+
+
+def down_blocks(place, act, y, wanted):
+    share = y.shape[1] // 4
     half = act.shape[1] // 2
-    for dst, h, pair in ((send_a, 0, (1, 3)), (send_b, 1, (2, 3)), (keep_a, 0, (0, 2)), (keep_b, 1, (0, 1))):
-        for slot, k in enumerate(pair):
-            cols = pl.ds(pl.multiple_of((me ^ k) * share, share), share)
-            dst[slot] = mm(act[:, h * half : (h + 1) * half], y[:, cols], TN).astype(BF16)
-    out.wait()
+    for h in (0, 1):
+        turned = jnp.transpose(act[:, h * half : (h + 1) * half])
+        for which, k, dst, slot in wanted:
+            if which == h:
+                cols = pl.ds(pl.multiple_of((place[0] ^ k) * share, share), share)
+                value = mm(turned, y[:, cols], NN).astype(BF16)
+                if slot is None:
+                    dst[...] = value
+                else:
+                    dst[slot] = value
+
+
+def down_keep_body(place, act, y, a0, a1, b0, b1):
+    down_blocks(place, act, y, ((0, 0, a0, None), (0, 2, a1, None), (1, 0, b0, None), (1, 1, b1, None)))
 
 
 def back_body(place, y, active, slope, own, from_x, from_y, diag_a, diag_b, gate_delta, up_delta, w, sems):
@@ -185,19 +196,34 @@
     lax.fori_loop(0, 2 * (hidden // tn), step, 0)
 
 
-def grad_body(send_pair, keep_pair, place, x, delta, send, keep):
-    me = place[0]
+def grad_blocks(place, x, wanted):
     share = x.shape[1] // 4
     tm = share // 2
-    for dst, pair in ((send, send_pair), (keep, keep_pair)):
-        for slot, k in enumerate(pair):
-
-            def step(i, _, dst=dst, slot=slot, k=k):
-                cols = pl.ds(pl.multiple_of((me ^ k) * share + i * tm, tm), tm)
-                dst[slot, pl.ds(pl.multiple_of(i * tm, tm), tm), :] = mm(x[:, cols], delta[...], TN).astype(BF16)
-                return 0
-
-            lax.fori_loop(0, 2, step, 0)
+    for k, targets in wanted:
+
+        def step(i, _, k=k, targets=targets):
+            cols = pl.ds(pl.multiple_of((place[0] ^ k) * share + i * tm, tm), tm)
+            turned = jnp.transpose(x[:, cols])
+            part = pl.ds(pl.multiple_of(i * tm, tm), tm)
+            for delta, dst, slot in targets:
+                value = mm(turned, delta[...], NN).astype(BF16)
+                if slot is None:
+                    dst[part, :] = value
+                else:
+                    dst[slot, part, :] = value
+            return 0
+
+        lax.fori_loop(0, 2, step, 0)
+
+
+def grad_send_body(place, x, gd, ud, gate_send, up_send):
+    grad_blocks(
+        place, x, ((1, [(gd, gate_send, 0)]), (3, [(gd, gate_send, 1), (ud, up_send, 1)]), (2, [(ud, up_send, 0)]))
+    )
+
+
+def grad_keep_body(place, x, gd, ud, g0, g1, u0, u1):
+    grad_blocks(place, x, ((2, [(gd, g1, None)]), (1, [(ud, u1, None)]), (0, [(gd, g0, None), (ud, u0, None)])))
 
 
 def pair_body(place, gate_delta, up_delta, *refs):
@@ -214,17 +240,16 @@
     for k in range(4):
         for c in started[k]:
             c.wait()
-    for dst, first in ((send, rows), (keep, 0)):
-
-        def step(i, _, dst=dst, first=first):
-            k, part = i // 2, pl.ds(pl.multiple_of(i % 2 * tn, tn), tn)
-            total = mm(gate_delta[first : first + rows, :], wg[k, part, :], NT)
-            total += mm(up_delta[first : first + rows, :], wu[k, part, :], NT)
-            cols = pl.ds(pl.multiple_of((me ^ k) * share + i % 2 * tn, tn), tn)
-            dst[:, cols] = total.astype(BF16)
+
+        def step(i, _, k=k):
+            part = pl.ds(pl.multiple_of(i * tn, tn), tn)
+            total = mm(gate_delta[...], wg[k, part, :], NT) + mm(up_delta[...], wu[k, part, :], NT)
+            cols = pl.ds(pl.multiple_of((me ^ k) * share + i * tn, tn), tn)
+            keep[:, cols] = total[:rows].astype(BF16)
+            send[:, cols] = total[rows:].astype(BF16)
             return 0
 
-        lax.fori_loop(0, 8, step, 0)
+        lax.fori_loop(0, 2, step, 0)
 
 
 def add(*terms):
@@ -304,13 +329,13 @@
         2 * (2 * rows * width + 2 * width * hidden) + 10 * rows * hidden,
     )
     piece = (2, half, share)
-    send_a, keep_a, send_b, keep_b, y = call(
-        functools.partial(down_body, experts),
-        [(piece, BF16, VMEM)] * 4 + [((rows, width), BF16, ANY)],
+    send_a, send_b, y = call(
+        functools.partial(down_send_body, experts),
+        [(piece, BF16, VMEM)] * 2 + [((rows, width), BF16, VMEM)],
         [(place, SMEM)] + [(a, ANY) for a in y_pieces] + [(act, VMEM)],
-        [pltpu.VMEM((rows, width + LANES), BF16), pltpu.VMEM((rows, width), BF16), dma(9)],
-        2 * rows * width * hidden,
-        2 * (2 * rows * width + rows * hidden + width * hidden),
+        [pltpu.VMEM((rows, width + LANES), BF16), dma(8)],
+        rows * width * hidden,
+        2 * (2 * rows * width + rows * hidden + width * hidden // 2),
     )
     got_a, got_b = to_x(send_a), to_y(send_b)
     gate_delta, up_delta = call(
@@ -321,22 +346,15 @@
         2 * rows * width * hidden,
         2 * (rows * width + width * hidden) + 12 * rows * hidden,
     )
-    piece = (2, share, hidden)
-
-    def grad(delta, send_pair, keep_pair):
-        return call(
-            functools.partial(grad_body, send_pair, keep_pair),
-            [(piece, BF16, VMEM)] * 2,
-            [(place, SMEM), (x, VMEM), (delta, VMEM)],
-            [],
-            2 * rows * width * hidden,
-            2 * (rows * width + rows * hidden + width * hidden),
-        )
-
-    gate_send, gate_keep = grad(gate_delta, (1, 3), (0, 2))
-    gate_got = to_x(gate_send)
-    up_send, up_keep = grad(up_delta, (2, 3), (0, 1))
-    up_got = to_y(up_send)
+    gate_send, up_send = call(
+        grad_send_body,
+        [((2, share, hidden), BF16, VMEM)] * 2,
+        [(place, SMEM), (x, VMEM), (gate_delta, VMEM), (up_delta, VMEM)],
+        [],
+        2 * rows * width * hidden,
+        2 * (rows * width + 2 * rows * hidden + width * hidden),
+    )
+    gate_got, up_got = to_x(gate_send), to_y(up_send)
     weight = pltpu.VMEM((4, share, hidden), BF16)
     pair_send, pair_keep = call(
         pair_body,
@@ -346,13 +364,30 @@
         4 * rows * width * hidden,
         2 * (rows * width + 2 * rows * hidden + 2 * width * hidden),
     )
-    down_a = add(keep_a[0], got_a[0]), to_y(add(keep_a[1], got_a[1]))
-    down_b = add(keep_b[0], got_b[0]), to_x(add(keep_b[1], got_b[1]))
-    down_grad = jnp.concatenate([add(*down_a), add(*down_b)], axis=0)
-    gate_grad = add(add(gate_keep[0], gate_got[0]), to_y(add(gate_keep[1], gate_got[1])))
-    up_grad = add(add(up_keep[0], up_got[0]), to_x(add(up_keep[1], up_got[1])))
-
     total = add(pair_keep, swap(pair_send)).reshape(chips, tok, width)
+    keep_a0, keep_a1, keep_b0, keep_b1 = call(
+        down_keep_body,
+        [((half, share), BF16, VMEM)] * 4,
+        [(place, SMEM), (act, VMEM), (y, VMEM)],
+        [],
+        rows * width * hidden,
+        2 * (rows * width + rows * hidden + width * hidden // 2),
+    )
+    gate0, gate1, up0, up1 = call(
+        grad_keep_body,
+        [((share, hidden), BF16, VMEM)] * 4,
+        [(place, SMEM), (x, VMEM), (gate_delta, VMEM), (up_delta, VMEM)],
+        [],
+        2 * rows * width * hidden,
+        2 * (rows * width + 2 * rows * hidden + width * hidden),
+    )
+    down_a, down_b = to_y(add(keep_a1, got_a[1])), to_x(add(keep_b1, got_b[1]))
+    gate_last = to_y(add(gate1, gate_got[1]))
+    up_last = to_x(add(up1, up_got[1]))
+    gate_sum, up_sum = lax.optimization_barrier((add(gate0, gate_got[0]), add(up0, up_got[0])))
+    down_grad = jnp.concatenate([add(keep_a0, got_a[0], down_a), add(keep_b0, got_b[0], down_b)], axis=0)
+    gate_grad, up_grad = add(gate_sum, gate_last), add(up_sum, up_last)
+
     far = hop(jnp.where(chip == 0, total[1], total[3]), [(3, 2), (0, 1)])
     right = hop(total[3], [(0, 1), (1, 2), (2, 3)])
     left = hop(total[1], [(1, 0), (2, 1), (3, 2)])

time: 305 us -> 302 us (level)
  Pallas kernels: 50.7 us -> 45.8 us
  local copies, waits for them, and re-layouts: 25.8 us -> 30.2 us
    pallas_call x7 -> x8, Pallas kernels: 50.7 us -> 45.8 us  [call(): pl.pallas_call(body, out_shape=[jax.ShapeDtypeStruct(s, d) for s, d, _ in...]
    unnamed x74 -> x84, local copies, waits for them, and re-layouts: 25.8 us -> 30.1 us
    ppermute x9, waiting for transfers between devices: 63.8 us -> 60 us  [to_y(): return lax.ppermute(block, 'dp', [(i, i ^ 2) for i in range(4)])]
  transfers between devices with their start and end apart: 41 -> 41, of which waited for: 13 -> 16; matrix products, arithmetic and copies ran while one was open for 4% -> 3% of each run, Pallas kernels for 17% -> 15%
where the time goes in v1:
time: 302 us; the launch traced here: 301 us
  waiting for transfers between devices  156 us (52%)
  starting transfers between devices  57.2 us (19%)
  Pallas kernels  45.8 us (15%)
  local copies, waits for them, and re-layouts  30.2 us (10%)
  other arithmetic  10.2 us (3%)
    ppermute x12, waiting for transfers between devices, hop(): lax.ppermute(block, 'expert', [(2 * a + c, 2 * b + c) for a, b in moves f...  85.7 us
    ppermute x9, waiting for transfers between devices, to_y(): return lax.ppermute(block, 'dp', [(i, i ^ 2) for i in range(4)])  60 us
    pallas_call x8, Pallas kernels, call(): pl.pallas_call(body, out_shape=[jax.ShapeDtypeStruct(s, d) for s, d, _ in...  45.8 us
    unnamed x84, local copies, waits for them, and re-layouts  30.1 us
    ppermute x12, starting transfers between devices, hop(): lax.ppermute(block, 'expert', [(2 * a + c, 2 * b + c) for a, b in moves f...  25.2 us
    ppermute x9, starting transfers between devices, to_y(): return lax.ppermute(block, 'dp', [(i, i ^ 2) for i in range(4)])  11.2 us
    ppermute x9, starting transfers between devices, to_x(): return lax.ppermute(block, 'dp', [(i, i ^ 1) for i in range(4)])  11 us
    ppermute x9, waiting for transfers between devices, to_x(): return lax.ppermute(block, 'dp', [(i, i ^ 1) for i in range(4)])  10.2 us
  transfers between devices with their start and end apart: 41, of which 16 were waited for; matrix products, arithmetic and copies ran while one was open for 3% of the time, Pallas kernels for 15%

profile of v1, /device:TPU:0, one launch (start us, length us, event | category | flops | bytes accessed | tf_op | source)
XLA Modules:
  0.0 300.7 jit_solution(16813832861918641635)
XLA Ops:
  0.6 4.1 %collective-permute-start.9 = (bf16[128,2048]{1,0:T(8,128)(2,1)}, bf16[128,2048]{1,0:T(8,128)(2,1)S(1)}, u32[]{:S(2)}, u32[]{:S(2)}) collective-permute-start(bf16[128,2048]{1,0:T(8,128)(2,1)} %refs_0_.1), channel_id=1, source_target_pairs={{0,4},{1,5},{2,6},{3,7},{4,0},{5,1},{6,2},{7,3},{8,12},{9,13},{10,... | collective-permute-start | bytes 1572872 | tf_op jit(solution)/shard_map/ppermute | solution.py:281
  4.8 3.5 %collective-permute-start.10 = (bf16[128,2048]{1,0:T(8,128)(2,1)}, bf16[128,2048]{1,0:T(8,128)(2,1)S(1)}, u32[]{:S(2)}, u32[]{:S(2)}) collective-permute-start(bf16[128,2048]{1,0:T(8,128)(2,1)} %refs_0_.1), channel_id=1, source_target_pairs={{0,2},{1,3},{2,4},{3,5},{4,6},{5,7},{8,10},{9,11},{10,12},{11,13},... | collective-permute-start | bytes 1572872 | tf_op jit(solution)/shard_map/ppermute | solution.py:281
  8.3 1.3 collective-permute-start.11
  12.2 2.1 collective-permute-start
  14.3 15.6 %collective-permute-done.9.refs_1_ = bf16[128,2048]{1,0:T(8,128)(2,1)S(1)} collective-permute-done((bf16[128,2048]{1,0:T(8,128)(2,1)}, bf16[128,2048]{1,0:T(8,128)(2,1)S(1)}, u32[]{:S(2)}, u32[]{:S(2)}) %collective-permute-start.9) | collective-permute-done | bytes 524320 | tf_op jit(solution)/shard_map/ppermute | solution.py:281
  29.9 2.0 collective-permute-start.1
  31.9 1.3 collective-permute-start.2
  34.4 1.5 collective-permute-start.18
  35.9 28.3 %collective-permute-done.refs_1_ = bf16[128,2176]{1,0:T(8,128)(2,1)S(1)} collective-permute-done((bf16[128,2176]{1,0:T(8,128)(2,1)S(1)}, bf16[128,2176]{1,0:T(8,128)(2,1)S(1)}, u32[]{:S(2)}, u32[]{:S(2)}) %collective-permute-start) | collective-permute-done | bytes 557088 | tf_op jit(solution)/shard_map/ppermute | solution.py:281
  64.2 1.8 collective-permute-start.22
  66.2 9.0 %collective-permute-done.2.refs_3_ = bf16[128,2176]{1,0:T(8,128)(2,1)S(1)} collective-permute-done((bf16[128,2176]{1,0:T(8,128)(2,1)S(1)}, bf16[128,2176]{1,0:T(8,128)(2,1)S(1)}, u32[]{:S(2)}, u32[]{:S(2)}) %collective-permute-start.2) | collective-permute-done | bytes 557088 | tf_op jit(solution)/shard_map/ppermute | solution.py:281
  75.2 1.5 collective-permute-start.21
  77.6 1.5 collective-permute-start.25
  79.9 5.0 %collective-permute-done.22.refs_16_.refs_6_ = bf16[512,768]{1,0:T(8,128)(2,1)} collective-permute-done((bf16[512,768]{1,0:T(8,128)(2,1)}, bf16[512,768]{1,0:T(8,128)(2,1)}, u32[]{:S(2)}, u32[]{:S(2)}) %collective-permute-start.22) | collective-permute-done | bytes 786464 | tf_op jit(solution)/shard_map/ppermute | solution.py:278
  84.9 1.3 collective-permute-start.12
  86.2 15.5 %collective-permute-done.19.refs_12_.refs_2_ = bf16[512,768]{1,0:T(8,128)(2,1)S(1)} collective-permute-done((bf16[512,768]{1,0:T(8,128)(2,1)}, bf16[512,768]{1,0:T(8,128)(2,1)S(1)}, u32[]{:S(2)}, u32[]{:S(2)}) %collective-permute-start.19) | collective-permute-done | bytes 786464 | tf_op jit(solution)/shard_map/ppermute | solution.py:278
  105.7 10.2 %collective-permute-done.25.from_y = bf16[768,512]{1,0:T(8,128)(2,1)S(1)} collective-permute-done((bf16[768,512]{1,0:T(8,128)(2,1)}, bf16[768,512]{1,0:T(8,128)(2,1)S(1)}, u32[]{:S(2)}, u32[]{:S(2)}) %collective-permute-start.25) | collective-permute-done | bytes 786464 | tf_op jit(solution)/shard_map/ppermute | solution.py:278
  116.0 1.9 collective-permute-start.16
  118.7 1.3 collective-permute-start.20
  120.0 1.5 collective-permute-start.23
  122.3 1.3 collective-permute-start.3
  125.2 2.4 collective-permute-start.17
  127.8 10.9 %collective-permute-done.3.refs_4_ = bf16[128,2176]{1,0:T(8,128)(2,1)} collective-permute-done((bf16[128,2176]{1,0:T(8,128)(2,1)S(1)}, bf16[128,2176]{1,0:T(8,128)(2,1)}, u32[]{:S(2)}, u32[]{:S(2)}) %collective-permute-start.3) | collective-permute-done | bytes 557088 | tf_op jit(solution)/shard_map/ppermute | solution.py:281
  139.5 1.9 collective-permute-start.7
  142.7 1.9 collective-permute-start.8
  144.7 1.1 copy-done.17
  145.8 1.1 copy-done.20
  146.9 1.1 copy-done.23
  148.1 1.0 copy-done.25
  149.1 1.0 copy-done.27
  151.2 1.0 copy-done.31
  156.4 10.9 %shard_map.103 = (bf16[1024,768]{1,0:T(8,128)(2,1)S(1)}, f32[1024,768]{1,0:T(8,128)S(1)}, f32[1024,768]{1,0:T(8,128)S(1)}, bf16[1024,2048]{1,0:T(8,128)(2,1)S(1)}) custom-call(s32[3]{0:T(128)S(1)} %pad_add_fusion.place, bf16[128,2048]{1,0:T(8,128)(2,1)S(1)} %copy-done.25, bf16[128,2048]{1,0:T(8,128)(2,1)S(1)} %copy-done.27, ...), custom_call_target="tpu_custom_call" | custom-call | flops 6442450944 | bytes 22544384 | tf_op jit(solution)/shard_map/pallas_call | solution.py:31
  167.3 2.0 copy-done.40
  169.4 6.0 %shard_map.104 = (bf16[2,384,512]{2,1,0:T(8,128)(2,1)}, bf16[2,384,512]{2,1,0:T(8,128)(2,1)}, bf16[1024,2048]{1,0:T(8,128)(2,1)S(1)}) custom-call(s32[3]{0:T(128)S(1)} %pad_add_fusion.place, bf16[128,2176]{1,0:T(8,128)(2,1)S(1)} %shard_map.102.refs_0_, bf16[128,2176]{1,0:T(8,128)(2,1)S(1)} %collective-permute-done.refs_1_, ...), custom_call_target="tpu_custom_call" | custom-call | flops 1610612736 | bytes 11534336 | tf_op jit(solution)/shard_map/pallas_call | solution.py:31
  175.4 1.3 collective-permute-start.37
  176.8 5.7 %shard_map.105 = (bf16[1024,768]{1,0:T(8,128)(2,1)S(1)}, bf16[1024,768]{1,0:T(8,128)(2,1)S(1)}) custom-call(s32[3]{0:T(128)S(1)} %pad_add_fusion.place, bf16[1024,2048]{1,0:T(8,128)(2,1)S(1)} %get-tuple-element.28.y, f32[1024,768]{1,0:T(8,128)S(1)} %get-tuple-element.29.active, f32[1024,768]{1,0:T(8,128)S(1)} %get-tuple-element.30.slope, ...), custom_call_target="tpu_custom_call" | custom-call | flops 3221225472 | bytes 16777216 | tf_op jit(solution)/shard_map/pallas_call | solution.py:31
  182.5 10.3 %shard_map.106 = (bf16[512,2048]{1,0:T(8,128)(2,1)}, bf16[512,2048]{1,0:T(8,128)(2,1)S(1)}) custom-call(s32[3]{0:T(128)S(1)} %pad_add_fusion.place, bf16[1024,768]{1,0:T(8,128)(2,1)S(1)} %get-tuple-element.31.gate_delta.gd, bf16[1024,768]{1,0:T(8,128)(2,1)S(1)} %get-tuple-element.32.up_delta.ud, bf16[512,768]{1,0:T(8,128)(2,1)S(1)} %bitcast.62, ...), custom_call_target="tpu_custom_call" | custom-call | flops 6442450944 | bytes 13631488 | tf_op jit(solution)/shard_map/pallas_call | solution.py:31
  193.1 1.5 collective-permute-start.39
  194.6 2.2 copy-done.1
  196.8 1.4 copy-done.3
  198.2 2.4 shard_map.109
  200.6 2.2 copy-done.41
  202.8 5.2 %shard_map.108 = (bf16[2,512,768]{2,1,0:T(8,128)(2,1)S(1)}, bf16[2,512,768]{2,1,0:T(8,128)(2,1)S(1)}) custom-call(s32[3]{0:T(128)S(1)} %pad_add_fusion.place, bf16[1024,2048]{1,0:T(8,128)(2,1)S(1)} %copy-done.41, bf16[1024,768]{1,0:T(8,128)(2,1)S(1)} %copy-done.13, bf16[1024,768]{1,0:T(8,128)(2,1)S(1)} %copy-done.15), custom_call_target="tpu_custom_call" | custom-call | flops 3221225472 | bytes 10485760 | tf_op jit(solution)/shard_map/pallas_call | solution.py:31
  208.7 5.1 %collective-permute-done.39 = bf16[2,384,512]{2,1,0:T(8,128)(2,1)} collective-permute-done((bf16[2,384,512]{2,1,0:T(8,128)(2,1)}, bf16[2,384,512]{2,1,0:T(8,128)(2,1)}, u32[]{:S(2)}, u32[]{:S(2)}) %collective-permute-start.39) | collective-permute-done | bytes 786464 | tf_op jit(solution)/shard_map/ppermute | solution.py:278
  213.8 1.1 fusion.6
  215.7 5.2 %shard_map.107 = (bf16[512,768]{1,0:T(8,128)(2,1)S(1)}, bf16[512,768]{1,0:T(8,128)(2,1)S(1)}, bf16[512,768]{1,0:T(8,128)(2,1)S(1)}, bf16[512,768]{1,0:T(8,128)(2,1)S(1)}) custom-call(s32[3]{0:T(128)S(1)} %pad_add_fusion.place, bf16[1024,2048]{1,0:T(8,128)(2,1)S(1)} %copy-done.41, bf16[1024,768]{1,0:T(8,128)(2,1)S(1)} %copy-done.13, ...), custom_call_target="tpu_custom_call" | custom-call | flops 3221225472 | bytes 10485760 | tf_op jit(solution)/shard_map/pallas_call | solution.py:31
  221.0 1.4 collective-permute-start.34
  222.3 1.5 collective-permute-start.33
  224.0 2.4 collective-permute-done.40
  226.4 1.1 fusion.8
  227.5 2.4 add_convert_fusion
  230.0 2.0 collective-permute-start.31
  232.1 23.8 %collective-permute-done.34 = bf16[2,512,768]{2,1,0:T(8,128)(2,1)S(1)} collective-permute-done((bf16[2,512,768]{2,1,0:T(8,128)(2,1)S(1)}, bf16[2,512,768]{2,1,0:T(8,128)(2,1)S(1)}, u32[]{:S(2)}, u32[]{:S(2)}) %collective-permute-start.34) | collective-permute-done | bytes 1572896 | tf_op jit(solution)/shard_map/ppermute | solution.py:278
  256.2 1.4 collective-permute-start.36
  257.6 2.5 collective-permute-done.33
  260.5 2.1 collective-permute-start.35
  263.6 1.7 collective-permute-start.29
  265.3 1.3 collective-permute-start.30
  266.7 3.3 %collective-permute-start.32 = (bf16[128,2048]{1,0:T(8,128)(2,1)S(1)}, bf16[128,2048]{1,0:T(8,128)(2,1)S(1)}, u32[]{:S(2)}, u32[]{:S(2)}) collective-permute-start(bf16[128,2048]{1,0:T(8,128)(2,1)S(1)} %add_convert_fusion.4), channel_id=1, source_target_pairs={{0,4},{1,5},{2,6},{3,7},{4,0},{5,1},{6,2},{7,3},{8,12},{9,13},{10,... | collective-permute-start | bytes 1572872 | tf_op jit(solution)/shard_map/ppermute | solution.py:281
  270.0 5.3 %collective-permute-done.36 = bf16[512,768]{1,0:T(8,128)(2,1)S(1)} collective-permute-done((bf16[512,768]{1,0:T(8,128)(2,1)S(1)}, bf16[512,768]{1,0:T(8,128)(2,1)S(1)}, u32[]{:S(2)}, u32[]{:S(2)}) %collective-permute-start.36) | collective-permute-done | bytes 786464 | tf_op jit(solution)/shard_map/ppermute | solution.py:275
  275.3 1.1 fusion.5
  276.9 1.1 fusion.4
  278.8 20.8 %collective-permute-done.32 = bf16[128,2048]{1,0:T(8,128)(2,1)S(1)} collective-permute-done((bf16[128,2048]{1,0:T(8,128)(2,1)S(1)}, bf16[128,2048]{1,0:T(8,128)(2,1)S(1)}, u32[]{:S(2)}, u32[]{:S(2)}) %collective-permute-start.32) | collective-permute-done | bytes 524320 | tf_op jit(solution)/shard_map/ppermute | solution.py:281
  299.6 1.1 add_convert_fusion.3
  (126 shorter events, 25.4 us)
Async XLA Ops:
  0.6 29.3 %collective-permute-start.9 = (bf16[128,2048]{1,0:T(8,128)(2,1)}, bf16[128,2048]{1,0:T(8,128)(2,1)S(1)}, u32[]{:S(2)}, u32[]{:S(2)}) collective-permute-start(bf16[128,2048]{1,0:T(8,128)(2,1)} %refs_0_.1), channel_id=1, source_target_pairs={{0,4},{1,5},{2,6},{3,7},{4,0},{5,1},{6,2},{7,3},{8,12},{9,13},{10,... | collective-permute-start | bytes 1572872 | tf_op jit(solution)/shard_map/ppermute | solution.py:281
  4.8 27.2 %collective-permute-start.10 = (bf16[128,2048]{1,0:T(8,128)(2,1)}, bf16[128,2048]{1,0:T(8,128)(2,1)S(1)}, u32[]{:S(2)}, u32[]{:S(2)}) collective-permute-start(bf16[128,2048]{1,0:T(8,128)(2,1)} %refs_0_.1), channel_id=1, source_target_pairs={{0,2},{1,3},{2,4},{3,5},{4,6},{5,7},{8,10},{9,11},{10,12},{11,13},... | collective-permute-start | bytes 1572872 | tf_op jit(solution)/shard_map/ppermute | solution.py:281
  8.3 25.3 %collective-permute-start.11 = (bf16[128,2048]{1,0:T(8,128)(2,1)}, bf16[128,2048]{1,0:T(8,128)(2,1)S(1)}, u32[]{:S(2)}, u32[]{:S(2)}) collective-permute-start(bf16[128,2048]{1,0:T(8,128)(2,1)} %refs_0_.1), channel_id=1, source_target_pairs={{2,0},{3,1},{4,2},{5,3},{6,4},{7,5},{10,8},{11,9},{12,10},{13,11},... | collective-permute-start | bytes 1572872 | tf_op jit(solution)/shard_map/ppermute | solution.py:281
  9.6 24.0 %collective-permute-start.13 = (bf16[128,2048]{1,0:T(8,128)(2,1)}, bf16[128,2048]{1,0:T(8,128)(2,1)S(1)}, u32[]{:S(2)}, u32[]{:S(2)}) collective-permute-start(bf16[128,2048]{1,0:T(8,128)(2,1)} %refs_0_.1), channel_id=1, source_target_pairs={{0,1},{1,0},{2,3},{3,2},{4,5},{5,4},{6,7},{7,6},{8,9},{9,8},{10,11... | collective-permute-start | bytes 1572872 | tf_op jit(solution)/shard_map/ppermute | solution.py:284
  9.7 1.0 copy-start.9
  12.2 52.0 %collective-permute-start = (bf16[128,2176]{1,0:T(8,128)(2,1)S(1)}, bf16[128,2176]{1,0:T(8,128)(2,1)S(1)}, u32[]{:S(2)}, u32[]{:S(2)}) collective-permute-start(bf16[128,2176]{1,0:T(8,128)(2,1)S(1)} %shard_map.102.refs_0_), channel_id=1, source_target_pairs={{0,4},{1,5},{2,6},{3,7},{4,0},{5,1},{6,2},{7,3},{8,12},{9,13},{10,... | collective-permute-start | bytes 1671176 | tf_op jit(solution)/shard_map/ppermute | solution.py:281
  29.9 36.1 %collective-permute-start.1 = (bf16[128,2176]{1,0:T(8,128)(2,1)S(1)}, bf16[128,2176]{1,0:T(8,128)(2,1)S(1)}, u32[]{:S(2)}, u32[]{:S(2)}) collective-permute-start(bf16[128,2176]{1,0:T(8,128)(2,1)S(1)} %shard_map.102.refs_0_), channel_id=1, source_target_pairs={{0,2},{1,3},{2,4},{3,5},{4,6},{5,7},{8,10},{9,11},{10,12},{11,13},... | collective-permute-start | bytes 1671176 | tf_op jit(solution)/shard_map/ppermute | solution.py:281
  31.9 43.3 %collective-permute-start.2 = (bf16[128,2176]{1,0:T(8,128)(2,1)S(1)}, bf16[128,2176]{1,0:T(8,128)(2,1)S(1)}, u32[]{:S(2)}, u32[]{:S(2)}) collective-permute-start(bf16[128,2176]{1,0:T(8,128)(2,1)S(1)} %shard_map.102.refs_0_), channel_id=1, source_target_pairs={{2,0},{3,1},{4,2},{5,3},{6,4},{7,5},{10,8},{11,9},{12,10},{13,11},... | collective-permute-start | bytes 1671176 | tf_op jit(solution)/shard_map/ppermute | solution.py:281
  33.6 43.2 %collective-permute-start.4 = (bf16[128,2176]{1,0:T(8,128)(2,1)S(1)}, bf16[128,2176]{1,0:T(8,128)(2,1)S(1)}, u32[]{:S(2)}, u32[]{:S(2)}) collective-permute-start(bf16[128,2176]{1,0:T(8,128)(2,1)S(1)} %shard_map.102.refs_0_), channel_id=1, source_target_pairs={{0,1},{1,0},{2,3},{3,2},{4,5},{5,4},{6,7},{7,6},{8,9},{9,8},{10,11... | collective-permute-start | bytes 1671176 | tf_op jit(solution)/shard_map/ppermute | solution.py:284
  34.4 44.8 %collective-permute-start.18 = (bf16[512,768]{1,0:T(8,128)(2,1)}, bf16[512,768]{1,0:T(8,128)(2,1)}, u32[]{:S(2)}, u32[]{:S(2)}) collective-permute-start(bf16[512,768]{1,0:T(8,128)(2,1)} %bitcast.59), channel_id=1, source_target_pairs={{0,8},{8,0},{16,24},{24,16},{1,9},{9,1},{17,25},{25,17},{2,10},{10... | collective-permute-start | bytes 2359304 | tf_op jit(solution)/shard_map/ppermute | solution.py:275
  64.2 20.7 %collective-permute-start.22 = (bf16[512,768]{1,0:T(8,128)(2,1)}, bf16[512,768]{1,0:T(8,128)(2,1)}, u32[]{:S(2)}, u32[]{:S(2)}) collective-permute-start(bf16[512,768]{1,0:T(8,128)(2,1)} %bitcast.63), channel_id=1, source_target_pairs={{0,16},{8,24},{16,0},{24,8},{1,17},{9,25},{17,1},{25,9},{2,18},{10... | collective-permute-start | bytes 2359304 | tf_op jit(solution)/shard_map/ppermute | solution.py:278
  66.0 35.6 %collective-permute-start.19 = (bf16[512,768]{1,0:T(8,128)(2,1)}, bf16[512,768]{1,0:T(8,128)(2,1)S(1)}, u32[]{:S(2)}, u32[]{:S(2)}) collective-permute-start(bf16[512,768]{1,0:T(8,128)(2,1)} %bitcast.60), channel_id=1, source_target_pairs={{0,16},{8,24},{16,0},{24,8},{1,17},{9,25},{17,1},{25,9},{2,18},{10... | collective-permute-start | bytes 2359304 | tf_op jit(solution)/shard_map/ppermute | solution.py:278
  75.2 1.5 copy-start.5
  75.2 28.1 %collective-permute-start.21 = (bf16[512,768]{1,0:T(8,128)(2,1)}, bf16[512,768]{1,0:T(8,128)(2,1)S(1)}, u32[]{:S(2)}, u32[]{:S(2)}) collective-permute-start(bf16[512,768]{1,0:T(8,128)(2,1)} %bitcast.64), channel_id=1, source_target_pairs={{0,8},{8,0},{16,24},{24,16},{1,9},{9,1},{17,25},{25,17},{2,10},{10... | collective-permute-start | bytes 2359304 | tf_op jit(solution)/shard_map/ppermute | solution.py:275
  77.6 38.4 %collective-permute-start.25 = (bf16[768,512]{1,0:T(8,128)(2,1)}, bf16[768,512]{1,0:T(8,128)(2,1)S(1)}, u32[]{:S(2)}, u32[]{:S(2)}) collective-permute-start(bf16[768,512]{1,0:T(8,128)(2,1)} %bitcast.54), channel_id=1, source_target_pairs={{0,16},{8,24},{16,0},{24,8},{1,17},{9,25},{17,1},{25,9},{2,18},{10... | collective-permute-start | bytes 2359304 | tf_op jit(solution)/shard_map/ppermute | solution.py:278
  79.1 39.6 %collective-permute-start.24 = (bf16[768,512]{1,0:T(8,128)(2,1)}, bf16[768,512]{1,0:T(8,128)(2,1)S(1)}, u32[]{:S(2)}, u32[]{:S(2)}) collective-permute-start(bf16[768,512]{1,0:T(8,128)(2,1)} %bitcast.55), channel_id=1, source_target_pairs={{0,8},{8,0},{16,24},{24,16},{1,9},{9,1},{17,25},{25,17},{2,10},{10... | collective-permute-start | bytes 2359304 | tf_op jit(solution)/shard_map/ppermute | solution.py:275
  84.9 35.1 %collective-permute-start.12 = (bf16[128,2048]{1,0:T(8,128)(2,1)S(1)}, bf16[128,2048]{1,0:T(8,128)(2,1)}, u32[]{:S(2)}, u32[]{:S(2)}) collective-permute-start(bf16[128,2048]{1,0:T(8,128)(2,1)S(1)} %collective-permute-done.9.refs_1_), channel_id=1, source_target_pairs={{4,6},{5,7},{2,0},{3,1},{12,14},{13,15},{10,8},{11,9},{20,22},{21,... | collective-permute-start | bytes 1572872 | tf_op jit(solution)/shard_map/ppermute | solution.py:281
  102.5 18.9 %collective-permute-start.14 = (bf16[128,2048]{1,0:T(8,128)(2,1)S(1)}, bf16[128,2048]{1,0:T(8,128)(2,1)S(1)}, u32[]{:S(2)}, u32[]{:S(2)}) collective-permute-start(bf16[128,2048]{1,0:T(8,128)(2,1)S(1)} %collective-permute-done.9.refs_1_), channel_id=1, source_target_pairs={{0,1},{1,0},{2,3},{3,2},{4,5},{5,4},{6,7},{7,6},{8,9},{9,8},{10,11... | collective-permute-start | bytes 1572872 | tf_op jit(solution)/shard_map/ppermute | solution.py:284
  104.2 19.4 %collective-permute-start.15 = (bf16[128,2048]{1,0:T(8,128)(2,1)S(1)}, bf16[128,2048]{1,0:T(8,128)(2,1)S(1)}, u32[]{:S(2)}, u32[]{:S(2)}) collective-permute-start(bf16[128,2048]{1,0:T(8,128)(2,1)S(1)} %collective-permute-done.10.refs_2_), channel_id=1, source_target_pairs={{2,3},{3,2},{4,5},{5,4},{6,7},{7,6},{10,11},{11,10},{12,13},{13,12... | collective-permute-start | bytes 1572872 | tf_op jit(solution)/shard_map/ppermute | solution.py:284
  116.0 8.5 %collective-permute-start.16 = (bf16[128,2048]{1,0:T(8,128)(2,1)S(1)}, bf16[128,2048]{1,0:T(8,128)(2,1)S(1)}, u32[]{:S(2)}, u32[]{:S(2)}) collective-permute-start(bf16[128,2048]{1,0:T(8,128)(2,1)S(1)} %collective-permute-done.11.refs_3_), channel_id=1, source_target_pairs={{0,1},{1,0},{2,3},{3,2},{4,5},{5,4},{8,9},{9,8},{10,11},{11,10},{1... | collective-permute-start | bytes 1572872 | tf_op jit(solution)/shard_map/ppermute | solution.py:284
  118.7 23.3 %collective-permute-start.20 = (bf16[512,768]{1,0:T(8,128)(2,1)}, bf16[512,768]{1,0:T(8,128)(2,1)}, u32[]{:S(2)}, u32[]{:S(2)}) collective-permute-start(bf16[512,768]{1,0:T(8,128)(2,1)} %collective-permute-done.18.refs_11_.refs_1_), channel_id=1, source_target_pairs={{0,16},{8,24},{16,0},{24,8},{1,17},{9,25},{17,1},{25,9},{2,18},{10... | collective-permute-start | bytes 2359304 | tf_op jit(solution)/shard_map/ppermute | solution.py:278
  120.0 22.7 %collective-permute-start.23 = (bf16[512,768]{1,0:T(8,128)(2,1)}, bf16[512,768]{1,0:T(8,128)(2,1)}, u32[]{:S(2)}, u32[]{:S(2)}) collective-permute-start(bf16[512,768]{1,0:T(8,128)(2,1)} %collective-permute-done.22.refs_16_.refs_6_), channel_id=1, source_target_pairs={{0,8},{8,0},{16,24},{24,16},{1,9},{9,1},{17,25},{25,17},{2,10},{10... | collective-permute-start | bytes 2359304 | tf_op jit(solution)/shard_map/ppermute | solution.py:275
  122.3 16.5 %collective-permute-start.3 = (bf16[128,2176]{1,0:T(8,128)(2,1)S(1)}, bf16[128,2176]{1,0:T(8,128)(2,1)}, u32[]{:S(2)}, u32[]{:S(2)}) collective-permute-start(bf16[128,2176]{1,0:T(8,128)(2,1)S(1)} %collective-permute-done.refs_1_), channel_id=1, source_target_pairs={{4,6},{5,7},{2,0},{3,1},{12,14},{13,15},{10,8},{11,9},{20,22},{21,... | collective-permute-start | bytes 1671176 | tf_op jit(solution)/shard_map/ppermute | solution.py:281
  124.4 15.0 %collective-permute-start.5 = (bf16[128,2176]{1,0:T(8,128)(2,1)S(1)}, bf16[128,2176]{1,0:T(8,128)(2,1)}, u32[]{:S(2)}, u32[]{:S(2)}) collective-permute-start(bf16[128,2176]{1,0:T(8,128)(2,1)S(1)} %collective-permute-done.refs_1_), channel_id=1, source_target_pairs={{0,1},{1,0},{2,3},{3,2},{4,5},{5,4},{6,7},{7,6},{8,9},{9,8},{10,11... | collective-permute-start | bytes 1671176 | tf_op jit(solution)/shard_map/ppermute | solution.py:284
  125.2 16.2 %collective-permute-start.17 = (bf16[128,2048]{1,0:T(8,128)(2,1)}, bf16[128,2048]{1,0:T(8,128)(2,1)}, u32[]{:S(2)}, u32[]{:S(2)}) collective-permute-start(bf16[128,2048]{1,0:T(8,128)(2,1)} %collective-permute-done.12.refs_4_), channel_id=1, source_target_pairs={{0,1},{1,0},{6,7},{7,6},{8,9},{9,8},{14,15},{15,14},{16,17},{17,16... | collective-permute-start | bytes 1572872 | tf_op jit(solution)/shard_map/ppermute | solution.py:284
  127.6 11.8 %copy-start.6 = (bf16[128,2176]{1,0:T(8,128)(2,1)S(1)}, bf16[128,2176]{1,0:T(8,128)(2,1)}, u32[]{:S(2)}) copy-start(bf16[128,2176]{1,0:T(8,128)(2,1)} %copy-done.5) | copy-start | bytes 1671172
  127.6 17.0 %copy-start.16 = (bf16[1,512,768]{2,1,0:T(8,128)(2,1)S(1)}, bf16[1,512,768]{2,1,0:T(8,128)(2,1)}, u32[]{:S(2)}) copy-start(bf16[1,512,768]{2,1,0:T(8,128)(2,1)} %param.11) | copy-start | bytes 2359300
  127.8 41.6 %copy-start.8 = (bf16[128,2176]{1,0:T(8,128)(2,1)S(1)}, bf16[128,2176]{1,0:T(8,128)(2,1)}, u32[]{:S(2)}) copy-start(bf16[128,2176]{1,0:T(8,128)(2,1)} %copy-done.7) | copy-start | bytes 1671172
  138.8 30.6 %collective-permute-start.6 = (bf16[128,2176]{1,0:T(8,128)(2,1)S(1)}, bf16[128,2176]{1,0:T(8,128)(2,1)S(1)}, u32[]{:S(2)}, u32[]{:S(2)}) collective-permute-start(bf16[128,2176]{1,0:T(8,128)(2,1)S(1)} %collective-permute-done.1.refs_2_), channel_id=1, source_target_pairs={{2,3},{3,2},{4,5},{5,4},{6,7},{7,6},{10,11},{11,10},{12,13},{13,12... | collective-permute-start | bytes 1671176 | tf_op jit(solution)/shard_map/ppermute | solution.py:284
  139.5 29.9 %collective-permute-start.7 = (bf16[128,2176]{1,0:T(8,128)(2,1)S(1)}, bf16[128,2176]{1,0:T(8,128)(2,1)S(1)}, u32[]{:S(2)}, u32[]{:S(2)}) collective-permute-start(bf16[128,2176]{1,0:T(8,128)(2,1)S(1)} %copy-done.6), channel_id=1, source_target_pairs={{0,1},{1,0},{2,3},{3,2},{4,5},{5,4},{8,9},{9,8},{10,11},{11,10},{1... | collective-permute-start | bytes 1671176 | tf_op jit(solution)/shard_map/ppermute | solution.py:284
  141.4 35.3 %collective-permute-start.26 = (bf16[384,512]{1,0:T(8,128)(2,1)S(1)}, bf16[384,512]{1,0:T(8,128)(2,1)S(1)}, u32[]{:S(2)}, u32[]{:S(2)}) collective-permute-start(bf16[384,512]{1,0:T(8,128)(2,1)S(1)} %slice.62), channel_id=1, source_target_pairs={{0,8},{8,0},{16,24},{24,16},{1,9},{9,1},{17,25},{25,17},{2,10},{10... | collective-permute-start | bytes 1179656 | tf_op jit(solution)/shard_map/ppermute | solution.py:275
  142.0 34.7 %collective-permute-start.27 = (bf16[384,512]{1,0:T(8,128)(2,1)S(1)}, bf16[384,512]{1,0:T(8,128)(2,1)S(1)}, u32[]{:S(2)}, u32[]{:S(2)}) collective-permute-start(bf16[384,512]{1,0:T(8,128)(2,1)S(1)} %slice.63), channel_id=1, source_target_pairs={{0,16},{8,24},{16,0},{24,8},{1,17},{9,25},{17,1},{25,9},{2,18},{10... | collective-permute-start | bytes 1179656 | tf_op jit(solution)/shard_map/ppermute | solution.py:278
  142.7 26.6 %collective-permute-start.8 = (bf16[128,2176]{1,0:T(8,128)(2,1)}, bf16[128,2176]{1,0:T(8,128)(2,1)S(1)}, u32[]{:S(2)}, u32[]{:S(2)}) collective-permute-start(bf16[128,2176]{1,0:T(8,128)(2,1)} %collective-permute-done.3.refs_4_), channel_id=1, source_target_pairs={{0,1},{1,0},{6,7},{7,6},{8,9},{9,8},{14,15},{15,14},{16,17},{17,16... | collective-permute-start | bytes 1671176 | tf_op jit(solution)/shard_map/ppermute | solution.py:284
  144.7 1.1 copy-start.17
  145.8 1.1 copy-start.20
  146.9 1.1 copy-start.23
  148.1 1.0 copy-start.25
  167.3 2.0 copy-start.40
  169.3 6.0 %copy-start.2 = (bf16[1024,768]{1,0:T(8,128)(2,1)}, bf16[1024,768]{1,0:T(8,128)(2,1)S(1)}, u32[]{:S(2)}) copy-start(bf16[1024,768]{1,0:T(8,128)(2,1)S(1)} %get-tuple-element.27.refs_10_.act) | copy-start | bytes 4718596
  169.4 7.4 %copy-start.4 = (bf16[1,768,512]{2,1,0:T(8,128)(2,1)S(1)}, bf16[1,768,512]{2,1,0:T(8,128)(2,1)}, u32[]{:S(2)}) copy-start(bf16[1,768,512]{2,1,0:T(8,128)(2,1)} %param.13) | copy-start | bytes 2359300
  175.4 7.1 %copy-start = (bf16[1024,2048]{1,0:T(8,128)(2,1)}, bf16[1024,2048]{1,0:T(8,128)(2,1)S(1)}, u32[]{:S(2)}) copy-start(bf16[1024,2048]{1,0:T(8,128)(2,1)S(1)} %get-tuple-element.28.y) | copy-start | bytes 12582916
  175.4 32.7 %collective-permute-start.37 = (bf16[2,384,512]{2,1,0:T(8,128)(2,1)}, bf16[2,384,512]{2,1,0:T(8,128)(2,1)S(1)}, u32[]{:S(2)}, u32[]{:S(2)}) collective-permute-start(bf16[2,384,512]{2,1,0:T(8,128)(2,1)} %get-tuple-element.45), channel_id=1, source_target_pairs={{0,8},{8,0},{16,24},{24,16},{1,9},{9,1},{17,25},{25,17},{2,10},{10... | collective-permute-start | bytes 2359304 | tf_op jit(solution)/shard_map/ppermute | solution.py:275
  176.7 5.7 %copy-start.18 = (bf16[1,512,768]{2,1,0:T(8,128)(2,1)S(1)}, bf16[1,512,768]{2,1,0:T(8,128)(2,1)}, u32[]{:S(2)}) copy-start(bf16[1,512,768]{2,1,0:T(8,128)(2,1)} %param.12) | copy-start | bytes 2359300
  176.8 5.7 %copy-start.21 = (bf16[512,768]{1,0:T(8,128)(2,1)S(1)}, bf16[512,768]{1,0:T(8,128)(2,1)}, u32[]{:S(2)}) copy-start(bf16[512,768]{1,0:T(8,128)(2,1)} %copy-done.19) | copy-start | bytes 2359300
  176.8 5.7 %copy-start.24 = (bf16[512,768]{1,0:T(8,128)(2,1)S(1)}, bf16[512,768]{1,0:T(8,128)(2,1)}, u32[]{:S(2)}) copy-start(bf16[512,768]{1,0:T(8,128)(2,1)} %copy-done.22) | copy-start | bytes 2359300
  182.5 10.3 %copy-start.12 = (bf16[1024,768]{1,0:T(8,128)(2,1)}, bf16[1024,768]{1,0:T(8,128)(2,1)S(1)}, u32[]{:S(2)}) copy-start(bf16[1024,768]{1,0:T(8,128)(2,1)S(1)} %get-tuple-element.31.gate_delta.gd) | copy-start | bytes 4718596
  182.5 10.3 %copy-start.14 = (bf16[1024,768]{1,0:T(8,128)(2,1)}, bf16[1024,768]{1,0:T(8,128)(2,1)S(1)}, u32[]{:S(2)}) copy-start(bf16[1024,768]{1,0:T(8,128)(2,1)S(1)} %get-tuple-element.32.up_delta.ud) | copy-start | bytes 4718596
  192.8 34.7 %collective-permute-start.28 = (bf16[512,2048]{1,0:T(8,128)(2,1)}, bf16[512,2048]{1,0:T(8,128)(2,1)}, u32[]{:S(2)}, u32[]{:S(2)}) collective-permute-start(bf16[512,2048]{1,0:T(8,128)(2,1)} %get-tuple-element.34), channel_id=1, source_target_pairs={{0,1},{1,0},{2,3},{3,2},{4,5},{5,4},{6,7},{7,6},{8,9},{9,8},{10,11... | collective-permute-start | bytes 6291464 | tf_op jit(solution)/shard_map/ppermute | solution.py:284
  193.1 20.7 %collective-permute-start.39 = (bf16[2,384,512]{2,1,0:T(8,128)(2,1)}, bf16[2,384,512]{2,1,0:T(8,128)(2,1)}, u32[]{:S(2)}, u32[]{:S(2)}) collective-permute-start(bf16[2,384,512]{2,1,0:T(8,128)(2,1)} %get-tuple-element.48), channel_id=1, source_target_pairs={{0,16},{8,24},{16,0},{24,8},{1,17},{9,25},{17,1},{25,9},{2,18},{10... | collective-permute-start | bytes 2359304 | tf_op jit(solution)/shard_map/ppermute | solution.py:278
  194.6 2.2 copy-start.1
  196.8 1.4 copy-start.3
  198.2 2.4 copy-start.13
  198.2 2.4 copy-start.15
  200.6 2.2 copy-start.41
  208.2 15.7 %collective-permute-start.38 = (bf16[384,512]{1,0:T(8,128)(2,1)S(1)}, bf16[384,512]{1,0:T(8,128)(2,1)S(1)}, u32[]{:S(2)}, u32[]{:S(2)}) collective-permute-start(bf16[384,512]{1,0:T(8,128)(2,1)S(1)} %fusion.9), channel_id=1, source_target_pairs={{0,16},{8,24},{16,0},{24,8},{1,17},{9,25},{17,1},{25,9},{2,18},{10... | collective-permute-start | bytes 1179656 | tf_op jit(solution)/shard_map/ppermute | solution.py:278
  214.9 11.5 %collective-permute-start.40 = (bf16[384,512]{1,0:T(8,128)(2,1)S(1)}, bf16[384,512]{1,0:T(8,128)(2,1)S(1)}, u32[]{:S(2)}, u32[]{:S(2)}) collective-permute-start(bf16[384,512]{1,0:T(8,128)(2,1)S(1)} %fusion.6), channel_id=1, source_target_pairs={{0,8},{8,0},{16,24},{24,16},{1,9},{9,1},{17,25},{25,17},{2,10},{10... | collective-permute-start | bytes 1179656 | tf_op jit(solution)/shard_map/ppermute | solution.py:275
  221.0 34.8 %collective-permute-start.34 = (bf16[2,512,768]{2,1,0:T(8,128)(2,1)S(1)}, bf16[2,512,768]{2,1,0:T(8,128)(2,1)S(1)}, u32[]{:S(2)}, u32[]{:S(2)}) collective-permute-start(bf16[2,512,768]{2,1,0:T(8,128)(2,1)S(1)} %get-tuple-element.39), channel_id=1, source_target_pairs={{0,16},{8,24},{16,0},{24,8},{1,17},{9,25},{17,1},{25,9},{2,18},{10... | collective-permute-start | bytes 4718600 | tf_op jit(solution)/shard_map/ppermute | solution.py:278
  222.3 37.8 %collective-permute-start.33 = (bf16[2,512,768]{2,1,0:T(8,128)(2,1)S(1)}, bf16[2,512,768]{2,1,0:T(8,128)(2,1)S(1)}, u32[]{:S(2)}, u32[]{:S(2)}) collective-permute-start(bf16[2,512,768]{2,1,0:T(8,128)(2,1)S(1)} %get-tuple-element.37), channel_id=1, source_target_pairs={{0,8},{8,0},{16,24},{24,16},{1,9},{9,1},{17,25},{25,17},{2,10},{10... | collective-permute-start | bytes 4718600 | tf_op jit(solution)/shard_map/ppermute | solution.py:275
  230.0 36.6 %collective-permute-start.31 = (bf16[128,2048]{1,0:T(8,128)(2,1)S(1)}, bf16[128,2048]{1,0:T(8,128)(2,1)S(1)}, u32[]{:S(2)}, u32[]{:S(2)}) collective-permute-start(bf16[128,2048]{1,0:T(8,128)(2,1)S(1)} %get-tuple-element.51), channel_id=1, source_target_pairs={{6,4},{7,5},{0,2},{1,3},{14,12},{15,13},{8,10},{9,11},{22,20},{23,... | collective-permute-start | bytes 1572872 | tf_op jit(solution)/shard_map/ppermute | solution.py:281
  256.2 19.1 %collective-permute-start.36 = (bf16[512,768]{1,0:T(8,128)(2,1)S(1)}, bf16[512,768]{1,0:T(8,128)(2,1)S(1)}, u32[]{:S(2)}, u32[]{:S(2)}) collective-permute-start(bf16[512,768]{1,0:T(8,128)(2,1)S(1)} %get-tuple-element.53), channel_id=1, source_target_pairs={{0,8},{8,0},{16,24},{24,16},{1,9},{9,1},{17,25},{25,17},{2,10},{10... | collective-permute-start | bytes 2359304 | tf_op jit(solution)/shard_map/ppermute | solution.py:275
  260.5 16.4 %collective-permute-start.35 = (bf16[512,768]{1,0:T(8,128)(2,1)S(1)}, bf16[512,768]{1,0:T(8,128)(2,1)S(1)}, u32[]{:S(2)}, u32[]{:S(2)}) collective-permute-start(bf16[512,768]{1,0:T(8,128)(2,1)S(1)} %get-tuple-element.56), channel_id=1, source_target_pairs={{0,16},{8,24},{16,0},{24,8},{1,17},{9,25},{17,1},{25,9},{2,18},{10... | collective-permute-start | bytes 2359304 | tf_op jit(solution)/shard_map/ppermute | solution.py:278
  263.6 14.4 %collective-permute-start.29 = (bf16[128,2048]{1,0:T(8,128)(2,1)S(1)}, bf16[128,2048]{1,0:T(8,128)(2,1)S(1)}, u32[]{:S(2)}, u32[]{:S(2)}) collective-permute-start(bf16[128,2048]{1,0:T(8,128)(2,1)S(1)} %get-tuple-element.50), channel_id=1, source_target_pairs={{0,2},{1,3},{2,4},{3,5},{4,6},{5,7},{8,10},{9,11},{10,12},{11,13},... | collective-permute-start | bytes 1572872 | tf_op jit(solution)/shard_map/ppermute | solution.py:281
  265.3 13.5 %collective-permute-start.30 = (bf16[128,2048]{1,0:T(8,128)(2,1)S(1)}, bf16[128,2048]{1,0:T(8,128)(2,1)S(1)}, u32[]{:S(2)}, u32[]{:S(2)}) collective-permute-start(bf16[128,2048]{1,0:T(8,128)(2,1)S(1)} %get-tuple-element.52), channel_id=1, source_target_pairs={{2,0},{3,1},{4,2},{5,3},{6,4},{7,5},{10,8},{11,9},{12,10},{13,11},... | collective-permute-start | bytes 1572872 | tf_op jit(solution)/shard_map/ppermute | solution.py:281
  266.7 32.8 %collective-permute-start.32 = (bf16[128,2048]{1,0:T(8,128)(2,1)S(1)}, bf16[128,2048]{1,0:T(8,128)(2,1)S(1)}, u32[]{:S(2)}, u32[]{:S(2)}) collective-permute-start(bf16[128,2048]{1,0:T(8,128)(2,1)S(1)} %add_convert_fusion.4), channel_id=1, source_target_pairs={{0,4},{1,5},{2,6},{3,7},{4,0},{5,1},{6,2},{7,3},{8,12},{9,13},{10,... | collective-permute-start | bytes 1572872 | tf_op jit(solution)/shard_map/ppermute | solution.py:281
  (19 other events, 16.8 us)

commit v2 on v1

--- a/solution.py
+++ b/solution.py
@@ -37,6 +37,11 @@
         compiler_params=pltpu.CompilerParams(vmem_limit_bytes=LIMIT),
         cost_estimate=pl.CostEstimate(flops=flops, bytes_accessed=moved, transcendentals=0),
     )(*[a for a, _ in ins])
+
+
+TWO = ((0, 2), (1, 3), (2, 0), (3, 1))
+OUTER = ((0, 1), (1, 0), (2, 3), (3, 2))
+INNER = ((1, 2), (2, 1))
 
 
 def prep_body(experts, routes, gates, rows, out):
@@ -81,14 +86,14 @@
 
 def load_rows(copies, chip, pieces, dst):
     tok = pieces[0].shape[0]
+    middle = jnp.logical_or(chip == 1, chip == 2)
     started = []
     for core in (0, 1):
-        own, two, right, left, far = pieces[5 * core : 5 * core + 5]
+        own, two, outer, inner, far = pieces[5 * core : 5 * core + 5]
         at = [dst.at[pl.ds((4 * core + s) * tok, tok)] for s in range(4)]
-        started.append(copies.start(own, at[0]))
-        started.append(copies.pick(chip == 0, far, right, at[1]))
-        started.append(copies.start(two, at[2]))
-        started.append(copies.pick(chip == 3, far, left, at[3]))
+        for src, to in zip((own, two, outer), at):
+            started.append(copies.start(src, to))
+        started.append(copies.pick(middle, inner, far, at[3]))
     return started
 
 
@@ -284,12 +289,12 @@
         return lax.ppermute(block, "expert", [(2 * z + c, 2 * z + 1 - c) for z in at for c in (0, 1)])
 
     def line(own):
-        two = hop(own, [(z, (z + 2) % 4) for z in range(4)])
-        right = hop(own, [(0, 1), (1, 2), (2, 3)])
-        left = hop(own, [(1, 0), (2, 1), (3, 2)])
-        far = hop(two, [(2, 3), (1, 0)])
-        return [own, two, right, left, far] + [
-            swap(own), swap(two), swap(right, (1, 2, 3)), swap(left, (0, 1, 2)), swap(far, (0, 3))
+        two = hop(own, TWO)
+        outer = hop(own, OUTER)
+        inner = hop(own, INNER)
+        far = hop(two, ((2, 3), (1, 0)))
+        return [own, two, outer, inner, far] + [
+            swap(own), swap(two), swap(outer), swap(inner, (1, 2)), swap(far, (0, 3))
         ]
 
     x_pieces = line(tokens)
@@ -388,11 +393,11 @@
     down_grad = jnp.concatenate([add(keep_a0, got_a[0], down_a), add(keep_b0, got_b[0], down_b)], axis=0)
     gate_grad, up_grad = add(gate_sum, gate_last), add(up_sum, up_last)
 
-    far = hop(jnp.where(chip == 0, total[1], total[3]), [(3, 2), (0, 1)])
-    right = hop(total[3], [(0, 1), (1, 2), (2, 3)])
-    left = hop(total[1], [(1, 0), (2, 1), (3, 2)])
-    two = hop(add(total[2], far), [(z, (z + 2) % 4) for z in range(4)])
-    input_grad = add(total[0], right, left, two)
+    far = hop(total[3], ((0, 1), (3, 2)))
+    inner = hop(total[3], INNER)
+    outer = hop(total[2], OUTER)
+    two = hop(add(total[1], far), TWO)
+    input_grad = add(total[0], inner, outer, two)
     return input_grad, gate_grad[None], up_grad[None], down_grad[None]
 
 

time: 302 us -> 293 us (0.970)
  waiting for transfers between devices: 156 us -> 168 us
  starting transfers between devices: 57.2 us -> 48.4 us
  local copies, waits for them, and re-layouts: 30.2 us -> 24.5 us
  other arithmetic: 10.2 us -> 6.69 us
    ppermute x9, waiting for transfers between devices: 60 us -> 76.2 us  [to_y(): return lax.ppermute(block, 'dp', [(i, i ^ 2) for i in range(4)])]
    ppermute x12, waiting for transfers between devices: 85.7 us -> 78.2 us  [hop(): lax.ppermute(block, 'expert', [(2 * a + c, 2 * b + c) for a, b in moves f...]
    unnamed x84 -> x68, local copies, waits for them, and re-layouts: 30.1 us -> 24.4 us
    ppermute x12, starting transfers between devices: 25.2 us -> 19.9 us  [hop(): lax.ppermute(block, 'expert', [(2 * a + c, 2 * b + c) for a, b in moves f...]
    convert_element_type x9, other arithmetic: 6.95 us -> 3.5 us  [add(): return total.astype(BF16)]
    ppermute x11, starting transfers between devices: 9.87 us -> 6.63 us  [swap(): lax.ppermute(block, 'expert', [(2 * z + c, 2 * z + 1 - c) for z in at for...]
  transfers between devices with their start and end apart: 41 -> 41, of which waited for: 16 -> 14; matrix products, arithmetic and copies ran while one was open for 3% -> 2% of each run, Pallas kernels for 15% -> 15%
where the time goes in v2:
time: 293 us; the launch traced here: 292 us
  waiting for transfers between devices  168 us (57%)
  starting transfers between devices  48.4 us (17%)
  Pallas kernels  43.7 us (15%)
  local copies, waits for them, and re-layouts  24.5 us (8%)
  other arithmetic  6.69 us (2%)
    ppermute x12, waiting for transfers between devices, hop(): lax.ppermute(block, 'expert', [(2 * a + c, 2 * b + c) for a, b in moves f...  78.2 us
    ppermute x9, waiting for transfers between devices, to_y(): return lax.ppermute(block, 'dp', [(i, i ^ 2) for i in range(4)])  76.2 us
    pallas_call x8, Pallas kernels, call(): pl.pallas_call(body, out_shape=[jax.ShapeDtypeStruct(s, d) for s, d, _ in...  43.7 us
    unnamed x68, local copies, waits for them, and re-layouts  24.4 us
    ppermute x12, starting transfers between devices, hop(): lax.ppermute(block, 'expert', [(2 * a + c, 2 * b + c) for a, b in moves f...  19.9 us
    ppermute x9, waiting for transfers between devices, to_x(): return lax.ppermute(block, 'dp', [(i, i ^ 1) for i in range(4)])  13 us
    ppermute x9, starting transfers between devices, to_x(): return lax.ppermute(block, 'dp', [(i, i ^ 1) for i in range(4)])  11.3 us
    ppermute x9, starting transfers between devices, to_y(): return lax.ppermute(block, 'dp', [(i, i ^ 2) for i in range(4)])  10.6 us
  transfers between devices with their start and end apart: 41, of which 14 were waited for; matrix products, arithmetic and copies ran while one was open for 2% of the time, Pallas kernels for 15%

profile of v2, /device:TPU:0, one launch (start us, length us, event | category | flops | bytes accessed | tf_op | source)
XLA Modules:
  0.0 292.0 jit_solution(13904353875743728319)
XLA Ops:
  0.6 4.1 %collective-permute-start.9 = (bf16[128,2048]{1,0:T(8,128)(2,1)}, bf16[128,2048]{1,0:T(8,128)(2,1)S(1)}, u32[]{:S(2)}, u32[]{:S(2)}) collective-permute-start(bf16[128,2048]{1,0:T(8,128)(2,1)} %refs_0_.1), channel_id=1, source_target_pairs={{0,4},{1,5},{2,6},{3,7},{4,0},{5,1},{6,2},{7,3},{8,12},{9,13},{10,... | collective-permute-start | bytes 1572872 | tf_op jit(solution)/shard_map/ppermute | solution.py:286
  4.8 1.6 collective-permute-start.10
  7.1 1.0 copy-done.5
  9.6 3.2 %collective-permute-start = (bf16[128,2176]{1,0:T(8,128)(2,1)S(1)}, bf16[128,2176]{1,0:T(8,128)(2,1)S(1)}, u32[]{:S(2)}, u32[]{:S(2)}) collective-permute-start(bf16[128,2176]{1,0:T(8,128)(2,1)S(1)} %shard_map.102.refs_0_), channel_id=1, source_target_pairs={{0,4},{1,5},{2,6},{3,7},{4,0},{5,1},{6,2},{7,3},{8,12},{9,13},{10,... | collective-permute-start | bytes 1671176 | tf_op jit(solution)/shard_map/ppermute | solution.py:286
  12.8 17.1 %collective-permute-done.9.refs_1_ = bf16[128,2048]{1,0:T(8,128)(2,1)S(1)} collective-permute-done((bf16[128,2048]{1,0:T(8,128)(2,1)}, bf16[128,2048]{1,0:T(8,128)(2,1)S(1)}, u32[]{:S(2)}, u32[]{:S(2)}) %collective-permute-start.9) | collective-permute-done | bytes 524320 | tf_op jit(solution)/shard_map/ppermute | solution.py:286
  30.7 0.8 copy-done.24
  31.5 2.0 collective-permute-start.18
  33.6 30.6 %collective-permute-done.refs_1_ = bf16[128,2176]{1,0:T(8,128)(2,1)S(1)} collective-permute-done((bf16[128,2176]{1,0:T(8,128)(2,1)S(1)}, bf16[128,2176]{1,0:T(8,128)(2,1)S(1)}, u32[]{:S(2)}, u32[]{:S(2)}) %collective-permute-start) | collective-permute-done | bytes 557088 | tf_op jit(solution)/shard_map/ppermute | solution.py:286
  64.1 1.8 collective-permute-start.22
  66.2 1.8 collective-permute-start.21
  68.0 0.9 copy-done.3
  68.9 1.5 collective-permute-start.25
  70.4 0.8 collective-permute-start.24
  71.2 13.7 %collective-permute-done.22.refs_16_.refs_6_ = bf16[512,768]{1,0:T(8,128)(2,1)} collective-permute-done((bf16[512,768]{1,0:T(8,128)(2,1)}, bf16[512,768]{1,0:T(8,128)(2,1)}, u32[]{:S(2)}, u32[]{:S(2)}) %collective-permute-start.22) | collective-permute-done | bytes 786464 | tf_op jit(solution)/shard_map/ppermute | solution.py:283
  84.9 1.3 collective-permute-start.12
  86.2 15.5 %collective-permute-done.19.refs_12_.refs_2_ = bf16[512,768]{1,0:T(8,128)(2,1)S(1)} collective-permute-done((bf16[512,768]{1,0:T(8,128)(2,1)}, bf16[512,768]{1,0:T(8,128)(2,1)S(1)}, u32[]{:S(2)}, u32[]{:S(2)}) %collective-permute-start.19) | collective-permute-done | bytes 786464 | tf_op jit(solution)/shard_map/ppermute | solution.py:283
  101.6 0.9 copy-done.11
  103.3 0.9 copy-done.14
  105.5 10.4 %collective-permute-done.25.from_y = bf16[768,512]{1,0:T(8,128)(2,1)S(1)} collective-permute-done((bf16[768,512]{1,0:T(8,128)(2,1)}, bf16[768,512]{1,0:T(8,128)(2,1)S(1)}, u32[]{:S(2)}, u32[]{:S(2)}) %collective-permute-start.25) | collective-permute-done | bytes 786464 | tf_op jit(solution)/shard_map/ppermute | solution.py:283
  117.4 1.3 collective-permute-start.20
  118.7 1.5 collective-permute-start.23
  121.0 1.3 collective-permute-start.3
  123.1 0.8 copy-done.30
  123.9 2.4 collective-permute-start.17
  126.5 11.5 %collective-permute-done.3.refs_4_ = bf16[128,2176]{1,0:T(8,128)(2,1)} collective-permute-done((bf16[128,2176]{1,0:T(8,128)(2,1)S(1)}, bf16[128,2176]{1,0:T(8,128)(2,1)}, u32[]{:S(2)}, u32[]{:S(2)}) %collective-permute-start.3) | collective-permute-done | bytes 557088 | tf_op jit(solution)/shard_map/ppermute | solution.py:286
  139.8 1.9 collective-permute-start.8
  141.8 1.1 copy-done.9
  142.9 1.1 copy-done.12
  144.0 1.1 copy-done.15
  145.1 1.0 copy-done.17
  146.2 1.0 copy-done.19
  147.2 1.0 copy-done.21
  148.3 1.0 copy-done.23
  149.3 1.0 copy-done.25
  150.4 1.0 copy-done.27
  151.4 1.0 copy-done.29
  152.4 1.0 copy-done.31
  153.5 11.0 %shard_map.103 = (bf16[1024,768]{1,0:T(8,128)(2,1)S(1)}, f32[1024,768]{1,0:T(8,128)S(1)}, f32[1024,768]{1,0:T(8,128)S(1)}, bf16[1024,2048]{1,0:T(8,128)(2,1)S(1)}) custom-call(s32[3]{0:T(128)S(1)} %pad_add_fusion.place, bf16[128,2048]{1,0:T(8,128)(2,1)S(1)} %copy-done.17, bf16[128,2048]{1,0:T(8,128)(2,1)S(1)} %copy-done.19, ...), custom_call_target="tpu_custom_call" | custom-call | flops 6442450944 | bytes 22544384 | tf_op jit(solution)/shard_map/pallas_call | solution.py:31
  164.5 2.0 copy-done.32
  166.5 5.0 %shard_map.104 = (bf16[2,384,512]{2,1,0:T(8,128)(2,1)S(1)}, bf16[2,384,512]{2,1,0:T(8,128)(2,1)S(1)}, bf16[1024,2048]{1,0:T(8,128)(2,1)S(1)}) custom-call(s32[3]{0:T(128)S(1)} %pad_add_fusion.place, bf16[128,2176]{1,0:T(8,128)(2,1)S(1)} %shard_map.102.refs_0_, bf16[128,2176]{1,0:T(8,128)(2,1)S(1)} %collective-permute-done.refs_1_, ...), custom_call_target="tpu_custom_call" | custom-call | flops 1610612736 | bytes 11534336 | tf_op jit(solution)/shard_map/pallas_call | solution.py:31
  171.6 1.6 collective-permute-start.37
  173.2 5.7 %shard_map.105 = (bf16[1024,768]{1,0:T(8,128)(2,1)S(1)}, bf16[1024,768]{1,0:T(8,128)(2,1)S(1)}) custom-call(s32[3]{0:T(128)S(1)} %pad_add_fusion.place, bf16[1024,2048]{1,0:T(8,128)(2,1)S(1)} %get-tuple-element.28.y, f32[1024,768]{1,0:T(8,128)S(1)} %get-tuple-element.29.active, f32[1024,768]{1,0:T(8,128)S(1)} %get-tuple-element.30.slope, ...), custom_call_target="tpu_custom_call" | custom-call | flops 3221225472 | bytes 16777216 | tf_op jit(solution)/shard_map/pallas_call | solution.py:31
  178.9 9.0 %shard_map.106 = (bf16[512,2048]{1,0:T(8,128)(2,1)S(1)}, bf16[512,2048]{1,0:T(8,128)(2,1)S(1)}) custom-call(s32[3]{0:T(128)S(1)} %pad_add_fusion.place, bf16[1024,768]{1,0:T(8,128)(2,1)S(1)} %get-tuple-element.31.gate_delta.gd, bf16[1024,768]{1,0:T(8,128)(2,1)S(1)} %get-tuple-element.32.up_delta.ud, bf16[512,768]{1,0:T(8,128)(2,1)S(1)} %bitcast.62, ...), custom_call_target="tpu_custom_call" | custom-call | flops 6442450944 | bytes 13631488 | tf_op jit(solution)/shard_map/pallas_call | solution.py:31
  188.1 1.5 collective-permute-start.39
  189.6 2.4 shard_map.109
  192.0 5.3 %shard_map.108 = (bf16[2,512,768]{2,1,0:T(8,128)(2,1)S(1)}, bf16[2,512,768]{2,1,0:T(8,128)(2,1)S(1)}) custom-call(s32[3]{0:T(128)S(1)} %pad_add_fusion.place, bf16[1024,2048]{1,0:T(8,128)(2,1)S(1)} %copy-done.33, bf16[1024,768]{1,0:T(8,128)(2,1)S(1)} %get-tuple-element.31.gate_delta.gd, bf16[1024,768]{1,0:T(8,128)(2,1)S(1)} %get-tuple-element.32.up_delta.ud), custom_call_target="tpu_custom_call" | custom-call | flops 3221225472 | bytes 10485760 | tf_op jit(solution)/shard_map/pallas_call | solution.py:31
  198.0 10.5 %collective-permute-done.39 = bf16[2,384,512]{2,1,0:T(8,128)(2,1)S(1)} collective-permute-done((bf16[2,384,512]{2,1,0:T(8,128)(2,1)S(1)}, bf16[2,384,512]{2,1,0:T(8,128)(2,1)S(1)}, u32[]{:S(2)}, u32[]{:S(2)}) %collective-permute-start.39) | collective-permute-done | bytes 786464 | tf_op jit(solution)/shard_map/ppermute | solution.py:283
  209.2 5.3 %shard_map.107 = (bf16[512,768]{1,0:T(8,128)(2,1)S(1)}, bf16[512,768]{1,0:T(8,128)(2,1)S(1)}, bf16[512,768]{1,0:T(8,128)(2,1)S(1)}, bf16[512,768]{1,0:T(8,128)(2,1)S(1)}) custom-call(s32[3]{0:T(128)S(1)} %pad_add_fusion.place, bf16[1024,2048]{1,0:T(8,128)(2,1)S(1)} %copy-done.33, bf16[1024,768]{1,0:T(8,128)(2,1)S(1)} %get-tuple-element.31.gate_delta.gd, ...), custom_call_target="tpu_custom_call" | custom-call | flops 3221225472 | bytes 10485760 | tf_op jit(solution)/shard_map/pallas_call | solution.py:31
  214.5 1.6 collective-permute-start.34
  216.1 1.5 collective-permute-start.33
  217.8 2.3 collective-permute-done.40
  220.2 0.9 add_convert_fusion
  221.2 3.1 %collective-permute-start.31 = (bf16[128,2048]{1,0:T(8,128)(2,1)S(1)}, bf16[128,2048]{1,0:T(8,128)(2,1)S(1)}, u32[]{:S(2)}, u32[]{:S(2)}) collective-permute-start(bf16[128,2048]{1,0:T(8,128)(2,1)S(1)} %get-tuple-element.51), channel_id=1, source_target_pairs={{0,2},{1,3},{6,4},{7,5},{8,10},{9,11},{14,12},{15,13},{16,18},{17,... | collective-permute-start | bytes 1572872 | tf_op jit(solution)/shard_map/ppermute | solution.py:286
  224.4 25.6 %collective-permute-done.34 = bf16[2,512,768]{2,1,0:T(8,128)(2,1)S(1)} collective-permute-done((bf16[2,512,768]{2,1,0:T(8,128)(2,1)S(1)}, bf16[2,512,768]{2,1,0:T(8,128)(2,1)S(1)}, u32[]{:S(2)}, u32[]{:S(2)}) %collective-permute-start.34) | collective-permute-done | bytes 1572896 | tf_op jit(solution)/shard_map/ppermute | solution.py:283
  250.4 0.9 collective-permute-start.36
  251.4 1.7 collective-permute-done.33
  253.5 1.6 collective-permute-start.35
  255.1 0.9 maximum_bitcast_fusion
  256.7 2.8 collective-permute-start.30
  260.0 9.0 %collective-permute-done.36 = bf16[512,768]{1,0:T(8,128)(2,1)S(1)} collective-permute-done((bf16[512,768]{1,0:T(8,128)(2,1)S(1)}, bf16[512,768]{1,0:T(8,128)(2,1)S(1)}, u32[]{:S(2)}, u32[]{:S(2)}) %collective-permute-start.36) | collective-permute-done | bytes 786464 | tf_op jit(solution)/shard_map/ppermute | solution.py:280
  269.0 1.1 fusion.5
  270.7 1.1 fusion.4
  271.8 19.0 %collective-permute-done.32 = bf16[128,2048]{1,0:T(8,128)(2,1)S(1)} collective-permute-done((bf16[128,2048]{1,0:T(8,128)(2,1)S(1)}, bf16[128,2048]{1,0:T(8,128)(2,1)S(1)}, u32[]{:S(2)}, u32[]{:S(2)}) %collective-permute-start.32) | collective-permute-done | bytes 524320 | tf_op jit(solution)/shard_map/ppermute | solution.py:286
  290.8 1.1 add_convert_fusion.3
  (110 shorter events, 15.1 us)
Async XLA Ops:
  0.6 29.3 %collective-permute-start.9 = (bf16[128,2048]{1,0:T(8,128)(2,1)}, bf16[128,2048]{1,0:T(8,128)(2,1)S(1)}, u32[]{:S(2)}, u32[]{:S(2)}) collective-permute-start(bf16[128,2048]{1,0:T(8,128)(2,1)} %refs_0_.1), channel_id=1, source_target_pairs={{0,4},{1,5},{2,6},{3,7},{4,0},{5,1},{6,2},{7,3},{8,12},{9,13},{10,... | collective-permute-start | bytes 1572872 | tf_op jit(solution)/shard_map/ppermute | solution.py:286
  4.8 25.1 %collective-permute-start.10 = (bf16[128,2048]{1,0:T(8,128)(2,1)}, bf16[128,2048]{1,0:T(8,128)(2,1)S(1)}, u32[]{:S(2)}, u32[]{:S(2)}) collective-permute-start(bf16[128,2048]{1,0:T(8,128)(2,1)} %refs_0_.1), channel_id=1, source_target_pairs={{0,2},{1,3},{2,0},{3,1},{4,6},{5,7},{6,4},{7,5},{8,10},{9,11},{10,... | collective-permute-start | bytes 1572872 | tf_op jit(solution)/shard_map/ppermute | solution.py:286
  6.3 24.3 %collective-permute-start.11 = (bf16[128,2048]{1,0:T(8,128)(2,1)}, bf16[128,2048]{1,0:T(8,128)(2,1)S(1)}, u32[]{:S(2)}, u32[]{:S(2)}) collective-permute-start(bf16[128,2048]{1,0:T(8,128)(2,1)} %refs_0_.1), channel_id=1, source_target_pairs={{2,4},{3,5},{4,2},{5,3},{10,12},{11,13},{12,10},{13,11},{18,20},{1... | collective-permute-start | bytes 1572872 | tf_op jit(solution)/shard_map/ppermute | solution.py:286
  7.0 23.7 %collective-permute-start.13 = (bf16[128,2048]{1,0:T(8,128)(2,1)}, bf16[128,2048]{1,0:T(8,128)(2,1)S(1)}, u32[]{:S(2)}, u32[]{:S(2)}) collective-permute-start(bf16[128,2048]{1,0:T(8,128)(2,1)} %refs_0_.1), channel_id=1, source_target_pairs={{0,1},{1,0},{2,3},{3,2},{4,5},{5,4},{6,7},{7,6},{8,9},{9,8},{10,11... | collective-permute-start | bytes 1572872 | tf_op jit(solution)/shard_map/ppermute | solution.py:289
  7.1 1.0 copy-start.5
  9.6 54.5 %collective-permute-start = (bf16[128,2176]{1,0:T(8,128)(2,1)S(1)}, bf16[128,2176]{1,0:T(8,128)(2,1)S(1)}, u32[]{:S(2)}, u32[]{:S(2)}) collective-permute-start(bf16[128,2176]{1,0:T(8,128)(2,1)S(1)} %shard_map.102.refs_0_), channel_id=1, source_target_pairs={{0,4},{1,5},{2,6},{3,7},{4,0},{5,1},{6,2},{7,3},{8,12},{9,13},{10,... | collective-permute-start | bytes 1671176 | tf_op jit(solution)/shard_map/ppermute | solution.py:286
  29.9 36.1 %collective-permute-start.1 = (bf16[128,2176]{1,0:T(8,128)(2,1)S(1)}, bf16[128,2176]{1,0:T(8,128)(2,1)S(1)}, u32[]{:S(2)}, u32[]{:S(2)}) collective-permute-start(bf16[128,2176]{1,0:T(8,128)(2,1)S(1)} %shard_map.102.refs_0_), channel_id=1, source_target_pairs={{0,2},{1,3},{2,0},{3,1},{4,6},{5,7},{6,4},{7,5},{8,10},{9,11},{10,... | collective-permute-start | bytes 1671176 | tf_op jit(solution)/shard_map/ppermute | solution.py:286
  29.9 36.3 %collective-permute-start.2 = (bf16[128,2176]{1,0:T(8,128)(2,1)S(1)}, bf16[128,2176]{1,0:T(8,128)(2,1)S(1)}, u32[]{:S(2)}, u32[]{:S(2)}) collective-permute-start(bf16[128,2176]{1,0:T(8,128)(2,1)S(1)} %shard_map.102.refs_0_), channel_id=1, source_target_pairs={{2,4},{3,5},{4,2},{5,3},{10,12},{11,13},{12,10},{13,11},{18,20},{1... | collective-permute-start | bytes 1671176 | tf_op jit(solution)/shard_map/ppermute | solution.py:286
  30.6 37.4 %collective-permute-start.4 = (bf16[128,2176]{1,0:T(8,128)(2,1)S(1)}, bf16[128,2176]{1,0:T(8,128)(2,1)S(1)}, u32[]{:S(2)}, u32[]{:S(2)}) collective-permute-start(bf16[128,2176]{1,0:T(8,128)(2,1)S(1)} %shard_map.102.refs_0_), channel_id=1, source_target_pairs={{0,1},{1,0},{2,3},{3,2},{4,5},{5,4},{6,7},{7,6},{8,9},{9,8},{10,11... | collective-permute-start | bytes 1671176 | tf_op jit(solution)/shard_map/ppermute | solution.py:289
  31.5 38.8 %collective-permute-start.18 = (bf16[512,768]{1,0:T(8,128)(2,1)}, bf16[512,768]{1,0:T(8,128)(2,1)}, u32[]{:S(2)}, u32[]{:S(2)}) collective-permute-start(bf16[512,768]{1,0:T(8,128)(2,1)} %bitcast.59), channel_id=1, source_target_pairs={{0,8},{8,0},{16,24},{24,16},{1,9},{9,1},{17,25},{25,17},{2,10},{10... | collective-permute-start | bytes 2359304 | tf_op jit(solution)/shard_map/ppermute | solution.py:280
  64.1 20.7 %collective-permute-start.22 = (bf16[512,768]{1,0:T(8,128)(2,1)}, bf16[512,768]{1,0:T(8,128)(2,1)}, u32[]{:S(2)}, u32[]{:S(2)}) collective-permute-start(bf16[512,768]{1,0:T(8,128)(2,1)} %bitcast.63), channel_id=1, source_target_pairs={{0,16},{8,24},{16,0},{24,8},{1,17},{9,25},{17,1},{25,9},{2,18},{10... | collective-permute-start | bytes 2359304 | tf_op jit(solution)/shard_map/ppermute | solution.py:283
  66.0 35.7 %collective-permute-start.19 = (bf16[512,768]{1,0:T(8,128)(2,1)}, bf16[512,768]{1,0:T(8,128)(2,1)S(1)}, u32[]{:S(2)}, u32[]{:S(2)}) collective-permute-start(bf16[512,768]{1,0:T(8,128)(2,1)} %bitcast.60), channel_id=1, source_target_pairs={{0,16},{8,24},{16,0},{24,8},{1,17},{9,25},{17,1},{25,9},{2,18},{10... | collective-permute-start | bytes 2359304 | tf_op jit(solution)/shard_map/ppermute | solution.py:283
  66.2 1.8 copy-start.1
  66.2 37.1 %collective-permute-start.21 = (bf16[512,768]{1,0:T(8,128)(2,1)}, bf16[512,768]{1,0:T(8,128)(2,1)S(1)}, u32[]{:S(2)}, u32[]{:S(2)}) collective-permute-start(bf16[512,768]{1,0:T(8,128)(2,1)} %bitcast.64), channel_id=1, source_target_pairs={{0,8},{8,0},{16,24},{24,16},{1,9},{9,1},{17,25},{25,17},{2,10},{10... | collective-permute-start | bytes 2359304 | tf_op jit(solution)/shard_map/ppermute | solution.py:280
  68.9 47.1 %collective-permute-start.25 = (bf16[768,512]{1,0:T(8,128)(2,1)}, bf16[768,512]{1,0:T(8,128)(2,1)S(1)}, u32[]{:S(2)}, u32[]{:S(2)}) collective-permute-start(bf16[768,512]{1,0:T(8,128)(2,1)} %bitcast.54), channel_id=1, source_target_pairs={{0,16},{8,24},{16,0},{24,8},{1,17},{9,25},{17,1},{25,9},{2,18},{10... | collective-permute-start | bytes 2359304 | tf_op jit(solution)/shard_map/ppermute | solution.py:283
  70.4 47.0 %collective-permute-start.24 = (bf16[768,512]{1,0:T(8,128)(2,1)}, bf16[768,512]{1,0:T(8,128)(2,1)S(1)}, u32[]{:S(2)}, u32[]{:S(2)}) collective-permute-start(bf16[768,512]{1,0:T(8,128)(2,1)} %bitcast.55), channel_id=1, source_target_pairs={{0,8},{8,0},{16,24},{24,16},{1,9},{9,1},{17,25},{25,17},{2,10},{10... | collective-permute-start | bytes 2359304 | tf_op jit(solution)/shard_map/ppermute | solution.py:280
  84.9 33.8 %collective-permute-start.12 = (bf16[128,2048]{1,0:T(8,128)(2,1)S(1)}, bf16[128,2048]{1,0:T(8,128)(2,1)}, u32[]{:S(2)}, u32[]{:S(2)}) collective-permute-start(bf16[128,2048]{1,0:T(8,128)(2,1)S(1)} %collective-permute-done.9.refs_1_), channel_id=1, source_target_pairs={{4,6},{5,7},{2,0},{3,1},{12,14},{13,15},{10,8},{11,9},{20,22},{21,... | collective-permute-start | bytes 1572872 | tf_op jit(solution)/shard_map/ppermute | solution.py:286
  102.5 17.7 %collective-permute-start.14 = (bf16[128,2048]{1,0:T(8,128)(2,1)S(1)}, bf16[128,2048]{1,0:T(8,128)(2,1)S(1)}, u32[]{:S(2)}, u32[]{:S(2)}) collective-permute-start(bf16[128,2048]{1,0:T(8,128)(2,1)S(1)} %collective-permute-done.9.refs_1_), channel_id=1, source_target_pairs={{0,1},{1,0},{2,3},{3,2},{4,5},{5,4},{6,7},{7,6},{8,9},{9,8},{10,11... | collective-permute-start | bytes 1572872 | tf_op jit(solution)/shard_map/ppermute | solution.py:289
  103.3 0.9 copy-start.14
  104.2 18.1 %collective-permute-start.15 = (bf16[128,2048]{1,0:T(8,128)(2,1)S(1)}, bf16[128,2048]{1,0:T(8,128)(2,1)S(1)}, u32[]{:S(2)}, u32[]{:S(2)}) collective-permute-start(bf16[128,2048]{1,0:T(8,128)(2,1)S(1)} %collective-permute-done.10.refs_2_), channel_id=1, source_target_pairs={{0,1},{1,0},{2,3},{3,2},{4,5},{5,4},{6,7},{7,6},{8,9},{9,8},{10,11... | collective-permute-start | bytes 1572872 | tf_op jit(solution)/shard_map/ppermute | solution.py:289
  115.9 7.2 %collective-permute-start.16 = (bf16[128,2048]{1,0:T(8,128)(2,1)S(1)}, bf16[128,2048]{1,0:T(8,128)(2,1)S(1)}, u32[]{:S(2)}, u32[]{:S(2)}) collective-permute-start(bf16[128,2048]{1,0:T(8,128)(2,1)S(1)} %collective-permute-done.11.refs_3_), channel_id=1, source_target_pairs={{2,3},{3,2},{4,5},{5,4},{10,11},{11,10},{12,13},{13,12},{18,19},{1... | collective-permute-start | bytes 1572872 | tf_op jit(solution)/shard_map/ppermute | solution.py:289
  117.4 21.9 %collective-permute-start.20 = (bf16[512,768]{1,0:T(8,128)(2,1)}, bf16[512,768]{1,0:T(8,128)(2,1)}, u32[]{:S(2)}, u32[]{:S(2)}) collective-permute-start(bf16[512,768]{1,0:T(8,128)(2,1)} %collective-permute-done.18.refs_11_.refs_1_), channel_id=1, source_target_pairs={{0,16},{8,24},{16,0},{24,8},{1,17},{9,25},{17,1},{25,9},{2,18},{10... | collective-permute-start | bytes 2359304 | tf_op jit(solution)/shard_map/ppermute | solution.py:283
  118.7 21.1 %collective-permute-start.23 = (bf16[512,768]{1,0:T(8,128)(2,1)}, bf16[512,768]{1,0:T(8,128)(2,1)}, u32[]{:S(2)}, u32[]{:S(2)}) collective-permute-start(bf16[512,768]{1,0:T(8,128)(2,1)} %collective-permute-done.22.refs_16_.refs_6_), channel_id=1, source_target_pairs={{0,8},{8,0},{16,24},{24,16},{1,9},{9,1},{17,25},{25,17},{2,10},{10... | collective-permute-start | bytes 2359304 | tf_op jit(solution)/shard_map/ppermute | solution.py:280
  121.0 17.0 %collective-permute-start.3 = (bf16[128,2176]{1,0:T(8,128)(2,1)S(1)}, bf16[128,2176]{1,0:T(8,128)(2,1)}, u32[]{:S(2)}, u32[]{:S(2)}) collective-permute-start(bf16[128,2176]{1,0:T(8,128)(2,1)S(1)} %collective-permute-done.refs_1_), channel_id=1, source_target_pairs={{4,6},{5,7},{2,0},{3,1},{12,14},{13,15},{10,8},{11,9},{20,22},{21,... | collective-permute-start | bytes 1671176 | tf_op jit(solution)/shard_map/ppermute | solution.py:286
  123.1 14.9 %collective-permute-start.5 = (bf16[128,2176]{1,0:T(8,128)(2,1)S(1)}, bf16[128,2176]{1,0:T(8,128)(2,1)}, u32[]{:S(2)}, u32[]{:S(2)}) collective-permute-start(bf16[128,2176]{1,0:T(8,128)(2,1)S(1)} %collective-permute-done.refs_1_), channel_id=1, source_target_pairs={{0,1},{1,0},{2,3},{3,2},{4,5},{5,4},{6,7},{7,6},{8,9},{9,8},{10,11... | collective-permute-start | bytes 1671176 | tf_op jit(solution)/shard_map/ppermute | solution.py:289
  123.9 14.8 %collective-permute-start.17 = (bf16[128,2048]{1,0:T(8,128)(2,1)}, bf16[128,2048]{1,0:T(8,128)(2,1)}, u32[]{:S(2)}, u32[]{:S(2)}) collective-permute-start(bf16[128,2048]{1,0:T(8,128)(2,1)} %collective-permute-done.12.refs_4_), channel_id=1, source_target_pairs={{0,1},{1,0},{6,7},{7,6},{8,9},{9,8},{14,15},{15,14},{16,17},{17,16... | collective-permute-start | bytes 1572872 | tf_op jit(solution)/shard_map/ppermute | solution.py:289
  126.3 11.7 %copy-start.2 = (bf16[128,2176]{1,0:T(8,128)(2,1)S(1)}, bf16[128,2176]{1,0:T(8,128)(2,1)}, u32[]{:S(2)}) copy-start(bf16[128,2176]{1,0:T(8,128)(2,1)} %copy-done.1) | copy-start | bytes 1671172
  126.3 15.4 %copy-start.8 = (bf16[1,512,768]{2,1,0:T(8,128)(2,1)S(1)}, bf16[1,512,768]{2,1,0:T(8,128)(2,1)}, u32[]{:S(2)}) copy-start(bf16[1,512,768]{2,1,0:T(8,128)(2,1)} %param.11) | copy-start | bytes 2359300
  126.5 40.0 %copy-start.4 = (bf16[128,2176]{1,0:T(8,128)(2,1)S(1)}, bf16[128,2176]{1,0:T(8,128)(2,1)}, u32[]{:S(2)}) copy-start(bf16[128,2176]{1,0:T(8,128)(2,1)} %copy-done.3) | copy-start | bytes 1671172
  138.0 28.5 %collective-permute-start.6 = (bf16[128,2176]{1,0:T(8,128)(2,1)S(1)}, bf16[128,2176]{1,0:T(8,128)(2,1)S(1)}, u32[]{:S(2)}, u32[]{:S(2)}) collective-permute-start(bf16[128,2176]{1,0:T(8,128)(2,1)S(1)} %collective-permute-done.1.refs_2_), channel_id=1, source_target_pairs={{0,1},{1,0},{2,3},{3,2},{4,5},{5,4},{6,7},{7,6},{8,9},{9,8},{10,11... | collective-permute-start | bytes 1671176 | tf_op jit(solution)/shard_map/ppermute | solution.py:289
  138.0 28.5 %collective-permute-start.7 = (bf16[128,2176]{1,0:T(8,128)(2,1)S(1)}, bf16[128,2176]{1,0:T(8,128)(2,1)S(1)}, u32[]{:S(2)}, u32[]{:S(2)}) collective-permute-start(bf16[128,2176]{1,0:T(8,128)(2,1)S(1)} %copy-done.2), channel_id=1, source_target_pairs={{2,3},{3,2},{4,5},{5,4},{10,11},{11,10},{12,13},{13,12},{18,19},{1... | collective-permute-start | bytes 1671176 | tf_op jit(solution)/shard_map/ppermute | solution.py:289
  138.7 34.4 %collective-permute-start.26 = (bf16[384,512]{1,0:T(8,128)(2,1)S(1)}, bf16[384,512]{1,0:T(8,128)(2,1)S(1)}, u32[]{:S(2)}, u32[]{:S(2)}) collective-permute-start(bf16[384,512]{1,0:T(8,128)(2,1)S(1)} %slice.61), channel_id=1, source_target_pairs={{0,8},{8,0},{16,24},{24,16},{1,9},{9,1},{17,25},{25,17},{2,10},{10... | collective-permute-start | bytes 1179656 | tf_op jit(solution)/shard_map/ppermute | solution.py:280
  139.3 33.8 %collective-permute-start.27 = (bf16[384,512]{1,0:T(8,128)(2,1)S(1)}, bf16[384,512]{1,0:T(8,128)(2,1)S(1)}, u32[]{:S(2)}, u32[]{:S(2)}) collective-permute-start(bf16[384,512]{1,0:T(8,128)(2,1)S(1)} %slice.62), channel_id=1, source_target_pairs={{0,16},{8,24},{16,0},{24,8},{1,17},{9,25},{17,1},{25,9},{2,18},{10... | collective-permute-start | bytes 1179656 | tf_op jit(solution)/shard_map/ppermute | solution.py:283
  139.8 26.7 %collective-permute-start.8 = (bf16[128,2176]{1,0:T(8,128)(2,1)}, bf16[128,2176]{1,0:T(8,128)(2,1)S(1)}, u32[]{:S(2)}, u32[]{:S(2)}) collective-permute-start(bf16[128,2176]{1,0:T(8,128)(2,1)} %collective-permute-done.3.refs_4_), channel_id=1, source_target_pairs={{0,1},{1,0},{6,7},{7,6},{8,9},{9,8},{14,15},{15,14},{16,17},{17,16... | collective-permute-start | bytes 1671176 | tf_op jit(solution)/shard_map/ppermute | solution.py:289
  141.7 1.1 copy-start.9
  142.9 1.1 copy-start.12
  144.0 1.1 copy-start.15
  145.1 1.0 copy-start.17
  146.2 1.0 copy-start.19
  147.2 1.0 copy-start.21
  148.3 1.0 copy-start.23
  149.3 1.0 copy-start.25
  150.4 1.0 copy-start.27
  151.4 1.0 copy-start.29
  152.4 1.0 copy-start.31
  164.5 2.0 copy-start.32
  166.5 6.6 %copy-start = (bf16[1,768,512]{2,1,0:T(8,128)(2,1)S(1)}, bf16[1,768,512]{2,1,0:T(8,128)(2,1)}, u32[]{:S(2)}) copy-start(bf16[1,768,512]{2,1,0:T(8,128)(2,1)} %param.13) | copy-start | bytes 2359300
  171.6 25.8 %collective-permute-start.37 = (bf16[2,384,512]{2,1,0:T(8,128)(2,1)S(1)}, bf16[2,384,512]{2,1,0:T(8,128)(2,1)S(1)}, u32[]{:S(2)}, u32[]{:S(2)}) collective-permute-start(bf16[2,384,512]{2,1,0:T(8,128)(2,1)S(1)} %get-tuple-element.45), channel_id=1, source_target_pairs={{0,8},{8,0},{16,24},{24,16},{1,9},{9,1},{17,25},{25,17},{2,10},{10... | collective-permute-start | bytes 2359304 | tf_op jit(solution)/shard_map/ppermute | solution.py:280
  173.1 5.7 %copy-start.10 = (bf16[1,512,768]{2,1,0:T(8,128)(2,1)S(1)}, bf16[1,512,768]{2,1,0:T(8,128)(2,1)}, u32[]{:S(2)}) copy-start(bf16[1,512,768]{2,1,0:T(8,128)(2,1)} %param.12) | copy-start | bytes 2359300
  173.2 5.7 %copy-start.13 = (bf16[512,768]{1,0:T(8,128)(2,1)S(1)}, bf16[512,768]{1,0:T(8,128)(2,1)}, u32[]{:S(2)}) copy-start(bf16[512,768]{1,0:T(8,128)(2,1)} %copy-done.11) | copy-start | bytes 2359300
  173.2 5.7 %copy-start.16 = (bf16[512,768]{1,0:T(8,128)(2,1)S(1)}, bf16[512,768]{1,0:T(8,128)(2,1)}, u32[]{:S(2)}) copy-start(bf16[512,768]{1,0:T(8,128)(2,1)} %copy-done.14) | copy-start | bytes 2359300
  187.8 32.4 %collective-permute-start.28 = (bf16[512,2048]{1,0:T(8,128)(2,1)S(1)}, bf16[512,2048]{1,0:T(8,128)(2,1)S(1)}, u32[]{:S(2)}, u32[]{:S(2)}) collective-permute-start(bf16[512,2048]{1,0:T(8,128)(2,1)S(1)} %get-tuple-element.34), channel_id=1, source_target_pairs={{0,1},{1,0},{2,3},{3,2},{4,5},{5,4},{6,7},{7,6},{8,9},{9,8},{10,11... | collective-permute-start | bytes 6291464 | tf_op jit(solution)/shard_map/ppermute | solution.py:289
  188.1 3.9 %copy-start.33 = (bf16[1024,2048]{1,0:T(8,128)(2,1)S(1)}, bf16[1024,2048]{1,0:T(8,128)(2,1)}, u32[]{:S(2)}) copy-start(bf16[1024,2048]{1,0:T(8,128)(2,1)} %copy-done.32) | copy-start | bytes 12582916
  188.1 20.4 %collective-permute-start.39 = (bf16[2,384,512]{2,1,0:T(8,128)(2,1)S(1)}, bf16[2,384,512]{2,1,0:T(8,128)(2,1)S(1)}, u32[]{:S(2)}, u32[]{:S(2)}) collective-permute-start(bf16[2,384,512]{2,1,0:T(8,128)(2,1)S(1)} %get-tuple-element.48), channel_id=1, source_target_pairs={{0,16},{8,24},{16,0},{24,8},{1,17},{9,25},{17,1},{25,9},{2,18},{10... | collective-permute-start | bytes 2359304 | tf_op jit(solution)/shard_map/ppermute | solution.py:283
  197.4 20.2 %collective-permute-start.38 = (bf16[384,512]{1,0:T(8,128)(2,1)S(1)}, bf16[384,512]{1,0:T(8,128)(2,1)S(1)}, u32[]{:S(2)}, u32[]{:S(2)}) collective-permute-start(bf16[384,512]{1,0:T(8,128)(2,1)S(1)} %fusion.9), channel_id=1, source_target_pairs={{0,16},{8,24},{16,0},{24,8},{1,17},{9,25},{17,1},{25,9},{2,18},{10... | collective-permute-start | bytes 1179656 | tf_op jit(solution)/shard_map/ppermute | solution.py:283
  208.6 11.4 %collective-permute-start.40 = (bf16[384,512]{1,0:T(8,128)(2,1)S(1)}, bf16[384,512]{1,0:T(8,128)(2,1)S(1)}, u32[]{:S(2)}, u32[]{:S(2)}) collective-permute-start(bf16[384,512]{1,0:T(8,128)(2,1)S(1)} %fusion.6), channel_id=1, source_target_pairs={{0,8},{8,0},{16,24},{24,16},{1,9},{9,1},{17,25},{25,17},{2,10},{10... | collective-permute-start | bytes 1179656 | tf_op jit(solution)/shard_map/ppermute | solution.py:280
  214.5 35.5 %collective-permute-start.34 = (bf16[2,512,768]{2,1,0:T(8,128)(2,1)S(1)}, bf16[2,512,768]{2,1,0:T(8,128)(2,1)S(1)}, u32[]{:S(2)}, u32[]{:S(2)}) collective-permute-start(bf16[2,512,768]{2,1,0:T(8,128)(2,1)S(1)} %get-tuple-element.39), channel_id=1, source_target_pairs={{0,16},{8,24},{16,0},{24,8},{1,17},{9,25},{17,1},{25,9},{2,18},{10... | collective-permute-start | bytes 4718600 | tf_op jit(solution)/shard_map/ppermute | solution.py:283
  216.1 36.9 %collective-permute-start.33 = (bf16[2,512,768]{2,1,0:T(8,128)(2,1)S(1)}, bf16[2,512,768]{2,1,0:T(8,128)(2,1)S(1)}, u32[]{:S(2)}, u32[]{:S(2)}) collective-permute-start(bf16[2,512,768]{2,1,0:T(8,128)(2,1)S(1)} %get-tuple-element.37), channel_id=1, source_target_pairs={{0,8},{8,0},{16,24},{24,16},{1,9},{9,1},{17,25},{25,17},{2,10},{10... | collective-permute-start | bytes 4718600 | tf_op jit(solution)/shard_map/ppermute | solution.py:280
  221.2 38.3 %collective-permute-start.31 = (bf16[128,2048]{1,0:T(8,128)(2,1)S(1)}, bf16[128,2048]{1,0:T(8,128)(2,1)S(1)}, u32[]{:S(2)}, u32[]{:S(2)}) collective-permute-start(bf16[128,2048]{1,0:T(8,128)(2,1)S(1)} %get-tuple-element.51), channel_id=1, source_target_pairs={{0,2},{1,3},{6,4},{7,5},{8,10},{9,11},{14,12},{15,13},{16,18},{17,... | collective-permute-start | bytes 1572872 | tf_op jit(solution)/shard_map/ppermute | solution.py:286
  250.4 18.6 %collective-permute-start.36 = (bf16[512,768]{1,0:T(8,128)(2,1)S(1)}, bf16[512,768]{1,0:T(8,128)(2,1)S(1)}, u32[]{:S(2)}, u32[]{:S(2)}) collective-permute-start(bf16[512,768]{1,0:T(8,128)(2,1)S(1)} %get-tuple-element.52), channel_id=1, source_target_pairs={{0,8},{8,0},{16,24},{24,16},{1,9},{9,1},{17,25},{25,17},{2,10},{10... | collective-permute-start | bytes 2359304 | tf_op jit(solution)/shard_map/ppermute | solution.py:280
  253.5 17.2 %collective-permute-start.35 = (bf16[512,768]{1,0:T(8,128)(2,1)S(1)}, bf16[512,768]{1,0:T(8,128)(2,1)S(1)}, u32[]{:S(2)}, u32[]{:S(2)}) collective-permute-start(bf16[512,768]{1,0:T(8,128)(2,1)S(1)} %get-tuple-element.55), channel_id=1, source_target_pairs={{0,16},{8,24},{16,0},{24,8},{1,17},{9,25},{17,1},{25,9},{2,18},{10... | collective-permute-start | bytes 2359304 | tf_op jit(solution)/shard_map/ppermute | solution.py:283
  256.0 15.8 %collective-permute-start.29 = (bf16[128,2048]{1,0:T(8,128)(2,1)S(1)}, bf16[128,2048]{1,0:T(8,128)(2,1)S(1)}, u32[]{:S(2)}, u32[]{:S(2)}) collective-permute-start(bf16[128,2048]{1,0:T(8,128)(2,1)S(1)} %get-tuple-element.51), channel_id=1, source_target_pairs={{2,4},{3,5},{4,2},{5,3},{10,12},{11,13},{12,10},{13,11},{18,20},{1... | collective-permute-start | bytes 1572872 | tf_op jit(solution)/shard_map/ppermute | solution.py:286
  256.7 15.2 %collective-permute-start.30 = (bf16[128,2048]{1,0:T(8,128)(2,1)S(1)}, bf16[128,2048]{1,0:T(8,128)(2,1)S(1)}, u32[]{:S(2)}, u32[]{:S(2)}) collective-permute-start(bf16[128,2048]{1,0:T(8,128)(2,1)S(1)} %get-tuple-element.50), channel_id=1, source_target_pairs={{0,2},{1,3},{2,0},{3,1},{4,6},{5,7},{6,4},{7,5},{8,10},{9,11},{10,... | collective-permute-start | bytes 1572872 | tf_op jit(solution)/shard_map/ppermute | solution.py:286
  259.7 31.2 %collective-permute-start.32 = (bf16[128,2048]{1,0:T(8,128)(2,1)S(1)}, bf16[128,2048]{1,0:T(8,128)(2,1)S(1)}, u32[]{:S(2)}, u32[]{:S(2)}) collective-permute-start(bf16[128,2048]{1,0:T(8,128)(2,1)S(1)} %add_convert_fusion.4), channel_id=1, source_target_pairs={{0,4},{1,5},{2,6},{3,7},{4,0},{5,1},{6,2},{7,3},{8,12},{9,13},{10,... | collective-permute-start | bytes 1572872 | tf_op jit(solution)/shard_map/ppermute | solution.py:286
  (11 other events, 8.7 us)

commit v3 on v2

--- a/solution.py
+++ b/solution.py
@@ -27,9 +27,10 @@
     return min(tok_rows, max(2, 9 * tok_rows * top_count // (8 * expert_count)))
 
 
-def call(body, outs, ins, scratch, flops, moved):
+def call(body, outs, ins, scratch, flops, moved, aliases=None):
     return pl.pallas_call(
         body,
+        input_output_aliases=aliases or {},
         out_shape=[jax.ShapeDtypeStruct(s, d) for s, d, _ in outs],
         in_specs=[s for _, s in ins],
         out_specs=[s for _, _, s in outs],
@@ -84,40 +85,25 @@
         return pltpu.make_async_copy(other, dst, sem)
 
 
-def load_rows(copies, chip, pieces, dst):
+def load_early(copies, pieces, dst):
+    tok = pieces[0].shape[0]
+    return [copies.start(src, dst.at[pl.ds(i * tok, tok)]) for i, src in enumerate(pieces)]
+
+
+def load_late(copies, chip, pieces, dst):
     tok = pieces[0].shape[0]
     middle = jnp.logical_or(chip == 1, chip == 2)
-    started = []
-    for core in (0, 1):
-        own, two, outer, inner, far = pieces[5 * core : 5 * core + 5]
-        at = [dst.at[pl.ds((4 * core + s) * tok, tok)] for s in range(4)]
-        for src, to in zip((own, two, outer), at):
-            started.append(copies.start(src, to))
-        started.append(copies.pick(middle, inner, far, at[3]))
-    return started
-
-
-def pre_body(place, *refs):
-    pieces, w_gate, w_up = refs[:10], refs[10:14], refs[14:18]
-    act, active_out, slope_out, x_out, x, wg, wu, sems = refs[18:]
-    me, chip = place[0], place[1]
-    copies = Copies(sems)
-    rows = load_rows(copies, chip, pieces, x)
-    share, hidden = w_gate[0].shape
-    weights = []
-    for k in range(4):
-        at = pl.ds((me ^ k) * share, share)
-        weights += [copies.start(w_gate[k], wg.at[at]), copies.start(w_up[k], wu.at[at])]
-    for c in rows:
-        c.wait()
-    out = copies.start(x, x_out)
-    for c in weights:
-        c.wait()
-    tm, tn = x.shape[0] // 2, 256
+    return [
+        copies.pick(middle, pieces[2 * core], pieces[2 * core + 1], dst.at[pl.ds(core * tok, tok)]) for core in (0, 1)
+    ]
+
+
+def pre_blocks(x, first, count, wg, wu, act, active_out, slope_out):
+    tn = 256
 
     def step(i, _):
-        r = pl.ds(pl.multiple_of(i // (hidden // tn) * tm, tm), tm)
-        c = pl.ds(pl.multiple_of(i % (hidden // tn) * tn, tn), tn)
+        r = slice(first, first + count)
+        c = pl.ds(pl.multiple_of(i * tn, tn), tn)
         lhs = x[r, :]
         gate = mm(lhs, wg[:, c], NN)
         up = mm(lhs, wu[:, c], NN)
@@ -128,29 +114,60 @@
         slope_out[r, c] = up * sigma * (1.0 + gate * (1.0 - sigma))
         return 0
 
-    lax.fori_loop(0, 2 * (hidden // tn), step, 0)
-    out.wait()
-
-
-def down_send_body(experts, place, *refs):
-    pieces, act = refs[:10], refs[10]
-    send_a, send_b, y, raw, sems = refs[11:]
-    chip, expert = place[1], place[2]
+    lax.fori_loop(0, wg.shape[1] // tn, step, 0)
+
+
+def pre_early_body(place, *refs):
+    pieces, w_gate, w_up = refs[:6], refs[6:10], refs[10:14]
+    act, active, slope, x, wg, wu, sems = refs[14:]
     copies = Copies(sems)
-    for c in load_rows(copies, chip, pieces, raw):
+    share = w_gate[0].shape[0]
+    started = load_early(copies, pieces, x)
+    for k in range(4):
+        at = pl.ds((place[0] ^ k) * share, share)
+        started += [copies.start(w_gate[k], wg.at[at]), copies.start(w_up[k], wu.at[at])]
+    for c in started:
         c.wait()
-    rows, width = y.shape
-    tok = rows // 8
+    pre_blocks(x, 0, x.shape[0] // 4 * 3, wg, wu, act, active, slope)
+
+
+def pre_late_body(place, *refs):
+    pieces, wg, wu = refs[:4], refs[4], refs[5]
+    act, active, slope, x, sems = refs[10:]
+    count = x.shape[0] // 4
+    for c in load_late(Copies(sems), place[1], pieces, x.at[pl.ds(3 * count, count)]):
+        c.wait()
+    pre_blocks(x, 3 * count, count, wg, wu, act, active, slope)
+
+
+def scale(experts, expert, raw, y, first):
+    tok, width = raw.shape[0] // 2, y.shape[1]
     lane = lax.broadcasted_iota(jnp.int32, (tok, LANES), 1)
     mine = jnp.logical_and(lane % experts == expert, lane < 3 * experts)
-
-    def scale(i, _):
-        r = pl.ds(pl.multiple_of(i * tok, tok), tok)
-        gate = jnp.sum(jnp.where(mine, raw[r, width:].astype(F32), 0.0), axis=1, keepdims=True)
-        y[r, :] = (raw[r, :width].astype(F32) * gate).astype(BF16)
-        return 0
-
-    lax.fori_loop(0, 8, scale, 0)
+    for i in (0, 1):
+        gate = jnp.sum(jnp.where(mine, raw[i * tok : (i + 1) * tok, width:].astype(F32), 0.0), axis=1, keepdims=True)
+        y[first + i * tok : first + (i + 1) * tok, :] = (raw[i * tok : (i + 1) * tok, :width].astype(F32) * gate).astype(
+            BF16
+        )
+
+
+def scale_early_body(experts, place, *refs):
+    pieces = refs[:6]
+    y, raw, sems = refs[6:]
+    tok = pieces[0].shape[0]
+    started = load_early(Copies(sems), pieces, raw)
+    for i in range(3):
+        started[2 * i].wait()
+        started[2 * i + 1].wait()
+        scale(experts, place[2], raw.at[pl.ds(2 * i * tok, 2 * tok)], y, 2 * i * tok)
+
+
+def down_send_body(experts, place, *refs):
+    pieces, act = refs[:4], refs[4]
+    send_a, send_b, y, raw, sems = refs[6:]
+    for c in load_late(Copies(sems), place[1], pieces, raw):
+        c.wait()
+    scale(experts, place[2], raw, y, y.shape[0] - raw.shape[0])
     down_blocks(place, act, y, ((0, 1, send_a, 0), (0, 3, send_a, 1), (1, 2, send_b, 0), (1, 3, send_b, 1)))
 
 
@@ -231,30 +248,20 @@
     grad_blocks(place, x, ((2, [(gd, g1, None)]), (1, [(ud, u1, None)]), (0, [(gd, g0, None), (ud, u0, None)])))
 
 
-def pair_body(place, gate_delta, up_delta, *refs):
-    w_gate, w_up = refs[:4], refs[4:8]
-    send, keep, wg, wu, sems = refs[8:]
-    me = place[0]
-    copies = Copies(sems)
-    started = []
-    for k in range(4):
-        started.append((copies.start(w_gate[k], wg.at[k]), copies.start(w_up[k], wu.at[k])))
-    share = wg.shape[1]
-    tn = share // 2
-    rows = keep.shape[0]
-    for k in range(4):
-        for c in started[k]:
-            c.wait()
-
-        def step(i, _, k=k):
-            part = pl.ds(pl.multiple_of(i * tn, tn), tn)
-            total = mm(gate_delta[...], wg[k, part, :], NT) + mm(up_delta[...], wu[k, part, :], NT)
-            cols = pl.ds(pl.multiple_of((me ^ k) * share + i * tn, tn), tn)
-            keep[:, cols] = total[:rows].astype(BF16)
-            send[:, cols] = total[rows:].astype(BF16)
-            return 0
-
-        lax.fori_loop(0, 2, step, 0)
+def pair_body(gate_delta, up_delta, wg, wu, send, keep):
+    tn = 256
+    part = keep.shape[0] // 4
+
+    def step(i, _):
+        c = pl.ds(pl.multiple_of(i * tn, tn), tn)
+        total = (mm(gate_delta[...], wg[c, :], NT) + mm(up_delta[...], wu[c, :], NT)).astype(BF16)
+        keep[: 3 * part, c] = total[: 3 * part]
+        send[: 3 * part, c] = total[3 * part : 6 * part]
+        keep[3 * part :, c] = total[6 * part : 7 * part]
+        send[3 * part :, c] = total[7 * part :]
+        return 0
+
+    lax.fori_loop(0, wg.shape[0] // tn, step, 0)
 
 
 def add(*terms):
@@ -293,11 +300,11 @@
         outer = hop(own, OUTER)
         inner = hop(own, INNER)
         far = hop(two, ((2, 3), (1, 0)))
-        return [own, two, outer, inner, far] + [
-            swap(own), swap(two), swap(outer), swap(inner, (1, 2)), swap(far, (0, 3))
-        ]
-
-    x_pieces = line(tokens)
+        early = [own, two, outer, swap(own), swap(two), swap(outer)]
+        late = [inner, far, swap(inner, (1, 2)), swap(far, (0, 3))]
+        return early, late
+
+    x_early, x_late = line(tokens)
     (y_own,) = call(
         functools.partial(prep_body, experts),
         [((tok, width + LANES), BF16, VMEM)],
@@ -306,7 +313,7 @@
         1000,
         4 * tok * width,
     )
-    y_pieces = line(y_own)
+    y_early, y_late = line(y_own)
 
     wg0, wu0, wd0 = w_gate[0], w_up[0], w_down[0]
     wg1, wu1 = to_x(wg0), to_y(wu0)
@@ -319,28 +326,50 @@
     def dma(n):
         return pltpu.SemaphoreType.DMA((n,))
 
-    weight = pltpu.VMEM((width, hidden), BF16)
+    def anys(arrays):
+        return [(a, ANY) for a in arrays]
+
+    pre_outs = [
+        ((rows, hidden), BF16, VMEM),
+        ((rows, hidden), F32, VMEM),
+        ((rows, hidden), F32, VMEM),
+        ((rows, width), BF16, VMEM),
+    ]
+    weight = ((width, hidden), BF16, VMEM)
+    *pre, wg, wu = call(
+        pre_early_body,
+        pre_outs + [weight] * 2,
+        [(place, SMEM)] + anys(x_early) + anys(w_g + w_u),
+        [dma(14)],
+        3 * rows * width * hidden,
+        3 * rows * width + 8 * width * hidden + 8 * rows * hidden,
+    )
     act, active, slope, x = call(
-        pre_body,
-        [
-            ((rows, hidden), BF16, VMEM),
-            ((rows, hidden), F32, VMEM),
-            ((rows, hidden), F32, VMEM),
-            ((rows, width), BF16, ANY),
-        ],
-        [(place, SMEM)] + [(a, ANY) for a in x_pieces] + [(a, ANY) for a in w_g + w_u],
-        [pltpu.VMEM((rows, width), BF16), weight, weight, dma(17)],
-        4 * rows * width * hidden,
-        2 * (2 * rows * width + 2 * width * hidden) + 10 * rows * hidden,
+        pre_late_body,
+        pre_outs,
+        [(place, SMEM)] + anys(x_late) + [(wg, VMEM), (wu, VMEM)] + [(a, VMEM) for a in pre],
+        [dma(2)],
+        rows * width * hidden,
+        rows * width + 4 * width * hidden + 3 * rows * hidden,
+        {7 + i: i for i in range(4)},
+    )
+    (y,) = call(
+        functools.partial(scale_early_body, experts),
+        [((rows, width), BF16, VMEM)],
+        [(place, SMEM)] + anys(y_early),
+        [pltpu.VMEM((6 * tok, width + LANES), BF16), dma(6)],
+        rows * width,
+        4 * rows * width,
     )
     piece = (2, half, share)
     send_a, send_b, y = call(
         functools.partial(down_send_body, experts),
         [(piece, BF16, VMEM)] * 2 + [((rows, width), BF16, VMEM)],
-        [(place, SMEM)] + [(a, ANY) for a in y_pieces] + [(act, VMEM)],
-        [pltpu.VMEM((rows, width + LANES), BF16), dma(8)],
+        [(place, SMEM)] + anys(y_late) + [(act, VMEM), (y, VMEM)],
+        [pltpu.VMEM((2 * tok, width + LANES), BF16), dma(2)],
         rows * width * hidden,
         2 * (2 * rows * width + rows * hidden + width * hidden // 2),
+        {6: 2},
     )
     got_a, got_b = to_x(send_a), to_y(send_b)
     gate_delta, up_delta = call(
@@ -360,12 +389,11 @@
         2 * (rows * width + 2 * rows * hidden + width * hidden),
     )
     gate_got, up_got = to_x(gate_send), to_y(up_send)
-    weight = pltpu.VMEM((4, share, hidden), BF16)
     pair_send, pair_keep = call(
         pair_body,
         [((rows // 2, width), BF16, VMEM)] * 2,
-        [(place, SMEM), (gate_delta, VMEM), (up_delta, VMEM)] + [(a, ANY) for a in w_g + w_u],
-        [weight, weight, dma(8)],
+        [(gate_delta, VMEM), (up_delta, VMEM), (wg, VMEM), (wu, VMEM)],
+        [],
         4 * rows * width * hidden,
         2 * (rows * width + 2 * rows * hidden + 2 * width * hidden),
     )
@@ -387,9 +415,10 @@
         2 * (rows * width + 2 * rows * hidden + width * hidden),
     )
     down_a, down_b = to_y(add(keep_a1, got_a[1])), to_x(add(keep_b1, got_b[1]))
-    gate_last = to_y(add(gate1, gate_got[1]))
-    up_last = to_x(add(up1, up_got[1]))
-    gate_sum, up_sum = lax.optimization_barrier((add(gate0, gate_got[0]), add(up0, up_got[0])))
+    gate1, up1 = add(gate1, gate_got[1]), add(up1, up_got[1])
+    sums = add(gate0, gate_got[0]), add(up0, up_got[0])
+    gate_last, up_last = to_y(gate1), to_x(up1)
+    gate_sum, up_sum = lax.optimization_barrier(sums)
     down_grad = jnp.concatenate([add(keep_a0, got_a[0], down_a), add(keep_b0, got_b[0], down_b)], axis=0)
     gate_grad, up_grad = add(gate_sum, gate_last), add(up_sum, up_last)
 

time: 293 us -> 297 us (1.014)
  starting transfers between devices: 48.4 us -> 51.7 us
  local copies, waits for them, and re-layouts: 24.5 us -> 21.3 us
  waiting for transfers between devices: 168 us -> 171 us
    ppermute x12, starting transfers between devices: 19.9 us -> 23.6 us  [hop(): lax.ppermute(block, 'expert', [(2 * a + c, 2 * b + c) for a, b in moves f...]
    ppermute x9, waiting for transfers between devices: 76.2 us -> 79.7 us  [to_y(): return lax.ppermute(block, 'dp', [(i, i ^ 2) for i in range(4)])]
    unnamed x68 -> x62, local copies, waits for them, and re-layouts: 24.4 us -> 21.2 us
    pallas_call x8 -> x10, Pallas kernels: 43.7 us -> 45.1 us  [call(): pl.pallas_call(body, input_output_aliases=aliases or {}, out_shape=[jax.S...]
  transfers between devices with their start and end apart: 41 -> 41, of which waited for: 14 -> 15; matrix products, arithmetic and copies ran while one was open for 2% -> 2% of each run, Pallas kernels for 15% -> 15%
where the time goes in v3:
time: 297 us
  waiting for transfers between devices  171 us (58%)
  starting transfers between devices  51.7 us (17%)
  Pallas kernels  45.1 us (15%)
  local copies, waits for them, and re-layouts  21.3 us (7%)
  other arithmetic  6.43 us (2%)
    ppermute x9, waiting for transfers between devices, to_y(): return lax.ppermute(block, 'dp', [(i, i ^ 2) for i in range(4)])  79.7 us
    ppermute x12, waiting for transfers between devices, hop(): lax.ppermute(block, 'expert', [(2 * a + c, 2 * b + c) for a, b in moves f...  79.6 us
    pallas_call x10, Pallas kernels, call(): pl.pallas_call(body, input_output_aliases=aliases or {}, out_shape=[jax.S...  45.1 us
    ppermute x12, starting transfers between devices, hop(): lax.ppermute(block, 'expert', [(2 * a + c, 2 * b + c) for a, b in moves f...  23.6 us
    unnamed x62, local copies, waits for them, and re-layouts  21.2 us
    ppermute x9, waiting for transfers between devices, to_x(): return lax.ppermute(block, 'dp', [(i, i ^ 1) for i in range(4)])  11.6 us
    ppermute x9, starting transfers between devices, to_x(): return lax.ppermute(block, 'dp', [(i, i ^ 1) for i in range(4)])  11.3 us
    ppermute x9, starting transfers between devices, to_y(): return lax.ppermute(block, 'dp', [(i, i ^ 2) for i in range(4)])  9.08 us
  transfers between devices with their start and end apart: 41, of which 15 were waited for; matrix products, arithmetic and copies ran while one was open for 2% of the time, Pallas kernels for 15%

profile of v3, /device:TPU:0, one launch (start us, length us, event | category | flops | bytes accessed | tf_op | source)
XLA Modules:
  0.0 296.6 jit_solution(11455655605974711228)
XLA Ops:
  0.6 4.1 %collective-permute-start.6 = (bf16[128,2048]{1,0:T(8,128)(2,1)}, bf16[128,2048]{1,0:T(8,128)(2,1)S(1)}, u32[]{:S(2)}, u32[]{:S(2)}) collective-permute-start(bf16[128,2048]{1,0:T(8,128)(2,1)} %refs_0_.1), channel_id=1, source_target_pairs={{0,4},{1,5},{2,6},{3,7},{4,0},{5,1},{6,2},{7,3},{8,12},{9,13},{10,... | collective-permute-start | bytes 1572872 | tf_op jit(solution)/shard_map/ppermute | solution.py:293
  4.8 1.6 collective-permute-start.10
  6.3 1.5 collective-permute-start.5
  7.8 1.0 copy-done.11
  10.3 2.4 collective-permute-start.1
  12.8 17.2 %collective-permute-done.6.refs_1_ = bf16[128,2048]{1,0:T(8,128)(2,1)S(1)} collective-permute-done((bf16[128,2048]{1,0:T(8,128)(2,1)}, bf16[128,2048]{1,0:T(8,128)(2,1)S(1)}, u32[]{:S(2)}, u32[]{:S(2)}) %collective-permute-start.6) | collective-permute-done | bytes 524320 | tf_op jit(solution)/shard_map/ppermute | solution.py:293
  29.9 0.8 copy-done.25
  30.7 1.5 collective-permute-start
  32.2 2.0 collective-permute-start.14
  34.2 29.9 %collective-permute-done.1.refs_1_ = bf16[128,2176]{1,0:T(8,128)(2,1)S(1)} collective-permute-done((bf16[128,2176]{1,0:T(8,128)(2,1)S(1)}, bf16[128,2176]{1,0:T(8,128)(2,1)S(1)}, u32[]{:S(2)}, u32[]{:S(2)}) %collective-permute-start.1) | collective-permute-done | bytes 557088 | tf_op jit(solution)/shard_map/ppermute | solution.py:293
  64.1 1.8 collective-permute-start.18
  66.2 0.8 copy-done.7
  67.0 1.8 collective-permute-start.17
  68.8 1.5 collective-permute-start.25
  70.8 14.0 %collective-permute-done.18.refs_12_ = bf16[512,768]{1,0:T(8,128)(2,1)} collective-permute-done((bf16[512,768]{1,0:T(8,128)(2,1)}, bf16[512,768]{1,0:T(8,128)(2,1)}, u32[]{:S(2)}, u32[]{:S(2)}) %collective-permute-start.18) | collective-permute-done | bytes 786464 | tf_op jit(solution)/shard_map/ppermute | solution.py:290
  84.9 16.7 %collective-permute-done.15.refs_8_ = bf16[512,768]{1,0:T(8,128)(2,1)S(1)} collective-permute-done((bf16[512,768]{1,0:T(8,128)(2,1)}, bf16[512,768]{1,0:T(8,128)(2,1)S(1)}, u32[]{:S(2)}, u32[]{:S(2)}) %collective-permute-start.15) | collective-permute-done | bytes 786464 | tf_op jit(solution)/shard_map/ppermute | solution.py:290
  101.6 0.9 copy-done.16
  102.5 0.8 copy-done.23
  103.3 0.9 copy-done.18
  104.7 11.2 %collective-permute-done.25.from_y = bf16[768,512]{1,0:T(8,128)(2,1)S(1)} collective-permute-done((bf16[768,512]{1,0:T(8,128)(2,1)}, bf16[768,512]{1,0:T(8,128)(2,1)S(1)}, u32[]{:S(2)}, u32[]{:S(2)}) %collective-permute-start.25) | collective-permute-done | bytes 786464 | tf_op jit(solution)/shard_map/ppermute | solution.py:290
  115.9 1.3 collective-permute-start.7
  118.0 1.3 collective-permute-start.16
  120.1 1.5 collective-permute-start.19
  122.4 7.4 %collective-permute-done.7.refs_1_ = bf16[128,2048]{1,0:T(8,128)(2,1)S(1)} collective-permute-done((bf16[128,2048]{1,0:T(8,128)(2,1)S(1)}, bf16[128,2048]{1,0:T(8,128)(2,1)S(1)}, u32[]{:S(2)}, u32[]{:S(2)}) %collective-permute-start.7) | collective-permute-done | bytes 524320 | tf_op jit(solution)/shard_map/ppermute | solution.py:293
  129.8 1.3 collective-permute-start.2
  131.1 0.8 copy-done.9
  131.9 1.5 collective-permute-start.8
  133.4 2.0 collective-permute-start.9
  135.7 2.7 shard_map.105.refs_5_
  138.4 1.5 collective-permute-start.3
  139.9 3.8 %collective-permute-done.2.refs_1_ = bf16[128,2176]{1,0:T(8,128)(2,1)} collective-permute-done((bf16[128,2176]{1,0:T(8,128)(2,1)S(1)}, bf16[128,2176]{1,0:T(8,128)(2,1)}, u32[]{:S(2)}, u32[]{:S(2)}) %collective-permute-start.2) | collective-permute-done | bytes 557088 | tf_op jit(solution)/shard_map/ppermute | solution.py:293
  143.7 1.7 collective-permute-start.26
  145.4 1.5 collective-permute-start.27
  146.9 1.9 collective-permute-start.4
  148.9 8.6 %shard_map.103 = (bf16[1024,768]{1,0:T(8,128)(2,1)S(1)}, f32[1024,768]{1,0:T(8,128)S(1)}, f32[1024,768]{1,0:T(8,128)S(1)}, bf16[1024,2048]{1,0:T(8,128)(2,1)S(1)...) custom-call(s32[3]{0:T(128)S(1)} %pad_add_fusion.place, bf16[128,2048]{1,0:T(8,128)(2,1)S(1)} %copy-done.20, ...), custom_call_target="tpu_custom_call" | custom-call | flops 4831838208 | bytes 25165824 | tf_op jit(solution)/shard_map/pallas_call | solution.py:31
  157.5 2.0 copy-done
  159.5 1.7 copy-done.2
  161.2 1.7 copy-done.4
  162.9 2.2 copy-done.1
  165.1 1.9 copy-done.3
  167.0 1.9 copy-done.5
  168.9 3.1 %shard_map.104 = (bf16[1024,768]{1,0:T(8,128)(2,1)S(1)}, f32[1024,768]{1,0:T(8,128)S(1)}, f32[1024,768]{1,0:T(8,128)S(1)}, bf16[1024,2048]{1,0:T(8,128)(2,1)S(1)}) custom-call(s32[3]{0:T(128)S(1)} %pad_add_fusion.place, bf16[128,2048]{1,0:T(8,128)(2,1)} %collective-permute-done.5.refs_0_, ...), custom_call_target="tpu_custom_call", output_to_operand_aliasing={{0}: (7, {}), {1}: (8, {}), {2}: (9, {}), {3}: (10, {})} | custom-call | flops 1610612736 | bytes 10747904 | tf_op jit(solution)/shard_map/pallas_call | solution.py:31
  172.0 4.0 %shard_map.106 = (bf16[2,384,512]{2,1,0:T(8,128)(2,1)S(1)}, bf16[2,384,512]{2,1,0:T(8,128)(2,1)S(1)}, bf16[1024,2048]{1,0:T(8,128)(2,1)S(1)}) custom-call(s32[3]{0:T(128)S(1)} %pad_add_fusion.place, bf16[128,2176]{1,0:T(8,128)(2,1)} %collective-permute-done.refs_0_, ...), custom_call_target="tpu_custom_call", output_to_operand_aliasing={{2}: (6, {})} | custom-call | flops 1610612736 | bytes 11534336 | tf_op jit(solution)/shard_map/pallas_call | solution.py:31
  176.6 5.6 %shard_map.107 = (bf16[1024,768]{1,0:T(8,128)(2,1)S(1)}, bf16[1024,768]{1,0:T(8,128)(2,1)S(1)}) custom-call(s32[3]{0:T(128)S(1)} %pad_add_fusion.place, bf16[1024,2048]{1,0:T(8,128)(2,1)S(1)} %get-tuple-element.40.y, f32[1024,768]{1,0:T(8,128)S(1)} %get-tuple-element.41.active, f32[1024,768]{1,0:T(8,128)S(1)} %get-tuple-element.42.slope, ...), custom_call_target="tpu_custom_call" | custom-call | flops 3221225472 | bytes 16777216 | tf_op jit(solution)/shard_map/pallas_call | solution.py:31
  182.2 8.1 %shard_map.108 = (bf16[512,2048]{1,0:T(8,128)(2,1)S(1)}, bf16[512,2048]{1,0:T(8,128)(2,1)S(1)}) custom-call(bf16[1024,768]{1,0:T(8,128)(2,1)S(1)} %get-tuple-element.43.gate_delta.gd, bf16[1024,768]{1,0:T(8,128)(2,1)S(1)} %get-tuple-element.44.up_delta.ud, bf16[2048,768]{1,0:T(8,128)(2,1)S(1)} %copy-done.3, bf16[2048,768]{1,0:T(8,128)(2,1)S(1)} %copy-done.5), custom_call_target="tpu_custom_call" | custom-call | flops 6442450944 | bytes 13631488 | tf_op jit(solution)/shard_map/pallas_call | solution.py:31
  190.9 2.4 shard_map.111
  193.3 5.3 %shard_map.110 = (bf16[2,512,768]{2,1,0:T(8,128)(2,1)S(1)}, bf16[2,512,768]{2,1,0:T(8,128)(2,1)S(1)}) custom-call(s32[3]{0:T(128)S(1)} %pad_add_fusion.place, bf16[1024,2048]{1,0:T(8,128)(2,1)S(1)} %get-tuple-element.47.x, bf16[1024,768]{1,0:T(8,128)(2,1)S(1)} %get-tuple-element.43.gate_delta.gd, bf16[1024,768]{1,0:T(8,128)(2,1)S(1)} %get-tuple-element.44.up_delta.ud), custom_call_target="tpu_custom_call" | custom-call | flops 3221225472 | bytes 10485760 | tf_op jit(solution)/shard_map/pallas_call | solution.py:31
  198.7 1.8 collective-permute-start.38
  200.5 10.6 %collective-permute-done.39 = bf16[2,384,512]{2,1,0:T(8,128)(2,1)S(1)} collective-permute-done((bf16[2,384,512]{2,1,0:T(8,128)(2,1)S(1)}, bf16[2,384,512]{2,1,0:T(8,128)(2,1)S(1)}, u32[]{:S(2)}, u32[]{:S(2)}) %collective-permute-start.39) | collective-permute-done | bytes 786464 | tf_op jit(solution)/shard_map/ppermute | solution.py:290
  211.1 1.6 collective-permute-start.40
  212.7 5.3 %shard_map.109 = (bf16[512,768]{1,0:T(8,128)(2,1)S(1)}, bf16[512,768]{1,0:T(8,128)(2,1)S(1)}, bf16[512,768]{1,0:T(8,128)(2,1)S(1)}, bf16[512,768]{1,0:T(8,128)(2,1)S(1)}) custom-call(s32[3]{0:T(128)S(1)} %pad_add_fusion.place, bf16[1024,2048]{1,0:T(8,128)(2,1)S(1)} %get-tuple-element.47.x, bf16[1024,768]{1,0:T(8,128)(2,1)S(1)} %get-tuple-element.43.gate_delta.gd, ...), custom_call_target="tpu_custom_call" | custom-call | flops 3221225472 | bytes 10485760 | tf_op jit(solution)/shard_map/pallas_call | solution.py:31
  219.0 3.7 %collective-permute-done.40 = bf16[384,512]{1,0:T(8,128)(2,1)S(1)} collective-permute-done((bf16[384,512]{1,0:T(8,128)(2,1)S(1)}, bf16[384,512]{1,0:T(8,128)(2,1)S(1)}, u32[]{:S(2)}, u32[]{:S(2)}) %collective-permute-start.40) | collective-permute-done | bytes 393248 | tf_op jit(solution)/shard_map/ppermute | solution.py:287
  223.7 2.3 collective-permute-start.31
  226.0 26.8 %collective-permute-done.34 = bf16[2,512,768]{2,1,0:T(8,128)(2,1)S(1)} collective-permute-done((bf16[2,512,768]{2,1,0:T(8,128)(2,1)S(1)}, bf16[2,512,768]{2,1,0:T(8,128)(2,1)S(1)}, u32[]{:S(2)}, u32[]{:S(2)}) %collective-permute-start.34) | collective-permute-done | bytes 1572896 | tf_op jit(solution)/shard_map/ppermute | solution.py:290
  253.2 1.2 collective-permute-start.36
  254.5 1.3 collective-permute-done.33
  256.3 0.9 maximum_bitcast_fusion
  257.9 6.6 %collective-permute-start.30 = (bf16[128,2048]{1,0:T(8,128)(2,1)S(1)}, bf16[128,2048]{1,0:T(8,128)(2,1)S(1)}, u32[]{:S(2)}, u32[]{:S(2)}) collective-permute-start(bf16[128,2048]{1,0:T(8,128)(2,1)S(1)} %get-tuple-element.62), channel_id=1, source_target_pairs={{0,2},{1,3},{2,0},{3,1},{4,6},{5,7},{6,4},{7,5},{8,10},{9,11},{10,... | collective-permute-start | bytes 1572872 | tf_op jit(solution)/shard_map/ppermute | solution.py:293
  265.0 6.5 %collective-permute-done.36 = bf16[512,768]{1,0:T(8,128)(2,1)S(1)} collective-permute-done((bf16[512,768]{1,0:T(8,128)(2,1)S(1)}, bf16[512,768]{1,0:T(8,128)(2,1)S(1)}, u32[]{:S(2)}, u32[]{:S(2)}) %collective-permute-start.36) | collective-permute-done | bytes 786464 | tf_op jit(solution)/shard_map/ppermute | solution.py:287
  271.6 1.1 fusion.5
  273.0 1.1 fusion.4
  274.1 2.7 collective-permute-done.30
  276.7 18.7 %collective-permute-done.32 = bf16[128,2048]{1,0:T(8,128)(2,1)S(1)} collective-permute-done((bf16[128,2048]{1,0:T(8,128)(2,1)S(1)}, bf16[128,2048]{1,0:T(8,128)(2,1)S(1)}, u32[]{:S(2)}, u32[]{:S(2)}) %collective-permute-start.32) | collective-permute-done | bytes 524320 | tf_op jit(solution)/shard_map/ppermute | solution.py:293
  295.4 1.1 add_convert_fusion.3
  (106 shorter events, 11.3 us)
Async XLA Ops:
  0.6 29.3 %collective-permute-start.6 = (bf16[128,2048]{1,0:T(8,128)(2,1)}, bf16[128,2048]{1,0:T(8,128)(2,1)S(1)}, u32[]{:S(2)}, u32[]{:S(2)}) collective-permute-start(bf16[128,2048]{1,0:T(8,128)(2,1)} %refs_0_.1), channel_id=1, source_target_pairs={{0,4},{1,5},{2,6},{3,7},{4,0},{5,1},{6,2},{7,3},{8,12},{9,13},{10,... | collective-permute-start | bytes 1572872 | tf_op jit(solution)/shard_map/ppermute | solution.py:293
  4.8 25.1 %collective-permute-start.10 = (bf16[128,2048]{1,0:T(8,128)(2,1)}, bf16[128,2048]{1,0:T(8,128)(2,1)S(1)}, u32[]{:S(2)}, u32[]{:S(2)}) collective-permute-start(bf16[128,2048]{1,0:T(8,128)(2,1)} %refs_0_.1), channel_id=1, source_target_pairs={{0,2},{1,3},{2,0},{3,1},{4,6},{5,7},{6,4},{7,5},{8,10},{9,11},{10,... | collective-permute-start | bytes 1572872 | tf_op jit(solution)/shard_map/ppermute | solution.py:293
  6.3 23.6 %collective-permute-start.11 = (bf16[128,2048]{1,0:T(8,128)(2,1)}, bf16[128,2048]{1,0:T(8,128)(2,1)S(1)}, u32[]{:S(2)}, u32[]{:S(2)}) collective-permute-start(bf16[128,2048]{1,0:T(8,128)(2,1)} %refs_0_.1), channel_id=1, source_target_pairs={{0,1},{1,0},{2,3},{3,2},{4,5},{5,4},{6,7},{7,6},{8,9},{9,8},{10,11... | collective-permute-start | bytes 1572872 | tf_op jit(solution)/shard_map/ppermute | solution.py:296
  6.3 25.9 %collective-permute-start.5 = (bf16[128,2048]{1,0:T(8,128)(2,1)}, bf16[128,2048]{1,0:T(8,128)(2,1)}, u32[]{:S(2)}, u32[]{:S(2)}) collective-permute-start(bf16[128,2048]{1,0:T(8,128)(2,1)} %refs_0_.1), channel_id=1, source_target_pairs={{2,4},{3,5},{4,2},{5,3},{10,12},{11,13},{12,10},{13,11},{18,20},{1... | collective-permute-start | bytes 1572872 | tf_op jit(solution)/shard_map/ppermute | solution.py:293
  7.8 1.0 copy-start.11
  10.3 53.8 %collective-permute-start.1 = (bf16[128,2176]{1,0:T(8,128)(2,1)S(1)}, bf16[128,2176]{1,0:T(8,128)(2,1)S(1)}, u32[]{:S(2)}, u32[]{:S(2)}) collective-permute-start(bf16[128,2176]{1,0:T(8,128)(2,1)S(1)} %shard_map.102.refs_0_), channel_id=1, source_target_pairs={{0,4},{1,5},{2,6},{3,7},{4,0},{5,1},{6,2},{7,3},{8,12},{9,13},{10,... | collective-permute-start | bytes 1671176 | tf_op jit(solution)/shard_map/ppermute | solution.py:293
  29.9 36.1 %collective-permute-start.20 = (bf16[128,2176]{1,0:T(8,128)(2,1)S(1)}, bf16[128,2176]{1,0:T(8,128)(2,1)}, u32[]{:S(2)}, u32[]{:S(2)}) collective-permute-start(bf16[128,2176]{1,0:T(8,128)(2,1)S(1)} %shard_map.102.refs_0_), channel_id=1, source_target_pairs={{0,2},{1,3},{2,0},{3,1},{4,6},{5,7},{6,4},{7,5},{8,10},{9,11},{10,... | collective-permute-start | bytes 1671176 | tf_op jit(solution)/shard_map/ppermute | solution.py:293
  29.9 36.3 %collective-permute-start.21 = (bf16[128,2176]{1,0:T(8,128)(2,1)S(1)}, bf16[128,2176]{1,0:T(8,128)(2,1)S(1)}, u32[]{:S(2)}, u32[]{:S(2)}) collective-permute-start(bf16[128,2176]{1,0:T(8,128)(2,1)S(1)} %shard_map.102.refs_0_), channel_id=1, source_target_pairs={{0,1},{1,0},{2,3},{3,2},{4,5},{5,4},{6,7},{7,6},{8,9},{9,8},{10,11... | collective-permute-start | bytes 1671176 | tf_op jit(solution)/shard_map/ppermute | solution.py:296
  29.9 0.8 copy-start.25
  30.7 38.0 %collective-permute-start = (bf16[128,2176]{1,0:T(8,128)(2,1)S(1)}, bf16[128,2176]{1,0:T(8,128)(2,1)}, u32[]{:S(2)}, u32[]{:S(2)}) collective-permute-start(bf16[128,2176]{1,0:T(8,128)(2,1)S(1)} %shard_map.102.refs_0_), channel_id=1, source_target_pairs={{2,4},{3,5},{4,2},{5,3},{10,12},{11,13},{12,10},{13,11},{18,20},{1... | collective-permute-start | bytes 1671176 | tf_op jit(solution)/shard_map/ppermute | solution.py:293
  32.2 38.1 %collective-permute-start.14 = (bf16[512,768]{1,0:T(8,128)(2,1)}, bf16[512,768]{1,0:T(8,128)(2,1)}, u32[]{:S(2)}, u32[]{:S(2)}) collective-permute-start(bf16[512,768]{1,0:T(8,128)(2,1)} %bitcast.59), channel_id=1, source_target_pairs={{0,8},{8,0},{16,24},{24,16},{1,9},{9,1},{17,25},{25,17},{2,10},{10... | collective-permute-start | bytes 2359304 | tf_op jit(solution)/shard_map/ppermute | solution.py:287
  64.1 20.7 %collective-permute-start.18 = (bf16[512,768]{1,0:T(8,128)(2,1)}, bf16[512,768]{1,0:T(8,128)(2,1)}, u32[]{:S(2)}, u32[]{:S(2)}) collective-permute-start(bf16[512,768]{1,0:T(8,128)(2,1)} %bitcast.62), channel_id=1, source_target_pairs={{0,16},{8,24},{16,0},{24,8},{1,17},{9,25},{17,1},{25,9},{2,18},{10... | collective-permute-start | bytes 2359304 | tf_op jit(solution)/shard_map/ppermute | solution.py:290
  66.0 35.7 %collective-permute-start.15 = (bf16[512,768]{1,0:T(8,128)(2,1)}, bf16[512,768]{1,0:T(8,128)(2,1)S(1)}, u32[]{:S(2)}, u32[]{:S(2)}) collective-permute-start(bf16[512,768]{1,0:T(8,128)(2,1)} %bitcast.60), channel_id=1, source_target_pairs={{0,16},{8,24},{16,0},{24,8},{1,17},{9,25},{17,1},{25,9},{2,18},{10... | collective-permute-start | bytes 2359304 | tf_op jit(solution)/shard_map/ppermute | solution.py:290
  67.0 36.3 %collective-permute-start.17 = (bf16[512,768]{1,0:T(8,128)(2,1)}, bf16[512,768]{1,0:T(8,128)(2,1)S(1)}, u32[]{:S(2)}, u32[]{:S(2)}) collective-permute-start(bf16[512,768]{1,0:T(8,128)(2,1)} %bitcast.63), channel_id=1, source_target_pairs={{0,8},{8,0},{16,24},{24,16},{1,9},{9,1},{17,25},{25,17},{2,10},{10... | collective-permute-start | bytes 2359304 | tf_op jit(solution)/shard_map/ppermute | solution.py:287
  68.8 47.1 %collective-permute-start.25 = (bf16[768,512]{1,0:T(8,128)(2,1)}, bf16[768,512]{1,0:T(8,128)(2,1)S(1)}, u32[]{:S(2)}, u32[]{:S(2)}) collective-permute-start(bf16[768,512]{1,0:T(8,128)(2,1)} %bitcast.54), channel_id=1, source_target_pairs={{0,16},{8,24},{16,0},{24,8},{1,17},{9,25},{17,1},{25,9},{2,18},{10... | collective-permute-start | bytes 2359304 | tf_op jit(solution)/shard_map/ppermute | solution.py:290
  70.3 47.7 %collective-permute-start.24 = (bf16[768,512]{1,0:T(8,128)(2,1)}, bf16[768,512]{1,0:T(8,128)(2,1)S(1)}, u32[]{:S(2)}, u32[]{:S(2)}) collective-permute-start(bf16[768,512]{1,0:T(8,128)(2,1)} %bitcast.55), channel_id=1, source_target_pairs={{0,8},{8,0},{16,24},{24,16},{1,9},{9,1},{17,25},{25,17},{2,10},{10... | collective-permute-start | bytes 2359304 | tf_op jit(solution)/shard_map/ppermute | solution.py:287
  84.9 34.4 %collective-permute-start.12 = (bf16[128,2048]{1,0:T(8,128)(2,1)S(1)}, bf16[128,2048]{1,0:T(8,128)(2,1)S(1)}, u32[]{:S(2)}, u32[]{:S(2)}) collective-permute-start(bf16[128,2048]{1,0:T(8,128)(2,1)S(1)} %collective-permute-done.6.refs_1_), channel_id=1, source_target_pairs={{0,1},{1,0},{2,3},{3,2},{4,5},{5,4},{6,7},{7,6},{8,9},{9,8},{10,11... | collective-permute-start | bytes 1572872 | tf_op jit(solution)/shard_map/ppermute | solution.py:296
  101.6 0.9 copy-start.16
  102.5 19.1 %collective-permute-start.13 = (bf16[128,2048]{1,0:T(8,128)(2,1)S(1)}, bf16[128,2048]{1,0:T(8,128)(2,1)S(1)}, u32[]{:S(2)}, u32[]{:S(2)}) collective-permute-start(bf16[128,2048]{1,0:T(8,128)(2,1)S(1)} %collective-permute-done.10.refs_2_), channel_id=1, source_target_pairs={{0,1},{1,0},{2,3},{3,2},{4,5},{5,4},{6,7},{7,6},{8,9},{9,8},{10,11... | collective-permute-start | bytes 1572872 | tf_op jit(solution)/shard_map/ppermute | solution.py:296
  103.3 0.9 copy-start.18
  104.2 26.9 %collective-permute-start.22 = (bf16[128,2176]{1,0:T(8,128)(2,1)S(1)}, bf16[128,2176]{1,0:T(8,128)(2,1)S(1)}, u32[]{:S(2)}, u32[]{:S(2)}) collective-permute-start(bf16[128,2176]{1,0:T(8,128)(2,1)S(1)} %collective-permute-done.1.refs_1_), channel_id=1, source_target_pairs={{0,1},{1,0},{2,3},{3,2},{4,5},{5,4},{6,7},{7,6},{8,9},{9,8},{10,11... | collective-permute-start | bytes 1671176 | tf_op jit(solution)/shard_map/ppermute | solution.py:296
  115.9 13.8 %collective-permute-start.7 = (bf16[128,2048]{1,0:T(8,128)(2,1)S(1)}, bf16[128,2048]{1,0:T(8,128)(2,1)S(1)}, u32[]{:S(2)}, u32[]{:S(2)}) collective-permute-start(bf16[128,2048]{1,0:T(8,128)(2,1)S(1)} %collective-permute-done.6.refs_1_), channel_id=1, source_target_pairs={{4,6},{5,7},{2,0},{3,1},{12,14},{13,15},{10,8},{11,9},{20,22},{21,... | collective-permute-start | bytes 1572872 | tf_op jit(solution)/shard_map/ppermute | solution.py:293
  118.0 27.4 %collective-permute-start.16 = (bf16[512,768]{1,0:T(8,128)(2,1)}, bf16[512,768]{1,0:T(8,128)(2,1)}, u32[]{:S(2)}, u32[]{:S(2)}) collective-permute-start(bf16[512,768]{1,0:T(8,128)(2,1)} %collective-permute-done.14.refs_7_), channel_id=1, source_target_pairs={{0,16},{8,24},{16,0},{24,8},{1,17},{9,25},{17,1},{25,9},{2,18},{10... | collective-permute-start | bytes 2359304 | tf_op jit(solution)/shard_map/ppermute | solution.py:290
  120.1 26.8 %collective-permute-start.19 = (bf16[512,768]{1,0:T(8,128)(2,1)}, bf16[512,768]{1,0:T(8,128)(2,1)}, u32[]{:S(2)}, u32[]{:S(2)}) collective-permute-start(bf16[512,768]{1,0:T(8,128)(2,1)} %collective-permute-done.18.refs_12_), channel_id=1, source_target_pairs={{0,8},{8,0},{16,24},{24,16},{1,9},{9,1},{17,25},{25,17},{2,10},{10... | collective-permute-start | bytes 2359304 | tf_op jit(solution)/shard_map/ppermute | solution.py:287
  122.4 11.0 %collective-permute-start.23 = (bf16[128,2176]{1,0:T(8,128)(2,1)}, bf16[128,2176]{1,0:T(8,128)(2,1)}, u32[]{:S(2)}, u32[]{:S(2)}) collective-permute-start(bf16[128,2176]{1,0:T(8,128)(2,1)} %collective-permute-done.20.refs_2_), channel_id=1, source_target_pairs={{0,1},{1,0},{2,3},{3,2},{4,5},{5,4},{6,7},{7,6},{8,9},{9,8},{10,11... | collective-permute-start | bytes 1671176 | tf_op jit(solution)/shard_map/ppermute | solution.py:296
  129.8 13.9 %collective-permute-start.2 = (bf16[128,2176]{1,0:T(8,128)(2,1)S(1)}, bf16[128,2176]{1,0:T(8,128)(2,1)}, u32[]{:S(2)}, u32[]{:S(2)}) collective-permute-start(bf16[128,2176]{1,0:T(8,128)(2,1)S(1)} %collective-permute-done.1.refs_1_), channel_id=1, source_target_pairs={{4,6},{5,7},{2,0},{3,1},{12,14},{13,15},{10,8},{11,9},{20,22},{21,... | collective-permute-start | bytes 1671176 | tf_op jit(solution)/shard_map/ppermute | solution.py:293
  131.9 6.5 %collective-permute-start.8 = (bf16[128,2048]{1,0:T(8,128)(2,1)}, bf16[128,2048]{1,0:T(8,128)(2,1)}, u32[]{:S(2)}, u32[]{:S(2)}) collective-permute-start(bf16[128,2048]{1,0:T(8,128)(2,1)} %collective-permute-done.5.refs_0_), channel_id=1, source_target_pairs={{2,3},{3,2},{4,5},{5,4},{10,11},{11,10},{12,13},{13,12},{18,19},{1... | collective-permute-start | bytes 1572872 | tf_op jit(solution)/shard_map/ppermute | solution.py:296
  133.3 2.2 copy-start.8
  133.4 2.2 copy-start.10
  133.4 29.5 %collective-permute-start.9 = (bf16[128,2048]{1,0:T(8,128)(2,1)S(1)}, bf16[128,2048]{1,0:T(8,128)(2,1)S(1)}, u32[]{:S(2)}, u32[]{:S(2)}) collective-permute-start(bf16[128,2048]{1,0:T(8,128)(2,1)S(1)} %collective-permute-done.7.refs_1_), channel_id=1, source_target_pairs={{0,1},{1,0},{6,7},{7,6},{8,9},{9,8},{14,15},{15,14},{16,17},{17,16... | collective-permute-start | bytes 1572872 | tf_op jit(solution)/shard_map/ppermute | solution.py:296
  135.6 13.3 %copy-start.14 = (bf16[1,512,768]{2,1,0:T(8,128)(2,1)S(1)}, bf16[1,512,768]{2,1,0:T(8,128)(2,1)}, u32[]{:S(2)}) copy-start(bf16[1,512,768]{2,1,0:T(8,128)(2,1)} %param.11) | copy-start | bytes 2359300
  135.6 13.2 %copy-start.15 = (bf16[1,512,768]{2,1,0:T(8,128)(2,1)S(1)}, bf16[1,512,768]{2,1,0:T(8,128)(2,1)}, u32[]{:S(2)}) copy-start(bf16[1,512,768]{2,1,0:T(8,128)(2,1)} %param.12) | copy-start | bytes 2359300
  135.6 13.2 %copy-start.17 = (bf16[512,768]{1,0:T(8,128)(2,1)S(1)}, bf16[512,768]{1,0:T(8,128)(2,1)}, u32[]{:S(2)}) copy-start(bf16[512,768]{1,0:T(8,128)(2,1)} %copy-done.16) | copy-start | bytes 2359300
  135.6 13.2 %copy-start.19 = (bf16[512,768]{1,0:T(8,128)(2,1)S(1)}, bf16[512,768]{1,0:T(8,128)(2,1)}, u32[]{:S(2)}) copy-start(bf16[512,768]{1,0:T(8,128)(2,1)} %copy-done.18) | copy-start | bytes 2359300
  135.6 13.2 %copy-start.20 = (bf16[128,2048]{1,0:T(8,128)(2,1)S(1)}, bf16[128,2048]{1,0:T(8,128)(2,1)}, u32[]{:S(2)}) copy-start(bf16[128,2048]{1,0:T(8,128)(2,1)} %refs_0_.1) | copy-start | bytes 1572868
  135.6 13.2 %copy-start.22 = (bf16[128,2048]{1,0:T(8,128)(2,1)S(1)}, bf16[128,2048]{1,0:T(8,128)(2,1)}, u32[]{:S(2)}) copy-start(bf16[128,2048]{1,0:T(8,128)(2,1)} %copy-done.21) | copy-start | bytes 1572868
  135.6 13.2 %copy-start.24 = (bf16[128,2048]{1,0:T(8,128)(2,1)S(1)}, bf16[128,2048]{1,0:T(8,128)(2,1)}, u32[]{:S(2)}) copy-start(bf16[128,2048]{1,0:T(8,128)(2,1)} %copy-done.23) | copy-start | bytes 1572868
  135.7 13.2 %copy-start.26 = (bf16[128,2048]{1,0:T(8,128)(2,1)S(1)}, bf16[128,2048]{1,0:T(8,128)(2,1)}, u32[]{:S(2)}) copy-start(bf16[128,2048]{1,0:T(8,128)(2,1)} %copy-done.25) | copy-start | bytes 1572868
  135.7 13.2 %copy-start.28 = (bf16[128,2048]{1,0:T(8,128)(2,1)S(1)}, bf16[128,2048]{1,0:T(8,128)(2,1)}, u32[]{:S(2)}) copy-start(bf16[128,2048]{1,0:T(8,128)(2,1)} %copy-done.27) | copy-start | bytes 1572868
  135.7 13.2 %copy-start.30 = (bf16[128,2048]{1,0:T(8,128)(2,1)S(1)}, bf16[128,2048]{1,0:T(8,128)(2,1)}, u32[]{:S(2)}) copy-start(bf16[128,2048]{1,0:T(8,128)(2,1)} %copy-done.29) | copy-start | bytes 1572868
  138.4 33.6 %collective-permute-start.3 = (bf16[128,2176]{1,0:T(8,128)(2,1)}, bf16[128,2176]{1,0:T(8,128)(2,1)}, u32[]{:S(2)}, u32[]{:S(2)}) collective-permute-start(bf16[128,2176]{1,0:T(8,128)(2,1)} %collective-permute-done.refs_0_), channel_id=1, source_target_pairs={{2,3},{3,2},{4,5},{5,4},{10,11},{11,10},{12,13},{13,12},{18,19},{1... | collective-permute-start | bytes 1671176 | tf_op jit(solution)/shard_map/ppermute | solution.py:296
  143.7 32.9 %collective-permute-start.26 = (bf16[384,512]{1,0:T(8,128)(2,1)S(1)}, bf16[384,512]{1,0:T(8,128)(2,1)S(1)}, u32[]{:S(2)}, u32[]{:S(2)}) collective-permute-start(bf16[384,512]{1,0:T(8,128)(2,1)S(1)} %slice.61), channel_id=1, source_target_pairs={{0,8},{8,0},{16,24},{24,16},{1,9},{9,1},{17,25},{25,17},{2,10},{10... | collective-permute-start | bytes 1179656 | tf_op jit(solution)/shard_map/ppermute | solution.py:287
  145.4 31.2 %collective-permute-start.27 = (bf16[384,512]{1,0:T(8,128)(2,1)S(1)}, bf16[384,512]{1,0:T(8,128)(2,1)S(1)}, u32[]{:S(2)}, u32[]{:S(2)}) collective-permute-start(bf16[384,512]{1,0:T(8,128)(2,1)S(1)} %slice.62), channel_id=1, source_target_pairs={{0,16},{8,24},{16,0},{24,8},{1,17},{9,25},{17,1},{25,9},{2,18},{10... | collective-permute-start | bytes 1179656 | tf_op jit(solution)/shard_map/ppermute | solution.py:290
  146.9 25.1 %collective-permute-start.4 = (bf16[128,2176]{1,0:T(8,128)(2,1)}, bf16[128,2176]{1,0:T(8,128)(2,1)}, u32[]{:S(2)}, u32[]{:S(2)}) collective-permute-start(bf16[128,2176]{1,0:T(8,128)(2,1)} %collective-permute-done.2.refs_1_), channel_id=1, source_target_pairs={{0,1},{1,0},{6,7},{7,6},{8,9},{9,8},{14,15},{15,14},{16,17},{17,16... | collective-permute-start | bytes 1671176 | tf_op jit(solution)/shard_map/ppermute | solution.py:296
  157.5 2.0 copy-start
  159.5 1.7 copy-start.2
  161.2 1.7 copy-start.4
  162.9 2.2 copy-start.1
  165.1 1.9 copy-start.3
  167.0 1.9 copy-start.5
  172.0 4.6 %copy-start.6 = (bf16[1,768,512]{2,1,0:T(8,128)(2,1)S(1)}, bf16[1,768,512]{2,1,0:T(8,128)(2,1)}, u32[]{:S(2)}) copy-start(bf16[1,768,512]{2,1,0:T(8,128)(2,1)} %param.13) | copy-start | bytes 2359300
  176.0 22.6 %collective-permute-start.37 = (bf16[2,384,512]{2,1,0:T(8,128)(2,1)S(1)}, bf16[2,384,512]{2,1,0:T(8,128)(2,1)S(1)}, u32[]{:S(2)}, u32[]{:S(2)}) collective-permute-start(bf16[2,384,512]{2,1,0:T(8,128)(2,1)S(1)} %get-tuple-element.57), channel_id=1, source_target_pairs={{0,8},{8,0},{16,24},{24,16},{1,9},{9,1},{17,25},{25,17},{2,10},{10... | collective-permute-start | bytes 2359304 | tf_op jit(solution)/shard_map/ppermute | solution.py:287
  190.3 32.5 %collective-permute-start.28 = (bf16[512,2048]{1,0:T(8,128)(2,1)S(1)}, bf16[512,2048]{1,0:T(8,128)(2,1)S(1)}, u32[]{:S(2)}, u32[]{:S(2)}) collective-permute-start(bf16[512,2048]{1,0:T(8,128)(2,1)S(1)} %get-tuple-element.46), channel_id=1, source_target_pairs={{0,1},{1,0},{2,3},{3,2},{4,5},{5,4},{6,7},{7,6},{8,9},{9,8},{10,11... | collective-permute-start | bytes 6291464 | tf_op jit(solution)/shard_map/ppermute | solution.py:296
  190.6 20.4 %collective-permute-start.39 = (bf16[2,384,512]{2,1,0:T(8,128)(2,1)S(1)}, bf16[2,384,512]{2,1,0:T(8,128)(2,1)S(1)}, u32[]{:S(2)}, u32[]{:S(2)}) collective-permute-start(bf16[2,384,512]{2,1,0:T(8,128)(2,1)S(1)} %get-tuple-element.60), channel_id=1, source_target_pairs={{0,16},{8,24},{16,0},{24,8},{1,17},{9,25},{17,1},{25,9},{2,18},{10... | collective-permute-start | bytes 2359304 | tf_op jit(solution)/shard_map/ppermute | solution.py:290
  198.7 20.2 %collective-permute-start.38 = (bf16[384,512]{1,0:T(8,128)(2,1)S(1)}, bf16[384,512]{1,0:T(8,128)(2,1)S(1)}, u32[]{:S(2)}, u32[]{:S(2)}) collective-permute-start(bf16[384,512]{1,0:T(8,128)(2,1)S(1)} %fusion.9), channel_id=1, source_target_pairs={{0,16},{8,24},{16,0},{24,8},{1,17},{9,25},{17,1},{25,9},{2,18},{10... | collective-permute-start | bytes 1179656 | tf_op jit(solution)/shard_map/ppermute | solution.py:290
  211.1 11.6 %collective-permute-start.40 = (bf16[384,512]{1,0:T(8,128)(2,1)S(1)}, bf16[384,512]{1,0:T(8,128)(2,1)S(1)}, u32[]{:S(2)}, u32[]{:S(2)}) collective-permute-start(bf16[384,512]{1,0:T(8,128)(2,1)S(1)} %fusion.6), channel_id=1, source_target_pairs={{0,8},{8,0},{16,24},{24,16},{1,9},{9,1},{17,25},{25,17},{2,10},{10... | collective-permute-start | bytes 1179656 | tf_op jit(solution)/shard_map/ppermute | solution.py:287
  218.0 34.8 %collective-permute-start.34 = (bf16[2,512,768]{2,1,0:T(8,128)(2,1)S(1)}, bf16[2,512,768]{2,1,0:T(8,128)(2,1)S(1)}, u32[]{:S(2)}, u32[]{:S(2)}) collective-permute-start(bf16[2,512,768]{2,1,0:T(8,128)(2,1)S(1)} %get-tuple-element.51), channel_id=1, source_target_pairs={{0,16},{8,24},{16,0},{24,8},{1,17},{9,25},{17,1},{25,9},{2,18},{10... | collective-permute-start | bytes 4718600 | tf_op jit(solution)/shard_map/ppermute | solution.py:290
  218.5 37.3 %collective-permute-start.33 = (bf16[2,512,768]{2,1,0:T(8,128)(2,1)S(1)}, bf16[2,512,768]{2,1,0:T(8,128)(2,1)S(1)}, u32[]{:S(2)}, u32[]{:S(2)}) collective-permute-start(bf16[2,512,768]{2,1,0:T(8,128)(2,1)S(1)} %get-tuple-element.49), channel_id=1, source_target_pairs={{0,8},{8,0},{16,24},{24,16},{1,9},{9,1},{17,25},{25,17},{2,10},{10... | collective-permute-start | bytes 4718600 | tf_op jit(solution)/shard_map/ppermute | solution.py:287
  223.7 40.7 %collective-permute-start.31 = (bf16[128,2048]{1,0:T(8,128)(2,1)S(1)}, bf16[128,2048]{1,0:T(8,128)(2,1)S(1)}, u32[]{:S(2)}, u32[]{:S(2)}) collective-permute-start(bf16[128,2048]{1,0:T(8,128)(2,1)S(1)} %get-tuple-element.63), channel_id=1, source_target_pairs={{0,2},{1,3},{6,4},{7,5},{8,10},{9,11},{14,12},{15,13},{16,18},{17,... | collective-permute-start | bytes 1572872 | tf_op jit(solution)/shard_map/ppermute | solution.py:293
  253.2 18.3 %collective-permute-start.36 = (bf16[512,768]{1,0:T(8,128)(2,1)S(1)}, bf16[512,768]{1,0:T(8,128)(2,1)S(1)}, u32[]{:S(2)}, u32[]{:S(2)}) collective-permute-start(bf16[512,768]{1,0:T(8,128)(2,1)S(1)} %get-tuple-element.64), channel_id=1, source_target_pairs={{0,8},{8,0},{16,24},{24,16},{1,9},{9,1},{17,25},{25,17},{2,10},{10... | collective-permute-start | bytes 2359304 | tf_op jit(solution)/shard_map/ppermute | solution.py:287
  256.2 16.8 %collective-permute-start.35 = (bf16[512,768]{1,0:T(8,128)(2,1)S(1)}, bf16[512,768]{1,0:T(8,128)(2,1)S(1)}, u32[]{:S(2)}, u32[]{:S(2)}) collective-permute-start(bf16[512,768]{1,0:T(8,128)(2,1)S(1)} %get-tuple-element.67), channel_id=1, source_target_pairs={{0,16},{8,24},{16,0},{24,8},{1,17},{9,25},{17,1},{25,9},{2,18},{10... | collective-permute-start | bytes 2359304 | tf_op jit(solution)/shard_map/ppermute | solution.py:290
  257.2 16.9 %collective-permute-start.29 = (bf16[128,2048]{1,0:T(8,128)(2,1)S(1)}, bf16[128,2048]{1,0:T(8,128)(2,1)S(1)}, u32[]{:S(2)}, u32[]{:S(2)}) collective-permute-start(bf16[128,2048]{1,0:T(8,128)(2,1)S(1)} %get-tuple-element.63), channel_id=1, source_target_pairs={{2,4},{3,5},{4,2},{5,3},{10,12},{11,13},{12,10},{13,11},{18,20},{1... | collective-permute-start | bytes 1572872 | tf_op jit(solution)/shard_map/ppermute | solution.py:293
  257.9 18.9 %collective-permute-start.30 = (bf16[128,2048]{1,0:T(8,128)(2,1)S(1)}, bf16[128,2048]{1,0:T(8,128)(2,1)S(1)}, u32[]{:S(2)}, u32[]{:S(2)}) collective-permute-start(bf16[128,2048]{1,0:T(8,128)(2,1)S(1)} %get-tuple-element.62), channel_id=1, source_target_pairs={{0,2},{1,3},{2,0},{3,1},{4,6},{5,7},{6,4},{7,5},{8,10},{9,11},{10,... | collective-permute-start | bytes 1572872 | tf_op jit(solution)/shard_map/ppermute | solution.py:293
  264.6 30.9 %collective-permute-start.32 = (bf16[128,2048]{1,0:T(8,128)(2,1)S(1)}, bf16[128,2048]{1,0:T(8,128)(2,1)S(1)}, u32[]{:S(2)}, u32[]{:S(2)}) collective-permute-start(bf16[128,2048]{1,0:T(8,128)(2,1)S(1)} %add_convert_fusion.4), channel_id=1, source_target_pairs={{0,4},{1,5},{2,6},{3,7},{4,0},{5,1},{6,2},{7,3},{8,12},{9,13},{10,... | collective-permute-start | bytes 1572872 | tf_op jit(solution)/shard_map/ppermute | solution.py:293
  (8 other events, 6.2 us)

commit v4 on v3

--- a/solution.py
+++ b/solution.py
@@ -85,9 +85,33 @@
         return pltpu.make_async_copy(other, dst, sem)
 
 
-def load_early(copies, pieces, dst):
+def load_early(copies, pieces, dst, first=0):
     tok = pieces[0].shape[0]
-    return [copies.start(src, dst.at[pl.ds(i * tok, tok)]) for i, src in enumerate(pieces)]
+    return [copies.start(src, dst.at[pl.ds((first + i) * tok, tok)]) for i, src in enumerate(pieces)]
+
+
+def load_weights(copies, place, which, pieces, wg, wu):
+    share = pieces[0].shape[0]
+    started = []
+    for i, k in enumerate(which):
+        at = pl.ds((place[0] ^ k) * share, share)
+        started += [copies.start(pieces[2 * i], wg.at[at]), copies.start(pieces[2 * i + 1], wu.at[at])]
+    return started
+
+
+def own_body(place, tokens, w_gate, w_up, x, wg, wu, sems):
+    copies = Copies(sems)
+    started = load_early(copies, (tokens,), x) + load_weights(copies, place, (0,), (w_gate, w_up), wg, wu)
+    for c in started:
+        c.wait()
+
+
+def near_body(place, *refs):
+    pieces, weights = refs[:5], refs[5:9]
+    x, wg, wu, sems = refs[12:]
+    copies = Copies(sems)
+    for c in load_early(copies, pieces, x, 1) + load_weights(copies, place, (1, 2), weights, wg, wu):
+        c.wait()
 
 
 def load_late(copies, chip, pieces, dst):
@@ -118,16 +142,10 @@
 
 
 def pre_early_body(place, *refs):
-    pieces, w_gate, w_up = refs[:6], refs[6:10], refs[10:14]
-    act, active, slope, x, wg, wu, sems = refs[14:]
-    copies = Copies(sems)
-    share = w_gate[0].shape[0]
-    started = load_early(copies, pieces, x)
-    for k in range(4):
-        at = pl.ds((place[0] ^ k) * share, share)
-        started += [copies.start(w_gate[k], wg.at[at]), copies.start(w_up[k], wu.at[at])]
-    for c in started:
+    act, active, slope, wg, wu, sems = refs[5:]
+    for c in load_weights(Copies(sems), place, (3,), refs[:2], wg, wu):
         c.wait()
+    x = refs[2]
     pre_blocks(x, 0, x.shape[0] // 4 * 3, wg, wu, act, active, slope)
 
 
@@ -316,10 +334,9 @@
     y_early, y_late = line(y_own)
 
     wg0, wu0, wd0 = w_gate[0], w_up[0], w_down[0]
-    wg1, wu1 = to_x(wg0), to_y(wu0)
-    wg2, wu2 = to_y(wg0), to_x(wu0)
-    wg3, wu3 = to_y(wg1), to_x(wu1)
-    w_g, w_u = (wg0, wg1, wg2, wg3), (wu0, wu2, wu1, wu3)
+    wg1, wu2 = to_x(wg0), to_y(wu0)
+    wg2, wu1 = to_y(wg0), to_x(wu0)
+    wg3, wu3 = to_y(wg1), to_x(wu2)
     wd1, wd2 = to_x(wd0), to_y(wd0)
     wd3a, wd3b = to_x(wd2[:half]), to_y(wd1[half:])
 
@@ -329,25 +346,40 @@
     def anys(arrays):
         return [(a, ANY) for a in arrays]
 
-    pre_outs = [
-        ((rows, hidden), BF16, VMEM),
-        ((rows, hidden), F32, VMEM),
-        ((rows, hidden), F32, VMEM),
-        ((rows, width), BF16, VMEM),
-    ]
+    x_out = ((rows, width), BF16, VMEM)
     weight = ((width, hidden), BF16, VMEM)
+    flat = ((rows, hidden), BF16, VMEM)
+    wide = ((rows, hidden), F32, VMEM)
+    x, wg, wu = call(
+        own_body,
+        [x_out, weight, weight],
+        [(place, SMEM)] + anys((tokens, wg0, wu0)),
+        [dma(3)],
+        1000,
+        width * (2 * tok + hidden),
+    )
+    x, wg, wu = call(
+        near_body,
+        [x_out, weight, weight],
+        [(place, SMEM)] + anys(x_early[1:]) + anys((wg1, wu1, wg2, wu2)) + [(x, VMEM), (wg, VMEM), (wu, VMEM)],
+        [dma(9)],
+        1000,
+        width * (10 * tok + 2 * hidden),
+        {10: 0, 11: 1, 12: 2},
+    )
     *pre, wg, wu = call(
         pre_early_body,
-        pre_outs + [weight] * 2,
-        [(place, SMEM)] + anys(x_early) + anys(w_g + w_u),
-        [dma(14)],
+        [flat, wide, wide, weight, weight],
+        [(place, SMEM)] + anys((wg3, wu3)) + [(x, VMEM), (wg, VMEM), (wu, VMEM)],
+        [dma(2)],
         3 * rows * width * hidden,
         3 * rows * width + 8 * width * hidden + 8 * rows * hidden,
+        {4: 3, 5: 4},
     )
     act, active, slope, x = call(
         pre_late_body,
-        pre_outs,
-        [(place, SMEM)] + anys(x_late) + [(wg, VMEM), (wu, VMEM)] + [(a, VMEM) for a in pre],
+        [flat, wide, wide, x_out],
+        [(place, SMEM)] + anys(x_late) + [(a, VMEM) for a in (wg, wu, *pre, x)],
         [dma(2)],
         rows * width * hidden,
         rows * width + 4 * width * hidden + 3 * rows * hidden,

time: 297 us -> 291 us (0.980)
  waiting for transfers between devices: 171 us -> 164 us
  starting transfers between devices: 51.7 us -> 57.9 us
  local copies, waits for them, and re-layouts: 21.3 us -> 15.5 us
    ppermute x12, starting transfers between devices: 23.6 us -> 30.6 us  [hop(): lax.ppermute(block, 'expert', [(2 * a + c, 2 * b + c) for a, b in moves f...]
    unnamed x62, local copies, waits for them, and re-layouts: 21.2 us -> 15.4 us
    ppermute x9, waiting for transfers between devices: 79.7 us -> 74.4 us  [to_y(): return lax.ppermute(block, 'dp', [(i, i ^ 2) for i in range(4)])]
    pallas_call x10 -> x12, Pallas kernels: 45.1 us -> 46.1 us  [call(): pl.pallas_call(body, input_output_aliases=aliases or {}, out_shape=[jax.S...]
  transfers between devices with their start and end apart: 41 -> 41, of which waited for: 15 -> 15; matrix products, arithmetic and copies ran while one was open for 2% -> 2% of each run, Pallas kernels for 15% -> 16%
where the time goes in v4:
time: 291 us
  waiting for transfers between devices  164 us (56%)
  starting transfers between devices  57.9 us (20%)
  Pallas kernels  46.1 us (16%)
  local copies, waits for them, and re-layouts  15.5 us (5%)
  other arithmetic  6.46 us (2%)
    ppermute x12, waiting for transfers between devices, hop(): lax.ppermute(block, 'expert', [(2 * a + c, 2 * b + c) for a, b in moves f...  79.4 us
    ppermute x9, waiting for transfers between devices, to_y(): return lax.ppermute(block, 'dp', [(i, i ^ 2) for i in range(4)])  74.4 us
    pallas_call x12, Pallas kernels, call(): pl.pallas_call(body, input_output_aliases=aliases or {}, out_shape=[jax.S...  46.1 us
    ppermute x12, starting transfers between devices, hop(): lax.ppermute(block, 'expert', [(2 * a + c, 2 * b + c) for a, b in moves f...  30.6 us
    unnamed x62, local copies, waits for them, and re-layouts  15.4 us
    ppermute x9, starting transfers between devices, to_x(): return lax.ppermute(block, 'dp', [(i, i ^ 1) for i in range(4)])  11.1 us
    ppermute x9, starting transfers between devices, to_y(): return lax.ppermute(block, 'dp', [(i, i ^ 2) for i in range(4)])  9.91 us
    ppermute x9, waiting for transfers between devices, to_x(): return lax.ppermute(block, 'dp', [(i, i ^ 1) for i in range(4)])  9.73 us
  transfers between devices with their start and end apart: 41, of which 15 were waited for; matrix products, arithmetic and copies ran while one was open for 2% of the time, Pallas kernels for 16%

profile of v4, /device:TPU:0, one launch (start us, length us, event | category | flops | bytes accessed | tf_op | source)
XLA Modules:
  0.0 290.6 jit_solution(11208369471567854144)
XLA Ops:
  0.6 4.1 %collective-permute-start.6 = (bf16[128,2048]{1,0:T(8,128)(2,1)}, bf16[128,2048]{1,0:T(8,128)(2,1)S(1)}, u32[]{:S(2)}, u32[]{:S(2)}) collective-permute-start(bf16[128,2048]{1,0:T(8,128)(2,1)} %tokens.1), channel_id=1, source_target_pairs={{0,4},{1,5},{2,6},{3,7},{4,0},{5,1},{6,2},{7,3},{8,12},{9,13},{10,... | collective-permute-start | bytes 1572872 | tf_op jit(solution)/shard_map/ppermute | solution.py:311
  4.8 1.6 collective-permute-start.14
  6.3 1.5 collective-permute-start.5
  7.8 1.0 copy-done.28
  10.3 2.4 collective-permute-start.1
  12.8 17.2 %collective-permute-done.6.refs_0_ = bf16[128,2048]{1,0:T(8,128)(2,1)S(1)} collective-permute-done((bf16[128,2048]{1,0:T(8,128)(2,1)}, bf16[128,2048]{1,0:T(8,128)(2,1)S(1)}, u32[]{:S(2)}, u32[]{:S(2)}) %collective-permute-start.6) | collective-permute-done | bytes 524320 | tf_op jit(solution)/shard_map/ppermute | solution.py:311
  29.9 0.8 copy-done.20
  30.8 1.5 collective-permute-start
  32.3 2.0 collective-permute-start.10
  34.3 29.9 %collective-permute-done.1.refs_1_ = bf16[128,2176]{1,0:T(8,128)(2,1)S(1)} collective-permute-done((bf16[128,2176]{1,0:T(8,128)(2,1)S(1)}, bf16[128,2176]{1,0:T(8,128)(2,1)S(1)}, u32[]{:S(2)}, u32[]{:S(2)}) %collective-permute-start.1) | collective-permute-done | bytes 557088 | tf_op jit(solution)/shard_map/ppermute | solution.py:311
  64.1 1.8 collective-permute-start.12
  66.0 1.5 collective-permute-start.18
  67.5 0.8 copy-done.11
  68.8 1.5 collective-permute-start.25
  70.9 13.9 %collective-permute-done.12.refs_8_ = bf16[512,768]{1,0:T(8,128)(2,1)S(1)} collective-permute-done((bf16[512,768]{1,0:T(8,128)(2,1)}, bf16[512,768]{1,0:T(8,128)(2,1)S(1)}, u32[]{:S(2)}, u32[]{:S(2)}) %collective-permute-start.12) | collective-permute-done | bytes 786464 | tf_op jit(solution)/shard_map/ppermute | solution.py:308
  84.8 1.8 collective-permute-done.18.refs_6_
  86.6 0.9 copy-done.4
  87.5 0.8 copy-done.18
  88.3 13.3 %collective-permute-done.19.refs_7_ = bf16[512,768]{1,0:T(8,128)(2,1)S(1)} collective-permute-done((bf16[512,768]{1,0:T(8,128)(2,1)}, bf16[512,768]{1,0:T(8,128)(2,1)S(1)}, u32[]{:S(2)}, u32[]{:S(2)}) %collective-permute-start.19) | collective-permute-done | bytes 786464 | tf_op jit(solution)/shard_map/ppermute | solution.py:308
  101.6 0.9 copy-done.6
  102.5 13.4 %collective-permute-done.25.from_y = bf16[768,512]{1,0:T(8,128)(2,1)S(1)} collective-permute-done((bf16[768,512]{1,0:T(8,128)(2,1)}, bf16[768,512]{1,0:T(8,128)(2,1)S(1)}, u32[]{:S(2)}, u32[]{:S(2)}) %collective-permute-start.25) | collective-permute-done | bytes 786464 | tf_op jit(solution)/shard_map/ppermute | solution.py:308
  115.9 1.3 collective-permute-start.7
  117.2 0.8 copy-done.16
  118.0 1.3 collective-permute-start.11
  120.1 1.5 collective-permute-start.13
  121.6 0.8 copy-done.26
  122.4 7.3 %collective-permute-done.7.refs_1_ = bf16[128,2048]{1,0:T(8,128)(2,1)S(1)} collective-permute-done((bf16[128,2048]{1,0:T(8,128)(2,1)S(1)}, bf16[128,2048]{1,0:T(8,128)(2,1)S(1)}, u32[]{:S(2)}, u32[]{:S(2)}) %collective-permute-start.7) | collective-permute-done | bytes 524320 | tf_op jit(solution)/shard_map/ppermute | solution.py:311
  129.8 1.3 collective-permute-start.2
  131.1 0.8 copy-done.13
  131.9 1.5 collective-permute-start.8
  133.4 1.9 collective-permute-start.9
  135.4 1.1 copy-done.8
  136.6 1.1 copy-done.9
  137.7 1.0 copy-done.15
  140.7 1.0 copy-done.27
  141.8 1.9 shard_map.104
  143.7 2.3 shard_map.107.refs_5_
  146.8 1.6 collective-permute-start.26
  148.3 1.5 collective-permute-start.27
  149.8 1.9 collective-permute-start.4
  151.8 7.6 %shard_map.105 = (bf16[1024,768]{1,0:T(8,128)(2,1)S(1)}, f32[1024,768]{1,0:T(8,128)S(1)}, f32[1024,768]{1,0:T(8,128)S(1)}, bf16[2048,768]{1,0:T(8,128)(2,1)S(1)}, bf16[2048,768]{1,0:T(8,128)(2,1)S(1)}) custom-call(s32[3]{0:T(128)S(1)} %pad_add_fusion.place, ...), custom_call_target="tpu_custom_call", output_to_operand_aliasing={{3}: (4, {}), {4}: (5, {})} | custom-call | flops 4831838208 | bytes 25165824 | tf_op jit(solution)/shard_map/pallas_call | solution.py:31
  159.4 2.9 shard_map.106
  162.4 3.9 %shard_map.108 = (bf16[2,384,512]{2,1,0:T(8,128)(2,1)S(1)}, bf16[2,384,512]{2,1,0:T(8,128)(2,1)S(1)}, bf16[1024,2048]{1,0:T(8,128)(2,1)S(1)}) custom-call(s32[3]{0:T(128)S(1)} %pad_add_fusion.place, bf16[128,2176]{1,0:T(8,128)(2,1)} %collective-permute-done.refs_0_, ...), custom_call_target="tpu_custom_call", output_to_operand_aliasing={{2}: (6, {})} | custom-call | flops 1610612736 | bytes 11534336 | tf_op jit(solution)/shard_map/pallas_call | solution.py:31
  167.0 5.6 %shard_map.109 = (bf16[1024,768]{1,0:T(8,128)(2,1)S(1)}, bf16[1024,768]{1,0:T(8,128)(2,1)S(1)}) custom-call(s32[3]{0:T(128)S(1)} %pad_add_fusion.place, bf16[1024,2048]{1,0:T(8,128)(2,1)S(1)} %get-tuple-element.50.y, f32[1024,768]{1,0:T(8,128)S(1)} %get-tuple-element.51.active, f32[1024,768]{1,0:T(8,128)S(1)} %get-tuple-element.52.slope, ...), custom_call_target="tpu_custom_call" | custom-call | flops 3221225472 | bytes 16777216 | tf_op jit(solution)/shard_map/pallas_call | solution.py:31
  172.6 8.1 %shard_map.110 = (bf16[512,2048]{1,0:T(8,128)(2,1)S(1)}, bf16[512,2048]{1,0:T(8,128)(2,1)S(1)}) custom-call(bf16[1024,768]{1,0:T(8,128)(2,1)S(1)} %get-tuple-element.53.gate_delta.gd, bf16[1024,768]{1,0:T(8,128)(2,1)S(1)} %get-tuple-element.54.up_delta.ud, bf16[2048,768]{1,0:T(8,128)(2,1)S(1)} %get-tuple-element.44.refs_4_.wg, ...), custom_call_target="tpu_custom_call" | custom-call | flops 6442450944 | bytes 13631488 | tf_op jit(solution)/shard_map/pallas_call | solution.py:31
  181.5 2.4 shard_map.113
  183.9 5.2 %shard_map.112 = (bf16[2,512,768]{2,1,0:T(8,128)(2,1)S(1)}, bf16[2,512,768]{2,1,0:T(8,128)(2,1)S(1)}) custom-call(s32[3]{0:T(128)S(1)} %pad_add_fusion.place, bf16[1024,2048]{1,0:T(8,128)(2,1)S(1)} %get-tuple-element.57.x, bf16[1024,768]{1,0:T(8,128)(2,1)S(1)} %get-tuple-element.53.gate_delta.gd, bf16[1024,768]{1,0:T(8,128)(2,1)S(1)} %get-tuple-element.54.up_delta.ud), custom_call_target="tpu_custom_call" | custom-call | flops 3221225472 | bytes 10485760 | tf_op jit(solution)/shard_map/pallas_call | solution.py:31
  189.2 1.6 collective-permute-start.38
  190.8 10.6 %collective-permute-done.39 = bf16[2,384,512]{2,1,0:T(8,128)(2,1)S(1)} collective-permute-done((bf16[2,384,512]{2,1,0:T(8,128)(2,1)S(1)}, bf16[2,384,512]{2,1,0:T(8,128)(2,1)S(1)}, u32[]{:S(2)}, u32[]{:S(2)}) %collective-permute-start.39) | collective-permute-done | bytes 786464 | tf_op jit(solution)/shard_map/ppermute | solution.py:308
  201.5 1.6 collective-permute-start.40
  203.1 5.2 %shard_map.111 = (bf16[512,768]{1,0:T(8,128)(2,1)S(1)}, bf16[512,768]{1,0:T(8,128)(2,1)S(1)}, bf16[512,768]{1,0:T(8,128)(2,1)S(1)}, bf16[512,768]{1,0:T(8,128)(2,1)S(1)}) custom-call(s32[3]{0:T(128)S(1)} %pad_add_fusion.place, bf16[1024,2048]{1,0:T(8,128)(2,1)S(1)} %get-tuple-element.57.x, bf16[1024,768]{1,0:T(8,128)(2,1)S(1)} %get-tuple-element.53.gate_delta.gd, ...), custom_call_target="tpu_custom_call" | custom-call | flops 3221225472 | bytes 10485760 | tf_op jit(solution)/shard_map/pallas_call | solution.py:31
  209.6 3.5 %collective-permute-done.40 = bf16[384,512]{1,0:T(8,128)(2,1)S(1)} collective-permute-done((bf16[384,512]{1,0:T(8,128)(2,1)S(1)}, bf16[384,512]{1,0:T(8,128)(2,1)S(1)}, u32[]{:S(2)}, u32[]{:S(2)}) %collective-permute-start.40) | collective-permute-done | bytes 393248 | tf_op jit(solution)/shard_map/ppermute | solution.py:305
  214.0 6.3 %collective-permute-start.31 = (bf16[128,2048]{1,0:T(8,128)(2,1)S(1)}, bf16[128,2048]{1,0:T(8,128)(2,1)S(1)}, u32[]{:S(2)}, u32[]{:S(2)}) collective-permute-start(bf16[128,2048]{1,0:T(8,128)(2,1)S(1)} %get-tuple-element.73), channel_id=1, source_target_pairs={{0,2},{1,3},{6,4},{7,5},{8,10},{9,11},{14,12},{15,13},{16,18},{17,... | collective-permute-start | bytes 1572872 | tf_op jit(solution)/shard_map/ppermute | solution.py:311
  220.4 22.7 %collective-permute-done.34 = bf16[2,512,768]{2,1,0:T(8,128)(2,1)S(1)} collective-permute-done((bf16[2,512,768]{2,1,0:T(8,128)(2,1)S(1)}, bf16[2,512,768]{2,1,0:T(8,128)(2,1)S(1)}, u32[]{:S(2)}, u32[]{:S(2)}) %collective-permute-start.34) | collective-permute-done | bytes 1572896 | tf_op jit(solution)/shard_map/ppermute | solution.py:308
  243.5 1.3 collective-permute-start.36
  244.8 1.3 collective-permute-done.33
  247.0 0.9 maximum_bitcast_fusion
  248.7 9.9 %collective-permute-start.30 = (bf16[128,2048]{1,0:T(8,128)(2,1)S(1)}, bf16[128,2048]{1,0:T(8,128)(2,1)S(1)}, u32[]{:S(2)}, u32[]{:S(2)}) collective-permute-start(bf16[128,2048]{1,0:T(8,128)(2,1)S(1)} %get-tuple-element.72), channel_id=1, source_target_pairs={{0,2},{1,3},{2,0},{3,1},{4,6},{5,7},{6,4},{7,5},{8,10},{9,11},{10,... | collective-permute-start | bytes 1572872 | tf_op jit(solution)/shard_map/ppermute | solution.py:311
  258.8 3.1 %collective-permute-done.36 = bf16[512,768]{1,0:T(8,128)(2,1)S(1)} collective-permute-done((bf16[512,768]{1,0:T(8,128)(2,1)S(1)}, bf16[512,768]{1,0:T(8,128)(2,1)S(1)}, u32[]{:S(2)}, u32[]{:S(2)}) %collective-permute-start.36) | collective-permute-done | bytes 786464 | tf_op jit(solution)/shard_map/ppermute | solution.py:305
  261.9 1.1 fusion.5
  263.4 1.1 fusion.4
  264.5 6.4 %collective-permute-done.30 = bf16[128,2048]{1,0:T(8,128)(2,1)S(1)} collective-permute-done((bf16[128,2048]{1,0:T(8,128)(2,1)S(1)}, bf16[128,2048]{1,0:T(8,128)(2,1)S(1)}, u32[]{:S(2)}, u32[]{:S(2)}) %collective-permute-start.30) | collective-permute-done | bytes 524320 | tf_op jit(solution)/shard_map/ppermute | solution.py:311
  270.9 18.6 %collective-permute-done.32 = bf16[128,2048]{1,0:T(8,128)(2,1)S(1)} collective-permute-done((bf16[128,2048]{1,0:T(8,128)(2,1)S(1)}, bf16[128,2048]{1,0:T(8,128)(2,1)S(1)}, u32[]{:S(2)}, u32[]{:S(2)}) %collective-permute-start.32) | collective-permute-done | bytes 524320 | tf_op jit(solution)/shard_map/ppermute | solution.py:311
  289.5 1.1 add_convert_fusion.3
  (108 shorter events, 12.5 us)
Async XLA Ops:
  0.6 29.3 %collective-permute-start.6 = (bf16[128,2048]{1,0:T(8,128)(2,1)}, bf16[128,2048]{1,0:T(8,128)(2,1)S(1)}, u32[]{:S(2)}, u32[]{:S(2)}) collective-permute-start(bf16[128,2048]{1,0:T(8,128)(2,1)} %tokens.1), channel_id=1, source_target_pairs={{0,4},{1,5},{2,6},{3,7},{4,0},{5,1},{6,2},{7,3},{8,12},{9,13},{10,... | collective-permute-start | bytes 1572872 | tf_op jit(solution)/shard_map/ppermute | solution.py:311
  4.8 25.1 %collective-permute-start.14 = (bf16[128,2048]{1,0:T(8,128)(2,1)}, bf16[128,2048]{1,0:T(8,128)(2,1)S(1)}, u32[]{:S(2)}, u32[]{:S(2)}) collective-permute-start(bf16[128,2048]{1,0:T(8,128)(2,1)} %tokens.1), channel_id=1, source_target_pairs={{0,2},{1,3},{2,0},{3,1},{4,6},{5,7},{6,4},{7,5},{8,10},{9,11},{10,... | collective-permute-start | bytes 1572872 | tf_op jit(solution)/shard_map/ppermute | solution.py:311
  6.3 23.6 %collective-permute-start.15 = (bf16[128,2048]{1,0:T(8,128)(2,1)}, bf16[128,2048]{1,0:T(8,128)(2,1)S(1)}, u32[]{:S(2)}, u32[]{:S(2)}) collective-permute-start(bf16[128,2048]{1,0:T(8,128)(2,1)} %tokens.1), channel_id=1, source_target_pairs={{0,1},{1,0},{2,3},{3,2},{4,5},{5,4},{6,7},{7,6},{8,9},{9,8},{10,11... | collective-permute-start | bytes 1572872 | tf_op jit(solution)/shard_map/ppermute | solution.py:314
  6.3 25.9 %collective-permute-start.5 = (bf16[128,2048]{1,0:T(8,128)(2,1)}, bf16[128,2048]{1,0:T(8,128)(2,1)}, u32[]{:S(2)}, u32[]{:S(2)}) collective-permute-start(bf16[128,2048]{1,0:T(8,128)(2,1)} %tokens.1), channel_id=1, source_target_pairs={{2,4},{3,5},{4,2},{5,3},{10,12},{11,13},{12,10},{13,11},{18,20},{1... | collective-permute-start | bytes 1572872 | tf_op jit(solution)/shard_map/ppermute | solution.py:311
  7.8 1.0 copy-start.28
  10.3 53.8 %collective-permute-start.1 = (bf16[128,2176]{1,0:T(8,128)(2,1)S(1)}, bf16[128,2176]{1,0:T(8,128)(2,1)S(1)}, u32[]{:S(2)}, u32[]{:S(2)}) collective-permute-start(bf16[128,2176]{1,0:T(8,128)(2,1)S(1)} %shard_map.102.refs_0_), channel_id=1, source_target_pairs={{0,4},{1,5},{2,6},{3,7},{4,0},{5,1},{6,2},{7,3},{8,12},{9,13},{10,... | collective-permute-start | bytes 1671176 | tf_op jit(solution)/shard_map/ppermute | solution.py:311
  29.9 36.1 %collective-permute-start.20 = (bf16[128,2176]{1,0:T(8,128)(2,1)S(1)}, bf16[128,2176]{1,0:T(8,128)(2,1)}, u32[]{:S(2)}, u32[]{:S(2)}) collective-permute-start(bf16[128,2176]{1,0:T(8,128)(2,1)S(1)} %shard_map.102.refs_0_), channel_id=1, source_target_pairs={{0,2},{1,3},{2,0},{3,1},{4,6},{5,7},{6,4},{7,5},{8,10},{9,11},{10,... | collective-permute-start | bytes 1671176 | tf_op jit(solution)/shard_map/ppermute | solution.py:311
  29.9 37.6 %collective-permute-start.21 = (bf16[128,2176]{1,0:T(8,128)(2,1)S(1)}, bf16[128,2176]{1,0:T(8,128)(2,1)S(1)}, u32[]{:S(2)}, u32[]{:S(2)}) collective-permute-start(bf16[128,2176]{1,0:T(8,128)(2,1)S(1)} %shard_map.102.refs_0_), channel_id=1, source_target_pairs={{0,1},{1,0},{2,3},{3,2},{4,5},{5,4},{6,7},{7,6},{8,9},{9,8},{10,11... | collective-permute-start | bytes 1671176 | tf_op jit(solution)/shard_map/ppermute | solution.py:314
  29.9 0.8 copy-start.20
  30.8 38.0 %collective-permute-start = (bf16[128,2176]{1,0:T(8,128)(2,1)S(1)}, bf16[128,2176]{1,0:T(8,128)(2,1)}, u32[]{:S(2)}, u32[]{:S(2)}) collective-permute-start(bf16[128,2176]{1,0:T(8,128)(2,1)S(1)} %shard_map.102.refs_0_), channel_id=1, source_target_pairs={{2,4},{3,5},{4,2},{5,3},{10,12},{11,13},{12,10},{13,11},{18,20},{1... | collective-permute-start | bytes 1671176 | tf_op jit(solution)/shard_map/ppermute | solution.py:311
  32.3 38.1 %collective-permute-start.10 = (bf16[512,768]{1,0:T(8,128)(2,1)}, bf16[512,768]{1,0:T(8,128)(2,1)}, u32[]{:S(2)}, u32[]{:S(2)}) collective-permute-start(bf16[512,768]{1,0:T(8,128)(2,1)} %bitcast.54), channel_id=1, source_target_pairs={{0,8},{8,0},{16,24},{24,16},{1,9},{9,1},{17,25},{25,17},{2,10},{10... | collective-permute-start | bytes 2359304 | tf_op jit(solution)/shard_map/ppermute | solution.py:305
  64.1 20.6 %collective-permute-start.12 = (bf16[512,768]{1,0:T(8,128)(2,1)}, bf16[512,768]{1,0:T(8,128)(2,1)S(1)}, u32[]{:S(2)}, u32[]{:S(2)}) collective-permute-start(bf16[512,768]{1,0:T(8,128)(2,1)} %bitcast.57), channel_id=1, source_target_pairs={{0,16},{8,24},{16,0},{24,8},{1,17},{9,25},{17,1},{25,9},{2,18},{10... | collective-permute-start | bytes 2359304 | tf_op jit(solution)/shard_map/ppermute | solution.py:308
  66.0 20.6 %collective-permute-start.18 = (bf16[512,768]{1,0:T(8,128)(2,1)}, bf16[512,768]{1,0:T(8,128)(2,1)S(1)}, u32[]{:S(2)}, u32[]{:S(2)}) collective-permute-start(bf16[512,768]{1,0:T(8,128)(2,1)} %bitcast.58), channel_id=1, source_target_pairs={{0,8},{8,0},{16,24},{24,16},{1,9},{9,1},{17,25},{25,17},{2,10},{10... | collective-permute-start | bytes 2359304 | tf_op jit(solution)/shard_map/ppermute | solution.py:305
  68.3 33.3 %collective-permute-start.19 = (bf16[512,768]{1,0:T(8,128)(2,1)}, bf16[512,768]{1,0:T(8,128)(2,1)S(1)}, u32[]{:S(2)}, u32[]{:S(2)}) collective-permute-start(bf16[512,768]{1,0:T(8,128)(2,1)} %bitcast.55), channel_id=1, source_target_pairs={{0,16},{8,24},{16,0},{24,8},{1,17},{9,25},{17,1},{25,9},{2,18},{10... | collective-permute-start | bytes 2359304 | tf_op jit(solution)/shard_map/ppermute | solution.py:308
  68.8 47.1 %collective-permute-start.25 = (bf16[768,512]{1,0:T(8,128)(2,1)}, bf16[768,512]{1,0:T(8,128)(2,1)S(1)}, u32[]{:S(2)}, u32[]{:S(2)}) collective-permute-start(bf16[768,512]{1,0:T(8,128)(2,1)} %bitcast.60), channel_id=1, source_target_pairs={{0,16},{8,24},{16,0},{24,8},{1,17},{9,25},{17,1},{25,9},{2,18},{10... | collective-permute-start | bytes 2359304 | tf_op jit(solution)/shard_map/ppermute | solution.py:308
  70.3 47.7 %collective-permute-start.24 = (bf16[768,512]{1,0:T(8,128)(2,1)}, bf16[768,512]{1,0:T(8,128)(2,1)S(1)}, u32[]{:S(2)}, u32[]{:S(2)}) collective-permute-start(bf16[768,512]{1,0:T(8,128)(2,1)} %bitcast.61), channel_id=1, source_target_pairs={{0,8},{8,0},{16,24},{24,16},{1,9},{9,1},{17,25},{25,17},{2,10},{10... | collective-permute-start | bytes 2359304 | tf_op jit(solution)/shard_map/ppermute | solution.py:305
  84.8 34.6 %collective-permute-start.16 = (bf16[128,2048]{1,0:T(8,128)(2,1)S(1)}, bf16[128,2048]{1,0:T(8,128)(2,1)S(1)}, u32[]{:S(2)}, u32[]{:S(2)}) collective-permute-start(bf16[128,2048]{1,0:T(8,128)(2,1)S(1)} %collective-permute-done.6.refs_0_), channel_id=1, source_target_pairs={{0,1},{1,0},{2,3},{3,2},{4,5},{5,4},{6,7},{7,6},{8,9},{9,8},{10,11... | collective-permute-start | bytes 1572872 | tf_op jit(solution)/shard_map/ppermute | solution.py:314
  86.6 0.9 copy-start.4
  87.5 34.2 %collective-permute-start.17 = (bf16[128,2048]{1,0:T(8,128)(2,1)S(1)}, bf16[128,2048]{1,0:T(8,128)(2,1)S(1)}, u32[]{:S(2)}, u32[]{:S(2)}) collective-permute-start(bf16[128,2048]{1,0:T(8,128)(2,1)S(1)} %collective-permute-done.14.refs_1_), channel_id=1, source_target_pairs={{0,1},{1,0},{2,3},{3,2},{4,5},{5,4},{6,7},{7,6},{8,9},{9,8},{10,11... | collective-permute-start | bytes 1572872 | tf_op jit(solution)/shard_map/ppermute | solution.py:314
  101.6 0.9 copy-start.6
  102.5 28.6 %collective-permute-start.22 = (bf16[128,2176]{1,0:T(8,128)(2,1)S(1)}, bf16[128,2176]{1,0:T(8,128)(2,1)S(1)}, u32[]{:S(2)}, u32[]{:S(2)}) collective-permute-start(bf16[128,2176]{1,0:T(8,128)(2,1)S(1)} %collective-permute-done.1.refs_1_), channel_id=1, source_target_pairs={{0,1},{1,0},{2,3},{3,2},{4,5},{5,4},{6,7},{7,6},{8,9},{9,8},{10,11... | collective-permute-start | bytes 1671176 | tf_op jit(solution)/shard_map/ppermute | solution.py:314
  115.9 23.6 %copy-start = (bf16[768,512]{1,0:T(8,128)(2,1)}, bf16[768,512]{1,0:T(8,128)(2,1)S(1)}, u32[]{:S(2)}) copy-start(bf16[768,512]{1,0:T(8,128)(2,1)S(1)} %collective-permute-done.25.from_y) | copy-start | bytes 2359300
  115.9 13.8 %collective-permute-start.7 = (bf16[128,2048]{1,0:T(8,128)(2,1)S(1)}, bf16[128,2048]{1,0:T(8,128)(2,1)S(1)}, u32[]{:S(2)}, u32[]{:S(2)}) collective-permute-start(bf16[128,2048]{1,0:T(8,128)(2,1)S(1)} %collective-permute-done.6.refs_0_), channel_id=1, source_target_pairs={{4,6},{5,7},{2,0},{3,1},{12,14},{13,15},{10,8},{11,9},{20,22},{21,... | collective-permute-start | bytes 1572872 | tf_op jit(solution)/shard_map/ppermute | solution.py:311
  118.0 21.5 %copy-start.2 = (bf16[768,512]{1,0:T(8,128)(2,1)}, bf16[768,512]{1,0:T(8,128)(2,1)S(1)}, u32[]{:S(2)}) copy-start(bf16[768,512]{1,0:T(8,128)(2,1)S(1)} %collective-permute-done.24.from_x) | copy-start | bytes 2359300
  118.0 30.3 %collective-permute-start.11 = (bf16[512,768]{1,0:T(8,128)(2,1)}, bf16[512,768]{1,0:T(8,128)(2,1)}, u32[]{:S(2)}, u32[]{:S(2)}) collective-permute-start(bf16[512,768]{1,0:T(8,128)(2,1)} %collective-permute-done.10.refs_5_), channel_id=1, source_target_pairs={{0,16},{8,24},{16,0},{24,8},{1,17},{9,25},{17,1},{25,9},{2,18},{10... | collective-permute-start | bytes 2359304 | tf_op jit(solution)/shard_map/ppermute | solution.py:308
  120.1 29.7 %collective-permute-start.13 = (bf16[512,768]{1,0:T(8,128)(2,1)S(1)}, bf16[512,768]{1,0:T(8,128)(2,1)}, u32[]{:S(2)}, u32[]{:S(2)}) collective-permute-start(bf16[512,768]{1,0:T(8,128)(2,1)S(1)} %collective-permute-done.12.refs_8_), channel_id=1, source_target_pairs={{0,8},{8,0},{16,24},{24,16},{1,9},{9,1},{17,25},{25,17},{2,10},{10... | collective-permute-start | bytes 2359304 | tf_op jit(solution)/shard_map/ppermute | solution.py:305
  122.4 11.0 %collective-permute-start.23 = (bf16[128,2176]{1,0:T(8,128)(2,1)}, bf16[128,2176]{1,0:T(8,128)(2,1)}, u32[]{:S(2)}, u32[]{:S(2)}) collective-permute-start(bf16[128,2176]{1,0:T(8,128)(2,1)} %collective-permute-done.20.refs_2_), channel_id=1, source_target_pairs={{0,1},{1,0},{2,3},{3,2},{4,5},{5,4},{6,7},{7,6},{8,9},{9,8},{10,11... | collective-permute-start | bytes 1671176 | tf_op jit(solution)/shard_map/ppermute | solution.py:314
  129.8 1.3 copy-start.22
  129.8 17.0 %collective-permute-start.2 = (bf16[128,2176]{1,0:T(8,128)(2,1)S(1)}, bf16[128,2176]{1,0:T(8,128)(2,1)}, u32[]{:S(2)}, u32[]{:S(2)}) collective-permute-start(bf16[128,2176]{1,0:T(8,128)(2,1)S(1)} %collective-permute-done.1.refs_1_), channel_id=1, source_target_pairs={{4,6},{5,7},{2,0},{3,1},{12,14},{13,15},{10,8},{11,9},{20,22},{21,... | collective-permute-start | bytes 1671176 | tf_op jit(solution)/shard_map/ppermute | solution.py:311
  131.9 14.1 %collective-permute-start.8 = (bf16[128,2048]{1,0:T(8,128)(2,1)}, bf16[128,2048]{1,0:T(8,128)(2,1)}, u32[]{:S(2)}, u32[]{:S(2)}) collective-permute-start(bf16[128,2048]{1,0:T(8,128)(2,1)} %collective-permute-done.5.refs_0_), channel_id=1, source_target_pairs={{2,3},{3,2},{4,5},{5,4},{10,11},{11,10},{12,13},{13,12},{18,19},{1... | collective-permute-start | bytes 1572872 | tf_op jit(solution)/shard_map/ppermute | solution.py:314
  133.4 26.0 %collective-permute-start.9 = (bf16[128,2048]{1,0:T(8,128)(2,1)}, bf16[128,2048]{1,0:T(8,128)(2,1)S(1)}, u32[]{:S(2)}, u32[]{:S(2)}) collective-permute-start(bf16[128,2048]{1,0:T(8,128)(2,1)} %copy-done.22), channel_id=1, source_target_pairs={{0,1},{1,0},{6,7},{7,6},{8,9},{9,8},{14,15},{15,14},{16,17},{17,16... | collective-permute-start | bytes 1572872 | tf_op jit(solution)/shard_map/ppermute | solution.py:314
  135.4 1.1 copy-start.8
  136.5 1.1 copy-start.9
  137.7 1.0 copy-start.15
  138.7 1.1 copy-start.5
  138.7 1.4 copy-start.7
  138.7 1.5 copy-start.17
  138.7 1.7 copy-start.19
  138.7 1.8 copy-start.21
  138.7 2.0 copy-start.25
  140.7 1.0 copy-start.27
  141.8 2.0 copy-start.12
  141.8 2.0 copy-start.14
  146.0 16.3 %collective-permute-start.3 = (bf16[128,2176]{1,0:T(8,128)(2,1)}, bf16[128,2176]{1,0:T(8,128)(2,1)S(1)}, u32[]{:S(2)}, u32[]{:S(2)}) collective-permute-start(bf16[128,2176]{1,0:T(8,128)(2,1)} %collective-permute-done.refs_0_), channel_id=1, source_target_pairs={{2,3},{3,2},{4,5},{5,4},{10,11},{11,10},{12,13},{13,12},{18,19},{1... | collective-permute-start | bytes 1671176 | tf_op jit(solution)/shard_map/ppermute | solution.py:314
  146.8 20.2 %collective-permute-start.26 = (bf16[384,512]{1,0:T(8,128)(2,1)S(1)}, bf16[384,512]{1,0:T(8,128)(2,1)S(1)}, u32[]{:S(2)}, u32[]{:S(2)}) collective-permute-start(bf16[384,512]{1,0:T(8,128)(2,1)S(1)} %slice.61), channel_id=1, source_target_pairs={{0,8},{8,0},{16,24},{24,16},{1,9},{9,1},{17,25},{25,17},{2,10},{10... | collective-permute-start | bytes 1179656 | tf_op jit(solution)/shard_map/ppermute | solution.py:305
  148.3 18.6 %collective-permute-start.27 = (bf16[384,512]{1,0:T(8,128)(2,1)S(1)}, bf16[384,512]{1,0:T(8,128)(2,1)S(1)}, u32[]{:S(2)}, u32[]{:S(2)}) collective-permute-start(bf16[384,512]{1,0:T(8,128)(2,1)S(1)} %slice.62), channel_id=1, source_target_pairs={{0,16},{8,24},{16,0},{24,8},{1,17},{9,25},{17,1},{25,9},{2,18},{10... | collective-permute-start | bytes 1179656 | tf_op jit(solution)/shard_map/ppermute | solution.py:308
  149.8 12.5 %collective-permute-start.4 = (bf16[128,2176]{1,0:T(8,128)(2,1)}, bf16[128,2176]{1,0:T(8,128)(2,1)S(1)}, u32[]{:S(2)}, u32[]{:S(2)}) collective-permute-start(bf16[128,2176]{1,0:T(8,128)(2,1)} %collective-permute-done.2.refs_1_), channel_id=1, source_target_pairs={{0,1},{1,0},{6,7},{7,6},{8,9},{9,8},{14,15},{15,14},{16,17},{17,16... | collective-permute-start | bytes 1671176 | tf_op jit(solution)/shard_map/ppermute | solution.py:314
  151.8 7.7 %copy-start.23 = (bf16[128,2048]{1,0:T(8,128)(2,1)S(1)}, bf16[128,2048]{1,0:T(8,128)(2,1)}, u32[]{:S(2)}) copy-start(bf16[128,2048]{1,0:T(8,128)(2,1)} %copy-done.22) | copy-start | bytes 1572868
  162.4 4.6 %copy-start.1 = (bf16[768,512]{1,0:T(8,128)(2,1)S(1)}, bf16[768,512]{1,0:T(8,128)(2,1)}, u32[]{:S(2)}) copy-start(bf16[768,512]{1,0:T(8,128)(2,1)} %copy-done) | copy-start | bytes 2359300
  162.4 4.6 %copy-start.3 = (bf16[768,512]{1,0:T(8,128)(2,1)S(1)}, bf16[768,512]{1,0:T(8,128)(2,1)}, u32[]{:S(2)}) copy-start(bf16[768,512]{1,0:T(8,128)(2,1)} %copy-done.2) | copy-start | bytes 2359300
  162.4 4.6 %copy-start.10 = (bf16[1,768,512]{2,1,0:T(8,128)(2,1)S(1)}, bf16[1,768,512]{2,1,0:T(8,128)(2,1)}, u32[]{:S(2)}) copy-start(bf16[1,768,512]{2,1,0:T(8,128)(2,1)} %param.13) | copy-start | bytes 2359300
  166.3 22.8 %collective-permute-start.37 = (bf16[2,384,512]{2,1,0:T(8,128)(2,1)S(1)}, bf16[2,384,512]{2,1,0:T(8,128)(2,1)S(1)}, u32[]{:S(2)}, u32[]{:S(2)}) collective-permute-start(bf16[2,384,512]{2,1,0:T(8,128)(2,1)S(1)} %get-tuple-element.67), channel_id=1, source_target_pairs={{0,8},{8,0},{16,24},{24,16},{1,9},{9,1},{17,25},{25,17},{2,10},{10... | collective-permute-start | bytes 2359304 | tf_op jit(solution)/shard_map/ppermute | solution.py:305
  180.7 32.5 %collective-permute-start.28 = (bf16[512,2048]{1,0:T(8,128)(2,1)S(1)}, bf16[512,2048]{1,0:T(8,128)(2,1)S(1)}, u32[]{:S(2)}, u32[]{:S(2)}) collective-permute-start(bf16[512,2048]{1,0:T(8,128)(2,1)S(1)} %get-tuple-element.56), channel_id=1, source_target_pairs={{0,1},{1,0},{2,3},{3,2},{4,5},{5,4},{6,7},{7,6},{8,9},{9,8},{10,11... | collective-permute-start | bytes 6291464 | tf_op jit(solution)/shard_map/ppermute | solution.py:314
  181.0 20.4 %collective-permute-start.39 = (bf16[2,384,512]{2,1,0:T(8,128)(2,1)S(1)}, bf16[2,384,512]{2,1,0:T(8,128)(2,1)S(1)}, u32[]{:S(2)}, u32[]{:S(2)}) collective-permute-start(bf16[2,384,512]{2,1,0:T(8,128)(2,1)S(1)} %get-tuple-element.70), channel_id=1, source_target_pairs={{0,16},{8,24},{16,0},{24,8},{1,17},{9,25},{17,1},{25,9},{2,18},{10... | collective-permute-start | bytes 2359304 | tf_op jit(solution)/shard_map/ppermute | solution.py:308
  189.2 20.2 %collective-permute-start.38 = (bf16[384,512]{1,0:T(8,128)(2,1)S(1)}, bf16[384,512]{1,0:T(8,128)(2,1)S(1)}, u32[]{:S(2)}, u32[]{:S(2)}) collective-permute-start(bf16[384,512]{1,0:T(8,128)(2,1)S(1)} %fusion.9), channel_id=1, source_target_pairs={{0,16},{8,24},{16,0},{24,8},{1,17},{9,25},{17,1},{25,9},{2,18},{10... | collective-permute-start | bytes 1179656 | tf_op jit(solution)/shard_map/ppermute | solution.py:308
  201.5 11.5 %collective-permute-start.40 = (bf16[384,512]{1,0:T(8,128)(2,1)S(1)}, bf16[384,512]{1,0:T(8,128)(2,1)S(1)}, u32[]{:S(2)}, u32[]{:S(2)}) collective-permute-start(bf16[384,512]{1,0:T(8,128)(2,1)S(1)} %fusion.6), channel_id=1, source_target_pairs={{0,8},{8,0},{16,24},{24,16},{1,9},{9,1},{17,25},{25,17},{2,10},{10... | collective-permute-start | bytes 1179656 | tf_op jit(solution)/shard_map/ppermute | solution.py:305
  208.3 34.8 %collective-permute-start.34 = (bf16[2,512,768]{2,1,0:T(8,128)(2,1)S(1)}, bf16[2,512,768]{2,1,0:T(8,128)(2,1)S(1)}, u32[]{:S(2)}, u32[]{:S(2)}) collective-permute-start(bf16[2,512,768]{2,1,0:T(8,128)(2,1)S(1)} %get-tuple-element.61), channel_id=1, source_target_pairs={{0,16},{8,24},{16,0},{24,8},{1,17},{9,25},{17,1},{25,9},{2,18},{10... | collective-permute-start | bytes 4718600 | tf_op jit(solution)/shard_map/ppermute | solution.py:308
  208.9 37.2 %collective-permute-start.33 = (bf16[2,512,768]{2,1,0:T(8,128)(2,1)S(1)}, bf16[2,512,768]{2,1,0:T(8,128)(2,1)S(1)}, u32[]{:S(2)}, u32[]{:S(2)}) collective-permute-start(bf16[2,512,768]{2,1,0:T(8,128)(2,1)S(1)} %get-tuple-element.59), channel_id=1, source_target_pairs={{0,8},{8,0},{16,24},{24,16},{1,9},{9,1},{17,25},{25,17},{2,10},{10... | collective-permute-start | bytes 4718600 | tf_op jit(solution)/shard_map/ppermute | solution.py:305
  214.0 44.5 %collective-permute-start.31 = (bf16[128,2048]{1,0:T(8,128)(2,1)S(1)}, bf16[128,2048]{1,0:T(8,128)(2,1)S(1)}, u32[]{:S(2)}, u32[]{:S(2)}) collective-permute-start(bf16[128,2048]{1,0:T(8,128)(2,1)S(1)} %get-tuple-element.73), channel_id=1, source_target_pairs={{0,2},{1,3},{6,4},{7,5},{8,10},{9,11},{14,12},{15,13},{16,18},{17,... | collective-permute-start | bytes 1572872 | tf_op jit(solution)/shard_map/ppermute | solution.py:311
  243.5 18.4 %collective-permute-start.36 = (bf16[512,768]{1,0:T(8,128)(2,1)S(1)}, bf16[512,768]{1,0:T(8,128)(2,1)S(1)}, u32[]{:S(2)}, u32[]{:S(2)}) collective-permute-start(bf16[512,768]{1,0:T(8,128)(2,1)S(1)} %get-tuple-element.74), channel_id=1, source_target_pairs={{0,8},{8,0},{16,24},{24,16},{1,9},{9,1},{17,25},{25,17},{2,10},{10... | collective-permute-start | bytes 2359304 | tf_op jit(solution)/shard_map/ppermute | solution.py:305
  246.5 16.9 %collective-permute-start.35 = (bf16[512,768]{1,0:T(8,128)(2,1)S(1)}, bf16[512,768]{1,0:T(8,128)(2,1)S(1)}, u32[]{:S(2)}, u32[]{:S(2)}) collective-permute-start(bf16[512,768]{1,0:T(8,128)(2,1)S(1)} %get-tuple-element.77), channel_id=1, source_target_pairs={{0,16},{8,24},{16,0},{24,8},{1,17},{9,25},{17,1},{25,9},{2,18},{10... | collective-permute-start | bytes 2359304 | tf_op jit(solution)/shard_map/ppermute | solution.py:308
  248.0 16.5 %collective-permute-start.29 = (bf16[128,2048]{1,0:T(8,128)(2,1)S(1)}, bf16[128,2048]{1,0:T(8,128)(2,1)S(1)}, u32[]{:S(2)}, u32[]{:S(2)}) collective-permute-start(bf16[128,2048]{1,0:T(8,128)(2,1)S(1)} %get-tuple-element.73), channel_id=1, source_target_pairs={{2,4},{3,5},{4,2},{5,3},{10,12},{11,13},{12,10},{13,11},{18,20},{1... | collective-permute-start | bytes 1572872 | tf_op jit(solution)/shard_map/ppermute | solution.py:311
  248.7 22.2 %collective-permute-start.30 = (bf16[128,2048]{1,0:T(8,128)(2,1)S(1)}, bf16[128,2048]{1,0:T(8,128)(2,1)S(1)}, u32[]{:S(2)}, u32[]{:S(2)}) collective-permute-start(bf16[128,2048]{1,0:T(8,128)(2,1)S(1)} %get-tuple-element.72), channel_id=1, source_target_pairs={{0,2},{1,3},{2,0},{3,1},{4,6},{5,7},{6,4},{7,5},{8,10},{9,11},{10,... | collective-permute-start | bytes 1572872 | tf_op jit(solution)/shard_map/ppermute | solution.py:311
  258.7 30.8 %collective-permute-start.32 = (bf16[128,2048]{1,0:T(8,128)(2,1)S(1)}, bf16[128,2048]{1,0:T(8,128)(2,1)S(1)}, u32[]{:S(2)}, u32[]{:S(2)}) collective-permute-start(bf16[128,2048]{1,0:T(8,128)(2,1)S(1)} %add_convert_fusion.4), channel_id=1, source_target_pairs={{0,4},{1,5},{2,6},{3,7},{4,0},{5,1},{6,2},{7,3},{8,12},{9,13},{10,... | collective-permute-start | bytes 1572872 | tf_op jit(solution)/shard_map/ppermute | solution.py:311
  (8 other events, 6.2 us)

commit v5 on v4

--- a/solution.py
+++ b/solution.py
@@ -1,5 +1,3 @@
-import functools
-
 import jax
 import jax.numpy as jnp
 from jax import lax
@@ -14,7 +12,6 @@
 VMEM = pl.BlockSpec(memory_space=pltpu.VMEM)
 SMEM = pl.BlockSpec(memory_space=pltpu.SMEM)
 LIMIT = 24 * 1024 * 1024
-LANES = 128
 NN = (((1,), (0,)), ((), ()))
 NT = (((1,), (1,)), ((), ()))
 
@@ -43,21 +40,6 @@
 TWO = ((0, 2), (1, 3), (2, 0), (3, 1))
 OUTER = ((0, 1), (1, 0), (2, 3), (3, 2))
 INNER = ((1, 2), (2, 1))
-
-
-def prep_body(experts, routes, gates, rows, out):
-    tok, width = rows.shape
-    line = lax.broadcasted_iota(jnp.int32, (LANES, tok), 0)
-    term, named = line // experts, line % experts
-    value = jnp.zeros((LANES, tok), F32)
-    for k in range(routes.shape[0]):
-        value += jnp.where(routes[k : k + 1, :] == named, gates[k : k + 1, :], 0.0)
-    high = value.astype(BF16).astype(F32)
-    mid = (value - high).astype(BF16).astype(F32)
-    low = value - high - mid
-    value = jnp.where(term == 0, high, jnp.where(term == 1, mid, jnp.where(term == 2, low, 0.0)))
-    out[:, :width] = rows[...]
-    out[:, width:] = jnp.transpose(value).astype(BF16)
 
 
 class Copies:
@@ -158,34 +140,40 @@
     pre_blocks(x, 3 * count, count, wg, wu, act, active, slope)
 
 
-def scale(experts, expert, raw, y, first):
-    tok, width = raw.shape[0] // 2, y.shape[1]
-    lane = lax.broadcasted_iota(jnp.int32, (tok, LANES), 1)
-    mine = jnp.logical_and(lane % experts == expert, lane < 3 * experts)
+def scale(gates, place, which, raw, y, first):
+    tok = raw.shape[0] // 2
+    chip, core = place[1], place[2] % 2
+    source = {"own": chip, "two": (chip + 2) % 4, "outer": chip ^ 1, "last": 3 - chip}[which]
+    column = jnp.transpose(gates[...])
+    lane = lax.broadcasted_iota(jnp.int32, column.shape, 1)
     for i in (0, 1):
-        gate = jnp.sum(jnp.where(mine, raw[i * tok : (i + 1) * tok, width:].astype(F32), 0.0), axis=1, keepdims=True)
-        y[first + i * tok : first + (i + 1) * tok, :] = (raw[i * tok : (i + 1) * tok, :width].astype(F32) * gate).astype(
-            BF16
-        )
-
-
-def scale_early_body(experts, place, *refs):
-    pieces = refs[:6]
-    y, raw, sems = refs[6:]
+        gate = jnp.sum(jnp.where(lane == 2 * source + (core ^ i), column, 0.0), axis=1, keepdims=True)
+        r = slice(i * tok, (i + 1) * tok)
+        y[pl.ds(first[i], tok), :] = (raw[r, :].astype(F32) * gate).astype(BF16)
+
+
+def scale_early_body(place, *refs):
+    pieces, gates = refs[:6], refs[6]
+    y, raw, sems = refs[7:]
     tok = pieces[0].shape[0]
-    started = load_early(Copies(sems), pieces, raw)
+    copies = Copies(sems)
+    started = []
     for i in range(3):
-        started[2 * i].wait()
-        started[2 * i + 1].wait()
-        scale(experts, place[2], raw.at[pl.ds(2 * i * tok, 2 * tok)], y, 2 * i * tok)
-
-
-def down_send_body(experts, place, *refs):
-    pieces, act = refs[:4], refs[4]
-    send_a, send_b, y, raw, sems = refs[6:]
+        at = [raw.at[pl.ds((2 * i + c) * tok, tok)] for c in (0, 1)]
+        started.append((copies.start(pieces[i], at[0]), copies.start(pieces[3 + i], at[1])))
+    for i, which in enumerate(("own", "two", "outer")):
+        for c in started[i]:
+            c.wait()
+        scale(gates, place, which, raw.at[pl.ds(2 * i * tok, 2 * tok)], y, (i * tok, (3 + i) * tok))
+
+
+def down_send_body(place, *refs):
+    pieces, gates, act = refs[:4], refs[4], refs[5]
+    send_a, send_b, y, raw, sems = refs[7:]
+    tok = raw.shape[0] // 2
     for c in load_late(Copies(sems), place[1], pieces, raw):
         c.wait()
-    scale(experts, place[2], raw, y, y.shape[0] - raw.shape[0])
+    scale(gates, place, "last", raw, y, (6 * tok, 7 * tok))
     down_blocks(place, act, y, ((0, 1, send_a, 0), (0, 3, send_a, 1), (1, 2, send_b, 0), (1, 3, send_b, 1)))
 
 
@@ -208,16 +196,16 @@
     down_blocks(place, act, y, ((0, 0, a0, None), (0, 2, a1, None), (1, 0, b0, None), (1, 1, b1, None)))
 
 
-def back_body(place, y, active, slope, own, from_x, from_y, diag_a, diag_b, gate_delta, up_delta, w, sems):
+def back_body(place, y, active, slope, *refs):
+    own, halves = refs[0], refs[1:7]
+    gate_delta, up_delta, w, sems = refs[7:]
     me = place[0]
     copies = Copies(sems)
     hidden, share = own.shape
     half = hidden // 2
-    started = []
-    for k, src in ((0, own), (1, from_x), (2, from_y)):
-        started.append(copies.start(src, w.at[me ^ k]))
-    started.append(copies.start(diag_a, w.at[me ^ 3, pl.ds(0, half)]))
-    started.append(copies.start(diag_b, w.at[me ^ 3, pl.ds(half, half)]))
+    started = [copies.start(own, w.at[me])]
+    for i, src in enumerate(halves):
+        started.append(copies.start(src, w.at[me ^ (1 + i // 2), pl.ds(i % 2 * half, half)]))
     for c in started:
         c.wait()
     rows = y.shape[0]
@@ -323,22 +311,20 @@
         return early, late
 
     x_early, x_late = line(tokens)
-    (y_own,) = call(
-        functools.partial(prep_body, experts),
-        [((tok, width + LANES), BF16, VMEM)],
-        [(routes.T, VMEM), (gate_values.T, VMEM), (out_grad, VMEM)],
-        [],
-        1000,
-        4 * tok * width,
-    )
-    y_early, y_late = line(y_own)
+    onehot = routes[:, :, None] == jnp.arange(experts, dtype=routes.dtype)
+    gates = jnp.sum(jnp.where(onehot, gate_values[:, :, None], 0.0), axis=1).T.reshape(experts, 1, tok)
+    gates = lax.all_to_all(gates, "expert", split_axis=0, concat_axis=0, tiled=True)
+    gates = gates.reshape(experts, tok)
+    y_early, y_late = line(out_grad)
 
     wg0, wu0, wd0 = w_gate[0], w_up[0], w_down[0]
     wg1, wu2 = to_x(wg0), to_y(wu0)
     wg2, wu1 = to_y(wg0), to_x(wu0)
     wg3, wu3 = to_y(wg1), to_x(wu2)
-    wd1, wd2 = to_x(wd0), to_y(wd0)
-    wd3a, wd3b = to_x(wd2[:half]), to_y(wd1[half:])
+    da0, db0 = wd0[:half], wd0[half:]
+    da1, db2 = to_x(da0), to_y(db0)
+    da2, db1 = to_y(da0), to_x(db0)
+    da3, db3 = to_y(da1), to_x(db2)
 
     def dma(n):
         return pltpu.SemaphoreType.DMA((n,))
@@ -386,29 +372,29 @@
         {7 + i: i for i in range(4)},
     )
     (y,) = call(
-        functools.partial(scale_early_body, experts),
+        scale_early_body,
         [((rows, width), BF16, VMEM)],
-        [(place, SMEM)] + anys(y_early),
-        [pltpu.VMEM((6 * tok, width + LANES), BF16), dma(6)],
+        [(place, SMEM)] + anys(y_early) + [(gates, VMEM)],
+        [pltpu.VMEM((6 * tok, width), BF16), dma(6)],
         rows * width,
         4 * rows * width,
     )
     piece = (2, half, share)
     send_a, send_b, y = call(
-        functools.partial(down_send_body, experts),
+        down_send_body,
         [(piece, BF16, VMEM)] * 2 + [((rows, width), BF16, VMEM)],
-        [(place, SMEM)] + anys(y_late) + [(act, VMEM), (y, VMEM)],
-        [pltpu.VMEM((2 * tok, width + LANES), BF16), dma(2)],
+        [(place, SMEM)] + anys(y_late) + [(gates, VMEM), (act, VMEM), (y, VMEM)],
+        [pltpu.VMEM((2 * tok, width), BF16), dma(2)],
         rows * width * hidden,
         2 * (2 * rows * width + rows * hidden + width * hidden // 2),
-        {6: 2},
+        {7: 2},
     )
     got_a, got_b = to_x(send_a), to_y(send_b)
     gate_delta, up_delta = call(
         back_body,
         [((rows, hidden), BF16, VMEM)] * 2,
-        [(place, SMEM), (y, VMEM), (active, VMEM), (slope, VMEM)] + [(a, ANY) for a in (wd0, wd1, wd2, wd3a, wd3b)],
-        [pltpu.VMEM((4, hidden, share), BF16), dma(5)],
+        [(place, SMEM), (y, VMEM), (active, VMEM), (slope, VMEM)] + anys((wd0, da1, db1, da2, db2, da3, db3)),
+        [pltpu.VMEM((4, hidden, share), BF16), dma(7)],
         2 * rows * width * hidden,
         2 * (rows * width + width * hidden) + 12 * rows * hidden,
     )

time: 291 us -> 287 us (0.986)
  waiting for transfers between devices: 164 us -> 143 us
  local copies, waits for them, and re-layouts: 15.5 us -> 28.7 us
    ppermute x12, waiting for transfers between devices: 79.4 us -> 63.7 us  [hop(): lax.ppermute(block, 'expert', [(2 * a + c, 2 * b + c) for a, b in moves f...]
    unnamed x62 -> x86, local copies, waits for them, and re-layouts: 15.4 us -> 27.4 us
    ppermute x12, starting transfers between devices: 30.6 us -> 19.7 us  [hop(): lax.ppermute(block, 'expert', [(2 * a + c, 2 * b + c) for a, b in moves f...]
    ppermute x9 -> x10, waiting for transfers between devices: 74.4 us -> 63.9 us  [to_y(): return lax.ppermute(block, 'dp', [(i, i ^ 2) for i in range(4)])]
    all_to_all x0 -> x1, starting transfers between devices: none -> 7.92 us  [dense(): lax.all_to_all(gates, 'expert', split_axis=0, concat_axis=0, tiled=True)]
    ppermute x9 -> x10, waiting for transfers between devices: 9.73 us -> 15.4 us  [to_x(): return lax.ppermute(block, 'dp', [(i, i ^ 1) for i in range(4)])]
    pallas_call x12 -> x11, Pallas kernels: 46.1 us -> 48.3 us  [call(): pl.pallas_call(body, input_output_aliases=aliases or {}, out_shape=[jax.S...]
    ppermute x9 -> x10, starting transfers between devices: 9.91 us -> 11.3 us  [to_y(): return lax.ppermute(block, 'dp', [(i, i ^ 2) for i in range(4)])]
  transfers between devices with their start and end apart: 41 -> 44, of which waited for: 15 -> 13; matrix products, arithmetic and copies ran while one was open for 2% -> 2% of each run, Pallas kernels for 16% -> 17%
where the time goes in v5:
time: 287 us; the launch traced here: 286 us
  waiting for transfers between devices  143 us (50%)
  starting transfers between devices  57.3 us (20%)
  Pallas kernels  48.3 us (17%)
  local copies, waits for them, and re-layouts  28.7 us (10%)
  other arithmetic  6.98 us (2%)
    ppermute x10, waiting for transfers between devices, to_y(): return lax.ppermute(block, 'dp', [(i, i ^ 2) for i in range(4)])  63.9 us
    ppermute x12, waiting for transfers between devices, hop(): lax.ppermute(block, 'expert', [(2 * a + c, 2 * b + c) for a, b in moves f...  63.7 us
    pallas_call x11, Pallas kernels, call(): pl.pallas_call(body, input_output_aliases=aliases or {}, out_shape=[jax.S...  48.3 us
    unnamed x86, local copies, waits for them, and re-layouts  27.4 us
    ppermute x12, starting transfers between devices, hop(): lax.ppermute(block, 'expert', [(2 * a + c, 2 * b + c) for a, b in moves f...  19.7 us
    ppermute x10, waiting for transfers between devices, to_x(): return lax.ppermute(block, 'dp', [(i, i ^ 1) for i in range(4)])  15.4 us
    ppermute x10, starting transfers between devices, to_y(): return lax.ppermute(block, 'dp', [(i, i ^ 2) for i in range(4)])  11.3 us
    ppermute x10, starting transfers between devices, to_x(): return lax.ppermute(block, 'dp', [(i, i ^ 1) for i in range(4)])  11.1 us
  transfers between devices with their start and end apart: 44, of which 13 were waited for; matrix products, arithmetic and copies ran while one was open for 2% of the time, Pallas kernels for 17%

profile of v5, /device:TPU:0, one launch (start us, length us, event | category | flops | bytes accessed | tf_op | source)
XLA Modules:
  0.0 285.5 jit_solution(8877366084579093751)
XLA Ops:
  0.7 1.3 slice_bitcast_fusion.8
  2.0 3.0 %collective-permute-start.24 = (bf16[384,512]{1,0:T(8,128)(2,1)S(1)}, bf16[384,512]{1,0:T(8,128)(2,1)S(1)}, u32[]{:S(2)}, u32[]{:S(2)}) collective-permute-start(bf16[384,512]{1,0:T(8,128)(2,1)S(1)} %get-tuple-element.79), channel_id=1, source_target_pairs={{0,8},{8,0},{16,24},{24,16},{1,9},{9,1},{17,25},{25,17},{2,10},{10... | collective-permute-start | bytes 1179656 | tf_op jit(solution)/shard_map/ppermute | solution.py:293
  5.0 1.5 collective-permute-start.27
  6.5 2.6 collective-permute-start.6
  9.1 1.6 collective-permute-start.14
  10.7 3.4 %collective-permute-done.24.refs_1_ = bf16[384,512]{1,0:T(8,128)(2,1)S(1)} collective-permute-done((bf16[384,512]{1,0:T(8,128)(2,1)S(1)}, bf16[384,512]{1,0:T(8,128)(2,1)S(1)}, u32[]{:S(2)}, u32[]{:S(2)}) %collective-permute-start.24) | collective-permute-done | bytes 393248 | tf_op jit(solution)/shard_map/ppermute | solution.py:293
  15.6 3.8 %collective-permute-start.1 = (bf16[128,2048]{1,0:T(8,128)(2,1)}, bf16[128,2048]{1,0:T(8,128)(2,1)}, u32[]{:S(2)}, u32[]{:S(2)}) collective-permute-start(bf16[128,2048]{1,0:T(8,128)(2,1)} %refs_0_.1), channel_id=1, source_target_pairs={{0,4},{1,5},{2,6},{3,7},{4,0},{5,1},{6,2},{7,3},{8,12},{9,13},{10,... | collective-permute-start | bytes 1572872 | tf_op jit(solution)/shard_map/ppermute | solution.py:299
  19.4 15.4 %collective-permute-done.6.refs_0_ = bf16[128,2048]{1,0:T(8,128)(2,1)S(1)} collective-permute-done((bf16[128,2048]{1,0:T(8,128)(2,1)}, bf16[128,2048]{1,0:T(8,128)(2,1)S(1)}, u32[]{:S(2)}, u32[]{:S(2)}) %collective-permute-start.6) | collective-permute-done | bytes 524320 | tf_op jit(solution)/shard_map/ppermute | solution.py:299
  35.6 1.4 collective-permute-start
  37.6 29.4 %collective-permute-done.1.refs_1_ = bf16[128,2048]{1,0:T(8,128)(2,1)} collective-permute-done((bf16[128,2048]{1,0:T(8,128)(2,1)}, bf16[128,2048]{1,0:T(8,128)(2,1)}, u32[]{:S(2)}, u32[]{:S(2)}) %collective-permute-start.1) | collective-permute-done | bytes 524320 | tf_op jit(solution)/shard_map/ppermute | solution.py:299
  68.8 1.5 collective-permute-start.19
  71.6 15.8 %collective-permute-done.12.refs_8_ = bf16[512,768]{1,0:T(8,128)(2,1)} collective-permute-done((bf16[512,768]{1,0:T(8,128)(2,1)S(1)}, bf16[512,768]{1,0:T(8,128)(2,1)}, u32[]{:S(2)}, u32[]{:S(2)}) %collective-permute-start.12) | collective-permute-done | bytes 786464 | tf_op jit(solution)/shard_map/ppermute | solution.py:296
  87.5 1.3 collective-permute-start.7
  89.5 0.9 copy-done.5
  91.9 9.2 %collective-permute-done.19.refs_7_ = bf16[512,768]{1,0:T(8,128)(2,1)S(1)} collective-permute-done((bf16[512,768]{1,0:T(8,128)(2,1)S(1)}, bf16[512,768]{1,0:T(8,128)(2,1)S(1)}, u32[]{:S(2)}, u32[]{:S(2)}) %collective-permute-start.19) | collective-permute-done | bytes 786464 | tf_op jit(solution)/shard_map/ppermute | solution.py:296
  106.7 1.3 collective-permute-start.2
  108.8 1.4 collective-permute-start.3
  111.0 1.9 collective-permute-start.9
  113.5 7.9 %all-to-all-start = ((f32[8,1,128]{2,1,0:T(1,128)}), f32[8,1,128]{2,1,0:T(1,128)S(1)}, u32[]{:S(2)}, u32[]{:S(2)}) async-start(f32[8,1,128]{2,1,0:T(1,128)} %bitcast.5), calls=%async_computation | async-start | bytes 8192 | tf_op jit(solution)/shard_map/all_to_all | solution.py:316
  121.6 1.2 copy-done.10
  122.8 1.1 copy-done.12
  123.9 1.0 copy-done.13
  126.0 1.0 copy-done.20
  127.1 1.0 copy-done.22
  128.1 1.0 copy-done.30
  129.1 1.0 copy-done.32
  130.2 2.2 shard_map.103
  132.4 2.0 copy-done
  134.4 1.7 copy-done.2
  136.1 1.0 copy-done.14
  137.2 1.0 copy-done.24
  138.2 1.0 copy-done.26
  139.3 1.0 copy-done.34
  140.3 1.0 copy-done.36
  141.3 2.6 shard_map.106.refs_6_
  144.0 1.6 collective-permute-start.25
  145.5 1.5 collective-permute-start.26
  148.1 1.9 collective-permute-start.4
  150.1 7.6 %shard_map.104 = (bf16[1024,768]{1,0:T(8,128)(2,1)S(1)}, f32[1024,768]{1,0:T(8,128)S(1)}, f32[1024,768]{1,0:T(8,128)S(1)}, bf16[2048,768]{1,0:T(8,128)(2,1)S(1)}, bf16[2048,768]{1,0:T(8,128)(2,1)S(1)}) custom-call(s32[3]{0:T(128)S(1)} %pad_add_fusion.place, ...), custom_call_target="tpu_custom_call", output_to_operand_aliasing={{3}: (4, {}), {4}: (5, {})} | custom-call | flops 4831838208 | bytes 25165824 | tf_op jit(solution)/shard_map/pallas_call | solution.py:28
  157.8 4.1 %shard_map.105 = (bf16[1024,768]{1,0:T(8,128)(2,1)S(1)}, f32[1024,768]{1,0:T(8,128)S(1)}, f32[1024,768]{1,0:T(8,128)S(1)}, bf16[1024,2048]{1,0:T(8,128)(2,1)S(1)}) custom-call(s32[3]{0:T(128)S(1)} %pad_add_fusion.place, bf16[128,2048]{1,0:T(8,128)(2,1)S(1)} %copy-done.16, ...), custom_call_target="tpu_custom_call", output_to_operand_aliasing={{0}: (7, {}), {1}: (8, {}), {2}: (9, {}), {3}: (10, {})} | custom-call | flops 1610612736 | bytes 10747904 | tf_op jit(solution)/shard_map/pallas_call | solution.py:28
  161.9 3.8 %shard_map.107 = (bf16[2,384,512]{2,1,0:T(8,128)(2,1)S(1)}, bf16[2,384,512]{2,1,0:T(8,128)(2,1)S(1)}, bf16[1024,2048]{1,0:T(8,128)(2,1)S(1)}) custom-call(s32[3]{0:T(128)S(1)} %pad_add_fusion.place, bf16[128,2048]{1,0:T(8,128)(2,1)} %collective-permute-done.refs_0_, ...), custom_call_target="tpu_custom_call", output_to_operand_aliasing={{2}: (7, {})} | custom-call | flops 1610612736 | bytes 11534336 | tf_op jit(solution)/shard_map/pallas_call | solution.py:28
  165.7 1.5 collective-permute-start.39
  167.3 6.3 %shard_map.108 = (bf16[1024,768]{1,0:T(8,128)(2,1)S(1)}, bf16[1024,768]{1,0:T(8,128)(2,1)S(1)}) custom-call(s32[3]{0:T(128)S(1)} %pad_add_fusion.place, bf16[1024,2048]{1,0:T(8,128)(2,1)S(1)} %get-tuple-element.50.y, f32[1024,768]{1,0:T(8,128)S(1)} %get-tuple-element.51.active, f32[1024,768]{1,0:T(8,128)S(1)} %get-tuple-element.52.slope, ...), custom_call_target="tpu_custom_call" | custom-call | flops 3221225472 | bytes 16777216 | tf_op jit(solution)/shard_map/pallas_call | solution.py:28
  173.6 8.1 %shard_map.109 = (bf16[512,2048]{1,0:T(8,128)(2,1)S(1)}, bf16[512,2048]{1,0:T(8,128)(2,1)S(1)}) custom-call(bf16[1024,768]{1,0:T(8,128)(2,1)S(1)} %get-tuple-element.53.gate_delta.gd, bf16[1024,768]{1,0:T(8,128)(2,1)S(1)} %get-tuple-element.54.up_delta.ud, bf16[2048,768]{1,0:T(8,128)(2,1)S(1)} %get-tuple-element.44.refs_4_.wg, ...), custom_call_target="tpu_custom_call" | custom-call | flops 6442450944 | bytes 13631488 | tf_op jit(solution)/shard_map/pallas_call | solution.py:28
  182.0 1.5 collective-permute-start.41
  183.5 2.4 shard_map.112
  185.9 5.3 %shard_map.111 = (bf16[2,512,768]{2,1,0:T(8,128)(2,1)S(1)}, bf16[2,512,768]{2,1,0:T(8,128)(2,1)S(1)}) custom-call(s32[3]{0:T(128)S(1)} %pad_add_fusion.place, bf16[1024,2048]{1,0:T(8,128)(2,1)S(1)} %get-tuple-element.57.x, bf16[1024,768]{1,0:T(8,128)(2,1)S(1)} %get-tuple-element.53.gate_delta.gd, bf16[1024,768]{1,0:T(8,128)(2,1)S(1)} %get-tuple-element.54.up_delta.ud), custom_call_target="tpu_custom_call" | custom-call | flops 3221225472 | bytes 10485760 | tf_op jit(solution)/shard_map/pallas_call | solution.py:28
  191.8 10.6 %collective-permute-done.41 = bf16[2,384,512]{2,1,0:T(8,128)(2,1)S(1)} collective-permute-done((bf16[2,384,512]{2,1,0:T(8,128)(2,1)S(1)}, bf16[2,384,512]{2,1,0:T(8,128)(2,1)S(1)}, u32[]{:S(2)}, u32[]{:S(2)}) %collective-permute-start.41) | collective-permute-done | bytes 786464 | tf_op jit(solution)/shard_map/ppermute | solution.py:296
  203.1 5.2 %shard_map.110 = (bf16[512,768]{1,0:T(8,128)(2,1)S(1)}, bf16[512,768]{1,0:T(8,128)(2,1)S(1)}, bf16[512,768]{1,0:T(8,128)(2,1)S(1)}, bf16[512,768]{1,0:T(8,128)(2,1)S(1)}) custom-call(s32[3]{0:T(128)S(1)} %pad_add_fusion.place, bf16[1024,2048]{1,0:T(8,128)(2,1)S(1)} %get-tuple-element.57.x, bf16[1024,768]{1,0:T(8,128)(2,1)S(1)} %get-tuple-element.53.gate_delta.gd, ...), custom_call_target="tpu_custom_call" | custom-call | flops 3221225472 | bytes 10485760 | tf_op jit(solution)/shard_map/pallas_call | solution.py:28
  208.3 1.6 collective-permute-start.36
  209.9 1.5 collective-permute-start.35
  211.6 2.4 collective-permute-done.42
  215.0 1.9 collective-permute-start.33
  216.9 27.0 %collective-permute-done.36 = bf16[2,512,768]{2,1,0:T(8,128)(2,1)S(1)} collective-permute-done((bf16[2,512,768]{2,1,0:T(8,128)(2,1)S(1)}, bf16[2,512,768]{2,1,0:T(8,128)(2,1)S(1)}, u32[]{:S(2)}, u32[]{:S(2)}) %collective-permute-start.36) | collective-permute-done | bytes 1572896 | tf_op jit(solution)/shard_map/ppermute | solution.py:296
  245.1 1.8 collective-permute-done.35
  247.3 1.6 collective-permute-start.37
  248.8 0.9 maximum_bitcast_fusion
  250.5 2.7 collective-permute-start.32
  253.3 1.8 collective-permute-start.34
  255.1 7.8 %collective-permute-done.38 = bf16[512,768]{1,0:T(8,128)(2,1)S(1)} collective-permute-done((bf16[512,768]{1,0:T(8,128)(2,1)S(1)}, bf16[512,768]{1,0:T(8,128)(2,1)S(1)}, u32[]{:S(2)}, u32[]{:S(2)}) %collective-permute-start.38) | collective-permute-done | bytes 786464 | tf_op jit(solution)/shard_map/ppermute | solution.py:293
  262.9 1.1 fusion.5
  264.4 1.1 fusion.4
  265.5 18.9 %collective-permute-done.34 = bf16[128,2048]{1,0:T(8,128)(2,1)S(1)} collective-permute-done((bf16[128,2048]{1,0:T(8,128)(2,1)S(1)}, bf16[128,2048]{1,0:T(8,128)(2,1)S(1)}, u32[]{:S(2)}, u32[]{:S(2)}) %collective-permute-start.34) | collective-permute-done | bytes 524320 | tf_op jit(solution)/shard_map/ppermute | solution.py:299
  284.4 1.1 add_convert_fusion.3
  (137 shorter events, 23.8 us)
Async XLA Ops:
  0.6 36.4 %copy-start.9 = (bf16[1,512,768]{2,1,0:T(8,128)(2,1)S(1)}, bf16[1,512,768]{2,1,0:T(8,128)(2,1)}, u32[]{:S(2)}) copy-start(bf16[1,512,768]{2,1,0:T(8,128)(2,1)} %param.11) | copy-start | bytes 2359300
  0.6 66.3 %copy-start.11 = (bf16[1,512,768]{2,1,0:T(8,128)(2,1)S(1)}, bf16[1,512,768]{2,1,0:T(8,128)(2,1)}, u32[]{:S(2)}) copy-start(bf16[1,512,768]{2,1,0:T(8,128)(2,1)} %param.12) | copy-start | bytes 2359300
  0.7 112.3 %copy-start.41 = (f32[128,4]{0,1:T(4,128)S(1)}, f32[128,4]{0,1:T(4,128)}, u32[]{:S(2)}) copy-start(f32[128,4]{0,1:T(4,128)} %param.10) | copy-start | bytes 6148
  0.7 112.3 %copy-start.42 = (s32[128,4]{0,1:T(4,128)S(1)}, s32[128,4]{0,1:T(4,128)}, u32[]{:S(2)}) copy-start(s32[128,4]{0,1:T(4,128)} %param.9) | copy-start | bytes 6148
  2.0 108.3 %copy-start.39 = (bf16[384,512]{1,0:T(8,128)(2,1)}, bf16[384,512]{1,0:T(8,128)(2,1)S(1)}, u32[]{:S(2)}) copy-start(bf16[384,512]{1,0:T(8,128)(2,1)S(1)} %get-tuple-element.79) | copy-start | bytes 1179652
  2.0 111.0 %copy-start.40 = (bf16[384,512]{1,0:T(8,128)(2,1)}, bf16[384,512]{1,0:T(8,128)(2,1)S(1)}, u32[]{:S(2)}) copy-start(bf16[384,512]{1,0:T(8,128)(2,1)S(1)} %get-tuple-element.78) | copy-start | bytes 1179652
  2.0 12.1 %collective-permute-start.24 = (bf16[384,512]{1,0:T(8,128)(2,1)S(1)}, bf16[384,512]{1,0:T(8,128)(2,1)S(1)}, u32[]{:S(2)}, u32[]{:S(2)}) collective-permute-start(bf16[384,512]{1,0:T(8,128)(2,1)S(1)} %get-tuple-element.79), channel_id=1, source_target_pairs={{0,8},{8,0},{16,24},{24,16},{1,9},{9,1},{17,25},{25,17},{2,10},{10... | collective-permute-start | bytes 1179656 | tf_op jit(solution)/shard_map/ppermute | solution.py:293
  5.0 10.6 %collective-permute-start.27 = (bf16[384,512]{1,0:T(8,128)(2,1)S(1)}, bf16[384,512]{1,0:T(8,128)(2,1)S(1)}, u32[]{:S(2)}, u32[]{:S(2)}) collective-permute-start(bf16[384,512]{1,0:T(8,128)(2,1)S(1)} %get-tuple-element.78), channel_id=1, source_target_pairs={{0,16},{8,24},{16,0},{24,8},{1,17},{9,25},{17,1},{25,9},{2,18},{10... | collective-permute-start | bytes 1179656 | tf_op jit(solution)/shard_map/ppermute | solution.py:296
  6.5 28.3 %collective-permute-start.6 = (bf16[128,2048]{1,0:T(8,128)(2,1)}, bf16[128,2048]{1,0:T(8,128)(2,1)S(1)}, u32[]{:S(2)}, u32[]{:S(2)}) collective-permute-start(bf16[128,2048]{1,0:T(8,128)(2,1)} %tokens.1), channel_id=1, source_target_pairs={{0,4},{1,5},{2,6},{3,7},{4,0},{5,1},{6,2},{7,3},{8,12},{9,13},{10,... | collective-permute-start | bytes 1572872 | tf_op jit(solution)/shard_map/ppermute | solution.py:299
  9.1 25.7 %collective-permute-start.14 = (bf16[128,2048]{1,0:T(8,128)(2,1)}, bf16[128,2048]{1,0:T(8,128)(2,1)S(1)}, u32[]{:S(2)}, u32[]{:S(2)}) collective-permute-start(bf16[128,2048]{1,0:T(8,128)(2,1)} %tokens.1), channel_id=1, source_target_pairs={{0,2},{1,3},{2,0},{3,1},{4,6},{5,7},{6,4},{7,5},{8,10},{9,11},{10,... | collective-permute-start | bytes 1572872 | tf_op jit(solution)/shard_map/ppermute | solution.py:299
  10.7 24.1 %collective-permute-start.15 = (bf16[128,2048]{1,0:T(8,128)(2,1)}, bf16[128,2048]{1,0:T(8,128)(2,1)S(1)}, u32[]{:S(2)}, u32[]{:S(2)}) collective-permute-start(bf16[128,2048]{1,0:T(8,128)(2,1)} %tokens.1), channel_id=1, source_target_pairs={{0,1},{1,0},{2,3},{3,2},{4,5},{5,4},{6,7},{7,6},{8,9},{9,8},{10,11... | collective-permute-start | bytes 1572872 | tf_op jit(solution)/shard_map/ppermute | solution.py:302
  14.1 22.9 %collective-permute-start.5 = (bf16[128,2048]{1,0:T(8,128)(2,1)}, bf16[128,2048]{1,0:T(8,128)(2,1)S(1)}, u32[]{:S(2)}, u32[]{:S(2)}) collective-permute-start(bf16[128,2048]{1,0:T(8,128)(2,1)} %tokens.1), channel_id=1, source_target_pairs={{2,4},{3,5},{4,2},{5,3},{10,12},{11,13},{12,10},{13,11},{18,20},{1... | collective-permute-start | bytes 1572872 | tf_op jit(solution)/shard_map/ppermute | solution.py:299
  15.6 3.8 %copy-start.37 = (bf16[384,512]{1,0:T(8,128)(2,1)}, bf16[384,512]{1,0:T(8,128)(2,1)S(1)}, u32[]{:S(2)}) copy-start(bf16[384,512]{1,0:T(8,128)(2,1)S(1)} %collective-permute-done.27.refs_4_) | copy-start | bytes 1179652
  15.6 51.4 %collective-permute-start.1 = (bf16[128,2048]{1,0:T(8,128)(2,1)}, bf16[128,2048]{1,0:T(8,128)(2,1)}, u32[]{:S(2)}, u32[]{:S(2)}) collective-permute-start(bf16[128,2048]{1,0:T(8,128)(2,1)} %refs_0_.1), channel_id=1, source_target_pairs={{0,4},{1,5},{2,6},{3,7},{4,0},{5,1},{6,2},{7,3},{8,12},{9,13},{10,... | collective-permute-start | bytes 1572872 | tf_op jit(solution)/shard_map/ppermute | solution.py:299
  34.8 32.7 %collective-permute-start.20 = (bf16[128,2048]{1,0:T(8,128)(2,1)}, bf16[128,2048]{1,0:T(8,128)(2,1)S(1)}, u32[]{:S(2)}, u32[]{:S(2)}) collective-permute-start(bf16[128,2048]{1,0:T(8,128)(2,1)} %refs_0_.1), channel_id=1, source_target_pairs={{0,2},{1,3},{2,0},{3,1},{4,6},{5,7},{6,4},{7,5},{8,10},{9,11},{10,... | collective-permute-start | bytes 1572872 | tf_op jit(solution)/shard_map/ppermute | solution.py:299
  34.8 33.2 %collective-permute-start.21 = (bf16[128,2048]{1,0:T(8,128)(2,1)}, bf16[128,2048]{1,0:T(8,128)(2,1)S(1)}, u32[]{:S(2)}, u32[]{:S(2)}) collective-permute-start(bf16[128,2048]{1,0:T(8,128)(2,1)} %refs_0_.1), channel_id=1, source_target_pairs={{0,1},{1,0},{2,3},{3,2},{4,5},{5,4},{6,7},{7,6},{8,9},{9,8},{10,11... | collective-permute-start | bytes 1572872 | tf_op jit(solution)/shard_map/ppermute | solution.py:302
  35.6 34.7 %collective-permute-start = (bf16[128,2048]{1,0:T(8,128)(2,1)}, bf16[128,2048]{1,0:T(8,128)(2,1)}, u32[]{:S(2)}, u32[]{:S(2)}) collective-permute-start(bf16[128,2048]{1,0:T(8,128)(2,1)} %refs_0_.1), channel_id=1, source_target_pairs={{2,4},{3,5},{4,2},{5,3},{10,12},{11,13},{12,10},{13,11},{18,20},{1... | collective-permute-start | bytes 1572872 | tf_op jit(solution)/shard_map/ppermute | solution.py:299
  37.1 33.3 %collective-permute-start.10 = (bf16[512,768]{1,0:T(8,128)(2,1)S(1)}, bf16[512,768]{1,0:T(8,128)(2,1)}, u32[]{:S(2)}, u32[]{:S(2)}) collective-permute-start(bf16[512,768]{1,0:T(8,128)(2,1)S(1)} %bitcast.63), channel_id=1, source_target_pairs={{0,8},{8,0},{16,24},{24,16},{1,9},{9,1},{17,25},{25,17},{2,10},{10... | collective-permute-start | bytes 2359304 | tf_op jit(solution)/shard_map/ppermute | solution.py:293
  66.9 20.5 %collective-permute-start.12 = (bf16[512,768]{1,0:T(8,128)(2,1)S(1)}, bf16[512,768]{1,0:T(8,128)(2,1)}, u32[]{:S(2)}, u32[]{:S(2)}) collective-permute-start(bf16[512,768]{1,0:T(8,128)(2,1)S(1)} %bitcast.66), channel_id=1, source_target_pairs={{0,16},{8,24},{16,0},{24,8},{1,17},{9,25},{17,1},{25,9},{2,18},{10... | collective-permute-start | bytes 2359304 | tf_op jit(solution)/shard_map/ppermute | solution.py:296
  67.5 22.1 %collective-permute-start.18 = (bf16[512,768]{1,0:T(8,128)(2,1)S(1)}, bf16[512,768]{1,0:T(8,128)(2,1)S(1)}, u32[]{:S(2)}, u32[]{:S(2)}) collective-permute-start(bf16[512,768]{1,0:T(8,128)(2,1)S(1)} %bitcast.67), channel_id=1, source_target_pairs={{0,8},{8,0},{16,24},{24,16},{1,9},{9,1},{17,25},{25,17},{2,10},{10... | collective-permute-start | bytes 2359304 | tf_op jit(solution)/shard_map/ppermute | solution.py:293
  68.8 32.3 %collective-permute-start.19 = (bf16[512,768]{1,0:T(8,128)(2,1)S(1)}, bf16[512,768]{1,0:T(8,128)(2,1)S(1)}, u32[]{:S(2)}, u32[]{:S(2)}) collective-permute-start(bf16[512,768]{1,0:T(8,128)(2,1)S(1)} %bitcast.64), channel_id=1, source_target_pairs={{0,16},{8,24},{16,0},{24,8},{1,17},{9,25},{17,1},{25,9},{2,18},{10... | collective-permute-start | bytes 2359304 | tf_op jit(solution)/shard_map/ppermute | solution.py:296
  70.3 31.7 %collective-permute-start.16 = (bf16[128,2048]{1,0:T(8,128)(2,1)S(1)}, bf16[128,2048]{1,0:T(8,128)(2,1)S(1)}, u32[]{:S(2)}, u32[]{:S(2)}) collective-permute-start(bf16[128,2048]{1,0:T(8,128)(2,1)S(1)} %collective-permute-done.6.refs_0_), channel_id=1, source_target_pairs={{0,1},{1,0},{2,3},{3,2},{4,5},{5,4},{6,7},{7,6},{8,9},{9,8},{10,11... | collective-permute-start | bytes 1572872 | tf_op jit(solution)/shard_map/ppermute | solution.py:302
  70.3 33.8 %collective-permute-start.17 = (bf16[128,2048]{1,0:T(8,128)(2,1)S(1)}, bf16[128,2048]{1,0:T(8,128)(2,1)S(1)}, u32[]{:S(2)}, u32[]{:S(2)}) collective-permute-start(bf16[128,2048]{1,0:T(8,128)(2,1)S(1)} %collective-permute-done.14.refs_1_), channel_id=1, source_target_pairs={{0,1},{1,0},{2,3},{3,2},{4,5},{5,4},{6,7},{7,6},{8,9},{9,8},{10,11... | collective-permute-start | bytes 1572872 | tf_op jit(solution)/shard_map/ppermute | solution.py:302
  87.5 18.0 %collective-permute-start.7 = (bf16[128,2048]{1,0:T(8,128)(2,1)S(1)}, bf16[128,2048]{1,0:T(8,128)(2,1)}, u32[]{:S(2)}, u32[]{:S(2)}) collective-permute-start(bf16[128,2048]{1,0:T(8,128)(2,1)S(1)} %collective-permute-done.6.refs_0_), channel_id=1, source_target_pairs={{4,6},{5,7},{2,0},{3,1},{12,14},{13,15},{10,8},{11,9},{20,22},{21,... | collective-permute-start | bytes 1572872 | tf_op jit(solution)/shard_map/ppermute | solution.py:299
  90.4 15.5 %collective-permute-start.8 = (bf16[128,2048]{1,0:T(8,128)(2,1)S(1)}, bf16[128,2048]{1,0:T(8,128)(2,1)S(1)}, u32[]{:S(2)}, u32[]{:S(2)}) collective-permute-start(bf16[128,2048]{1,0:T(8,128)(2,1)S(1)} %collective-permute-done.5.refs_0_), channel_id=1, source_target_pairs={{2,3},{3,2},{4,5},{5,4},{10,11},{11,10},{12,13},{13,12},{18,19},{1... | collective-permute-start | bytes 1572872 | tf_op jit(solution)/shard_map/ppermute | solution.py:302
  102.0 5.9 %collective-permute-start.22 = (bf16[128,2048]{1,0:T(8,128)(2,1)}, bf16[128,2048]{1,0:T(8,128)(2,1)S(1)}, u32[]{:S(2)}, u32[]{:S(2)}) collective-permute-start(bf16[128,2048]{1,0:T(8,128)(2,1)} %collective-permute-done.1.refs_1_), channel_id=1, source_target_pairs={{0,1},{1,0},{2,3},{3,2},{4,5},{5,4},{6,7},{7,6},{8,9},{9,8},{10,11... | collective-permute-start | bytes 1572872 | tf_op jit(solution)/shard_map/ppermute | solution.py:302
  102.8 7.4 %collective-permute-start.23 = (bf16[128,2048]{1,0:T(8,128)(2,1)S(1)}, bf16[128,2048]{1,0:T(8,128)(2,1)S(1)}, u32[]{:S(2)}, u32[]{:S(2)}) collective-permute-start(bf16[128,2048]{1,0:T(8,128)(2,1)S(1)} %collective-permute-done.20.refs_2_), channel_id=1, source_target_pairs={{0,1},{1,0},{2,3},{3,2},{4,5},{5,4},{6,7},{7,6},{8,9},{9,8},{10,11... | collective-permute-start | bytes 1572872 | tf_op jit(solution)/shard_map/ppermute | solution.py:302
  104.9 42.6 %collective-permute-start.11 = (bf16[512,768]{1,0:T(8,128)(2,1)}, bf16[512,768]{1,0:T(8,128)(2,1)}, u32[]{:S(2)}, u32[]{:S(2)}) collective-permute-start(bf16[512,768]{1,0:T(8,128)(2,1)} %collective-permute-done.10.refs_5_), channel_id=1, source_target_pairs={{0,16},{8,24},{16,0},{24,8},{1,17},{9,25},{17,1},{25,9},{2,18},{10... | collective-permute-start | bytes 2359304 | tf_op jit(solution)/shard_map/ppermute | solution.py:296
  105.4 42.7 %collective-permute-start.13 = (bf16[512,768]{1,0:T(8,128)(2,1)}, bf16[512,768]{1,0:T(8,128)(2,1)}, u32[]{:S(2)}, u32[]{:S(2)}) collective-permute-start(bf16[512,768]{1,0:T(8,128)(2,1)} %collective-permute-done.12.refs_8_), channel_id=1, source_target_pairs={{0,8},{8,0},{16,24},{24,16},{1,9},{9,1},{17,25},{25,17},{2,10},{10... | collective-permute-start | bytes 2359304 | tf_op jit(solution)/shard_map/ppermute | solution.py:293
  106.7 37.3 %collective-permute-start.2 = (bf16[128,2048]{1,0:T(8,128)(2,1)}, bf16[128,2048]{1,0:T(8,128)(2,1)}, u32[]{:S(2)}, u32[]{:S(2)}) collective-permute-start(bf16[128,2048]{1,0:T(8,128)(2,1)} %collective-permute-done.1.refs_1_), channel_id=1, source_target_pairs={{4,6},{5,7},{2,0},{3,1},{12,14},{13,15},{10,8},{11,9},{20,22},{21,... | collective-permute-start | bytes 1572872 | tf_op jit(solution)/shard_map/ppermute | solution.py:299
  108.8 36.8 %collective-permute-start.3 = (bf16[128,2048]{1,0:T(8,128)(2,1)}, bf16[128,2048]{1,0:T(8,128)(2,1)}, u32[]{:S(2)}, u32[]{:S(2)}) collective-permute-start(bf16[128,2048]{1,0:T(8,128)(2,1)} %collective-permute-done.refs_0_), channel_id=1, source_target_pairs={{2,3},{3,2},{4,5},{5,4},{10,11},{11,10},{12,13},{13,12},{18,19},{1... | collective-permute-start | bytes 1572872 | tf_op jit(solution)/shard_map/ppermute | solution.py:302
  111.0 36.0 %collective-permute-start.9 = (bf16[128,2048]{1,0:T(8,128)(2,1)}, bf16[128,2048]{1,0:T(8,128)(2,1)}, u32[]{:S(2)}, u32[]{:S(2)}) collective-permute-start(bf16[128,2048]{1,0:T(8,128)(2,1)} %collective-permute-done.7.refs_1_), channel_id=1, source_target_pairs={{0,1},{1,0},{6,7},{7,6},{8,9},{9,8},{14,15},{15,14},{16,17},{17,16... | collective-permute-start | bytes 1572872 | tf_op jit(solution)/shard_map/ppermute | solution.py:302
  113.5 22.6 %all-to-all-start = ((f32[8,1,128]{2,1,0:T(1,128)}), f32[8,1,128]{2,1,0:T(1,128)S(1)}, u32[]{:S(2)}, u32[]{:S(2)}) async-start(f32[8,1,128]{2,1,0:T(1,128)} %bitcast.5), calls=%async_computation | async-start | bytes 8192 | tf_op jit(solution)/shard_map/all_to_all | solution.py:316
  121.5 4.2 %copy-start.6 = (bf16[512,768]{1,0:T(8,128)(2,1)S(1)}, bf16[512,768]{1,0:T(8,128)(2,1)}, u32[]{:S(2)}) copy-start(bf16[512,768]{1,0:T(8,128)(2,1)} %copy-done.5) | copy-start | bytes 2359300
  121.5 4.2 %copy-start.8 = (bf16[512,768]{1,0:T(8,128)(2,1)S(1)}, bf16[512,768]{1,0:T(8,128)(2,1)}, u32[]{:S(2)}) copy-start(bf16[512,768]{1,0:T(8,128)(2,1)} %copy-done.7) | copy-start | bytes 2359300
  121.6 1.2 copy-start.10
  122.8 1.1 copy-start.12
  132.4 2.0 copy-start
  134.4 1.7 copy-start.2
  136.1 1.0 copy-start.14
  141.3 8.7 %copy-start.1 = (bf16[1024,2048]{1,0:T(8,128)(2,1)S(1)}, bf16[1024,2048]{1,0:T(8,128)(2,1)}, u32[]{:S(2)}) copy-start(bf16[1024,2048]{1,0:T(8,128)(2,1)} %copy-done) | copy-start | bytes 12582916
  141.3 8.7 %copy-start.3 = (bf16[2048,768]{1,0:T(8,128)(2,1)S(1)}, bf16[2048,768]{1,0:T(8,128)(2,1)}, u32[]{:S(2)}) copy-start(bf16[2048,768]{1,0:T(8,128)(2,1)} %copy-done.2) | copy-start | bytes 9437188
  144.0 23.2 %collective-permute-start.25 = (bf16[384,512]{1,0:T(8,128)(2,1)}, bf16[384,512]{1,0:T(8,128)(2,1)S(1)}, u32[]{:S(2)}, u32[]{:S(2)}) collective-permute-start(bf16[384,512]{1,0:T(8,128)(2,1)} %copy-done.40), channel_id=1, source_target_pairs={{0,8},{8,0},{16,24},{24,16},{1,9},{9,1},{17,25},{25,17},{2,10},{10... | collective-permute-start | bytes 1179656 | tf_op jit(solution)/shard_map/ppermute | solution.py:293
  145.5 21.7 %collective-permute-start.26 = (bf16[384,512]{1,0:T(8,128)(2,1)}, bf16[384,512]{1,0:T(8,128)(2,1)S(1)}, u32[]{:S(2)}, u32[]{:S(2)}) collective-permute-start(bf16[384,512]{1,0:T(8,128)(2,1)} %copy-done.39), channel_id=1, source_target_pairs={{0,16},{8,24},{16,0},{24,8},{1,17},{9,25},{17,1},{25,9},{2,18},{10... | collective-permute-start | bytes 1179656 | tf_op jit(solution)/shard_map/ppermute | solution.py:296
  147.1 20.2 %collective-permute-start.28 = (bf16[384,512]{1,0:T(8,128)(2,1)S(1)}, bf16[384,512]{1,0:T(8,128)(2,1)S(1)}, u32[]{:S(2)}, u32[]{:S(2)}) collective-permute-start(bf16[384,512]{1,0:T(8,128)(2,1)S(1)} %collective-permute-done.24.refs_1_), channel_id=1, source_target_pairs={{0,16},{8,24},{16,0},{24,8},{1,17},{9,25},{17,1},{25,9},{2,18},{10... | collective-permute-start | bytes 1179656 | tf_op jit(solution)/shard_map/ppermute | solution.py:296
  147.6 19.7 %collective-permute-start.29 = (bf16[384,512]{1,0:T(8,128)(2,1)}, bf16[384,512]{1,0:T(8,128)(2,1)S(1)}, u32[]{:S(2)}, u32[]{:S(2)}) collective-permute-start(bf16[384,512]{1,0:T(8,128)(2,1)} %copy-done.37), channel_id=1, source_target_pairs={{0,8},{8,0},{16,24},{24,16},{1,9},{9,1},{17,25},{25,17},{2,10},{10... | collective-permute-start | bytes 1179656 | tf_op jit(solution)/shard_map/ppermute | solution.py:293
  148.1 13.7 %collective-permute-start.4 = (bf16[128,2048]{1,0:T(8,128)(2,1)}, bf16[128,2048]{1,0:T(8,128)(2,1)S(1)}, u32[]{:S(2)}, u32[]{:S(2)}) collective-permute-start(bf16[128,2048]{1,0:T(8,128)(2,1)} %collective-permute-done.2.refs_1_), channel_id=1, source_target_pairs={{0,1},{1,0},{6,7},{7,6},{8,9},{9,8},{14,15},{15,14},{16,17},{17,16... | collective-permute-start | bytes 1572872 | tf_op jit(solution)/shard_map/ppermute | solution.py:302
  150.1 7.7 %copy-start.16 = (bf16[128,2048]{1,0:T(8,128)(2,1)S(1)}, bf16[128,2048]{1,0:T(8,128)(2,1)}, u32[]{:S(2)}) copy-start(bf16[128,2048]{1,0:T(8,128)(2,1)} %copy-done.15) | copy-start | bytes 1572868
  150.1 7.7 %copy-start.28 = (bf16[128,2048]{1,0:T(8,128)(2,1)S(1)}, bf16[128,2048]{1,0:T(8,128)(2,1)}, u32[]{:S(2)}) copy-start(bf16[128,2048]{1,0:T(8,128)(2,1)} %copy-done.27) | copy-start | bytes 1572868
  161.9 5.4 %copy-start.4 = (bf16[1,768,512]{2,1,0:T(8,128)(2,1)S(1)}, bf16[1,768,512]{2,1,0:T(8,128)(2,1)}, u32[]{:S(2)}) copy-start(bf16[1,768,512]{2,1,0:T(8,128)(2,1)} %param.13) | copy-start | bytes 2359300
  161.9 5.4 %copy-start.38 = (bf16[384,512]{1,0:T(8,128)(2,1)S(1)}, bf16[384,512]{1,0:T(8,128)(2,1)}, u32[]{:S(2)}) copy-start(bf16[384,512]{1,0:T(8,128)(2,1)} %copy-done.37) | copy-start | bytes 1179652
  165.7 25.4 %collective-permute-start.39 = (bf16[2,384,512]{2,1,0:T(8,128)(2,1)S(1)}, bf16[2,384,512]{2,1,0:T(8,128)(2,1)S(1)}, u32[]{:S(2)}, u32[]{:S(2)}) collective-permute-start(bf16[2,384,512]{2,1,0:T(8,128)(2,1)S(1)} %get-tuple-element.67), channel_id=1, source_target_pairs={{0,8},{8,0},{16,24},{24,16},{1,9},{9,1},{17,25},{25,17},{2,10},{10... | collective-permute-start | bytes 2359304 | tf_op jit(solution)/shard_map/ppermute | solution.py:293
  181.7 32.4 %collective-permute-start.30 = (bf16[512,2048]{1,0:T(8,128)(2,1)S(1)}, bf16[512,2048]{1,0:T(8,128)(2,1)S(1)}, u32[]{:S(2)}, u32[]{:S(2)}) collective-permute-start(bf16[512,2048]{1,0:T(8,128)(2,1)S(1)} %get-tuple-element.56), channel_id=1, source_target_pairs={{0,1},{1,0},{2,3},{3,2},{4,5},{5,4},{6,7},{7,6},{8,9},{9,8},{10,11... | collective-permute-start | bytes 6291464 | tf_op jit(solution)/shard_map/ppermute | solution.py:302
  182.0 20.4 %collective-permute-start.41 = (bf16[2,384,512]{2,1,0:T(8,128)(2,1)S(1)}, bf16[2,384,512]{2,1,0:T(8,128)(2,1)S(1)}, u32[]{:S(2)}, u32[]{:S(2)}) collective-permute-start(bf16[2,384,512]{2,1,0:T(8,128)(2,1)S(1)} %get-tuple-element.70), channel_id=1, source_target_pairs={{0,16},{8,24},{16,0},{24,8},{1,17},{9,25},{17,1},{25,9},{2,18},{10... | collective-permute-start | bytes 2359304 | tf_op jit(solution)/shard_map/ppermute | solution.py:296
  191.2 20.1 %collective-permute-start.40 = (bf16[384,512]{1,0:T(8,128)(2,1)S(1)}, bf16[384,512]{1,0:T(8,128)(2,1)S(1)}, u32[]{:S(2)}, u32[]{:S(2)}) collective-permute-start(bf16[384,512]{1,0:T(8,128)(2,1)S(1)} %fusion.9), channel_id=1, source_target_pairs={{0,16},{8,24},{16,0},{24,8},{1,17},{9,25},{17,1},{25,9},{2,18},{10... | collective-permute-start | bytes 1179656 | tf_op jit(solution)/shard_map/ppermute | solution.py:296
  202.5 11.5 %collective-permute-start.42 = (bf16[384,512]{1,0:T(8,128)(2,1)S(1)}, bf16[384,512]{1,0:T(8,128)(2,1)S(1)}, u32[]{:S(2)}, u32[]{:S(2)}) collective-permute-start(bf16[384,512]{1,0:T(8,128)(2,1)S(1)} %fusion.6), channel_id=1, source_target_pairs={{0,8},{8,0},{16,24},{24,16},{1,9},{9,1},{17,25},{25,17},{2,10},{10... | collective-permute-start | bytes 1179656 | tf_op jit(solution)/shard_map/ppermute | solution.py:293
  208.3 35.5 %collective-permute-start.36 = (bf16[2,512,768]{2,1,0:T(8,128)(2,1)S(1)}, bf16[2,512,768]{2,1,0:T(8,128)(2,1)S(1)}, u32[]{:S(2)}, u32[]{:S(2)}) collective-permute-start(bf16[2,512,768]{2,1,0:T(8,128)(2,1)S(1)} %get-tuple-element.61), channel_id=1, source_target_pairs={{0,16},{8,24},{16,0},{24,8},{1,17},{9,25},{17,1},{25,9},{2,18},{10... | collective-permute-start | bytes 4718600 | tf_op jit(solution)/shard_map/ppermute | solution.py:296
  209.9 37.0 %collective-permute-start.35 = (bf16[2,512,768]{2,1,0:T(8,128)(2,1)S(1)}, bf16[2,512,768]{2,1,0:T(8,128)(2,1)S(1)}, u32[]{:S(2)}, u32[]{:S(2)}) collective-permute-start(bf16[2,512,768]{2,1,0:T(8,128)(2,1)S(1)} %get-tuple-element.59), channel_id=1, source_target_pairs={{0,8},{8,0},{16,24},{24,16},{1,9},{9,1},{17,25},{25,17},{2,10},{10... | collective-permute-start | bytes 4718600 | tf_op jit(solution)/shard_map/ppermute | solution.py:293
  215.0 38.2 %collective-permute-start.33 = (bf16[128,2048]{1,0:T(8,128)(2,1)S(1)}, bf16[128,2048]{1,0:T(8,128)(2,1)S(1)}, u32[]{:S(2)}, u32[]{:S(2)}) collective-permute-start(bf16[128,2048]{1,0:T(8,128)(2,1)S(1)} %get-tuple-element.73), channel_id=1, source_target_pairs={{0,2},{1,3},{6,4},{7,5},{8,10},{9,11},{14,12},{15,13},{16,18},{17,... | collective-permute-start | bytes 1572872 | tf_op jit(solution)/shard_map/ppermute | solution.py:299
  244.2 18.7 %collective-permute-start.38 = (bf16[512,768]{1,0:T(8,128)(2,1)S(1)}, bf16[512,768]{1,0:T(8,128)(2,1)S(1)}, u32[]{:S(2)}, u32[]{:S(2)}) collective-permute-start(bf16[512,768]{1,0:T(8,128)(2,1)S(1)} %get-tuple-element.74), channel_id=1, source_target_pairs={{0,8},{8,0},{16,24},{24,16},{1,9},{9,1},{17,25},{25,17},{2,10},{10... | collective-permute-start | bytes 2359304 | tf_op jit(solution)/shard_map/ppermute | solution.py:293
  247.3 17.2 %collective-permute-start.37 = (bf16[512,768]{1,0:T(8,128)(2,1)S(1)}, bf16[512,768]{1,0:T(8,128)(2,1)S(1)}, u32[]{:S(2)}, u32[]{:S(2)}) collective-permute-start(bf16[512,768]{1,0:T(8,128)(2,1)S(1)} %get-tuple-element.77), channel_id=1, source_target_pairs={{0,16},{8,24},{16,0},{24,8},{1,17},{9,25},{17,1},{25,9},{2,18},{10... | collective-permute-start | bytes 2359304 | tf_op jit(solution)/shard_map/ppermute | solution.py:296
  249.8 15.7 %collective-permute-start.31 = (bf16[128,2048]{1,0:T(8,128)(2,1)S(1)}, bf16[128,2048]{1,0:T(8,128)(2,1)S(1)}, u32[]{:S(2)}, u32[]{:S(2)}) collective-permute-start(bf16[128,2048]{1,0:T(8,128)(2,1)S(1)} %get-tuple-element.73), channel_id=1, source_target_pairs={{2,4},{3,5},{4,2},{5,3},{10,12},{11,13},{12,10},{13,11},{18,20},{1... | collective-permute-start | bytes 1572872 | tf_op jit(solution)/shard_map/ppermute | solution.py:299
  250.5 15.0 %collective-permute-start.32 = (bf16[128,2048]{1,0:T(8,128)(2,1)S(1)}, bf16[128,2048]{1,0:T(8,128)(2,1)S(1)}, u32[]{:S(2)}, u32[]{:S(2)}) collective-permute-start(bf16[128,2048]{1,0:T(8,128)(2,1)S(1)} %get-tuple-element.72), channel_id=1, source_target_pairs={{0,2},{1,3},{2,0},{3,1},{4,6},{5,7},{6,4},{7,5},{8,10},{9,11},{10,... | collective-permute-start | bytes 1572872 | tf_op jit(solution)/shard_map/ppermute | solution.py:299
  253.3 31.1 %collective-permute-start.34 = (bf16[128,2048]{1,0:T(8,128)(2,1)S(1)}, bf16[128,2048]{1,0:T(8,128)(2,1)S(1)}, u32[]{:S(2)}, u32[]{:S(2)}) collective-permute-start(bf16[128,2048]{1,0:T(8,128)(2,1)S(1)} %add_convert_fusion.4), channel_id=1, source_target_pairs={{0,4},{1,5},{2,6},{3,7},{4,0},{5,1},{6,2},{7,3},{8,12},{9,13},{10,... | collective-permute-start | bytes 1572872 | tf_op jit(solution)/shard_map/ppermute | solution.py:299
  (23 other events, 21.0 us)

commit v6 on v5

--- a/solution.py
+++ b/solution.py
@@ -11,7 +11,7 @@
 ANY = pl.BlockSpec(memory_space=pl.ANY)
 VMEM = pl.BlockSpec(memory_space=pltpu.VMEM)
 SMEM = pl.BlockSpec(memory_space=pltpu.SMEM)
-LIMIT = 24 * 1024 * 1024
+LIMIT = 12 * 1024 * 1024
 NN = (((1,), (0,)), ((), ()))
 NT = (((1,), (1,)), ((), ()))
 
@@ -81,9 +81,10 @@
     return started
 
 
-def own_body(place, tokens, w_gate, w_up, x, wg, wu, sems):
+def own_body(place, gates, tokens, w_gate, w_up, column, x, wg, wu, sems):
     copies = Copies(sems)
     started = load_early(copies, (tokens,), x) + load_weights(copies, place, (0,), (w_gate, w_up), wg, wu)
+    column[...] = jnp.transpose(gates[...])
     for c in started:
         c.wait()
 
@@ -144,10 +145,9 @@
     tok = raw.shape[0] // 2
     chip, core = place[1], place[2] % 2
     source = {"own": chip, "two": (chip + 2) % 4, "outer": chip ^ 1, "last": 3 - chip}[which]
-    column = jnp.transpose(gates[...])
-    lane = lax.broadcasted_iota(jnp.int32, column.shape, 1)
+    lane = lax.broadcasted_iota(jnp.int32, gates.shape, 1)
     for i in (0, 1):
-        gate = jnp.sum(jnp.where(lane == 2 * source + (core ^ i), column, 0.0), axis=1, keepdims=True)
+        gate = jnp.sum(jnp.where(lane == 2 * source + (core ^ i), gates[...], 0.0), axis=1, keepdims=True)
         r = slice(i * tok, (i + 1) * tok)
         y[pl.ds(first[i], tok), :] = (raw[r, :].astype(F32) * gate).astype(BF16)
 
@@ -336,10 +336,10 @@
     weight = ((width, hidden), BF16, VMEM)
     flat = ((rows, hidden), BF16, VMEM)
     wide = ((rows, hidden), F32, VMEM)
-    x, wg, wu = call(
+    gates, x, wg, wu = call(
         own_body,
-        [x_out, weight, weight],
-        [(place, SMEM)] + anys((tokens, wg0, wu0)),
+        [((tok, experts), F32, VMEM), x_out, weight, weight],
+        [(place, SMEM), (gates, VMEM)] + anys((tokens, wg0, wu0)),
         [dma(3)],
         1000,
         width * (2 * tok + hidden),

time: 287 us -> 277 us (0.965)
  local copies, waits for them, and re-layouts: 28.7 us -> 15.9 us
  waiting for transfers between devices: 143 us -> 151 us
  starting transfers between devices: 57.3 us -> 53.7 us
    unnamed x86 -> x74, local copies, waits for them, and re-layouts: 27.4 us -> 14.6 us
    all_to_all x1, waiting for transfers between devices: 0.01 us -> 5.51 us  [dense(): lax.all_to_all(gates, 'expert', split_axis=0, concat_axis=0, tiled=True)]
    ppermute x12, starting transfers between devices: 19.7 us -> 16 us  [hop(): lax.ppermute(block, 'expert', [(2 * a + c, 2 * b + c) for a, b in moves f...]
    ppermute x10, waiting for transfers between devices: 15.4 us -> 18.5 us  [to_x(): return lax.ppermute(block, 'dp', [(i, i ^ 1) for i in range(4)])]
  transfers between devices with their start and end apart: 44 -> 44, of which waited for: 13 -> 14; matrix products, arithmetic and copies ran while one was open for 2% -> 2% of each run, Pallas kernels for 17% -> 17%
where the time goes in v6:
time: 277 us; the launch traced here: 276 us
  waiting for transfers between devices  151 us (55%)
  starting transfers between devices  53.7 us (19%)
  Pallas kernels  46.9 us (17%)
  local copies, waits for them, and re-layouts  15.9 us (6%)
  other arithmetic  7.26 us (3%)
    ppermute x10, waiting for transfers between devices, to_y(): return lax.ppermute(block, 'dp', [(i, i ^ 2) for i in range(4)])  65.2 us
    ppermute x12, waiting for transfers between devices, hop(): lax.ppermute(block, 'expert', [(2 * a + c, 2 * b + c) for a, b in moves f...  62.2 us
    pallas_call x11, Pallas kernels, call(): pl.pallas_call(body, input_output_aliases=aliases or {}, out_shape=[jax.S...  46.9 us
    ppermute x10, waiting for transfers between devices, to_x(): return lax.ppermute(block, 'dp', [(i, i ^ 1) for i in range(4)])  18.5 us
    ppermute x12, starting transfers between devices, hop(): lax.ppermute(block, 'expert', [(2 * a + c, 2 * b + c) for a, b in moves f...  16 us
    unnamed x74, local copies, waits for them, and re-layouts  14.6 us
    ppermute x10, starting transfers between devices, to_y(): return lax.ppermute(block, 'dp', [(i, i ^ 2) for i in range(4)])  11.3 us
    ppermute x10, starting transfers between devices, to_x(): return lax.ppermute(block, 'dp', [(i, i ^ 1) for i in range(4)])  11.2 us
  transfers between devices with their start and end apart: 44, of which 14 were waited for; matrix products, arithmetic and copies ran while one was open for 2% of the time, Pallas kernels for 17%

profile of v6, /device:TPU:0, one launch (start us, length us, event | category | flops | bytes accessed | tf_op | source)
XLA Modules:
  0.0 276.2 jit_solution(7122554268409595652)
XLA Ops:
  0.7 1.3 slice_bitcast_fusion.8
  2.0 3.0 %collective-permute-start.24 = (bf16[384,512]{1,0:T(8,128)(2,1)S(1)}, bf16[384,512]{1,0:T(8,128)(2,1)S(1)}, u32[]{:S(2)}, u32[]{:S(2)}) collective-permute-start(bf16[384,512]{1,0:T(8,128)(2,1)S(1)} %get-tuple-element.81), channel_id=1, source_target_pairs={{0,8},{8,0},{16,24},{24,16},{1,9},{9,1},{17,25},{25,17},{2,10},{10... | collective-permute-start | bytes 1179656 | tf_op jit(solution)/shard_map/ppermute | solution.py:293
  5.0 1.5 collective-permute-start.27
  6.5 2.6 collective-permute-start.6
  9.1 1.6 collective-permute-start.14
  10.7 3.4 %collective-permute-done.24.refs_1_ = bf16[384,512]{1,0:T(8,128)(2,1)S(1)} collective-permute-done((bf16[384,512]{1,0:T(8,128)(2,1)S(1)}, bf16[384,512]{1,0:T(8,128)(2,1)S(1)}, u32[]{:S(2)}, u32[]{:S(2)}) %collective-permute-start.24) | collective-permute-done | bytes 393248 | tf_op jit(solution)/shard_map/ppermute | solution.py:293
  15.6 3.8 %collective-permute-start.1 = (bf16[128,2048]{1,0:T(8,128)(2,1)}, bf16[128,2048]{1,0:T(8,128)(2,1)}, u32[]{:S(2)}, u32[]{:S(2)}) collective-permute-start(bf16[128,2048]{1,0:T(8,128)(2,1)} %refs_0_.1), channel_id=1, source_target_pairs={{0,4},{1,5},{2,6},{3,7},{4,0},{5,1},{6,2},{7,3},{8,12},{9,13},{10,... | collective-permute-start | bytes 1572872 | tf_op jit(solution)/shard_map/ppermute | solution.py:299
  19.4 15.4 %collective-permute-done.6.refs_0_ = bf16[128,2048]{1,0:T(8,128)(2,1)S(1)} collective-permute-done((bf16[128,2048]{1,0:T(8,128)(2,1)}, bf16[128,2048]{1,0:T(8,128)(2,1)S(1)}, u32[]{:S(2)}, u32[]{:S(2)}) %collective-permute-start.6) | collective-permute-done | bytes 524320 | tf_op jit(solution)/shard_map/ppermute | solution.py:299
  34.8 0.8 copy-done.13
  35.6 1.4 collective-permute-start
  37.6 29.3 %collective-permute-done.1.refs_1_ = bf16[128,2048]{1,0:T(8,128)(2,1)} collective-permute-done((bf16[128,2048]{1,0:T(8,128)(2,1)}, bf16[128,2048]{1,0:T(8,128)(2,1)}, u32[]{:S(2)}, u32[]{:S(2)}) %collective-permute-start.1) | collective-permute-done | bytes 524320 | tf_op jit(solution)/shard_map/ppermute | solution.py:299
  68.0 0.8 copy-done.17
  68.8 1.5 collective-permute-start.19
  71.6 15.7 %collective-permute-done.12.refs_8_ = bf16[512,768]{1,0:T(8,128)(2,1)S(1)} collective-permute-done((bf16[512,768]{1,0:T(8,128)(2,1)S(1)}, bf16[512,768]{1,0:T(8,128)(2,1)S(1)}, u32[]{:S(2)}, u32[]{:S(2)}) %collective-permute-start.12) | collective-permute-done | bytes 786464 | tf_op jit(solution)/shard_map/ppermute | solution.py:296
  87.4 1.3 collective-permute-start.7
  90.9 10.2 %collective-permute-done.19.refs_7_ = bf16[512,768]{1,0:T(8,128)(2,1)S(1)} collective-permute-done((bf16[512,768]{1,0:T(8,128)(2,1)S(1)}, bf16[512,768]{1,0:T(8,128)(2,1)S(1)}, u32[]{:S(2)}, u32[]{:S(2)}) %collective-permute-start.19) | collective-permute-done | bytes 786464 | tf_op jit(solution)/shard_map/ppermute | solution.py:296
  101.2 0.8 copy-done.21
  102.5 0.8 copy-done.15
  103.3 0.9 copy-done.23
  105.1 0.8 copy-done.19
  105.9 1.3 collective-permute-start.2
  107.2 0.9 copy-done.25
  108.0 1.5 collective-permute-start.3
  109.5 0.8 copy-done.27
  110.3 1.9 collective-permute-start.9
  112.8 7.9 %all-to-all-start = ((f32[8,1,128]{2,1,0:T(1,128)}), f32[8,1,128]{2,1,0:T(1,128)S(1)}, u32[]{:S(2)}, u32[]{:S(2)}) async-start(f32[8,1,128]{2,1,0:T(1,128)} %bitcast.5), calls=%async_computation | async-start | bytes 8192 | tf_op jit(solution)/shard_map/all_to_all | solution.py:316
  120.8 5.5 %all-to-all-done = f32[8,1,128]{2,1,0:T(1,128)S(1)} async-done(((f32[8,1,128]{2,1,0:T(1,128)}), f32[8,1,128]{2,1,0:T(1,128)S(1)}, u32[]{:S(2)}, u32[]{:S(2)}) %all-to-all-start) | async-done | bytes 4128 | tf_op jit(solution)/shard_map/all_to_all | solution.py:316
  126.3 1.1 copy-done.2
  127.5 1.1 copy-done.4
  128.6 1.0 copy-done.5
  129.6 0.8 shard_map.102
  131.1 1.0 copy-done.24
  132.2 1.0 shard_map.103
  133.9 2.2 shard_map.106.refs_6_
  136.1 1.6 collective-permute-start.25
  137.7 1.5 collective-permute-start.26
  140.2 1.9 collective-permute-start.4
  142.2 7.6 %shard_map.104 = (bf16[1024,768]{1,0:T(8,128)(2,1)S(1)}, f32[1024,768]{1,0:T(8,128)S(1)}, f32[1024,768]{1,0:T(8,128)S(1)}, bf16[2048,768]{1,0:T(8,128)(2,1)S(1)}, bf16[2048,768]{1,0:T(8,128)(2,1)S(1)}) custom-call(s32[3]{0:T(128)S(1)} %pad_add_fusion.place, ...), custom_call_target="tpu_custom_call", output_to_operand_aliasing={{3}: (4, {}), {4}: (5, {})} | custom-call | flops 4831838208 | bytes 25165824 | tf_op jit(solution)/shard_map/pallas_call | solution.py:28
  149.8 4.0 %shard_map.105 = (bf16[1024,768]{1,0:T(8,128)(2,1)S(1)}, f32[1024,768]{1,0:T(8,128)S(1)}, f32[1024,768]{1,0:T(8,128)S(1)}, bf16[1024,2048]{1,0:T(8,128)(2,1)S(1)}) custom-call(s32[3]{0:T(128)S(1)} %pad_add_fusion.place, bf16[128,2048]{1,0:T(8,128)(2,1)S(1)} %copy-done.8, ...), custom_call_target="tpu_custom_call", output_to_operand_aliasing={{0}: (7, {}), {1}: (8, {}), {2}: (9, {}), {3}: (10, {})} | custom-call | flops 1610612736 | bytes 10747904 | tf_op jit(solution)/shard_map/pallas_call | solution.py:28
  153.9 3.8 %shard_map.107 = (bf16[2,384,512]{2,1,0:T(8,128)(2,1)S(1)}, bf16[2,384,512]{2,1,0:T(8,128)(2,1)S(1)}, bf16[1024,2048]{1,0:T(8,128)(2,1)S(1)}) custom-call(s32[3]{0:T(128)S(1)} %pad_add_fusion.place, bf16[128,2048]{1,0:T(8,128)(2,1)} %collective-permute-done.refs_0_, ...), custom_call_target="tpu_custom_call", output_to_operand_aliasing={{2}: (7, {})} | custom-call | flops 1610612736 | bytes 11534336 | tf_op jit(solution)/shard_map/pallas_call | solution.py:28
  157.7 1.6 collective-permute-start.39
  159.3 6.3 %shard_map.108 = (bf16[1024,768]{1,0:T(8,128)(2,1)S(1)}, bf16[1024,768]{1,0:T(8,128)(2,1)S(1)}) custom-call(s32[3]{0:T(128)S(1)} %pad_add_fusion.place, bf16[1024,2048]{1,0:T(8,128)(2,1)S(1)} %get-tuple-element.52.y, f32[1024,768]{1,0:T(8,128)S(1)} %get-tuple-element.53.active, f32[1024,768]{1,0:T(8,128)S(1)} %get-tuple-element.54.slope, ...), custom_call_target="tpu_custom_call" | custom-call | flops 3221225472 | bytes 16777216 | tf_op jit(solution)/shard_map/pallas_call | solution.py:28
  165.7 8.1 %shard_map.109 = (bf16[512,2048]{1,0:T(8,128)(2,1)S(1)}, bf16[512,2048]{1,0:T(8,128)(2,1)S(1)}) custom-call(bf16[1024,768]{1,0:T(8,128)(2,1)S(1)} %get-tuple-element.55.gate_delta.gd, bf16[1024,768]{1,0:T(8,128)(2,1)S(1)} %get-tuple-element.56.up_delta.ud, bf16[2048,768]{1,0:T(8,128)(2,1)S(1)} %get-tuple-element.46.refs_4_.wg, ...), custom_call_target="tpu_custom_call" | custom-call | flops 6442450944 | bytes 13631488 | tf_op jit(solution)/shard_map/pallas_call | solution.py:28
  174.0 1.5 collective-permute-start.41
  175.6 2.4 shard_map.112
  177.9 5.3 %shard_map.111 = (bf16[2,512,768]{2,1,0:T(8,128)(2,1)S(1)}, bf16[2,512,768]{2,1,0:T(8,128)(2,1)S(1)}) custom-call(s32[3]{0:T(128)S(1)} %pad_add_fusion.place, bf16[1024,2048]{1,0:T(8,128)(2,1)S(1)} %get-tuple-element.59.x, bf16[1024,768]{1,0:T(8,128)(2,1)S(1)} %get-tuple-element.55.gate_delta.gd, bf16[1024,768]{1,0:T(8,128)(2,1)S(1)} %get-tuple-element.56.up_delta.ud), custom_call_target="tpu_custom_call" | custom-call | flops 3221225472 | bytes 10485760 | tf_op jit(solution)/shard_map/pallas_call | solution.py:28
  183.9 10.6 %collective-permute-done.41 = bf16[2,384,512]{2,1,0:T(8,128)(2,1)S(1)} collective-permute-done((bf16[2,384,512]{2,1,0:T(8,128)(2,1)S(1)}, bf16[2,384,512]{2,1,0:T(8,128)(2,1)S(1)}, u32[]{:S(2)}, u32[]{:S(2)}) %collective-permute-start.41) | collective-permute-done | bytes 786464 | tf_op jit(solution)/shard_map/ppermute | solution.py:296
  195.2 5.3 %shard_map.110 = (bf16[512,768]{1,0:T(8,128)(2,1)S(1)}, bf16[512,768]{1,0:T(8,128)(2,1)S(1)}, bf16[512,768]{1,0:T(8,128)(2,1)S(1)}, bf16[512,768]{1,0:T(8,128)(2,1)S(1)}) custom-call(s32[3]{0:T(128)S(1)} %pad_add_fusion.place, bf16[1024,2048]{1,0:T(8,128)(2,1)S(1)} %get-tuple-element.59.x, bf16[1024,768]{1,0:T(8,128)(2,1)S(1)} %get-tuple-element.55.gate_delta.gd, ...), custom_call_target="tpu_custom_call" | custom-call | flops 3221225472 | bytes 10485760 | tf_op jit(solution)/shard_map/pallas_call | solution.py:28
  200.4 1.6 collective-permute-start.36
  202.0 1.5 collective-permute-start.35
  203.6 2.4 collective-permute-done.42
  206.2 0.9 add_convert_fusion
  207.2 1.3 collective-permute-start.33
  208.5 27.4 %collective-permute-done.36 = bf16[2,512,768]{2,1,0:T(8,128)(2,1)S(1)} collective-permute-done((bf16[2,512,768]{2,1,0:T(8,128)(2,1)S(1)}, bf16[2,512,768]{2,1,0:T(8,128)(2,1)S(1)}, u32[]{:S(2)}, u32[]{:S(2)}) %collective-permute-start.36) | collective-permute-done | bytes 1572896 | tf_op jit(solution)/shard_map/ppermute | solution.py:296
  236.3 0.9 collective-permute-start.38
  237.2 1.7 collective-permute-done.35
  239.4 1.6 collective-permute-start.37
  241.0 0.9 maximum_bitcast_fusion
  243.1 1.0 collective-permute-start.34
  244.1 10.9 %collective-permute-done.38 = bf16[512,768]{1,0:T(8,128)(2,1)S(1)} collective-permute-done((bf16[512,768]{1,0:T(8,128)(2,1)S(1)}, bf16[512,768]{1,0:T(8,128)(2,1)S(1)}, u32[]{:S(2)}, u32[]{:S(2)}) %collective-permute-start.38) | collective-permute-done | bytes 786464 | tf_op jit(solution)/shard_map/ppermute | solution.py:293
  255.0 1.1 fusion.5
  256.5 1.1 fusion.4
  257.6 17.4 %collective-permute-done.34 = bf16[128,2048]{1,0:T(8,128)(2,1)S(1)} collective-permute-done((bf16[128,2048]{1,0:T(8,128)(2,1)S(1)}, bf16[128,2048]{1,0:T(8,128)(2,1)S(1)}, u32[]{:S(2)}, u32[]{:S(2)}) %collective-permute-start.34) | collective-permute-done | bytes 524320 | tf_op jit(solution)/shard_map/ppermute | solution.py:299
  275.1 1.1 add_convert_fusion.3
  (125 shorter events, 15.7 us)
Async XLA Ops:
  0.6 36.5 %copy-start.1 = (bf16[1,512,768]{2,1,0:T(8,128)(2,1)S(1)}, bf16[1,512,768]{2,1,0:T(8,128)(2,1)}, u32[]{:S(2)}) copy-start(bf16[1,512,768]{2,1,0:T(8,128)(2,1)} %param.11) | copy-start | bytes 2359300
  0.6 66.3 %copy-start.3 = (bf16[1,512,768]{2,1,0:T(8,128)(2,1)S(1)}, bf16[1,512,768]{2,1,0:T(8,128)(2,1)}, u32[]{:S(2)}) copy-start(bf16[1,512,768]{2,1,0:T(8,128)(2,1)} %param.12) | copy-start | bytes 2359300
  0.7 111.6 %copy-start.35 = (f32[128,4]{0,1:T(4,128)S(1)}, f32[128,4]{0,1:T(4,128)}, u32[]{:S(2)}) copy-start(f32[128,4]{0,1:T(4,128)} %param.10) | copy-start | bytes 6148
  0.7 111.6 %copy-start.36 = (s32[128,4]{0,1:T(4,128)S(1)}, s32[128,4]{0,1:T(4,128)}, u32[]{:S(2)}) copy-start(s32[128,4]{0,1:T(4,128)} %param.9) | copy-start | bytes 6148
  2.0 107.5 %copy-start.31 = (bf16[384,512]{1,0:T(8,128)(2,1)}, bf16[384,512]{1,0:T(8,128)(2,1)S(1)}, u32[]{:S(2)}) copy-start(bf16[384,512]{1,0:T(8,128)(2,1)S(1)} %get-tuple-element.81) | copy-start | bytes 1179652
  2.0 110.2 %copy-start.33 = (bf16[384,512]{1,0:T(8,128)(2,1)}, bf16[384,512]{1,0:T(8,128)(2,1)S(1)}, u32[]{:S(2)}) copy-start(bf16[384,512]{1,0:T(8,128)(2,1)S(1)} %get-tuple-element.80) | copy-start | bytes 1179652
  2.0 12.1 %collective-permute-start.24 = (bf16[384,512]{1,0:T(8,128)(2,1)S(1)}, bf16[384,512]{1,0:T(8,128)(2,1)S(1)}, u32[]{:S(2)}, u32[]{:S(2)}) collective-permute-start(bf16[384,512]{1,0:T(8,128)(2,1)S(1)} %get-tuple-element.81), channel_id=1, source_target_pairs={{0,8},{8,0},{16,24},{24,16},{1,9},{9,1},{17,25},{25,17},{2,10},{10... | collective-permute-start | bytes 1179656 | tf_op jit(solution)/shard_map/ppermute | solution.py:293
  5.0 10.6 %collective-permute-start.27 = (bf16[384,512]{1,0:T(8,128)(2,1)S(1)}, bf16[384,512]{1,0:T(8,128)(2,1)S(1)}, u32[]{:S(2)}, u32[]{:S(2)}) collective-permute-start(bf16[384,512]{1,0:T(8,128)(2,1)S(1)} %get-tuple-element.80), channel_id=1, source_target_pairs={{0,16},{8,24},{16,0},{24,8},{1,17},{9,25},{17,1},{25,9},{2,18},{10... | collective-permute-start | bytes 1179656 | tf_op jit(solution)/shard_map/ppermute | solution.py:296
  6.5 28.3 %collective-permute-start.6 = (bf16[128,2048]{1,0:T(8,128)(2,1)}, bf16[128,2048]{1,0:T(8,128)(2,1)S(1)}, u32[]{:S(2)}, u32[]{:S(2)}) collective-permute-start(bf16[128,2048]{1,0:T(8,128)(2,1)} %tokens.1), channel_id=1, source_target_pairs={{0,4},{1,5},{2,6},{3,7},{4,0},{5,1},{6,2},{7,3},{8,12},{9,13},{10,... | collective-permute-start | bytes 1572872 | tf_op jit(solution)/shard_map/ppermute | solution.py:299
  9.1 25.7 %collective-permute-start.14 = (bf16[128,2048]{1,0:T(8,128)(2,1)}, bf16[128,2048]{1,0:T(8,128)(2,1)S(1)}, u32[]{:S(2)}, u32[]{:S(2)}) collective-permute-start(bf16[128,2048]{1,0:T(8,128)(2,1)} %tokens.1), channel_id=1, source_target_pairs={{0,2},{1,3},{2,0},{3,1},{4,6},{5,7},{6,4},{7,5},{8,10},{9,11},{10,... | collective-permute-start | bytes 1572872 | tf_op jit(solution)/shard_map/ppermute | solution.py:299
  10.7 24.1 %collective-permute-start.15 = (bf16[128,2048]{1,0:T(8,128)(2,1)}, bf16[128,2048]{1,0:T(8,128)(2,1)S(1)}, u32[]{:S(2)}, u32[]{:S(2)}) collective-permute-start(bf16[128,2048]{1,0:T(8,128)(2,1)} %tokens.1), channel_id=1, source_target_pairs={{0,1},{1,0},{2,3},{3,2},{4,5},{5,4},{6,7},{7,6},{8,9},{9,8},{10,11... | collective-permute-start | bytes 1572872 | tf_op jit(solution)/shard_map/ppermute | solution.py:302
  14.1 23.0 %collective-permute-start.5 = (bf16[128,2048]{1,0:T(8,128)(2,1)}, bf16[128,2048]{1,0:T(8,128)(2,1)S(1)}, u32[]{:S(2)}, u32[]{:S(2)}) collective-permute-start(bf16[128,2048]{1,0:T(8,128)(2,1)} %tokens.1), channel_id=1, source_target_pairs={{2,4},{3,5},{4,2},{5,3},{10,12},{11,13},{12,10},{13,11},{18,20},{1... | collective-permute-start | bytes 1572872 | tf_op jit(solution)/shard_map/ppermute | solution.py:299
  15.6 3.8 %copy-start.29 = (bf16[384,512]{1,0:T(8,128)(2,1)}, bf16[384,512]{1,0:T(8,128)(2,1)S(1)}, u32[]{:S(2)}) copy-start(bf16[384,512]{1,0:T(8,128)(2,1)S(1)} %collective-permute-done.27.refs_4_) | copy-start | bytes 1179652
  15.6 51.4 %collective-permute-start.1 = (bf16[128,2048]{1,0:T(8,128)(2,1)}, bf16[128,2048]{1,0:T(8,128)(2,1)}, u32[]{:S(2)}, u32[]{:S(2)}) collective-permute-start(bf16[128,2048]{1,0:T(8,128)(2,1)} %refs_0_.1), channel_id=1, source_target_pairs={{0,4},{1,5},{2,6},{3,7},{4,0},{5,1},{6,2},{7,3},{8,12},{9,13},{10,... | collective-permute-start | bytes 1572872 | tf_op jit(solution)/shard_map/ppermute | solution.py:299
  34.8 32.7 %collective-permute-start.20 = (bf16[128,2048]{1,0:T(8,128)(2,1)}, bf16[128,2048]{1,0:T(8,128)(2,1)S(1)}, u32[]{:S(2)}, u32[]{:S(2)}) collective-permute-start(bf16[128,2048]{1,0:T(8,128)(2,1)} %refs_0_.1), channel_id=1, source_target_pairs={{0,2},{1,3},{2,0},{3,1},{4,6},{5,7},{6,4},{7,5},{8,10},{9,11},{10,... | collective-permute-start | bytes 1572872 | tf_op jit(solution)/shard_map/ppermute | solution.py:299
  34.8 33.2 %collective-permute-start.21 = (bf16[128,2048]{1,0:T(8,128)(2,1)}, bf16[128,2048]{1,0:T(8,128)(2,1)S(1)}, u32[]{:S(2)}, u32[]{:S(2)}) collective-permute-start(bf16[128,2048]{1,0:T(8,128)(2,1)} %refs_0_.1), channel_id=1, source_target_pairs={{0,1},{1,0},{2,3},{3,2},{4,5},{5,4},{6,7},{7,6},{8,9},{9,8},{10,11... | collective-permute-start | bytes 1572872 | tf_op jit(solution)/shard_map/ppermute | solution.py:302
  35.6 34.7 %collective-permute-start = (bf16[128,2048]{1,0:T(8,128)(2,1)}, bf16[128,2048]{1,0:T(8,128)(2,1)}, u32[]{:S(2)}, u32[]{:S(2)}) collective-permute-start(bf16[128,2048]{1,0:T(8,128)(2,1)} %refs_0_.1), channel_id=1, source_target_pairs={{2,4},{3,5},{4,2},{5,3},{10,12},{11,13},{12,10},{13,11},{18,20},{1... | collective-permute-start | bytes 1572872 | tf_op jit(solution)/shard_map/ppermute | solution.py:299
  37.1 33.2 %collective-permute-start.10 = (bf16[512,768]{1,0:T(8,128)(2,1)S(1)}, bf16[512,768]{1,0:T(8,128)(2,1)S(1)}, u32[]{:S(2)}, u32[]{:S(2)}) collective-permute-start(bf16[512,768]{1,0:T(8,128)(2,1)S(1)} %bitcast.63), channel_id=1, source_target_pairs={{0,8},{8,0},{16,24},{24,16},{1,9},{9,1},{17,25},{25,17},{2,10},{10... | collective-permute-start | bytes 2359304 | tf_op jit(solution)/shard_map/ppermute | solution.py:293
  66.9 20.4 %collective-permute-start.12 = (bf16[512,768]{1,0:T(8,128)(2,1)S(1)}, bf16[512,768]{1,0:T(8,128)(2,1)S(1)}, u32[]{:S(2)}, u32[]{:S(2)}) collective-permute-start(bf16[512,768]{1,0:T(8,128)(2,1)S(1)} %bitcast.66), channel_id=1, source_target_pairs={{0,16},{8,24},{16,0},{24,8},{1,17},{9,25},{17,1},{25,9},{2,18},{10... | collective-permute-start | bytes 2359304 | tf_op jit(solution)/shard_map/ppermute | solution.py:296
  67.5 22.0 %collective-permute-start.18 = (bf16[512,768]{1,0:T(8,128)(2,1)S(1)}, bf16[512,768]{1,0:T(8,128)(2,1)S(1)}, u32[]{:S(2)}, u32[]{:S(2)}) collective-permute-start(bf16[512,768]{1,0:T(8,128)(2,1)S(1)} %bitcast.67), channel_id=1, source_target_pairs={{0,8},{8,0},{16,24},{24,16},{1,9},{9,1},{17,25},{25,17},{2,10},{10... | collective-permute-start | bytes 2359304 | tf_op jit(solution)/shard_map/ppermute | solution.py:293
  68.8 32.3 %collective-permute-start.19 = (bf16[512,768]{1,0:T(8,128)(2,1)S(1)}, bf16[512,768]{1,0:T(8,128)(2,1)S(1)}, u32[]{:S(2)}, u32[]{:S(2)}) collective-permute-start(bf16[512,768]{1,0:T(8,128)(2,1)S(1)} %bitcast.64), channel_id=1, source_target_pairs={{0,16},{8,24},{16,0},{24,8},{1,17},{9,25},{17,1},{25,9},{2,18},{10... | collective-permute-start | bytes 2359304 | tf_op jit(solution)/shard_map/ppermute | solution.py:296
  70.3 30.8 %collective-permute-start.16 = (bf16[128,2048]{1,0:T(8,128)(2,1)S(1)}, bf16[128,2048]{1,0:T(8,128)(2,1)S(1)}, u32[]{:S(2)}, u32[]{:S(2)}) collective-permute-start(bf16[128,2048]{1,0:T(8,128)(2,1)S(1)} %collective-permute-done.6.refs_0_), channel_id=1, source_target_pairs={{0,1},{1,0},{2,3},{3,2},{4,5},{5,4},{6,7},{7,6},{8,9},{9,8},{10,11... | collective-permute-start | bytes 1572872 | tf_op jit(solution)/shard_map/ppermute | solution.py:302
  70.3 32.9 %collective-permute-start.17 = (bf16[128,2048]{1,0:T(8,128)(2,1)S(1)}, bf16[128,2048]{1,0:T(8,128)(2,1)S(1)}, u32[]{:S(2)}, u32[]{:S(2)}) collective-permute-start(bf16[128,2048]{1,0:T(8,128)(2,1)S(1)} %collective-permute-done.14.refs_1_), channel_id=1, source_target_pairs={{0,1},{1,0},{2,3},{3,2},{4,5},{5,4},{6,7},{7,6},{8,9},{9,8},{10,11... | collective-permute-start | bytes 1572872 | tf_op jit(solution)/shard_map/ppermute | solution.py:302
  87.4 17.3 %collective-permute-start.7 = (bf16[128,2048]{1,0:T(8,128)(2,1)S(1)}, bf16[128,2048]{1,0:T(8,128)(2,1)}, u32[]{:S(2)}, u32[]{:S(2)}) collective-permute-start(bf16[128,2048]{1,0:T(8,128)(2,1)S(1)} %collective-permute-done.6.refs_0_), channel_id=1, source_target_pairs={{4,6},{5,7},{2,0},{3,1},{12,14},{13,15},{10,8},{11,9},{20,22},{21,... | collective-permute-start | bytes 1572872 | tf_op jit(solution)/shard_map/ppermute | solution.py:299
  89.4 15.6 %collective-permute-start.8 = (bf16[128,2048]{1,0:T(8,128)(2,1)S(1)}, bf16[128,2048]{1,0:T(8,128)(2,1)S(1)}, u32[]{:S(2)}, u32[]{:S(2)}) collective-permute-start(bf16[128,2048]{1,0:T(8,128)(2,1)S(1)} %collective-permute-done.5.refs_0_), channel_id=1, source_target_pairs={{2,3},{3,2},{4,5},{5,4},{10,11},{11,10},{12,13},{13,12},{18,19},{1... | collective-permute-start | bytes 1572872 | tf_op jit(solution)/shard_map/ppermute | solution.py:302
  101.1 6.0 %collective-permute-start.22 = (bf16[128,2048]{1,0:T(8,128)(2,1)}, bf16[128,2048]{1,0:T(8,128)(2,1)S(1)}, u32[]{:S(2)}, u32[]{:S(2)}) collective-permute-start(bf16[128,2048]{1,0:T(8,128)(2,1)} %collective-permute-done.1.refs_1_), channel_id=1, source_target_pairs={{0,1},{1,0},{2,3},{3,2},{4,5},{5,4},{6,7},{7,6},{8,9},{9,8},{10,11... | collective-permute-start | bytes 1572872 | tf_op jit(solution)/shard_map/ppermute | solution.py:302
  102.0 7.5 %collective-permute-start.23 = (bf16[128,2048]{1,0:T(8,128)(2,1)S(1)}, bf16[128,2048]{1,0:T(8,128)(2,1)S(1)}, u32[]{:S(2)}, u32[]{:S(2)}) collective-permute-start(bf16[128,2048]{1,0:T(8,128)(2,1)S(1)} %collective-permute-done.20.refs_2_), channel_id=1, source_target_pairs={{0,1},{1,0},{2,3},{3,2},{4,5},{5,4},{6,7},{7,6},{8,9},{9,8},{10,11... | collective-permute-start | bytes 1572872 | tf_op jit(solution)/shard_map/ppermute | solution.py:302
  104.1 35.6 %collective-permute-start.11 = (bf16[512,768]{1,0:T(8,128)(2,1)S(1)}, bf16[512,768]{1,0:T(8,128)(2,1)}, u32[]{:S(2)}, u32[]{:S(2)}) collective-permute-start(bf16[512,768]{1,0:T(8,128)(2,1)S(1)} %collective-permute-done.10.refs_5_), channel_id=1, source_target_pairs={{0,16},{8,24},{16,0},{24,8},{1,17},{9,25},{17,1},{25,9},{2,18},{10... | collective-permute-start | bytes 2359304 | tf_op jit(solution)/shard_map/ppermute | solution.py:296
  104.6 35.6 %collective-permute-start.13 = (bf16[512,768]{1,0:T(8,128)(2,1)S(1)}, bf16[512,768]{1,0:T(8,128)(2,1)}, u32[]{:S(2)}, u32[]{:S(2)}) collective-permute-start(bf16[512,768]{1,0:T(8,128)(2,1)S(1)} %collective-permute-done.12.refs_8_), channel_id=1, source_target_pairs={{0,8},{8,0},{16,24},{24,16},{1,9},{9,1},{17,25},{25,17},{2,10},{10... | collective-permute-start | bytes 2359304 | tf_op jit(solution)/shard_map/ppermute | solution.py:293
  105.9 30.2 %collective-permute-start.2 = (bf16[128,2048]{1,0:T(8,128)(2,1)}, bf16[128,2048]{1,0:T(8,128)(2,1)}, u32[]{:S(2)}, u32[]{:S(2)}) collective-permute-start(bf16[128,2048]{1,0:T(8,128)(2,1)} %collective-permute-done.1.refs_1_), channel_id=1, source_target_pairs={{4,6},{5,7},{2,0},{3,1},{12,14},{13,15},{10,8},{11,9},{20,22},{21,... | collective-permute-start | bytes 1572872 | tf_op jit(solution)/shard_map/ppermute | solution.py:299
  108.0 29.6 %collective-permute-start.3 = (bf16[128,2048]{1,0:T(8,128)(2,1)}, bf16[128,2048]{1,0:T(8,128)(2,1)}, u32[]{:S(2)}, u32[]{:S(2)}) collective-permute-start(bf16[128,2048]{1,0:T(8,128)(2,1)} %collective-permute-done.refs_0_), channel_id=1, source_target_pairs={{2,3},{3,2},{4,5},{5,4},{10,11},{11,10},{12,13},{13,12},{18,19},{1... | collective-permute-start | bytes 1572872 | tf_op jit(solution)/shard_map/ppermute | solution.py:302
  110.3 28.9 %collective-permute-start.9 = (bf16[128,2048]{1,0:T(8,128)(2,1)}, bf16[128,2048]{1,0:T(8,128)(2,1)}, u32[]{:S(2)}, u32[]{:S(2)}) collective-permute-start(bf16[128,2048]{1,0:T(8,128)(2,1)} %collective-permute-done.7.refs_1_), channel_id=1, source_target_pairs={{0,1},{1,0},{6,7},{7,6},{8,9},{9,8},{14,15},{15,14},{16,17},{17,16... | collective-permute-start | bytes 1572872 | tf_op jit(solution)/shard_map/ppermute | solution.py:302
  112.8 13.5 %all-to-all-start = ((f32[8,1,128]{2,1,0:T(1,128)}), f32[8,1,128]{2,1,0:T(1,128)S(1)}, u32[]{:S(2)}, u32[]{:S(2)}) async-start(f32[8,1,128]{2,1,0:T(1,128)} %bitcast.5), calls=%async_computation | async-start | bytes 8192 | tf_op jit(solution)/shard_map/all_to_all | solution.py:316
  129.6 1.2 copy-start.12
  129.6 1.4 copy-start.14
  129.6 1.5 copy-start.22
  132.2 1.2 copy-start.16
  132.2 1.4 copy-start.18
  132.2 1.5 copy-start.26
  132.2 1.7 copy-start.28
  133.9 2.2 copy-start.34
  133.9 3.8 %copy-start.32 = (bf16[384,512]{1,0:T(8,128)(2,1)S(1)}, bf16[384,512]{1,0:T(8,128)(2,1)}, u32[]{:S(2)}) copy-start(bf16[384,512]{1,0:T(8,128)(2,1)} %copy-done.31) | copy-start | bytes 1179652
  133.9 5.8 %copy-start.30 = (bf16[384,512]{1,0:T(8,128)(2,1)S(1)}, bf16[384,512]{1,0:T(8,128)(2,1)}, u32[]{:S(2)}) copy-start(bf16[384,512]{1,0:T(8,128)(2,1)} %copy-done.29) | copy-start | bytes 1179652
  136.1 23.2 %collective-permute-start.25 = (bf16[384,512]{1,0:T(8,128)(2,1)S(1)}, bf16[384,512]{1,0:T(8,128)(2,1)S(1)}, u32[]{:S(2)}, u32[]{:S(2)}) collective-permute-start(bf16[384,512]{1,0:T(8,128)(2,1)S(1)} %copy-done.34), channel_id=1, source_target_pairs={{0,8},{8,0},{16,24},{24,16},{1,9},{9,1},{17,25},{25,17},{2,10},{10... | collective-permute-start | bytes 1179656 | tf_op jit(solution)/shard_map/ppermute | solution.py:293
  137.7 21.6 %collective-permute-start.26 = (bf16[384,512]{1,0:T(8,128)(2,1)S(1)}, bf16[384,512]{1,0:T(8,128)(2,1)S(1)}, u32[]{:S(2)}, u32[]{:S(2)}) collective-permute-start(bf16[384,512]{1,0:T(8,128)(2,1)S(1)} %copy-done.32), channel_id=1, source_target_pairs={{0,16},{8,24},{16,0},{24,8},{1,17},{9,25},{17,1},{25,9},{2,18},{10... | collective-permute-start | bytes 1179656 | tf_op jit(solution)/shard_map/ppermute | solution.py:296
  139.2 20.1 %collective-permute-start.28 = (bf16[384,512]{1,0:T(8,128)(2,1)S(1)}, bf16[384,512]{1,0:T(8,128)(2,1)S(1)}, u32[]{:S(2)}, u32[]{:S(2)}) collective-permute-start(bf16[384,512]{1,0:T(8,128)(2,1)S(1)} %collective-permute-done.24.refs_1_), channel_id=1, source_target_pairs={{0,16},{8,24},{16,0},{24,8},{1,17},{9,25},{17,1},{25,9},{2,18},{10... | collective-permute-start | bytes 1179656 | tf_op jit(solution)/shard_map/ppermute | solution.py:296
  139.7 19.6 %collective-permute-start.29 = (bf16[384,512]{1,0:T(8,128)(2,1)S(1)}, bf16[384,512]{1,0:T(8,128)(2,1)S(1)}, u32[]{:S(2)}, u32[]{:S(2)}) collective-permute-start(bf16[384,512]{1,0:T(8,128)(2,1)S(1)} %copy-done.30), channel_id=1, source_target_pairs={{0,8},{8,0},{16,24},{24,16},{1,9},{9,1},{17,25},{25,17},{2,10},{10... | collective-permute-start | bytes 1179656 | tf_op jit(solution)/shard_map/ppermute | solution.py:293
  140.2 13.7 %collective-permute-start.4 = (bf16[128,2048]{1,0:T(8,128)(2,1)}, bf16[128,2048]{1,0:T(8,128)(2,1)S(1)}, u32[]{:S(2)}, u32[]{:S(2)}) collective-permute-start(bf16[128,2048]{1,0:T(8,128)(2,1)} %collective-permute-done.2.refs_1_), channel_id=1, source_target_pairs={{0,1},{1,0},{6,7},{7,6},{8,9},{9,8},{14,15},{15,14},{16,17},{17,16... | collective-permute-start | bytes 1572872 | tf_op jit(solution)/shard_map/ppermute | solution.py:302
  142.2 7.7 %copy-start.8 = (bf16[128,2048]{1,0:T(8,128)(2,1)S(1)}, bf16[128,2048]{1,0:T(8,128)(2,1)}, u32[]{:S(2)}) copy-start(bf16[128,2048]{1,0:T(8,128)(2,1)} %copy-done.7) | copy-start | bytes 1572868
  142.2 7.7 %copy-start.20 = (bf16[128,2048]{1,0:T(8,128)(2,1)S(1)}, bf16[128,2048]{1,0:T(8,128)(2,1)}, u32[]{:S(2)}) copy-start(bf16[128,2048]{1,0:T(8,128)(2,1)} %copy-done.19) | copy-start | bytes 1572868
  153.9 5.4 %copy-start = (bf16[1,768,512]{2,1,0:T(8,128)(2,1)S(1)}, bf16[1,768,512]{2,1,0:T(8,128)(2,1)}, u32[]{:S(2)}) copy-start(bf16[1,768,512]{2,1,0:T(8,128)(2,1)} %param.13) | copy-start | bytes 2359300
  157.7 25.5 %collective-permute-start.39 = (bf16[2,384,512]{2,1,0:T(8,128)(2,1)S(1)}, bf16[2,384,512]{2,1,0:T(8,128)(2,1)S(1)}, u32[]{:S(2)}, u32[]{:S(2)}) collective-permute-start(bf16[2,384,512]{2,1,0:T(8,128)(2,1)S(1)} %get-tuple-element.69), channel_id=1, source_target_pairs={{0,8},{8,0},{16,24},{24,16},{1,9},{9,1},{17,25},{25,17},{2,10},{10... | collective-permute-start | bytes 2359304 | tf_op jit(solution)/shard_map/ppermute | solution.py:293
  173.8 32.4 %collective-permute-start.30 = (bf16[512,2048]{1,0:T(8,128)(2,1)S(1)}, bf16[512,2048]{1,0:T(8,128)(2,1)S(1)}, u32[]{:S(2)}, u32[]{:S(2)}) collective-permute-start(bf16[512,2048]{1,0:T(8,128)(2,1)S(1)} %get-tuple-element.58), channel_id=1, source_target_pairs={{0,1},{1,0},{2,3},{3,2},{4,5},{5,4},{6,7},{7,6},{8,9},{9,8},{10,11... | collective-permute-start | bytes 6291464 | tf_op jit(solution)/shard_map/ppermute | solution.py:302
  174.0 20.4 %collective-permute-start.41 = (bf16[2,384,512]{2,1,0:T(8,128)(2,1)S(1)}, bf16[2,384,512]{2,1,0:T(8,128)(2,1)S(1)}, u32[]{:S(2)}, u32[]{:S(2)}) collective-permute-start(bf16[2,384,512]{2,1,0:T(8,128)(2,1)S(1)} %get-tuple-element.72), channel_id=1, source_target_pairs={{0,16},{8,24},{16,0},{24,8},{1,17},{9,25},{17,1},{25,9},{2,18},{10... | collective-permute-start | bytes 2359304 | tf_op jit(solution)/shard_map/ppermute | solution.py:296
  183.3 20.2 %collective-permute-start.40 = (bf16[384,512]{1,0:T(8,128)(2,1)S(1)}, bf16[384,512]{1,0:T(8,128)(2,1)S(1)}, u32[]{:S(2)}, u32[]{:S(2)}) collective-permute-start(bf16[384,512]{1,0:T(8,128)(2,1)S(1)} %fusion.9), channel_id=1, source_target_pairs={{0,16},{8,24},{16,0},{24,8},{1,17},{9,25},{17,1},{25,9},{2,18},{10... | collective-permute-start | bytes 1179656 | tf_op jit(solution)/shard_map/ppermute | solution.py:296
  194.6 11.5 %collective-permute-start.42 = (bf16[384,512]{1,0:T(8,128)(2,1)S(1)}, bf16[384,512]{1,0:T(8,128)(2,1)S(1)}, u32[]{:S(2)}, u32[]{:S(2)}) collective-permute-start(bf16[384,512]{1,0:T(8,128)(2,1)S(1)} %fusion.6), channel_id=1, source_target_pairs={{0,8},{8,0},{16,24},{24,16},{1,9},{9,1},{17,25},{25,17},{2,10},{10... | collective-permute-start | bytes 1179656 | tf_op jit(solution)/shard_map/ppermute | solution.py:293
  200.4 35.5 %collective-permute-start.36 = (bf16[2,512,768]{2,1,0:T(8,128)(2,1)S(1)}, bf16[2,512,768]{2,1,0:T(8,128)(2,1)S(1)}, u32[]{:S(2)}, u32[]{:S(2)}) collective-permute-start(bf16[2,512,768]{2,1,0:T(8,128)(2,1)S(1)} %get-tuple-element.63), channel_id=1, source_target_pairs={{0,16},{8,24},{16,0},{24,8},{1,17},{9,25},{17,1},{25,9},{2,18},{10... | collective-permute-start | bytes 4718600 | tf_op jit(solution)/shard_map/ppermute | solution.py:296
  202.0 37.0 %collective-permute-start.35 = (bf16[2,512,768]{2,1,0:T(8,128)(2,1)S(1)}, bf16[2,512,768]{2,1,0:T(8,128)(2,1)S(1)}, u32[]{:S(2)}, u32[]{:S(2)}) collective-permute-start(bf16[2,512,768]{2,1,0:T(8,128)(2,1)S(1)} %get-tuple-element.61), channel_id=1, source_target_pairs={{0,8},{8,0},{16,24},{24,16},{1,9},{9,1},{17,25},{25,17},{2,10},{10... | collective-permute-start | bytes 4718600 | tf_op jit(solution)/shard_map/ppermute | solution.py:293
  207.2 35.8 %collective-permute-start.33 = (bf16[128,2048]{1,0:T(8,128)(2,1)S(1)}, bf16[128,2048]{1,0:T(8,128)(2,1)S(1)}, u32[]{:S(2)}, u32[]{:S(2)}) collective-permute-start(bf16[128,2048]{1,0:T(8,128)(2,1)S(1)} %get-tuple-element.75), channel_id=1, source_target_pairs={{0,2},{1,3},{6,4},{7,5},{8,10},{9,11},{14,12},{15,13},{16,18},{17,... | collective-permute-start | bytes 1572872 | tf_op jit(solution)/shard_map/ppermute | solution.py:299
  236.3 18.6 %collective-permute-start.38 = (bf16[512,768]{1,0:T(8,128)(2,1)S(1)}, bf16[512,768]{1,0:T(8,128)(2,1)S(1)}, u32[]{:S(2)}, u32[]{:S(2)}) collective-permute-start(bf16[512,768]{1,0:T(8,128)(2,1)S(1)} %get-tuple-element.76), channel_id=1, source_target_pairs={{0,8},{8,0},{16,24},{24,16},{1,9},{9,1},{17,25},{25,17},{2,10},{10... | collective-permute-start | bytes 2359304 | tf_op jit(solution)/shard_map/ppermute | solution.py:293
  239.4 17.2 %collective-permute-start.37 = (bf16[512,768]{1,0:T(8,128)(2,1)S(1)}, bf16[512,768]{1,0:T(8,128)(2,1)S(1)}, u32[]{:S(2)}, u32[]{:S(2)}) collective-permute-start(bf16[512,768]{1,0:T(8,128)(2,1)S(1)} %get-tuple-element.79), channel_id=1, source_target_pairs={{0,16},{8,24},{16,0},{24,8},{1,17},{9,25},{17,1},{25,9},{2,18},{10... | collective-permute-start | bytes 2359304 | tf_op jit(solution)/shard_map/ppermute | solution.py:296
  241.9 15.7 %collective-permute-start.31 = (bf16[128,2048]{1,0:T(8,128)(2,1)S(1)}, bf16[128,2048]{1,0:T(8,128)(2,1)S(1)}, u32[]{:S(2)}, u32[]{:S(2)}) collective-permute-start(bf16[128,2048]{1,0:T(8,128)(2,1)S(1)} %get-tuple-element.75), channel_id=1, source_target_pairs={{2,4},{3,5},{4,2},{5,3},{10,12},{11,13},{12,10},{13,11},{18,20},{1... | collective-permute-start | bytes 1572872 | tf_op jit(solution)/shard_map/ppermute | solution.py:299
  242.6 15.1 %collective-permute-start.32 = (bf16[128,2048]{1,0:T(8,128)(2,1)S(1)}, bf16[128,2048]{1,0:T(8,128)(2,1)S(1)}, u32[]{:S(2)}, u32[]{:S(2)}) collective-permute-start(bf16[128,2048]{1,0:T(8,128)(2,1)S(1)} %get-tuple-element.74), channel_id=1, source_target_pairs={{0,2},{1,3},{2,0},{3,1},{4,6},{5,7},{6,4},{7,5},{8,10},{9,11},{10,... | collective-permute-start | bytes 1572872 | tf_op jit(solution)/shard_map/ppermute | solution.py:299
  243.1 32.0 %collective-permute-start.34 = (bf16[128,2048]{1,0:T(8,128)(2,1)S(1)}, bf16[128,2048]{1,0:T(8,128)(2,1)S(1)}, u32[]{:S(2)}, u32[]{:S(2)}) collective-permute-start(bf16[128,2048]{1,0:T(8,128)(2,1)S(1)} %add_convert_fusion.4), channel_id=1, source_target_pairs={{0,4},{1,5},{2,6},{3,7},{4,0},{5,1},{6,2},{7,3},{8,12},{9,13},{10,... | collective-permute-start | bytes 1572872 | tf_op jit(solution)/shard_map/ppermute | solution.py:299
  (17 other events, 15.4 us)

commit v7 on v4

--- a/solution.py
+++ b/solution.py
@@ -13,7 +13,7 @@
 ANY = pl.BlockSpec(memory_space=pl.ANY)
 VMEM = pl.BlockSpec(memory_space=pltpu.VMEM)
 SMEM = pl.BlockSpec(memory_space=pltpu.SMEM)
-LIMIT = 24 * 1024 * 1024
+LIMIT = 12 * 1024 * 1024
 LANES = 128
 NN = (((1,), (0,)), ((), ()))
 NT = (((1,), (1,)), ((), ()))
@@ -208,16 +208,16 @@
     down_blocks(place, act, y, ((0, 0, a0, None), (0, 2, a1, None), (1, 0, b0, None), (1, 1, b1, None)))
 
 
-def back_body(place, y, active, slope, own, from_x, from_y, diag_a, diag_b, gate_delta, up_delta, w, sems):
+def back_body(place, y, active, slope, *refs):
+    own, halves = refs[0], refs[1:7]
+    gate_delta, up_delta, w, sems = refs[7:]
     me = place[0]
     copies = Copies(sems)
     hidden, share = own.shape
     half = hidden // 2
-    started = []
-    for k, src in ((0, own), (1, from_x), (2, from_y)):
-        started.append(copies.start(src, w.at[me ^ k]))
-    started.append(copies.start(diag_a, w.at[me ^ 3, pl.ds(0, half)]))
-    started.append(copies.start(diag_b, w.at[me ^ 3, pl.ds(half, half)]))
+    started = [copies.start(own, w.at[me])]
+    for i, src in enumerate(halves):
+        started.append(copies.start(src, w.at[me ^ (1 + i // 2), pl.ds(i % 2 * half, half)]))
     for c in started:
         c.wait()
     rows = y.shape[0]
@@ -337,8 +337,10 @@
     wg1, wu2 = to_x(wg0), to_y(wu0)
     wg2, wu1 = to_y(wg0), to_x(wu0)
     wg3, wu3 = to_y(wg1), to_x(wu2)
-    wd1, wd2 = to_x(wd0), to_y(wd0)
-    wd3a, wd3b = to_x(wd2[:half]), to_y(wd1[half:])
+    da0, db0 = wd0[:half], wd0[half:]
+    da1, db2 = to_x(da0), to_y(db0)
+    da2, db1 = to_y(da0), to_x(db0)
+    da3, db3 = to_y(da1), to_x(db2)
 
     def dma(n):
         return pltpu.SemaphoreType.DMA((n,))
@@ -407,8 +409,8 @@
     gate_delta, up_delta = call(
         back_body,
         [((rows, hidden), BF16, VMEM)] * 2,
-        [(place, SMEM), (y, VMEM), (active, VMEM), (slope, VMEM)] + [(a, ANY) for a in (wd0, wd1, wd2, wd3a, wd3b)],
-        [pltpu.VMEM((4, hidden, share), BF16), dma(5)],
+        [(place, SMEM), (y, VMEM), (active, VMEM), (slope, VMEM)] + anys((wd0, da1, db1, da2, db2, da3, db3)),
+        [pltpu.VMEM((4, hidden, share), BF16), dma(7)],
         2 * rows * width * hidden,
         2 * (rows * width + width * hidden) + 12 * rows * hidden,
     )

time: 291 us -> 273 us (0.938)
  waiting for transfers between devices: 164 us -> 147 us
  starting transfers between devices: 57.9 us -> 51.9 us
  local copies, waits for them, and re-layouts: 15.5 us -> 18.7 us
    ppermute x9 -> x10, waiting for transfers between devices: 74.4 us -> 62.8 us  [to_y(): return lax.ppermute(block, 'dp', [(i, i ^ 2) for i in range(4)])]
    ppermute x12, starting transfers between devices: 30.6 us -> 22.8 us  [hop(): lax.ppermute(block, 'expert', [(2 * a + c, 2 * b + c) for a, b in moves f...]
    ppermute x12, waiting for transfers between devices: 79.4 us -> 71.8 us  [hop(): lax.ppermute(block, 'expert', [(2 * a + c, 2 * b + c) for a, b in moves f...]
    ppermute x9 -> x10, waiting for transfers between devices: 9.73 us -> 12.1 us  [to_x(): return lax.ppermute(block, 'dp', [(i, i ^ 1) for i in range(4)])]
    unnamed x62 -> x84, local copies, waits for them, and re-layouts: 15.4 us -> 17.3 us
    ppermute x9 -> x10, starting transfers between devices: 9.91 us -> 11.4 us  [to_y(): return lax.ppermute(block, 'dp', [(i, i ^ 2) for i in range(4)])]
    ppermute x9 -> x10, starting transfers between devices: 11.1 us -> 10.9 us  [to_x(): return lax.ppermute(block, 'dp', [(i, i ^ 1) for i in range(4)])]
  transfers between devices with their start and end apart: 41 -> 43, of which waited for: 15 -> 15; matrix products, arithmetic and copies ran while one was open for 2% -> 2% of each run, Pallas kernels for 16% -> 17%
where the time goes in v7:
time: 273 us; the launch traced here: 272 us
  waiting for transfers between devices  147 us (54%)
  starting transfers between devices  51.9 us (19%)
  Pallas kernels  47.1 us (17%)
  local copies, waits for them, and re-layouts  18.7 us (7%)
  other arithmetic  6.67 us (2%)
    ppermute x12, waiting for transfers between devices, hop(): lax.ppermute(block, 'expert', [(2 * a + c, 2 * b + c) for a, b in moves f...  71.8 us
    ppermute x10, waiting for transfers between devices, to_y(): return lax.ppermute(block, 'dp', [(i, i ^ 2) for i in range(4)])  62.8 us
    pallas_call x12, Pallas kernels, call(): pl.pallas_call(body, input_output_aliases=aliases or {}, out_shape=[jax.S...  47.1 us
    ppermute x12, starting transfers between devices, hop(): lax.ppermute(block, 'expert', [(2 * a + c, 2 * b + c) for a, b in moves f...  22.8 us
    unnamed x84, local copies, waits for them, and re-layouts  17.3 us
    ppermute x10, waiting for transfers between devices, to_x(): return lax.ppermute(block, 'dp', [(i, i ^ 1) for i in range(4)])  12.1 us
    ppermute x10, starting transfers between devices, to_y(): return lax.ppermute(block, 'dp', [(i, i ^ 2) for i in range(4)])  11.4 us
    ppermute x10, starting transfers between devices, to_x(): return lax.ppermute(block, 'dp', [(i, i ^ 1) for i in range(4)])  10.9 us
  transfers between devices with their start and end apart: 43, of which 15 were waited for; matrix products, arithmetic and copies ran while one was open for 2% of the time, Pallas kernels for 17%

profile of v7, /device:TPU:0, one launch (start us, length us, event | category | flops | bytes accessed | tf_op | source)
XLA Modules:
  0.0 272.4 jit_solution(14274399729819762161)
XLA Ops:
  0.7 1.3 slice_bitcast_fusion.8
  2.0 3.0 %collective-permute-start.24 = (bf16[384,512]{1,0:T(8,128)(2,1)S(1)}, bf16[384,512]{1,0:T(8,128)(2,1)S(1)}, u32[]{:S(2)}, u32[]{:S(2)}) collective-permute-start(bf16[384,512]{1,0:T(8,128)(2,1)S(1)} %get-tuple-element.79), channel_id=1, source_target_pairs={{0,8},{8,0},{16,24},{24,16},{1,9},{9,1},{17,25},{25,17},{2,10},{10... | collective-permute-start | bytes 1179656 | tf_op jit(solution)/shard_map/ppermute | solution.py:305
  5.1 1.5 collective-permute-start.27
  6.6 2.6 collective-permute-start.6
  9.2 1.6 collective-permute-start.14
  10.9 3.3 %collective-permute-done.24.refs_1_ = bf16[384,512]{1,0:T(8,128)(2,1)S(1)} collective-permute-done((bf16[384,512]{1,0:T(8,128)(2,1)S(1)}, bf16[384,512]{1,0:T(8,128)(2,1)S(1)}, u32[]{:S(2)}, u32[]{:S(2)}) %collective-permute-start.24) | collective-permute-done | bytes 393248 | tf_op jit(solution)/shard_map/ppermute | solution.py:305
  14.2 2.8 %collective-permute-start.1 = (bf16[128,2176]{1,0:T(8,128)(2,1)S(1)}, bf16[128,2176]{1,0:T(8,128)(2,1)}, u32[]{:S(2)}, u32[]{:S(2)}) collective-permute-start(bf16[128,2176]{1,0:T(8,128)(2,1)S(1)} %shard_map.102.refs_0_), channel_id=1, source_target_pairs={{0,4},{1,5},{2,6},{3,7},{4,0},{5,1},{6,2},{7,3},{8,12},{9,13},{10,... | collective-permute-start | bytes 1671176 | tf_op jit(solution)/shard_map/ppermute | solution.py:311
  17.7 16.9 %collective-permute-done.6.refs_0_ = bf16[128,2048]{1,0:T(8,128)(2,1)S(1)} collective-permute-done((bf16[128,2048]{1,0:T(8,128)(2,1)S(1)}, bf16[128,2048]{1,0:T(8,128)(2,1)S(1)}, u32[]{:S(2)}, u32[]{:S(2)}) %collective-permute-start.6) | collective-permute-done | bytes 524320 | tf_op jit(solution)/shard_map/ppermute | solution.py:311
  36.8 20.2 %collective-permute-done.1.refs_1_ = bf16[128,2176]{1,0:T(8,128)(2,1)} collective-permute-done((bf16[128,2176]{1,0:T(8,128)(2,1)S(1)}, bf16[128,2176]{1,0:T(8,128)(2,1)}, u32[]{:S(2)}, u32[]{:S(2)}) %collective-permute-start.1) | collective-permute-done | bytes 557088 | tf_op jit(solution)/shard_map/ppermute | solution.py:311
  58.1 0.8 copy-done.9
  58.9 1.5 collective-permute-start.19
  60.9 0.8 copy-done.21
  61.8 15.7 %collective-permute-done.12.refs_8_ = bf16[512,768]{1,0:T(8,128)(2,1)S(1)} collective-permute-done((bf16[512,768]{1,0:T(8,128)(2,1)S(1)}, bf16[512,768]{1,0:T(8,128)(2,1)S(1)}, u32[]{:S(2)}, u32[]{:S(2)}) %collective-permute-start.12) | collective-permute-done | bytes 786464 | tf_op jit(solution)/shard_map/ppermute | solution.py:308
  77.4 1.3 collective-permute-start.7
  79.5 11.7 %collective-permute-done.19.refs_7_ = bf16[512,768]{1,0:T(8,128)(2,1)S(1)} collective-permute-done((bf16[512,768]{1,0:T(8,128)(2,1)S(1)}, bf16[512,768]{1,0:T(8,128)(2,1)S(1)}, u32[]{:S(2)}, u32[]{:S(2)}) %collective-permute-start.19) | collective-permute-done | bytes 786464 | tf_op jit(solution)/shard_map/ppermute | solution.py:308
  91.2 0.9 copy-done.1
  93.6 0.8 copy-done.27
  95.2 0.8 copy-done.29
  96.6 7.4 %collective-permute-done.7.refs_1_ = bf16[128,2048]{1,0:T(8,128)(2,1)} collective-permute-done((bf16[128,2048]{1,0:T(8,128)(2,1)S(1)}, bf16[128,2048]{1,0:T(8,128)(2,1)}, u32[]{:S(2)}, u32[]{:S(2)}) %collective-permute-start.7) | collective-permute-done | bytes 524320 | tf_op jit(solution)/shard_map/ppermute | solution.py:311
  105.3 1.3 collective-permute-start.2
  106.6 0.8 copy-done.11
  107.4 1.5 collective-permute-start.3
  108.9 0.9 copy-done.13
  109.7 1.9 collective-permute-start.9
  111.8 1.2 copy-done.4
  113.0 1.1 copy-done.6
  114.1 1.0 copy-done.16
  116.4 1.0 copy-done.24
  117.4 1.0 copy-done.28
  118.4 1.0 copy-done.30
  119.5 1.0 shard_map.104
  121.1 2.5 shard_map.107.refs_5_
  123.5 3.9 %collective-permute-done.2.refs_1_ = bf16[128,2176]{1,0:T(8,128)(2,1)} collective-permute-done((bf16[128,2176]{1,0:T(8,128)(2,1)}, bf16[128,2176]{1,0:T(8,128)(2,1)}, u32[]{:S(2)}, u32[]{:S(2)}) %collective-permute-start.2) | collective-permute-done | bytes 557088 | tf_op jit(solution)/shard_map/ppermute | solution.py:311
  128.2 1.5 collective-permute-start.26
  130.3 1.3 collective-permute-start.29
  131.5 1.9 collective-permute-start.4
  133.5 7.6 %shard_map.105 = (bf16[1024,768]{1,0:T(8,128)(2,1)S(1)}, f32[1024,768]{1,0:T(8,128)S(1)}, f32[1024,768]{1,0:T(8,128)S(1)}, bf16[2048,768]{1,0:T(8,128)(2,1)S(1)}, bf16[2048,768]{1,0:T(8,128)(2,1)S(1)}) custom-call(s32[3]{0:T(128)S(1)} %pad_add_fusion.place, ...), custom_call_target="tpu_custom_call", output_to_operand_aliasing={{3}: (4, {}), {4}: (5, {})} | custom-call | flops 4831838208 | bytes 25165824 | tf_op jit(solution)/shard_map/pallas_call | solution.py:31
  141.1 4.0 %shard_map.106 = (bf16[1024,768]{1,0:T(8,128)(2,1)S(1)}, f32[1024,768]{1,0:T(8,128)S(1)}, f32[1024,768]{1,0:T(8,128)S(1)}, bf16[1024,2048]{1,0:T(8,128)(2,1)S(1)}) custom-call(s32[3]{0:T(128)S(1)} %pad_add_fusion.place, bf16[128,2048]{1,0:T(8,128)(2,1)S(1)} %copy-done.18, ...), custom_call_target="tpu_custom_call", output_to_operand_aliasing={{0}: (7, {}), {1}: (8, {}), {2}: (9, {}), {3}: (10, {})} | custom-call | flops 1610612736 | bytes 10747904 | tf_op jit(solution)/shard_map/pallas_call | solution.py:31
  145.2 3.8 %shard_map.108 = (bf16[2,384,512]{2,1,0:T(8,128)(2,1)S(1)}, bf16[2,384,512]{2,1,0:T(8,128)(2,1)S(1)}, bf16[1024,2048]{1,0:T(8,128)(2,1)S(1)}) custom-call(s32[3]{0:T(128)S(1)} %pad_add_fusion.place, bf16[128,2176]{1,0:T(8,128)(2,1)S(1)} %collective-permute-done.refs_0_, ...), custom_call_target="tpu_custom_call", output_to_operand_aliasing={{2}: (6, {})} | custom-call | flops 1610612736 | bytes 11534336 | tf_op jit(solution)/shard_map/pallas_call | solution.py:31
  149.0 0.8 collective-permute-start.39
  149.9 6.3 %shard_map.109 = (bf16[1024,768]{1,0:T(8,128)(2,1)S(1)}, bf16[1024,768]{1,0:T(8,128)(2,1)S(1)}) custom-call(s32[3]{0:T(128)S(1)} %pad_add_fusion.place, bf16[1024,2048]{1,0:T(8,128)(2,1)S(1)} %get-tuple-element.50.y, f32[1024,768]{1,0:T(8,128)S(1)} %get-tuple-element.51.active, f32[1024,768]{1,0:T(8,128)S(1)} %get-tuple-element.52.slope, ...), custom_call_target="tpu_custom_call" | custom-call | flops 3221225472 | bytes 16777216 | tf_op jit(solution)/shard_map/pallas_call | solution.py:31
  156.2 8.1 %shard_map.110 = (bf16[512,2048]{1,0:T(8,128)(2,1)S(1)}, bf16[512,2048]{1,0:T(8,128)(2,1)S(1)}) custom-call(bf16[1024,768]{1,0:T(8,128)(2,1)S(1)} %get-tuple-element.53.gate_delta.gd, bf16[1024,768]{1,0:T(8,128)(2,1)S(1)} %get-tuple-element.54.up_delta.ud, bf16[2048,768]{1,0:T(8,128)(2,1)S(1)} %get-tuple-element.44.refs_4_.wg, ...), custom_call_target="tpu_custom_call" | custom-call | flops 6442450944 | bytes 13631488 | tf_op jit(solution)/shard_map/pallas_call | solution.py:31
  164.6 1.5 collective-permute-start.41
  166.1 2.4 shard_map.113
  168.5 5.3 %shard_map.112 = (bf16[2,512,768]{2,1,0:T(8,128)(2,1)S(1)}, bf16[2,512,768]{2,1,0:T(8,128)(2,1)S(1)}) custom-call(s32[3]{0:T(128)S(1)} %pad_add_fusion.place, bf16[1024,2048]{1,0:T(8,128)(2,1)S(1)} %get-tuple-element.57.x, bf16[1024,768]{1,0:T(8,128)(2,1)S(1)} %get-tuple-element.53.gate_delta.gd, bf16[1024,768]{1,0:T(8,128)(2,1)S(1)} %get-tuple-element.54.up_delta.ud), custom_call_target="tpu_custom_call" | custom-call | flops 3221225472 | bytes 10485760 | tf_op jit(solution)/shard_map/pallas_call | solution.py:31
  174.4 10.6 %collective-permute-done.41 = bf16[2,384,512]{2,1,0:T(8,128)(2,1)S(1)} collective-permute-done((bf16[2,384,512]{2,1,0:T(8,128)(2,1)S(1)}, bf16[2,384,512]{2,1,0:T(8,128)(2,1)S(1)}, u32[]{:S(2)}, u32[]{:S(2)}) %collective-permute-start.41) | collective-permute-done | bytes 786464 | tf_op jit(solution)/shard_map/ppermute | solution.py:308
  185.1 1.3 collective-permute-start.42
  186.4 5.2 %shard_map.111 = (bf16[512,768]{1,0:T(8,128)(2,1)S(1)}, bf16[512,768]{1,0:T(8,128)(2,1)S(1)}, bf16[512,768]{1,0:T(8,128)(2,1)S(1)}, bf16[512,768]{1,0:T(8,128)(2,1)S(1)}) custom-call(s32[3]{0:T(128)S(1)} %pad_add_fusion.place, bf16[1024,2048]{1,0:T(8,128)(2,1)S(1)} %get-tuple-element.57.x, bf16[1024,768]{1,0:T(8,128)(2,1)S(1)} %get-tuple-element.53.gate_delta.gd, ...), custom_call_target="tpu_custom_call" | custom-call | flops 3221225472 | bytes 10485760 | tf_op jit(solution)/shard_map/pallas_call | solution.py:31
  191.7 1.6 collective-permute-start.36
  194.2 1.7 collective-permute-done.42
  196.1 0.9 add_convert_fusion
  197.1 4.8 %collective-permute-start.33 = (bf16[128,2048]{1,0:T(8,128)(2,1)S(1)}, bf16[128,2048]{1,0:T(8,128)(2,1)S(1)}, u32[]{:S(2)}, u32[]{:S(2)}) collective-permute-start(bf16[128,2048]{1,0:T(8,128)(2,1)S(1)} %get-tuple-element.73), channel_id=1, source_target_pairs={{0,2},{1,3},{6,4},{7,5},{8,10},{9,11},{14,12},{15,13},{16,18},{17,... | collective-permute-start | bytes 1572872 | tf_op jit(solution)/shard_map/ppermute | solution.py:311
  201.9 24.7 %collective-permute-done.36 = bf16[2,512,768]{2,1,0:T(8,128)(2,1)S(1)} collective-permute-done((bf16[2,512,768]{2,1,0:T(8,128)(2,1)S(1)}, bf16[2,512,768]{2,1,0:T(8,128)(2,1)S(1)}, u32[]{:S(2)}, u32[]{:S(2)}) %collective-permute-start.36) | collective-permute-done | bytes 1572896 | tf_op jit(solution)/shard_map/ppermute | solution.py:308
  227.0 1.3 collective-permute-start.38
  228.2 1.9 collective-permute-done.35
  230.5 1.7 collective-permute-start.37
  232.2 0.9 maximum_bitcast_fusion
  233.8 6.3 %collective-permute-start.32 = (bf16[128,2048]{1,0:T(8,128)(2,1)S(1)}, bf16[128,2048]{1,0:T(8,128)(2,1)S(1)}, u32[]{:S(2)}, u32[]{:S(2)}) collective-permute-start(bf16[128,2048]{1,0:T(8,128)(2,1)S(1)} %get-tuple-element.72), channel_id=1, source_target_pairs={{0,2},{1,3},{2,0},{3,1},{4,6},{5,7},{6,4},{7,5},{8,10},{9,11},{10,... | collective-permute-start | bytes 1572872 | tf_op jit(solution)/shard_map/ppermute | solution.py:311
  240.3 5.2 %collective-permute-done.38 = bf16[512,768]{1,0:T(8,128)(2,1)S(1)} collective-permute-done((bf16[512,768]{1,0:T(8,128)(2,1)S(1)}, bf16[512,768]{1,0:T(8,128)(2,1)S(1)}, u32[]{:S(2)}, u32[]{:S(2)}) %collective-permute-start.38) | collective-permute-done | bytes 786464 | tf_op jit(solution)/shard_map/ppermute | solution.py:305
  245.5 1.1 fusion.5
  246.8 1.1 fusion.4
  247.9 4.5 %collective-permute-done.32 = bf16[128,2048]{1,0:T(8,128)(2,1)S(1)} collective-permute-done((bf16[128,2048]{1,0:T(8,128)(2,1)S(1)}, bf16[128,2048]{1,0:T(8,128)(2,1)S(1)}, u32[]{:S(2)}, u32[]{:S(2)}) %collective-permute-start.32) | collective-permute-done | bytes 524320 | tf_op jit(solution)/shard_map/ppermute | solution.py:311
  252.4 18.8 %collective-permute-done.34 = bf16[128,2048]{1,0:T(8,128)(2,1)S(1)} collective-permute-done((bf16[128,2048]{1,0:T(8,128)(2,1)S(1)}, bf16[128,2048]{1,0:T(8,128)(2,1)S(1)}, u32[]{:S(2)}, u32[]{:S(2)}) %collective-permute-start.34) | collective-permute-done | bytes 524320 | tf_op jit(solution)/shard_map/ppermute | solution.py:311
  271.2 1.1 add_convert_fusion.3
  (133 shorter events, 16.7 us)
Async XLA Ops:
  0.6 6.0 %copy-start.15 = (bf16[128,2048]{1,0:T(8,128)(2,1)S(1)}, bf16[128,2048]{1,0:T(8,128)(2,1)}, u32[]{:S(2)}) copy-start(bf16[128,2048]{1,0:T(8,128)(2,1)} %tokens.1) | copy-start | bytes 1572868
  0.6 10.1 %copy-start.36 = (s32[128,4]{0,1:T(4,128)S(1)}, s32[128,4]{0,1:T(4,128)}, u32[]{:S(2)}) copy-start(s32[128,4]{0,1:T(4,128)} %param.9) | copy-start | bytes 6148
  0.7 10.1 %copy-start.37 = (f32[128,4]{0,1:T(4,128)S(1)}, f32[128,4]{0,1:T(4,128)}, u32[]{:S(2)}) copy-start(f32[128,4]{0,1:T(4,128)} %param.10) | copy-start | bytes 6148
  0.7 10.1 %copy-start.31 = (bf16[128,2048]{1,0:T(8,128)(2,1)S(1)}, bf16[128,2048]{1,0:T(8,128)(2,1)}, u32[]{:S(2)}) copy-start(bf16[128,2048]{1,0:T(8,128)(2,1)} %rows.1) | copy-start | bytes 1572868
  0.7 35.5 %copy-start.3 = (bf16[1,512,768]{2,1,0:T(8,128)(2,1)S(1)}, bf16[1,512,768]{2,1,0:T(8,128)(2,1)}, u32[]{:S(2)}) copy-start(bf16[1,512,768]{2,1,0:T(8,128)(2,1)} %param.11) | copy-start | bytes 2359300
  0.7 56.3 %copy-start.5 = (bf16[1,512,768]{2,1,0:T(8,128)(2,1)S(1)}, bf16[1,512,768]{2,1,0:T(8,128)(2,1)}, u32[]{:S(2)}) copy-start(bf16[1,512,768]{2,1,0:T(8,128)(2,1)} %param.12) | copy-start | bytes 2359300
  2.0 109.6 %copy-start.38 = (bf16[384,512]{1,0:T(8,128)(2,1)}, bf16[384,512]{1,0:T(8,128)(2,1)S(1)}, u32[]{:S(2)}) copy-start(bf16[384,512]{1,0:T(8,128)(2,1)S(1)} %get-tuple-element.79) | copy-start | bytes 1179652
  2.0 109.6 %copy-start.40 = (bf16[384,512]{1,0:T(8,128)(2,1)}, bf16[384,512]{1,0:T(8,128)(2,1)S(1)}, u32[]{:S(2)}) copy-start(bf16[384,512]{1,0:T(8,128)(2,1)S(1)} %get-tuple-element.78) | copy-start | bytes 1179652
  2.0 12.1 %collective-permute-start.24 = (bf16[384,512]{1,0:T(8,128)(2,1)S(1)}, bf16[384,512]{1,0:T(8,128)(2,1)S(1)}, u32[]{:S(2)}, u32[]{:S(2)}) collective-permute-start(bf16[384,512]{1,0:T(8,128)(2,1)S(1)} %get-tuple-element.79), channel_id=1, source_target_pairs={{0,8},{8,0},{16,24},{24,16},{1,9},{9,1},{17,25},{25,17},{2,10},{10... | collective-permute-start | bytes 1179656 | tf_op jit(solution)/shard_map/ppermute | solution.py:305
  5.1 12.0 %collective-permute-start.27 = (bf16[384,512]{1,0:T(8,128)(2,1)S(1)}, bf16[384,512]{1,0:T(8,128)(2,1)S(1)}, u32[]{:S(2)}, u32[]{:S(2)}) collective-permute-start(bf16[384,512]{1,0:T(8,128)(2,1)S(1)} %get-tuple-element.78), channel_id=1, source_target_pairs={{0,16},{8,24},{16,0},{24,8},{1,17},{9,25},{17,1},{25,9},{2,18},{10... | collective-permute-start | bytes 1179656 | tf_op jit(solution)/shard_map/ppermute | solution.py:308
  6.6 28.1 %collective-permute-start.6 = (bf16[128,2048]{1,0:T(8,128)(2,1)S(1)}, bf16[128,2048]{1,0:T(8,128)(2,1)S(1)}, u32[]{:S(2)}, u32[]{:S(2)}) collective-permute-start(bf16[128,2048]{1,0:T(8,128)(2,1)S(1)} %copy-done.15), channel_id=1, source_target_pairs={{0,4},{1,5},{2,6},{3,7},{4,0},{5,1},{6,2},{7,3},{8,12},{9,13},{10,... | collective-permute-start | bytes 1572872 | tf_op jit(solution)/shard_map/ppermute | solution.py:311
  9.2 25.5 %collective-permute-start.14 = (bf16[128,2048]{1,0:T(8,128)(2,1)S(1)}, bf16[128,2048]{1,0:T(8,128)(2,1)S(1)}, u32[]{:S(2)}, u32[]{:S(2)}) collective-permute-start(bf16[128,2048]{1,0:T(8,128)(2,1)S(1)} %copy-done.15), channel_id=1, source_target_pairs={{0,2},{1,3},{2,0},{3,1},{4,6},{5,7},{6,4},{7,5},{8,10},{9,11},{10,... | collective-permute-start | bytes 1572872 | tf_op jit(solution)/shard_map/ppermute | solution.py:311
  10.8 23.9 %collective-permute-start.15 = (bf16[128,2048]{1,0:T(8,128)(2,1)S(1)}, bf16[128,2048]{1,0:T(8,128)(2,1)S(1)}, u32[]{:S(2)}, u32[]{:S(2)}) collective-permute-start(bf16[128,2048]{1,0:T(8,128)(2,1)S(1)} %copy-done.15), channel_id=1, source_target_pairs={{0,1},{1,0},{2,3},{3,2},{4,5},{5,4},{6,7},{7,6},{8,9},{9,8},{10,11... | collective-permute-start | bytes 1572872 | tf_op jit(solution)/shard_map/ppermute | solution.py:314
  14.2 94.7 %copy-start.32 = (bf16[384,512]{1,0:T(8,128)(2,1)}, bf16[384,512]{1,0:T(8,128)(2,1)S(1)}, u32[]{:S(2)}) copy-start(bf16[384,512]{1,0:T(8,128)(2,1)S(1)} %collective-permute-done.24.refs_1_) | copy-start | bytes 1179652
  14.2 42.8 %collective-permute-start.1 = (bf16[128,2176]{1,0:T(8,128)(2,1)S(1)}, bf16[128,2176]{1,0:T(8,128)(2,1)}, u32[]{:S(2)}, u32[]{:S(2)}) collective-permute-start(bf16[128,2176]{1,0:T(8,128)(2,1)S(1)} %shard_map.102.refs_0_), channel_id=1, source_target_pairs={{0,4},{1,5},{2,6},{3,7},{4,0},{5,1},{6,2},{7,3},{8,12},{9,13},{10,... | collective-permute-start | bytes 1671176 | tf_op jit(solution)/shard_map/ppermute | solution.py:311
  17.0 94.6 %copy-start.34 = (bf16[384,512]{1,0:T(8,128)(2,1)}, bf16[384,512]{1,0:T(8,128)(2,1)S(1)}, u32[]{:S(2)}) copy-start(bf16[384,512]{1,0:T(8,128)(2,1)S(1)} %collective-permute-done.27.refs_4_) | copy-start | bytes 1179652
  17.0 19.1 %collective-permute-start.5 = (bf16[128,2048]{1,0:T(8,128)(2,1)S(1)}, bf16[128,2048]{1,0:T(8,128)(2,1)S(1)}, u32[]{:S(2)}, u32[]{:S(2)}) collective-permute-start(bf16[128,2048]{1,0:T(8,128)(2,1)S(1)} %copy-done.15), channel_id=1, source_target_pairs={{2,4},{3,5},{4,2},{5,3},{10,12},{11,13},{12,10},{13,11},{18,20},{1... | collective-permute-start | bytes 1572872 | tf_op jit(solution)/shard_map/ppermute | solution.py:311
  34.6 22.9 %collective-permute-start.20 = (bf16[128,2176]{1,0:T(8,128)(2,1)S(1)}, bf16[128,2176]{1,0:T(8,128)(2,1)S(1)}, u32[]{:S(2)}, u32[]{:S(2)}) collective-permute-start(bf16[128,2176]{1,0:T(8,128)(2,1)S(1)} %shard_map.102.refs_0_), channel_id=1, source_target_pairs={{0,2},{1,3},{2,0},{3,1},{4,6},{5,7},{6,4},{7,5},{8,10},{9,11},{10,... | collective-permute-start | bytes 1671176 | tf_op jit(solution)/shard_map/ppermute | solution.py:311
  34.7 23.4 %collective-permute-start.21 = (bf16[128,2176]{1,0:T(8,128)(2,1)S(1)}, bf16[128,2176]{1,0:T(8,128)(2,1)S(1)}, u32[]{:S(2)}, u32[]{:S(2)}) collective-permute-start(bf16[128,2176]{1,0:T(8,128)(2,1)S(1)} %shard_map.102.refs_0_), channel_id=1, source_target_pairs={{0,1},{1,0},{2,3},{3,2},{4,5},{5,4},{6,7},{7,6},{8,9},{9,8},{10,11... | collective-permute-start | bytes 1671176 | tf_op jit(solution)/shard_map/ppermute | solution.py:314
  35.5 24.9 %collective-permute-start = (bf16[128,2176]{1,0:T(8,128)(2,1)S(1)}, bf16[128,2176]{1,0:T(8,128)(2,1)S(1)}, u32[]{:S(2)}, u32[]{:S(2)}) collective-permute-start(bf16[128,2176]{1,0:T(8,128)(2,1)S(1)} %shard_map.102.refs_0_), channel_id=1, source_target_pairs={{2,4},{3,5},{4,2},{5,3},{10,12},{11,13},{12,10},{13,11},{18,20},{1... | collective-permute-start | bytes 1671176 | tf_op jit(solution)/shard_map/ppermute | solution.py:311
  36.2 24.2 %collective-permute-start.10 = (bf16[512,768]{1,0:T(8,128)(2,1)S(1)}, bf16[512,768]{1,0:T(8,128)(2,1)S(1)}, u32[]{:S(2)}, u32[]{:S(2)}) collective-permute-start(bf16[512,768]{1,0:T(8,128)(2,1)S(1)} %bitcast.59), channel_id=1, source_target_pairs={{0,8},{8,0},{16,24},{24,16},{1,9},{9,1},{17,25},{25,17},{2,10},{10... | collective-permute-start | bytes 2359304 | tf_op jit(solution)/shard_map/ppermute | solution.py:305
  57.0 20.4 %collective-permute-start.12 = (bf16[512,768]{1,0:T(8,128)(2,1)S(1)}, bf16[512,768]{1,0:T(8,128)(2,1)S(1)}, u32[]{:S(2)}, u32[]{:S(2)}) collective-permute-start(bf16[512,768]{1,0:T(8,128)(2,1)S(1)} %bitcast.62), channel_id=1, source_target_pairs={{0,16},{8,24},{16,0},{24,8},{1,17},{9,25},{17,1},{25,9},{2,18},{10... | collective-permute-start | bytes 2359304 | tf_op jit(solution)/shard_map/ppermute | solution.py:308
  57.5 22.0 %collective-permute-start.18 = (bf16[512,768]{1,0:T(8,128)(2,1)S(1)}, bf16[512,768]{1,0:T(8,128)(2,1)S(1)}, u32[]{:S(2)}, u32[]{:S(2)}) collective-permute-start(bf16[512,768]{1,0:T(8,128)(2,1)S(1)} %bitcast.63), channel_id=1, source_target_pairs={{0,8},{8,0},{16,24},{24,16},{1,9},{9,1},{17,25},{25,17},{2,10},{10... | collective-permute-start | bytes 2359304 | tf_op jit(solution)/shard_map/ppermute | solution.py:305
  58.9 32.3 %collective-permute-start.19 = (bf16[512,768]{1,0:T(8,128)(2,1)S(1)}, bf16[512,768]{1,0:T(8,128)(2,1)S(1)}, u32[]{:S(2)}, u32[]{:S(2)}) collective-permute-start(bf16[512,768]{1,0:T(8,128)(2,1)S(1)} %bitcast.60), channel_id=1, source_target_pairs={{0,16},{8,24},{16,0},{24,8},{1,17},{9,25},{17,1},{25,9},{2,18},{10... | collective-permute-start | bytes 2359304 | tf_op jit(solution)/shard_map/ppermute | solution.py:308
  60.4 33.2 %collective-permute-start.16 = (bf16[128,2048]{1,0:T(8,128)(2,1)S(1)}, bf16[128,2048]{1,0:T(8,128)(2,1)S(1)}, u32[]{:S(2)}, u32[]{:S(2)}) collective-permute-start(bf16[128,2048]{1,0:T(8,128)(2,1)S(1)} %collective-permute-done.6.refs_0_), channel_id=1, source_target_pairs={{0,1},{1,0},{2,3},{3,2},{4,5},{5,4},{6,7},{7,6},{8,9},{9,8},{10,11... | collective-permute-start | bytes 1572872 | tf_op jit(solution)/shard_map/ppermute | solution.py:314
  60.4 34.8 %collective-permute-start.17 = (bf16[128,2048]{1,0:T(8,128)(2,1)S(1)}, bf16[128,2048]{1,0:T(8,128)(2,1)S(1)}, u32[]{:S(2)}, u32[]{:S(2)}) collective-permute-start(bf16[128,2048]{1,0:T(8,128)(2,1)S(1)} %collective-permute-done.14.refs_1_), channel_id=1, source_target_pairs={{0,1},{1,0},{2,3},{3,2},{4,5},{5,4},{6,7},{7,6},{8,9},{9,8},{10,11... | collective-permute-start | bytes 1572872 | tf_op jit(solution)/shard_map/ppermute | solution.py:314
  77.4 26.5 %collective-permute-start.7 = (bf16[128,2048]{1,0:T(8,128)(2,1)S(1)}, bf16[128,2048]{1,0:T(8,128)(2,1)}, u32[]{:S(2)}, u32[]{:S(2)}) collective-permute-start(bf16[128,2048]{1,0:T(8,128)(2,1)S(1)} %collective-permute-done.6.refs_0_), channel_id=1, source_target_pairs={{4,6},{5,7},{2,0},{3,1},{12,14},{13,15},{10,8},{11,9},{20,22},{21,... | collective-permute-start | bytes 1572872 | tf_op jit(solution)/shard_map/ppermute | solution.py:311
  79.5 27.0 %collective-permute-start.22 = (bf16[128,2176]{1,0:T(8,128)(2,1)}, bf16[128,2176]{1,0:T(8,128)(2,1)S(1)}, u32[]{:S(2)}, u32[]{:S(2)}) collective-permute-start(bf16[128,2176]{1,0:T(8,128)(2,1)} %collective-permute-done.1.refs_1_), channel_id=1, source_target_pairs={{0,1},{1,0},{2,3},{3,2},{4,5},{5,4},{6,7},{7,6},{8,9},{9,8},{10,11... | collective-permute-start | bytes 1671176 | tf_op jit(solution)/shard_map/ppermute | solution.py:314
  92.1 12.4 %collective-permute-start.8 = (bf16[128,2048]{1,0:T(8,128)(2,1)S(1)}, bf16[128,2048]{1,0:T(8,128)(2,1)S(1)}, u32[]{:S(2)}, u32[]{:S(2)}) collective-permute-start(bf16[128,2048]{1,0:T(8,128)(2,1)S(1)} %collective-permute-done.5.refs_0_), channel_id=1, source_target_pairs={{2,3},{3,2},{4,5},{5,4},{10,11},{11,10},{12,13},{13,12},{18,19},{1... | collective-permute-start | bytes 1572872 | tf_op jit(solution)/shard_map/ppermute | solution.py:314
  94.4 14.5 %collective-permute-start.23 = (bf16[128,2176]{1,0:T(8,128)(2,1)S(1)}, bf16[128,2176]{1,0:T(8,128)(2,1)S(1)}, u32[]{:S(2)}, u32[]{:S(2)}) collective-permute-start(bf16[128,2176]{1,0:T(8,128)(2,1)S(1)} %collective-permute-done.20.refs_2_), channel_id=1, source_target_pairs={{0,1},{1,0},{2,3},{3,2},{4,5},{5,4},{6,7},{7,6},{8,9},{9,8},{10,11... | collective-permute-start | bytes 1671176 | tf_op jit(solution)/shard_map/ppermute | solution.py:314
  96.0 34.2 %collective-permute-start.11 = (bf16[512,768]{1,0:T(8,128)(2,1)S(1)}, bf16[512,768]{1,0:T(8,128)(2,1)}, u32[]{:S(2)}, u32[]{:S(2)}) collective-permute-start(bf16[512,768]{1,0:T(8,128)(2,1)S(1)} %collective-permute-done.10.refs_5_), channel_id=1, source_target_pairs={{0,16},{8,24},{16,0},{24,8},{1,17},{9,25},{17,1},{25,9},{2,18},{10... | collective-permute-start | bytes 2359304 | tf_op jit(solution)/shard_map/ppermute | solution.py:308
  103.9 27.6 %collective-permute-start.13 = (bf16[512,768]{1,0:T(8,128)(2,1)S(1)}, bf16[512,768]{1,0:T(8,128)(2,1)}, u32[]{:S(2)}, u32[]{:S(2)}) collective-permute-start(bf16[512,768]{1,0:T(8,128)(2,1)S(1)} %collective-permute-done.12.refs_8_), channel_id=1, source_target_pairs={{0,8},{8,0},{16,24},{24,16},{1,9},{9,1},{17,25},{25,17},{2,10},{10... | collective-permute-start | bytes 2359304 | tf_op jit(solution)/shard_map/ppermute | solution.py:305
  105.3 22.1 %collective-permute-start.2 = (bf16[128,2176]{1,0:T(8,128)(2,1)}, bf16[128,2176]{1,0:T(8,128)(2,1)}, u32[]{:S(2)}, u32[]{:S(2)}) collective-permute-start(bf16[128,2176]{1,0:T(8,128)(2,1)} %collective-permute-done.1.refs_1_), channel_id=1, source_target_pairs={{4,6},{5,7},{2,0},{3,1},{12,14},{13,15},{10,8},{11,9},{20,22},{21,... | collective-permute-start | bytes 1671176 | tf_op jit(solution)/shard_map/ppermute | solution.py:311
  107.4 20.8 %collective-permute-start.3 = (bf16[128,2176]{1,0:T(8,128)(2,1)S(1)}, bf16[128,2176]{1,0:T(8,128)(2,1)}, u32[]{:S(2)}, u32[]{:S(2)}) collective-permute-start(bf16[128,2176]{1,0:T(8,128)(2,1)S(1)} %collective-permute-done.refs_0_), channel_id=1, source_target_pairs={{2,3},{3,2},{4,5},{5,4},{10,11},{11,10},{12,13},{13,12},{18,19},{1... | collective-permute-start | bytes 1671176 | tf_op jit(solution)/shard_map/ppermute | solution.py:314
  109.7 20.0 %collective-permute-start.9 = (bf16[128,2048]{1,0:T(8,128)(2,1)}, bf16[128,2048]{1,0:T(8,128)(2,1)}, u32[]{:S(2)}, u32[]{:S(2)}) collective-permute-start(bf16[128,2048]{1,0:T(8,128)(2,1)} %collective-permute-done.7.refs_1_), channel_id=1, source_target_pairs={{0,1},{1,0},{6,7},{7,6},{8,9},{9,8},{14,15},{15,14},{16,17},{17,16... | collective-permute-start | bytes 1572872 | tf_op jit(solution)/shard_map/ppermute | solution.py:314
  111.7 4.2 %copy-start.2 = (bf16[512,768]{1,0:T(8,128)(2,1)S(1)}, bf16[512,768]{1,0:T(8,128)(2,1)}, u32[]{:S(2)}) copy-start(bf16[512,768]{1,0:T(8,128)(2,1)} %copy-done.1) | copy-start | bytes 2359300
  119.5 1.2 copy-start.10
  119.5 1.4 copy-start.12
  119.5 1.6 copy-start.14
  121.0 6.4 %copy-start.41 = (bf16[384,512]{1,0:T(8,128)(2,1)S(1)}, bf16[384,512]{1,0:T(8,128)(2,1)}, u32[]{:S(2)}) copy-start(bf16[384,512]{1,0:T(8,128)(2,1)} %copy-done.40) | copy-start | bytes 1179652
  121.0 7.2 %copy-start.39 = (bf16[384,512]{1,0:T(8,128)(2,1)S(1)}, bf16[384,512]{1,0:T(8,128)(2,1)}, u32[]{:S(2)}) copy-start(bf16[384,512]{1,0:T(8,128)(2,1)} %copy-done.38) | copy-start | bytes 1179652
  121.0 8.7 %copy-start.33 = (bf16[384,512]{1,0:T(8,128)(2,1)S(1)}, bf16[384,512]{1,0:T(8,128)(2,1)}, u32[]{:S(2)}) copy-start(bf16[384,512]{1,0:T(8,128)(2,1)} %copy-done.32) | copy-start | bytes 1179652
  121.0 9.2 %copy-start.35 = (bf16[384,512]{1,0:T(8,128)(2,1)S(1)}, bf16[384,512]{1,0:T(8,128)(2,1)}, u32[]{:S(2)}) copy-start(bf16[384,512]{1,0:T(8,128)(2,1)} %copy-done.34) | copy-start | bytes 1179652
  127.4 22.4 %collective-permute-start.25 = (bf16[384,512]{1,0:T(8,128)(2,1)S(1)}, bf16[384,512]{1,0:T(8,128)(2,1)S(1)}, u32[]{:S(2)}, u32[]{:S(2)}) collective-permute-start(bf16[384,512]{1,0:T(8,128)(2,1)S(1)} %copy-done.41), channel_id=1, source_target_pairs={{0,8},{8,0},{16,24},{24,16},{1,9},{9,1},{17,25},{25,17},{2,10},{10... | collective-permute-start | bytes 1179656 | tf_op jit(solution)/shard_map/ppermute | solution.py:305
  128.2 21.6 %collective-permute-start.26 = (bf16[384,512]{1,0:T(8,128)(2,1)S(1)}, bf16[384,512]{1,0:T(8,128)(2,1)S(1)}, u32[]{:S(2)}, u32[]{:S(2)}) collective-permute-start(bf16[384,512]{1,0:T(8,128)(2,1)S(1)} %copy-done.39), channel_id=1, source_target_pairs={{0,16},{8,24},{16,0},{24,8},{1,17},{9,25},{17,1},{25,9},{2,18},{10... | collective-permute-start | bytes 1179656 | tf_op jit(solution)/shard_map/ppermute | solution.py:308
  129.7 20.1 %collective-permute-start.28 = (bf16[384,512]{1,0:T(8,128)(2,1)S(1)}, bf16[384,512]{1,0:T(8,128)(2,1)S(1)}, u32[]{:S(2)}, u32[]{:S(2)}) collective-permute-start(bf16[384,512]{1,0:T(8,128)(2,1)S(1)} %copy-done.33), channel_id=1, source_target_pairs={{0,16},{8,24},{16,0},{24,8},{1,17},{9,25},{17,1},{25,9},{2,18},{10... | collective-permute-start | bytes 1179656 | tf_op jit(solution)/shard_map/ppermute | solution.py:308
  130.3 19.6 %collective-permute-start.29 = (bf16[384,512]{1,0:T(8,128)(2,1)S(1)}, bf16[384,512]{1,0:T(8,128)(2,1)S(1)}, u32[]{:S(2)}, u32[]{:S(2)}) collective-permute-start(bf16[384,512]{1,0:T(8,128)(2,1)S(1)} %copy-done.35), channel_id=1, source_target_pairs={{0,8},{8,0},{16,24},{24,16},{1,9},{9,1},{17,25},{25,17},{2,10},{10... | collective-permute-start | bytes 1179656 | tf_op jit(solution)/shard_map/ppermute | solution.py:305
  131.5 13.6 %collective-permute-start.4 = (bf16[128,2176]{1,0:T(8,128)(2,1)}, bf16[128,2176]{1,0:T(8,128)(2,1)S(1)}, u32[]{:S(2)}, u32[]{:S(2)}) collective-permute-start(bf16[128,2176]{1,0:T(8,128)(2,1)} %collective-permute-done.2.refs_1_), channel_id=1, source_target_pairs={{0,1},{1,0},{6,7},{7,6},{8,9},{9,8},{14,15},{15,14},{16,17},{17,16... | collective-permute-start | bytes 1671176 | tf_op jit(solution)/shard_map/ppermute | solution.py:314
  133.4 7.7 %copy-start.18 = (bf16[128,2048]{1,0:T(8,128)(2,1)S(1)}, bf16[128,2048]{1,0:T(8,128)(2,1)}, u32[]{:S(2)}) copy-start(bf16[128,2048]{1,0:T(8,128)(2,1)} %copy-done.17) | copy-start | bytes 1572868
  133.4 7.7 %copy-start.26 = (bf16[128,2048]{1,0:T(8,128)(2,1)S(1)}, bf16[128,2048]{1,0:T(8,128)(2,1)}, u32[]{:S(2)}) copy-start(bf16[128,2048]{1,0:T(8,128)(2,1)} %copy-done.25) | copy-start | bytes 1572868
  145.2 4.7 %copy-start = (bf16[1,768,512]{2,1,0:T(8,128)(2,1)S(1)}, bf16[1,768,512]{2,1,0:T(8,128)(2,1)}, u32[]{:S(2)}) copy-start(bf16[1,768,512]{2,1,0:T(8,128)(2,1)} %param.13) | copy-start | bytes 2359300
  149.0 24.7 %collective-permute-start.39 = (bf16[2,384,512]{2,1,0:T(8,128)(2,1)S(1)}, bf16[2,384,512]{2,1,0:T(8,128)(2,1)S(1)}, u32[]{:S(2)}, u32[]{:S(2)}) collective-permute-start(bf16[2,384,512]{2,1,0:T(8,128)(2,1)S(1)} %get-tuple-element.67), channel_id=1, source_target_pairs={{0,8},{8,0},{16,24},{24,16},{1,9},{9,1},{17,25},{25,17},{2,10},{10... | collective-permute-start | bytes 2359304 | tf_op jit(solution)/shard_map/ppermute | solution.py:305
  164.3 31.7 %collective-permute-start.30 = (bf16[512,2048]{1,0:T(8,128)(2,1)S(1)}, bf16[512,2048]{1,0:T(8,128)(2,1)S(1)}, u32[]{:S(2)}, u32[]{:S(2)}) collective-permute-start(bf16[512,2048]{1,0:T(8,128)(2,1)S(1)} %get-tuple-element.56), channel_id=1, source_target_pairs={{0,1},{1,0},{2,3},{3,2},{4,5},{5,4},{6,7},{7,6},{8,9},{9,8},{10,11... | collective-permute-start | bytes 6291464 | tf_op jit(solution)/shard_map/ppermute | solution.py:314
  164.6 20.4 %collective-permute-start.41 = (bf16[2,384,512]{2,1,0:T(8,128)(2,1)S(1)}, bf16[2,384,512]{2,1,0:T(8,128)(2,1)S(1)}, u32[]{:S(2)}, u32[]{:S(2)}) collective-permute-start(bf16[2,384,512]{2,1,0:T(8,128)(2,1)S(1)} %get-tuple-element.70), channel_id=1, source_target_pairs={{0,16},{8,24},{16,0},{24,8},{1,17},{9,25},{17,1},{25,9},{2,18},{10... | collective-permute-start | bytes 2359304 | tf_op jit(solution)/shard_map/ppermute | solution.py:308
  173.9 20.2 %collective-permute-start.40 = (bf16[384,512]{1,0:T(8,128)(2,1)S(1)}, bf16[384,512]{1,0:T(8,128)(2,1)S(1)}, u32[]{:S(2)}, u32[]{:S(2)}) collective-permute-start(bf16[384,512]{1,0:T(8,128)(2,1)S(1)} %fusion.9), channel_id=1, source_target_pairs={{0,16},{8,24},{16,0},{24,8},{1,17},{9,25},{17,1},{25,9},{2,18},{10... | collective-permute-start | bytes 1179656 | tf_op jit(solution)/shard_map/ppermute | solution.py:308
  185.1 10.8 %collective-permute-start.42 = (bf16[384,512]{1,0:T(8,128)(2,1)S(1)}, bf16[384,512]{1,0:T(8,128)(2,1)S(1)}, u32[]{:S(2)}, u32[]{:S(2)}) collective-permute-start(bf16[384,512]{1,0:T(8,128)(2,1)S(1)} %fusion.6), channel_id=1, source_target_pairs={{0,8},{8,0},{16,24},{24,16},{1,9},{9,1},{17,25},{25,17},{2,10},{10... | collective-permute-start | bytes 1179656 | tf_op jit(solution)/shard_map/ppermute | solution.py:305
  191.7 34.9 %collective-permute-start.36 = (bf16[2,512,768]{2,1,0:T(8,128)(2,1)S(1)}, bf16[2,512,768]{2,1,0:T(8,128)(2,1)S(1)}, u32[]{:S(2)}, u32[]{:S(2)}) collective-permute-start(bf16[2,512,768]{2,1,0:T(8,128)(2,1)S(1)} %get-tuple-element.61), channel_id=1, source_target_pairs={{0,16},{8,24},{16,0},{24,8},{1,17},{9,25},{17,1},{25,9},{2,18},{10... | collective-permute-start | bytes 4718600 | tf_op jit(solution)/shard_map/ppermute | solution.py:308
  193.3 36.8 %collective-permute-start.35 = (bf16[2,512,768]{2,1,0:T(8,128)(2,1)S(1)}, bf16[2,512,768]{2,1,0:T(8,128)(2,1)S(1)}, u32[]{:S(2)}, u32[]{:S(2)}) collective-permute-start(bf16[2,512,768]{2,1,0:T(8,128)(2,1)S(1)} %get-tuple-element.59), channel_id=1, source_target_pairs={{0,8},{8,0},{16,24},{24,16},{1,9},{9,1},{17,25},{25,17},{2,10},{10... | collective-permute-start | bytes 4718600 | tf_op jit(solution)/shard_map/ppermute | solution.py:305
  197.1 43.0 %collective-permute-start.33 = (bf16[128,2048]{1,0:T(8,128)(2,1)S(1)}, bf16[128,2048]{1,0:T(8,128)(2,1)S(1)}, u32[]{:S(2)}, u32[]{:S(2)}) collective-permute-start(bf16[128,2048]{1,0:T(8,128)(2,1)S(1)} %get-tuple-element.73), channel_id=1, source_target_pairs={{0,2},{1,3},{6,4},{7,5},{8,10},{9,11},{14,12},{15,13},{16,18},{17,... | collective-permute-start | bytes 1572872 | tf_op jit(solution)/shard_map/ppermute | solution.py:311
  227.0 18.6 %collective-permute-start.38 = (bf16[512,768]{1,0:T(8,128)(2,1)S(1)}, bf16[512,768]{1,0:T(8,128)(2,1)S(1)}, u32[]{:S(2)}, u32[]{:S(2)}) collective-permute-start(bf16[512,768]{1,0:T(8,128)(2,1)S(1)} %get-tuple-element.74), channel_id=1, source_target_pairs={{0,8},{8,0},{16,24},{24,16},{1,9},{9,1},{17,25},{25,17},{2,10},{10... | collective-permute-start | bytes 2359304 | tf_op jit(solution)/shard_map/ppermute | solution.py:305
  230.5 16.3 %collective-permute-start.37 = (bf16[512,768]{1,0:T(8,128)(2,1)S(1)}, bf16[512,768]{1,0:T(8,128)(2,1)S(1)}, u32[]{:S(2)}, u32[]{:S(2)}) collective-permute-start(bf16[512,768]{1,0:T(8,128)(2,1)S(1)} %get-tuple-element.77), channel_id=1, source_target_pairs={{0,16},{8,24},{16,0},{24,8},{1,17},{9,25},{17,1},{25,9},{2,18},{10... | collective-permute-start | bytes 2359304 | tf_op jit(solution)/shard_map/ppermute | solution.py:308
  233.1 14.8 %collective-permute-start.31 = (bf16[128,2048]{1,0:T(8,128)(2,1)S(1)}, bf16[128,2048]{1,0:T(8,128)(2,1)S(1)}, u32[]{:S(2)}, u32[]{:S(2)}) collective-permute-start(bf16[128,2048]{1,0:T(8,128)(2,1)S(1)} %get-tuple-element.73), channel_id=1, source_target_pairs={{2,4},{3,5},{4,2},{5,3},{10,12},{11,13},{12,10},{13,11},{18,20},{1... | collective-permute-start | bytes 1572872 | tf_op jit(solution)/shard_map/ppermute | solution.py:311
  233.8 18.6 %collective-permute-start.32 = (bf16[128,2048]{1,0:T(8,128)(2,1)S(1)}, bf16[128,2048]{1,0:T(8,128)(2,1)S(1)}, u32[]{:S(2)}, u32[]{:S(2)}) collective-permute-start(bf16[128,2048]{1,0:T(8,128)(2,1)S(1)} %get-tuple-element.72), channel_id=1, source_target_pairs={{0,2},{1,3},{2,0},{3,1},{4,6},{5,7},{6,4},{7,5},{8,10},{9,11},{10,... | collective-permute-start | bytes 1572872 | tf_op jit(solution)/shard_map/ppermute | solution.py:311
  240.2 31.0 %collective-permute-start.34 = (bf16[128,2048]{1,0:T(8,128)(2,1)S(1)}, bf16[128,2048]{1,0:T(8,128)(2,1)S(1)}, u32[]{:S(2)}, u32[]{:S(2)}) collective-permute-start(bf16[128,2048]{1,0:T(8,128)(2,1)S(1)} %add_convert_fusion.4), channel_id=1, source_target_pairs={{0,4},{1,5},{2,6},{3,7},{4,0},{5,1},{6,2},{7,3},{8,12},{9,13},{10,... | collective-permute-start | bytes 1572872 | tf_op jit(solution)/shard_map/ppermute | solution.py:311
  (21 other events, 19.7 us)

commit v8 on v7

--- a/solution.py
+++ b/solution.py
@@ -180,32 +180,61 @@
         scale(experts, place[2], raw.at[pl.ds(2 * i * tok, 2 * tok)], y, 2 * i * tok)
 
 
+def down_blocks(place, act, y, first, count, wanted, put):
+    share = y.shape[1] // 4
+    half = act.shape[1] // 2
+    rows = slice(first, first + count)
+    for h in (0, 1):
+        turned = jnp.transpose(act[rows, h * half : (h + 1) * half])
+        for which, k, target in wanted:
+            if which == h:
+                cols = pl.ds(pl.multiple_of((place[0] ^ k) * share, share), share)
+                put(target, mm(turned, y[rows, cols], NN))
+
+
+def down_early_body(place, act, y, part):
+    def put(target, value):
+        part[target] = value
+
+    early = y.shape[0] // 4 * 3
+    down_blocks(place, act, y, 0, early, ((0, 1, 0), (0, 3, 1), (1, 2, 2), (1, 3, 3)), put)
+
+
 def down_send_body(experts, place, *refs):
-    pieces, act = refs[:4], refs[4]
-    send_a, send_b, y, raw, sems = refs[6:]
+    pieces, act, part = refs[:4], refs[4], refs[5]
+    send_a, send_b, y, raw, sems = refs[7:]
     for c in load_late(Copies(sems), place[1], pieces, raw):
         c.wait()
-    scale(experts, place[2], raw, y, y.shape[0] - raw.shape[0])
-    down_blocks(place, act, y, ((0, 1, send_a, 0), (0, 3, send_a, 1), (1, 2, send_b, 0), (1, 3, send_b, 1)))
-
-
-def down_blocks(place, act, y, wanted):
-    share = y.shape[1] // 4
-    half = act.shape[1] // 2
-    for h in (0, 1):
-        turned = jnp.transpose(act[:, h * half : (h + 1) * half])
-        for which, k, dst, slot in wanted:
-            if which == h:
-                cols = pl.ds(pl.multiple_of((place[0] ^ k) * share, share), share)
-                value = mm(turned, y[:, cols], NN).astype(BF16)
-                if slot is None:
-                    dst[...] = value
-                else:
-                    dst[slot] = value
+    count = raw.shape[0]
+    first = y.shape[0] - count
+    scale(experts, place[2], raw, y, first)
+
+    def put(target, value):
+        dst = (send_a, send_b)[target // 2]
+        dst[target % 2] = (part[target] + value).astype(BF16)
+
+    down_blocks(place, act, y, first, count, ((0, 1, 0), (0, 3, 1), (1, 2, 2), (1, 3, 3)), put)
 
 
 def down_keep_body(place, act, y, a0, a1, b0, b1):
-    down_blocks(place, act, y, ((0, 0, a0, None), (0, 2, a1, None), (1, 0, b0, None), (1, 1, b1, None)))
+    def put(target, value):
+        target[...] = value.astype(BF16)
+
+    down_blocks(place, act, y, 0, y.shape[0], ((0, 0, a0), (0, 2, a1), (1, 0, b0), (1, 1, b1)), put)
+
+
+def last_body(gate_sum, gate_last, up_sum, up_last, gate_out, up_out, gate, up, sems):
+    copies = Copies(sems)
+    part = gate.shape[1] // 2
+    started = []
+    for total, last, held, out in ((gate_sum, gate_last, gate, gate_out), (up_sum, up_last, up, up_out)):
+        for i in (0, 1):
+            r = slice(i * part, (i + 1) * part)
+            held[0, r, :] = (total[r, :].astype(F32) + last[r, :].astype(F32)).astype(BF16)
+            at = pl.ds(i * part, part)
+            started.append(copies.start(held.at[0, at], out.at[0, at]))
+    for c in started:
+        c.wait()
 
 
 def back_body(place, y, active, slope, *refs):
@@ -396,14 +425,22 @@
         4 * rows * width,
     )
     piece = (2, half, share)
+    (part,) = call(
+        down_early_body,
+        [((4, half, share), F32, VMEM)],
+        [(place, SMEM), (act, VMEM), (y, VMEM)],
+        [],
+        3 * rows * width * hidden // 4,
+        2 * (rows * width + rows * hidden + width * hidden),
+    )
     send_a, send_b, y = call(
         functools.partial(down_send_body, experts),
         [(piece, BF16, VMEM)] * 2 + [((rows, width), BF16, VMEM)],
-        [(place, SMEM)] + anys(y_late) + [(act, VMEM), (y, VMEM)],
+        [(place, SMEM)] + anys(y_late) + [(act, VMEM), (part, VMEM), (y, VMEM)],
         [pltpu.VMEM((2 * tok, width + LANES), BF16), dma(2)],
-        rows * width * hidden,
-        2 * (2 * rows * width + rows * hidden + width * hidden // 2),
-        {6: 2},
+        rows * width * hidden // 4,
+        2 * (rows * width + rows * hidden // 4 + width * hidden),
+        {7: 2},
     )
     got_a, got_b = to_x(send_a), to_y(send_b)
     gate_delta, up_delta = call(
@@ -454,14 +491,22 @@
     gate_last, up_last = to_y(gate1), to_x(up1)
     gate_sum, up_sum = lax.optimization_barrier(sums)
     down_grad = jnp.concatenate([add(keep_a0, got_a[0], down_a), add(keep_b0, got_b[0], down_b)], axis=0)
-    gate_grad, up_grad = add(gate_sum, gate_last), add(up_sum, up_last)
+    result = (1, share, hidden)
+    gate_grad, up_grad = call(
+        last_body,
+        [(result, BF16, ANY)] * 2,
+        [(a, VMEM) for a in (gate_sum, gate_last, up_sum, up_last)],
+        [pltpu.VMEM(result, BF16)] * 2 + [dma(4)],
+        share * hidden,
+        12 * share * hidden,
+    )
 
     far = hop(total[3], ((0, 1), (3, 2)))
     inner = hop(total[3], INNER)
     outer = hop(total[2], OUTER)
     two = hop(add(total[1], far), TWO)
     input_grad = add(total[0], inner, outer, two)
-    return input_grad, gate_grad[None], up_grad[None], down_grad[None]
+    return input_grad, gate_grad, up_grad, down_grad[None]
 
 
 def routed(tokens, out_grad, routes, gate_values, w_gate, w_up, w_down):

time: 273 us -> 265 us (0.971)
  waiting for transfers between devices: 147 us -> 136 us
    ppermute x12, waiting for transfers between devices: 71.8 us -> 66 us  [hop(): lax.ppermute(block, 'expert', [(2 * a + c, 2 * b + c) for a, b in moves f...]
    ppermute x10, waiting for transfers between devices: 62.8 us -> 57.3 us  [to_y(): return lax.ppermute(block, 'dp', [(i, i ^ 2) for i in range(4)])]
    pallas_call x12 -> x14, Pallas kernels: 47.1 us -> 49.1 us  [call(): pl.pallas_call(body, input_output_aliases=aliases or {}, out_shape=[jax.S...]
  transfers between devices with their start and end apart: 43 -> 43, of which waited for: 15 -> 14; matrix products, arithmetic and copies ran while one was open for 2% -> 1% of each run, Pallas kernels for 17% -> 13%
where the time goes in v8:
time: 265 us; the launch traced here: 264 us
  waiting for transfers between devices  136 us (51%)
  starting transfers between devices  51.6 us (19%)
  Pallas kernels  49.1 us (19%)
  local copies, waits for them, and re-layouts  21.1 us (8%)
  other arithmetic  4.41 us (2%)
    ppermute x12, waiting for transfers between devices, hop(): lax.ppermute(block, 'expert', [(2 * a + c, 2 * b + c) for a, b in moves f...  66 us
    ppermute x10, waiting for transfers between devices, to_y(): return lax.ppermute(block, 'dp', [(i, i ^ 2) for i in range(4)])  57.3 us
    pallas_call x14, Pallas kernels, call(): pl.pallas_call(body, input_output_aliases=aliases or {}, out_shape=[jax.S...  49.1 us
    ppermute x12, starting transfers between devices, hop(): lax.ppermute(block, 'expert', [(2 * a + c, 2 * b + c) for a, b in moves f...  22.2 us
    unnamed x84, local copies, waits for them, and re-layouts  19.7 us
    ppermute x10, waiting for transfers between devices, to_x(): return lax.ppermute(block, 'dp', [(i, i ^ 1) for i in range(4)])  12.9 us
    ppermute x10, starting transfers between devices, to_y(): return lax.ppermute(block, 'dp', [(i, i ^ 2) for i in range(4)])  11.3 us
    ppermute x10, starting transfers between devices, to_x(): return lax.ppermute(block, 'dp', [(i, i ^ 1) for i in range(4)])  10.9 us
  transfers between devices with their start and end apart: 43, of which 14 were waited for; matrix products, arithmetic and copies ran while one was open for 1% of the time, Pallas kernels for 13%

profile of v8, /device:TPU:0, one launch (start us, length us, event | category | flops | bytes accessed | tf_op | source)
XLA Modules:
  0.0 263.7 jit_solution(7162027449905167840)
XLA Ops:
  0.7 1.3 slice_bitcast_fusion.8
  2.0 3.0 %collective-permute-start.24 = (bf16[384,512]{1,0:T(8,128)(2,1)S(1)}, bf16[384,512]{1,0:T(8,128)(2,1)S(1)}, u32[]{:S(2)}, u32[]{:S(2)}) collective-permute-start(bf16[384,512]{1,0:T(8,128)(2,1)S(1)} %get-tuple-element.83), channel_id=1, source_target_pairs={{0,8},{8,0},{16,24},{24,16},{1,9},{9,1},{17,25},{25,17},{2,10},{10... | collective-permute-start | bytes 1179656 | tf_op jit(solution)/shard_map/ppermute | solution.py:334
  5.0 1.5 collective-permute-start.27
  6.6 2.6 collective-permute-start.6
  9.1 1.6 collective-permute-start.14
  10.7 1.0 copy-done.31
  13.2 0.9 collective-permute-done.24.refs_1_
  14.2 2.8 %collective-permute-start.1 = (bf16[128,2176]{1,0:T(8,128)(2,1)S(1)}, bf16[128,2176]{1,0:T(8,128)(2,1)}, u32[]{:S(2)}, u32[]{:S(2)}) collective-permute-start(bf16[128,2176]{1,0:T(8,128)(2,1)S(1)} %shard_map.102.refs_0_), channel_id=1, source_target_pairs={{0,4},{1,5},{2,6},{3,7},{4,0},{5,1},{6,2},{7,3},{8,12},{9,13},{10,... | collective-permute-start | bytes 1671176 | tf_op jit(solution)/shard_map/ppermute | solution.py:340
  17.7 17.1 %collective-permute-done.6.refs_0_ = bf16[128,2048]{1,0:T(8,128)(2,1)S(1)} collective-permute-done((bf16[128,2048]{1,0:T(8,128)(2,1)}, bf16[128,2048]{1,0:T(8,128)(2,1)S(1)}, u32[]{:S(2)}, u32[]{:S(2)}) %collective-permute-start.6) | collective-permute-done | bytes 524320 | tf_op jit(solution)/shard_map/ppermute | solution.py:340
  36.9 20.2 %collective-permute-done.1.refs_1_ = bf16[128,2176]{1,0:T(8,128)(2,1)} collective-permute-done((bf16[128,2176]{1,0:T(8,128)(2,1)S(1)}, bf16[128,2176]{1,0:T(8,128)(2,1)}, u32[]{:S(2)}, u32[]{:S(2)}) %collective-permute-start.1) | collective-permute-done | bytes 557088 | tf_op jit(solution)/shard_map/ppermute | solution.py:340
  58.2 0.8 copy-done.9
  59.0 1.5 collective-permute-start.19
  61.1 0.8 copy-done.21
  61.9 15.7 %collective-permute-done.12.refs_8_ = bf16[512,768]{1,0:T(8,128)(2,1)S(1)} collective-permute-done((bf16[512,768]{1,0:T(8,128)(2,1)S(1)}, bf16[512,768]{1,0:T(8,128)(2,1)S(1)}, u32[]{:S(2)}, u32[]{:S(2)}) %collective-permute-start.12) | collective-permute-done | bytes 786464 | tf_op jit(solution)/shard_map/ppermute | solution.py:337
  77.6 1.3 collective-permute-start.7
  79.7 11.7 %collective-permute-done.19.refs_7_ = bf16[512,768]{1,0:T(8,128)(2,1)S(1)} collective-permute-done((bf16[512,768]{1,0:T(8,128)(2,1)S(1)}, bf16[512,768]{1,0:T(8,128)(2,1)S(1)}, u32[]{:S(2)}, u32[]{:S(2)}) %collective-permute-start.19) | collective-permute-done | bytes 786464 | tf_op jit(solution)/shard_map/ppermute | solution.py:337
  91.4 0.9 copy-done.1
  93.7 0.8 copy-done.27
  95.4 0.8 copy-done.29
  96.7 7.4 %collective-permute-done.7.refs_1_ = bf16[128,2048]{1,0:T(8,128)(2,1)} collective-permute-done((bf16[128,2048]{1,0:T(8,128)(2,1)S(1)}, bf16[128,2048]{1,0:T(8,128)(2,1)}, u32[]{:S(2)}, u32[]{:S(2)}) %collective-permute-start.7) | collective-permute-done | bytes 524320 | tf_op jit(solution)/shard_map/ppermute | solution.py:340
  105.4 1.3 collective-permute-start.2
  106.7 0.8 copy-done.11
  107.5 1.5 collective-permute-start.3
  109.0 0.8 copy-done.13
  109.9 1.9 collective-permute-start.9
  111.9 1.2 copy-done.4
  113.1 1.1 copy-done.6
  114.3 1.0 copy-done.16
  116.5 1.0 copy-done.24
  117.5 1.0 copy-done.28
  118.6 1.0 copy-done.30
  119.6 1.0 shard_map.104
  121.2 2.5 shard_map.107.y.refs_6_
  123.7 3.9 %collective-permute-done.2.refs_1_ = bf16[128,2176]{1,0:T(8,128)(2,1)} collective-permute-done((bf16[128,2176]{1,0:T(8,128)(2,1)}, bf16[128,2176]{1,0:T(8,128)(2,1)}, u32[]{:S(2)}, u32[]{:S(2)}) %collective-permute-start.2) | collective-permute-done | bytes 557088 | tf_op jit(solution)/shard_map/ppermute | solution.py:340
  128.4 1.5 collective-permute-start.26
  130.4 1.3 collective-permute-start.29
  131.7 1.9 collective-permute-start.4
  133.6 7.6 %shard_map.105 = (bf16[1024,768]{1,0:T(8,128)(2,1)S(1)}, f32[1024,768]{1,0:T(8,128)S(1)}, f32[1024,768]{1,0:T(8,128)S(1)}, bf16[2048,768]{1,0:T(8,128)(2,1)S(1)}, bf16[2048,768]{1,0:T(8,128)(2,1)S(1)}) custom-call(s32[3]{0:T(128)S(1)} %pad_add_fusion.place, ...), custom_call_target="tpu_custom_call", output_to_operand_aliasing={{3}: (4, {}), {4}: (5, {})} | custom-call | flops 4831838208 | bytes 25165824 | tf_op jit(solution)/shard_map/pallas_call | solution.py:31
  141.3 4.0 %shard_map.106 = (bf16[1024,768]{1,0:T(8,128)(2,1)S(1)}, f32[1024,768]{1,0:T(8,128)S(1)}, f32[1024,768]{1,0:T(8,128)S(1)}, bf16[1024,2048]{1,0:T(8,128)(2,1)S(1)}) custom-call(s32[3]{0:T(128)S(1)} %pad_add_fusion.place, bf16[128,2048]{1,0:T(8,128)(2,1)S(1)} %copy-done.18, ...), custom_call_target="tpu_custom_call", output_to_operand_aliasing={{0}: (7, {}), {1}: (8, {}), {2}: (9, {}), {3}: (10, {})} | custom-call | flops 1610612736 | bytes 10747904 | tf_op jit(solution)/shard_map/pallas_call | solution.py:31
  145.3 2.0 shard_map.108.refs_5_
  147.3 2.6 shard_map.109
  150.0 6.3 %shard_map.110 = (bf16[1024,768]{1,0:T(8,128)(2,1)S(1)}, bf16[1024,768]{1,0:T(8,128)(2,1)S(1)}) custom-call(s32[3]{0:T(128)S(1)} %pad_add_fusion.place, bf16[1024,2048]{1,0:T(8,128)(2,1)S(1)} %get-tuple-element.52.y, f32[1024,768]{1,0:T(8,128)S(1)} %get-tuple-element.53.active, f32[1024,768]{1,0:T(8,128)S(1)} %get-tuple-element.54.slope, ...), custom_call_target="tpu_custom_call" | custom-call | flops 3221225472 | bytes 16777216 | tf_op jit(solution)/shard_map/pallas_call | solution.py:31
  156.3 8.1 %shard_map.111 = (bf16[512,2048]{1,0:T(8,128)(2,1)S(1)}, bf16[512,2048]{1,0:T(8,128)(2,1)S(1)}) custom-call(bf16[1024,768]{1,0:T(8,128)(2,1)S(1)} %get-tuple-element.55.gate_delta.gd, bf16[1024,768]{1,0:T(8,128)(2,1)S(1)} %get-tuple-element.56.up_delta.ud, bf16[2048,768]{1,0:T(8,128)(2,1)S(1)} %get-tuple-element.46.refs_4_.wg, ...), custom_call_target="tpu_custom_call" | custom-call | flops 6442450944 | bytes 13631488 | tf_op jit(solution)/shard_map/pallas_call | solution.py:31
  165.7 1.5 collective-permute-start.41
  167.3 5.3 %shard_map.113 = (bf16[2,512,768]{2,1,0:T(8,128)(2,1)S(1)}, bf16[2,512,768]{2,1,0:T(8,128)(2,1)S(1)}) custom-call(s32[3]{0:T(128)S(1)} %pad_add_fusion.place, bf16[1024,2048]{1,0:T(8,128)(2,1)S(1)} %get-tuple-element.59.x, bf16[1024,768]{1,0:T(8,128)(2,1)S(1)} %get-tuple-element.55.gate_delta.gd, bf16[1024,768]{1,0:T(8,128)(2,1)S(1)} %get-tuple-element.56.up_delta.ud), custom_call_target="tpu_custom_call" | custom-call | flops 3221225472 | bytes 10485760 | tf_op jit(solution)/shard_map/pallas_call | solution.py:31
  173.1 1.3 collective-permute-start.35
  174.4 2.4 shard_map.115
  176.7 5.3 %shard_map.112 = (bf16[512,768]{1,0:T(8,128)(2,1)S(1)}, bf16[512,768]{1,0:T(8,128)(2,1)S(1)}, bf16[512,768]{1,0:T(8,128)(2,1)S(1)}, bf16[512,768]{1,0:T(8,128)(2,1)S(1)}) custom-call(s32[3]{0:T(128)S(1)} %pad_add_fusion.place, bf16[1024,2048]{1,0:T(8,128)(2,1)S(1)} %get-tuple-element.59.x, bf16[1024,768]{1,0:T(8,128)(2,1)S(1)} %get-tuple-element.55.gate_delta.gd, ...), custom_call_target="tpu_custom_call" | custom-call | flops 3221225472 | bytes 10485760 | tf_op jit(solution)/shard_map/pallas_call | solution.py:31
  182.0 3.4 %collective-permute-done.39 = bf16[2,384,512]{2,1,0:T(8,128)(2,1)S(1)} collective-permute-done((bf16[2,384,512]{2,1,0:T(8,128)(2,1)S(1)}, bf16[2,384,512]{2,1,0:T(8,128)(2,1)S(1)}, u32[]{:S(2)}, u32[]{:S(2)}) %collective-permute-start.39) | collective-permute-done | bytes 786464 | tf_op jit(solution)/shard_map/ppermute | solution.py:334
  185.5 1.6 collective-permute-start.40
  187.2 0.8 collective-permute-start.42
  188.9 5.3 %collective-permute-start.33 = (bf16[128,2048]{1,0:T(8,128)(2,1)S(1)}, bf16[128,2048]{1,0:T(8,128)(2,1)S(1)}, u32[]{:S(2)}, u32[]{:S(2)}) collective-permute-start(bf16[128,2048]{1,0:T(8,128)(2,1)S(1)} %get-tuple-element.77), channel_id=1, source_target_pairs={{0,2},{1,3},{6,4},{7,5},{8,10},{9,11},{14,12},{15,13},{16,18},{17,... | collective-permute-start | bytes 1572872 | tf_op jit(solution)/shard_map/ppermute | solution.py:340
  194.2 25.6 %collective-permute-done.36 = bf16[2,512,768]{2,1,0:T(8,128)(2,1)S(1)} collective-permute-done((bf16[2,512,768]{2,1,0:T(8,128)(2,1)S(1)}, bf16[2,512,768]{2,1,0:T(8,128)(2,1)S(1)}, u32[]{:S(2)}, u32[]{:S(2)}) %collective-permute-start.36) | collective-permute-done | bytes 1572896 | tf_op jit(solution)/shard_map/ppermute | solution.py:337
  220.3 1.3 collective-permute-start.38
  222.1 1.6 collective-permute-start.37
  224.5 3.8 %collective-permute-done.40 = bf16[384,512]{1,0:T(8,128)(2,1)S(1)} collective-permute-done((bf16[384,512]{1,0:T(8,128)(2,1)S(1)}, bf16[384,512]{1,0:T(8,128)(2,1)S(1)}, u32[]{:S(2)}, u32[]{:S(2)}) %collective-permute-start.40) | collective-permute-done | bytes 393248 | tf_op jit(solution)/shard_map/ppermute | solution.py:337
  228.3 3.4 %collective-permute-start.32 = (bf16[128,2048]{1,0:T(8,128)(2,1)S(1)}, bf16[128,2048]{1,0:T(8,128)(2,1)S(1)}, u32[]{:S(2)}, u32[]{:S(2)}) collective-permute-start(bf16[128,2048]{1,0:T(8,128)(2,1)S(1)} %get-tuple-element.76), channel_id=1, source_target_pairs={{0,2},{1,3},{2,0},{3,1},{4,6},{5,7},{6,4},{7,5},{8,10},{9,11},{10,... | collective-permute-start | bytes 1572872 | tf_op jit(solution)/shard_map/ppermute | solution.py:340
  231.7 1.9 collective-permute-start.34
  233.9 0.9 maximum_bitcast_fusion
  234.8 8.6 %collective-permute-done.38.up_last = bf16[512,768]{1,0:T(8,128)(2,1)S(1)} collective-permute-done((bf16[512,768]{1,0:T(8,128)(2,1)S(1)}, bf16[512,768]{1,0:T(8,128)(2,1)S(1)}, u32[]{:S(2)}, u32[]{:S(2)}) %collective-permute-start.38) | collective-permute-done | bytes 786464 | tf_op jit(solution)/shard_map/ppermute | solution.py:334
  244.0 1.3 shard_map.114
  245.3 1.8 collective-permute-done.32
  247.1 15.5 %collective-permute-done.34 = bf16[128,2048]{1,0:T(8,128)(2,1)S(1)} collective-permute-done((bf16[128,2048]{1,0:T(8,128)(2,1)S(1)}, bf16[128,2048]{1,0:T(8,128)(2,1)S(1)}, u32[]{:S(2)}, u32[]{:S(2)}) %collective-permute-start.34) | collective-permute-done | bytes 524320 | tf_op jit(solution)/shard_map/ppermute | solution.py:340
  262.6 1.1 add_convert_fusion.1
  (133 shorter events, 19.3 us)
Async XLA Ops:
  0.6 16.4 %copy-start.15 = (bf16[128,2048]{1,0:T(8,128)(2,1)S(1)}, bf16[128,2048]{1,0:T(8,128)(2,1)}, u32[]{:S(2)}) copy-start(bf16[128,2048]{1,0:T(8,128)(2,1)} %tokens.1) | copy-start | bytes 1572868
  0.6 35.7 %copy-start.3 = (bf16[1,512,768]{2,1,0:T(8,128)(2,1)S(1)}, bf16[1,512,768]{2,1,0:T(8,128)(2,1)}, u32[]{:S(2)}) copy-start(bf16[1,512,768]{2,1,0:T(8,128)(2,1)} %param.11) | copy-start | bytes 2359300
  0.7 56.5 %copy-start.5 = (bf16[1,512,768]{2,1,0:T(8,128)(2,1)S(1)}, bf16[1,512,768]{2,1,0:T(8,128)(2,1)}, u32[]{:S(2)}) copy-start(bf16[1,512,768]{2,1,0:T(8,128)(2,1)} %param.12) | copy-start | bytes 2359300
  2.0 109.8 %copy-start.38 = (bf16[384,512]{1,0:T(8,128)(2,1)}, bf16[384,512]{1,0:T(8,128)(2,1)S(1)}, u32[]{:S(2)}) copy-start(bf16[384,512]{1,0:T(8,128)(2,1)S(1)} %get-tuple-element.83) | copy-start | bytes 1179652
  2.0 109.8 %copy-start.40 = (bf16[384,512]{1,0:T(8,128)(2,1)}, bf16[384,512]{1,0:T(8,128)(2,1)S(1)}, u32[]{:S(2)}) copy-start(bf16[384,512]{1,0:T(8,128)(2,1)S(1)} %get-tuple-element.82) | copy-start | bytes 1179652
  2.0 12.1 %collective-permute-start.24 = (bf16[384,512]{1,0:T(8,128)(2,1)S(1)}, bf16[384,512]{1,0:T(8,128)(2,1)S(1)}, u32[]{:S(2)}, u32[]{:S(2)}) collective-permute-start(bf16[384,512]{1,0:T(8,128)(2,1)S(1)} %get-tuple-element.83), channel_id=1, source_target_pairs={{0,8},{8,0},{16,24},{24,16},{1,9},{9,1},{17,25},{25,17},{2,10},{10... | collective-permute-start | bytes 1179656 | tf_op jit(solution)/shard_map/ppermute | solution.py:334
  5.0 12.0 %collective-permute-start.27 = (bf16[384,512]{1,0:T(8,128)(2,1)S(1)}, bf16[384,512]{1,0:T(8,128)(2,1)S(1)}, u32[]{:S(2)}, u32[]{:S(2)}) collective-permute-start(bf16[384,512]{1,0:T(8,128)(2,1)S(1)} %get-tuple-element.82), channel_id=1, source_target_pairs={{0,16},{8,24},{16,0},{24,8},{1,17},{9,25},{17,1},{25,9},{2,18},{10... | collective-permute-start | bytes 1179656 | tf_op jit(solution)/shard_map/ppermute | solution.py:337
  6.6 28.3 %collective-permute-start.6 = (bf16[128,2048]{1,0:T(8,128)(2,1)}, bf16[128,2048]{1,0:T(8,128)(2,1)S(1)}, u32[]{:S(2)}, u32[]{:S(2)}) collective-permute-start(bf16[128,2048]{1,0:T(8,128)(2,1)} %tokens.1), channel_id=1, source_target_pairs={{0,4},{1,5},{2,6},{3,7},{4,0},{5,1},{6,2},{7,3},{8,12},{9,13},{10,... | collective-permute-start | bytes 1572872 | tf_op jit(solution)/shard_map/ppermute | solution.py:340
  9.1 25.7 %collective-permute-start.14 = (bf16[128,2048]{1,0:T(8,128)(2,1)}, bf16[128,2048]{1,0:T(8,128)(2,1)S(1)}, u32[]{:S(2)}, u32[]{:S(2)}) collective-permute-start(bf16[128,2048]{1,0:T(8,128)(2,1)} %tokens.1), channel_id=1, source_target_pairs={{0,2},{1,3},{2,0},{3,1},{4,6},{5,7},{6,4},{7,5},{8,10},{9,11},{10,... | collective-permute-start | bytes 1572872 | tf_op jit(solution)/shard_map/ppermute | solution.py:340
  10.7 24.1 %collective-permute-start.15 = (bf16[128,2048]{1,0:T(8,128)(2,1)}, bf16[128,2048]{1,0:T(8,128)(2,1)S(1)}, u32[]{:S(2)}, u32[]{:S(2)}) collective-permute-start(bf16[128,2048]{1,0:T(8,128)(2,1)} %tokens.1), channel_id=1, source_target_pairs={{0,1},{1,0},{2,3},{3,2},{4,5},{5,4},{6,7},{7,6},{8,9},{9,8},{10,11... | collective-permute-start | bytes 1572872 | tf_op jit(solution)/shard_map/ppermute | solution.py:343
  14.1 94.9 %copy-start.32 = (bf16[384,512]{1,0:T(8,128)(2,1)}, bf16[384,512]{1,0:T(8,128)(2,1)S(1)}, u32[]{:S(2)}) copy-start(bf16[384,512]{1,0:T(8,128)(2,1)S(1)} %collective-permute-done.24.refs_1_) | copy-start | bytes 1179652
  14.2 43.0 %collective-permute-start.1 = (bf16[128,2176]{1,0:T(8,128)(2,1)S(1)}, bf16[128,2176]{1,0:T(8,128)(2,1)}, u32[]{:S(2)}, u32[]{:S(2)}) collective-permute-start(bf16[128,2176]{1,0:T(8,128)(2,1)S(1)} %shard_map.102.refs_0_), channel_id=1, source_target_pairs={{0,4},{1,5},{2,6},{3,7},{4,0},{5,1},{6,2},{7,3},{8,12},{9,13},{10,... | collective-permute-start | bytes 1671176 | tf_op jit(solution)/shard_map/ppermute | solution.py:340
  17.0 94.8 %copy-start.34 = (bf16[384,512]{1,0:T(8,128)(2,1)}, bf16[384,512]{1,0:T(8,128)(2,1)S(1)}, u32[]{:S(2)}) copy-start(bf16[384,512]{1,0:T(8,128)(2,1)S(1)} %collective-permute-done.27.refs_4_) | copy-start | bytes 1179652
  17.0 19.3 %collective-permute-start.5 = (bf16[128,2048]{1,0:T(8,128)(2,1)S(1)}, bf16[128,2048]{1,0:T(8,128)(2,1)S(1)}, u32[]{:S(2)}, u32[]{:S(2)}) collective-permute-start(bf16[128,2048]{1,0:T(8,128)(2,1)S(1)} %copy-done.15), channel_id=1, source_target_pairs={{2,4},{3,5},{4,2},{5,3},{10,12},{11,13},{12,10},{13,11},{18,20},{1... | collective-permute-start | bytes 1572872 | tf_op jit(solution)/shard_map/ppermute | solution.py:340
  34.8 22.9 %collective-permute-start.20 = (bf16[128,2176]{1,0:T(8,128)(2,1)S(1)}, bf16[128,2176]{1,0:T(8,128)(2,1)S(1)}, u32[]{:S(2)}, u32[]{:S(2)}) collective-permute-start(bf16[128,2176]{1,0:T(8,128)(2,1)S(1)} %shard_map.102.refs_0_), channel_id=1, source_target_pairs={{0,2},{1,3},{2,0},{3,1},{4,6},{5,7},{6,4},{7,5},{8,10},{9,11},{10,... | collective-permute-start | bytes 1671176 | tf_op jit(solution)/shard_map/ppermute | solution.py:340
  34.8 23.4 %collective-permute-start.21 = (bf16[128,2176]{1,0:T(8,128)(2,1)S(1)}, bf16[128,2176]{1,0:T(8,128)(2,1)S(1)}, u32[]{:S(2)}, u32[]{:S(2)}) collective-permute-start(bf16[128,2176]{1,0:T(8,128)(2,1)S(1)} %shard_map.102.refs_0_), channel_id=1, source_target_pairs={{0,1},{1,0},{2,3},{3,2},{4,5},{5,4},{6,7},{7,6},{8,9},{9,8},{10,11... | collective-permute-start | bytes 1671176 | tf_op jit(solution)/shard_map/ppermute | solution.py:343
  35.6 24.9 %collective-permute-start = (bf16[128,2176]{1,0:T(8,128)(2,1)S(1)}, bf16[128,2176]{1,0:T(8,128)(2,1)S(1)}, u32[]{:S(2)}, u32[]{:S(2)}) collective-permute-start(bf16[128,2176]{1,0:T(8,128)(2,1)S(1)} %shard_map.102.refs_0_), channel_id=1, source_target_pairs={{2,4},{3,5},{4,2},{5,3},{10,12},{11,13},{12,10},{13,11},{18,20},{1... | collective-permute-start | bytes 1671176 | tf_op jit(solution)/shard_map/ppermute | solution.py:340
  36.3 24.2 %collective-permute-start.10 = (bf16[512,768]{1,0:T(8,128)(2,1)S(1)}, bf16[512,768]{1,0:T(8,128)(2,1)S(1)}, u32[]{:S(2)}, u32[]{:S(2)}) collective-permute-start(bf16[512,768]{1,0:T(8,128)(2,1)S(1)} %bitcast.55), channel_id=1, source_target_pairs={{0,8},{8,0},{16,24},{24,16},{1,9},{9,1},{17,25},{25,17},{2,10},{10... | collective-permute-start | bytes 2359304 | tf_op jit(solution)/shard_map/ppermute | solution.py:334
  57.2 20.4 %collective-permute-start.12 = (bf16[512,768]{1,0:T(8,128)(2,1)S(1)}, bf16[512,768]{1,0:T(8,128)(2,1)S(1)}, u32[]{:S(2)}, u32[]{:S(2)}) collective-permute-start(bf16[512,768]{1,0:T(8,128)(2,1)S(1)} %bitcast.58), channel_id=1, source_target_pairs={{0,16},{8,24},{16,0},{24,8},{1,17},{9,25},{17,1},{25,9},{2,18},{10... | collective-permute-start | bytes 2359304 | tf_op jit(solution)/shard_map/ppermute | solution.py:337
  57.7 22.0 %collective-permute-start.18 = (bf16[512,768]{1,0:T(8,128)(2,1)S(1)}, bf16[512,768]{1,0:T(8,128)(2,1)S(1)}, u32[]{:S(2)}, u32[]{:S(2)}) collective-permute-start(bf16[512,768]{1,0:T(8,128)(2,1)S(1)} %bitcast.59), channel_id=1, source_target_pairs={{0,8},{8,0},{16,24},{24,16},{1,9},{9,1},{17,25},{25,17},{2,10},{10... | collective-permute-start | bytes 2359304 | tf_op jit(solution)/shard_map/ppermute | solution.py:334
  59.0 32.3 %collective-permute-start.19 = (bf16[512,768]{1,0:T(8,128)(2,1)S(1)}, bf16[512,768]{1,0:T(8,128)(2,1)S(1)}, u32[]{:S(2)}, u32[]{:S(2)}) collective-permute-start(bf16[512,768]{1,0:T(8,128)(2,1)S(1)} %bitcast.56), channel_id=1, source_target_pairs={{0,16},{8,24},{16,0},{24,8},{1,17},{9,25},{17,1},{25,9},{2,18},{10... | collective-permute-start | bytes 2359304 | tf_op jit(solution)/shard_map/ppermute | solution.py:337
  60.6 33.2 %collective-permute-start.16 = (bf16[128,2048]{1,0:T(8,128)(2,1)S(1)}, bf16[128,2048]{1,0:T(8,128)(2,1)S(1)}, u32[]{:S(2)}, u32[]{:S(2)}) collective-permute-start(bf16[128,2048]{1,0:T(8,128)(2,1)S(1)} %collective-permute-done.6.refs_0_), channel_id=1, source_target_pairs={{0,1},{1,0},{2,3},{3,2},{4,5},{5,4},{6,7},{7,6},{8,9},{9,8},{10,11... | collective-permute-start | bytes 1572872 | tf_op jit(solution)/shard_map/ppermute | solution.py:343
  60.6 34.8 %collective-permute-start.17 = (bf16[128,2048]{1,0:T(8,128)(2,1)S(1)}, bf16[128,2048]{1,0:T(8,128)(2,1)S(1)}, u32[]{:S(2)}, u32[]{:S(2)}) collective-permute-start(bf16[128,2048]{1,0:T(8,128)(2,1)S(1)} %collective-permute-done.14.refs_1_), channel_id=1, source_target_pairs={{0,1},{1,0},{2,3},{3,2},{4,5},{5,4},{6,7},{7,6},{8,9},{9,8},{10,11... | collective-permute-start | bytes 1572872 | tf_op jit(solution)/shard_map/ppermute | solution.py:343
  77.6 26.5 %collective-permute-start.7 = (bf16[128,2048]{1,0:T(8,128)(2,1)S(1)}, bf16[128,2048]{1,0:T(8,128)(2,1)}, u32[]{:S(2)}, u32[]{:S(2)}) collective-permute-start(bf16[128,2048]{1,0:T(8,128)(2,1)S(1)} %collective-permute-done.6.refs_0_), channel_id=1, source_target_pairs={{4,6},{5,7},{2,0},{3,1},{12,14},{13,15},{10,8},{11,9},{20,22},{21,... | collective-permute-start | bytes 1572872 | tf_op jit(solution)/shard_map/ppermute | solution.py:340
  79.7 27.0 %collective-permute-start.22 = (bf16[128,2176]{1,0:T(8,128)(2,1)}, bf16[128,2176]{1,0:T(8,128)(2,1)S(1)}, u32[]{:S(2)}, u32[]{:S(2)}) collective-permute-start(bf16[128,2176]{1,0:T(8,128)(2,1)} %collective-permute-done.1.refs_1_), channel_id=1, source_target_pairs={{0,1},{1,0},{2,3},{3,2},{4,5},{5,4},{6,7},{7,6},{8,9},{9,8},{10,11... | collective-permute-start | bytes 1671176 | tf_op jit(solution)/shard_map/ppermute | solution.py:343
  92.3 12.4 %collective-permute-start.8 = (bf16[128,2048]{1,0:T(8,128)(2,1)S(1)}, bf16[128,2048]{1,0:T(8,128)(2,1)S(1)}, u32[]{:S(2)}, u32[]{:S(2)}) collective-permute-start(bf16[128,2048]{1,0:T(8,128)(2,1)S(1)} %collective-permute-done.5.refs_0_), channel_id=1, source_target_pairs={{2,3},{3,2},{4,5},{5,4},{10,11},{11,10},{12,13},{13,12},{18,19},{1... | collective-permute-start | bytes 1572872 | tf_op jit(solution)/shard_map/ppermute | solution.py:343
  94.6 14.4 %collective-permute-start.23 = (bf16[128,2176]{1,0:T(8,128)(2,1)S(1)}, bf16[128,2176]{1,0:T(8,128)(2,1)S(1)}, u32[]{:S(2)}, u32[]{:S(2)}) collective-permute-start(bf16[128,2176]{1,0:T(8,128)(2,1)S(1)} %collective-permute-done.20.refs_2_), channel_id=1, source_target_pairs={{0,1},{1,0},{2,3},{3,2},{4,5},{5,4},{6,7},{7,6},{8,9},{9,8},{10,11... | collective-permute-start | bytes 1671176 | tf_op jit(solution)/shard_map/ppermute | solution.py:343
  96.2 34.2 %collective-permute-start.11 = (bf16[512,768]{1,0:T(8,128)(2,1)S(1)}, bf16[512,768]{1,0:T(8,128)(2,1)}, u32[]{:S(2)}, u32[]{:S(2)}) collective-permute-start(bf16[512,768]{1,0:T(8,128)(2,1)S(1)} %collective-permute-done.10.refs_5_), channel_id=1, source_target_pairs={{0,16},{8,24},{16,0},{24,8},{1,17},{9,25},{17,1},{25,9},{2,18},{10... | collective-permute-start | bytes 2359304 | tf_op jit(solution)/shard_map/ppermute | solution.py:337
  104.1 27.6 %collective-permute-start.13 = (bf16[512,768]{1,0:T(8,128)(2,1)S(1)}, bf16[512,768]{1,0:T(8,128)(2,1)}, u32[]{:S(2)}, u32[]{:S(2)}) collective-permute-start(bf16[512,768]{1,0:T(8,128)(2,1)S(1)} %collective-permute-done.12.refs_8_), channel_id=1, source_target_pairs={{0,8},{8,0},{16,24},{24,16},{1,9},{9,1},{17,25},{25,17},{2,10},{10... | collective-permute-start | bytes 2359304 | tf_op jit(solution)/shard_map/ppermute | solution.py:334
  105.4 22.2 %collective-permute-start.2 = (bf16[128,2176]{1,0:T(8,128)(2,1)}, bf16[128,2176]{1,0:T(8,128)(2,1)}, u32[]{:S(2)}, u32[]{:S(2)}) collective-permute-start(bf16[128,2176]{1,0:T(8,128)(2,1)} %collective-permute-done.1.refs_1_), channel_id=1, source_target_pairs={{4,6},{5,7},{2,0},{3,1},{12,14},{13,15},{10,8},{11,9},{20,22},{21,... | collective-permute-start | bytes 1671176 | tf_op jit(solution)/shard_map/ppermute | solution.py:340
  107.5 20.8 %collective-permute-start.3 = (bf16[128,2176]{1,0:T(8,128)(2,1)S(1)}, bf16[128,2176]{1,0:T(8,128)(2,1)}, u32[]{:S(2)}, u32[]{:S(2)}) collective-permute-start(bf16[128,2176]{1,0:T(8,128)(2,1)S(1)} %collective-permute-done.refs_0_), channel_id=1, source_target_pairs={{2,3},{3,2},{4,5},{5,4},{10,11},{11,10},{12,13},{13,12},{18,19},{1... | collective-permute-start | bytes 1671176 | tf_op jit(solution)/shard_map/ppermute | solution.py:343
  109.9 20.0 %collective-permute-start.9 = (bf16[128,2048]{1,0:T(8,128)(2,1)}, bf16[128,2048]{1,0:T(8,128)(2,1)}, u32[]{:S(2)}, u32[]{:S(2)}) collective-permute-start(bf16[128,2048]{1,0:T(8,128)(2,1)} %collective-permute-done.7.refs_1_), channel_id=1, source_target_pairs={{0,1},{1,0},{6,7},{7,6},{8,9},{9,8},{14,15},{15,14},{16,17},{17,16... | collective-permute-start | bytes 1572872 | tf_op jit(solution)/shard_map/ppermute | solution.py:343
  111.8 4.2 %copy-start.2 = (bf16[512,768]{1,0:T(8,128)(2,1)S(1)}, bf16[512,768]{1,0:T(8,128)(2,1)}, u32[]{:S(2)}) copy-start(bf16[512,768]{1,0:T(8,128)(2,1)} %copy-done.1) | copy-start | bytes 2359300
  111.9 1.2 copy-start.4
  113.1 1.1 copy-start.6
  115.3 1.2 copy-start.22
  119.6 1.2 copy-start.10
  119.6 1.4 copy-start.12
  119.6 1.6 copy-start.14
  121.2 6.4 %copy-start.41 = (bf16[384,512]{1,0:T(8,128)(2,1)S(1)}, bf16[384,512]{1,0:T(8,128)(2,1)}, u32[]{:S(2)}) copy-start(bf16[384,512]{1,0:T(8,128)(2,1)} %copy-done.40) | copy-start | bytes 1179652
  121.2 7.2 %copy-start.39 = (bf16[384,512]{1,0:T(8,128)(2,1)S(1)}, bf16[384,512]{1,0:T(8,128)(2,1)}, u32[]{:S(2)}) copy-start(bf16[384,512]{1,0:T(8,128)(2,1)} %copy-done.38) | copy-start | bytes 1179652
  121.2 8.7 %copy-start.33 = (bf16[384,512]{1,0:T(8,128)(2,1)S(1)}, bf16[384,512]{1,0:T(8,128)(2,1)}, u32[]{:S(2)}) copy-start(bf16[384,512]{1,0:T(8,128)(2,1)} %copy-done.32) | copy-start | bytes 1179652
  121.2 9.2 %copy-start.35 = (bf16[384,512]{1,0:T(8,128)(2,1)S(1)}, bf16[384,512]{1,0:T(8,128)(2,1)}, u32[]{:S(2)}) copy-start(bf16[384,512]{1,0:T(8,128)(2,1)} %copy-done.34) | copy-start | bytes 1179652
  127.6 22.3 %collective-permute-start.25 = (bf16[384,512]{1,0:T(8,128)(2,1)S(1)}, bf16[384,512]{1,0:T(8,128)(2,1)S(1)}, u32[]{:S(2)}, u32[]{:S(2)}) collective-permute-start(bf16[384,512]{1,0:T(8,128)(2,1)S(1)} %copy-done.41), channel_id=1, source_target_pairs={{0,8},{8,0},{16,24},{24,16},{1,9},{9,1},{17,25},{25,17},{2,10},{10... | collective-permute-start | bytes 1179656 | tf_op jit(solution)/shard_map/ppermute | solution.py:334
  128.4 21.5 %collective-permute-start.26 = (bf16[384,512]{1,0:T(8,128)(2,1)S(1)}, bf16[384,512]{1,0:T(8,128)(2,1)S(1)}, u32[]{:S(2)}, u32[]{:S(2)}) collective-permute-start(bf16[384,512]{1,0:T(8,128)(2,1)S(1)} %copy-done.39), channel_id=1, source_target_pairs={{0,16},{8,24},{16,0},{24,8},{1,17},{9,25},{17,1},{25,9},{2,18},{10... | collective-permute-start | bytes 1179656 | tf_op jit(solution)/shard_map/ppermute | solution.py:337
  129.9 20.0 %collective-permute-start.28 = (bf16[384,512]{1,0:T(8,128)(2,1)S(1)}, bf16[384,512]{1,0:T(8,128)(2,1)S(1)}, u32[]{:S(2)}, u32[]{:S(2)}) collective-permute-start(bf16[384,512]{1,0:T(8,128)(2,1)S(1)} %copy-done.33), channel_id=1, source_target_pairs={{0,16},{8,24},{16,0},{24,8},{1,17},{9,25},{17,1},{25,9},{2,18},{10... | collective-permute-start | bytes 1179656 | tf_op jit(solution)/shard_map/ppermute | solution.py:337
  130.4 19.5 %collective-permute-start.29 = (bf16[384,512]{1,0:T(8,128)(2,1)S(1)}, bf16[384,512]{1,0:T(8,128)(2,1)S(1)}, u32[]{:S(2)}, u32[]{:S(2)}) collective-permute-start(bf16[384,512]{1,0:T(8,128)(2,1)S(1)} %copy-done.35), channel_id=1, source_target_pairs={{0,8},{8,0},{16,24},{24,16},{1,9},{9,1},{17,25},{25,17},{2,10},{10... | collective-permute-start | bytes 1179656 | tf_op jit(solution)/shard_map/ppermute | solution.py:334
  131.7 15.6 %collective-permute-start.4 = (bf16[128,2176]{1,0:T(8,128)(2,1)}, bf16[128,2176]{1,0:T(8,128)(2,1)S(1)}, u32[]{:S(2)}, u32[]{:S(2)}) collective-permute-start(bf16[128,2176]{1,0:T(8,128)(2,1)} %collective-permute-done.2.refs_1_), channel_id=1, source_target_pairs={{0,1},{1,0},{6,7},{7,6},{8,9},{9,8},{14,15},{15,14},{16,17},{17,16... | collective-permute-start | bytes 1671176 | tf_op jit(solution)/shard_map/ppermute | solution.py:343
  133.6 7.7 %copy-start.18 = (bf16[128,2048]{1,0:T(8,128)(2,1)S(1)}, bf16[128,2048]{1,0:T(8,128)(2,1)}, u32[]{:S(2)}) copy-start(bf16[128,2048]{1,0:T(8,128)(2,1)} %copy-done.17) | copy-start | bytes 1572868
  133.6 7.7 %copy-start.26 = (bf16[128,2048]{1,0:T(8,128)(2,1)S(1)}, bf16[128,2048]{1,0:T(8,128)(2,1)}, u32[]{:S(2)}) copy-start(bf16[128,2048]{1,0:T(8,128)(2,1)} %copy-done.25) | copy-start | bytes 1572868
  147.3 2.7 %copy-start = (bf16[1,768,512]{2,1,0:T(8,128)(2,1)S(1)}, bf16[1,768,512]{2,1,0:T(8,128)(2,1)}, u32[]{:S(2)}) copy-start(bf16[1,768,512]{2,1,0:T(8,128)(2,1)} %param.13) | copy-start | bytes 2359300
  164.4 23.6 %collective-permute-start.30 = (bf16[512,2048]{1,0:T(8,128)(2,1)S(1)}, bf16[512,2048]{1,0:T(8,128)(2,1)S(1)}, u32[]{:S(2)}, u32[]{:S(2)}) collective-permute-start(bf16[512,2048]{1,0:T(8,128)(2,1)S(1)} %get-tuple-element.58), channel_id=1, source_target_pairs={{0,1},{1,0},{2,3},{3,2},{4,5},{5,4},{6,7},{7,6},{8,9},{9,8},{10,11... | collective-permute-start | bytes 6291464 | tf_op jit(solution)/shard_map/ppermute | solution.py:343
  165.0 20.4 %collective-permute-start.39 = (bf16[2,384,512]{2,1,0:T(8,128)(2,1)S(1)}, bf16[2,384,512]{2,1,0:T(8,128)(2,1)S(1)}, u32[]{:S(2)}, u32[]{:S(2)}) collective-permute-start(bf16[2,384,512]{2,1,0:T(8,128)(2,1)S(1)} %get-tuple-element.71), channel_id=1, source_target_pairs={{0,8},{8,0},{16,24},{24,16},{1,9},{9,1},{17,25},{25,17},{2,10},{10... | collective-permute-start | bytes 2359304 | tf_op jit(solution)/shard_map/ppermute | solution.py:334
  165.7 21.3 %collective-permute-start.41 = (bf16[2,384,512]{2,1,0:T(8,128)(2,1)S(1)}, bf16[2,384,512]{2,1,0:T(8,128)(2,1)S(1)}, u32[]{:S(2)}, u32[]{:S(2)}) collective-permute-start(bf16[2,384,512]{2,1,0:T(8,128)(2,1)S(1)} %get-tuple-element.74), channel_id=1, source_target_pairs={{0,16},{8,24},{16,0},{24,8},{1,17},{9,25},{17,1},{25,9},{2,18},{10... | collective-permute-start | bytes 2359304 | tf_op jit(solution)/shard_map/ppermute | solution.py:337
  172.5 47.3 %collective-permute-start.36 = (bf16[2,512,768]{2,1,0:T(8,128)(2,1)S(1)}, bf16[2,512,768]{2,1,0:T(8,128)(2,1)S(1)}, u32[]{:S(2)}, u32[]{:S(2)}) collective-permute-start(bf16[2,512,768]{2,1,0:T(8,128)(2,1)S(1)} %get-tuple-element.63), channel_id=1, source_target_pairs={{0,16},{8,24},{16,0},{24,8},{1,17},{9,25},{17,1},{25,9},{2,18},{10... | collective-permute-start | bytes 4718600 | tf_op jit(solution)/shard_map/ppermute | solution.py:337
  173.1 48.5 %collective-permute-start.35 = (bf16[2,512,768]{2,1,0:T(8,128)(2,1)S(1)}, bf16[2,512,768]{2,1,0:T(8,128)(2,1)S(1)}, u32[]{:S(2)}, u32[]{:S(2)}) collective-permute-start(bf16[2,512,768]{2,1,0:T(8,128)(2,1)S(1)} %get-tuple-element.61), channel_id=1, source_target_pairs={{0,8},{8,0},{16,24},{24,16},{1,9},{9,1},{17,25},{25,17},{2,10},{10... | collective-permute-start | bytes 4718600 | tf_op jit(solution)/shard_map/ppermute | solution.py:334
  185.5 42.8 %collective-permute-start.40 = (bf16[384,512]{1,0:T(8,128)(2,1)S(1)}, bf16[384,512]{1,0:T(8,128)(2,1)S(1)}, u32[]{:S(2)}, u32[]{:S(2)}) collective-permute-start(bf16[384,512]{1,0:T(8,128)(2,1)S(1)} %fusion.7), channel_id=1, source_target_pairs={{0,16},{8,24},{16,0},{24,8},{1,17},{9,25},{17,1},{25,9},{2,18},{10... | collective-permute-start | bytes 1179656 | tf_op jit(solution)/shard_map/ppermute | solution.py:337
  187.2 44.5 %collective-permute-start.42 = (bf16[384,512]{1,0:T(8,128)(2,1)S(1)}, bf16[384,512]{1,0:T(8,128)(2,1)S(1)}, u32[]{:S(2)}, u32[]{:S(2)}) collective-permute-start(bf16[384,512]{1,0:T(8,128)(2,1)S(1)} %fusion.4), channel_id=1, source_target_pairs={{0,8},{8,0},{16,24},{24,16},{1,9},{9,1},{17,25},{25,17},{2,10},{10... | collective-permute-start | bytes 1179656 | tf_op jit(solution)/shard_map/ppermute | solution.py:334
  188.9 34.8 %collective-permute-start.33 = (bf16[128,2048]{1,0:T(8,128)(2,1)S(1)}, bf16[128,2048]{1,0:T(8,128)(2,1)S(1)}, u32[]{:S(2)}, u32[]{:S(2)}) collective-permute-start(bf16[128,2048]{1,0:T(8,128)(2,1)S(1)} %get-tuple-element.77), channel_id=1, source_target_pairs={{0,2},{1,3},{6,4},{7,5},{8,10},{9,11},{14,12},{15,13},{16,18},{17,... | collective-permute-start | bytes 1572872 | tf_op jit(solution)/shard_map/ppermute | solution.py:340
  220.3 23.2 %collective-permute-start.38 = (bf16[512,768]{1,0:T(8,128)(2,1)S(1)}, bf16[512,768]{1,0:T(8,128)(2,1)S(1)}, u32[]{:S(2)}, u32[]{:S(2)}) collective-permute-start(bf16[512,768]{1,0:T(8,128)(2,1)S(1)} %get-tuple-element.78), channel_id=1, source_target_pairs={{0,8},{8,0},{16,24},{24,16},{1,9},{9,1},{17,25},{25,17},{2,10},{10... | collective-permute-start | bytes 2359304 | tf_op jit(solution)/shard_map/ppermute | solution.py:334
  222.1 21.9 %collective-permute-start.37 = (bf16[512,768]{1,0:T(8,128)(2,1)S(1)}, bf16[512,768]{1,0:T(8,128)(2,1)S(1)}, u32[]{:S(2)}, u32[]{:S(2)}) collective-permute-start(bf16[512,768]{1,0:T(8,128)(2,1)S(1)} %get-tuple-element.80), channel_id=1, source_target_pairs={{0,16},{8,24},{16,0},{24,8},{1,17},{9,25},{17,1},{25,9},{2,18},{10... | collective-permute-start | bytes 2359304 | tf_op jit(solution)/shard_map/ppermute | solution.py:337
  223.7 21.6 %collective-permute-start.31 = (bf16[128,2048]{1,0:T(8,128)(2,1)S(1)}, bf16[128,2048]{1,0:T(8,128)(2,1)S(1)}, u32[]{:S(2)}, u32[]{:S(2)}) collective-permute-start(bf16[128,2048]{1,0:T(8,128)(2,1)S(1)} %get-tuple-element.77), channel_id=1, source_target_pairs={{2,4},{3,5},{4,2},{5,3},{10,12},{11,13},{12,10},{13,11},{18,20},{1... | collective-permute-start | bytes 1572872 | tf_op jit(solution)/shard_map/ppermute | solution.py:340
  228.3 18.8 %collective-permute-start.32 = (bf16[128,2048]{1,0:T(8,128)(2,1)S(1)}, bf16[128,2048]{1,0:T(8,128)(2,1)S(1)}, u32[]{:S(2)}, u32[]{:S(2)}) collective-permute-start(bf16[128,2048]{1,0:T(8,128)(2,1)S(1)} %get-tuple-element.76), channel_id=1, source_target_pairs={{0,2},{1,3},{2,0},{3,1},{4,6},{5,7},{6,4},{7,5},{8,10},{9,11},{10,... | collective-permute-start | bytes 1572872 | tf_op jit(solution)/shard_map/ppermute | solution.py:340
  231.7 30.9 %collective-permute-start.34 = (bf16[128,2048]{1,0:T(8,128)(2,1)S(1)}, bf16[128,2048]{1,0:T(8,128)(2,1)S(1)}, u32[]{:S(2)}, u32[]{:S(2)}) collective-permute-start(bf16[128,2048]{1,0:T(8,128)(2,1)S(1)} %add_convert_fusion.2), channel_id=1, source_target_pairs={{0,4},{1,5},{2,6},{3,7},{4,0},{5,1},{6,2},{7,3},{8,12},{9,13},{10,... | collective-permute-start | bytes 1572872 | tf_op jit(solution)/shard_map/ppermute | solution.py:340
  (21 other events, 18.5 us)

commit v9 on v8

--- a/solution.py
+++ b/solution.py
@@ -131,22 +131,57 @@
         lhs = x[r, :]
         gate = mm(lhs, wg[:, c], NN)
         up = mm(lhs, wu[:, c], NN)
-        sigma = jax.nn.sigmoid(gate)
-        active = gate * sigma
-        act[r, c] = (active * up).astype(BF16)
-        active_out[r, c] = active
-        slope_out[r, c] = up * sigma * (1.0 + gate * (1.0 - sigma))
+        activate(gate, up, r, c, act, active_out, slope_out)
         return 0
 
     lax.fori_loop(0, wg.shape[1] // tn, step, 0)
 
 
+def activate(gate, up, r, c, act, active_out, slope_out):
+    sigma = jax.nn.sigmoid(gate)
+    active = gate * sigma
+    act[r, c] = (active * up).astype(BF16)
+    active_out[r, c] = active
+    slope_out[r, c] = up * sigma * (1.0 + gate * (1.0 - sigma))
+
+
+def pre_part_body(place, x, wg, wu, gate_part, up_part):
+    tn, share = 256, wg.shape[0] // 4
+    r = slice(0, x.shape[0] // 4 * 3)
+
+    def step(i, _):
+        c = pl.ds(pl.multiple_of(i * tn, tn), tn)
+        gate = up = None
+        for k in range(3):
+            block = pl.ds(pl.multiple_of((place[0] ^ k) * share, share), share)
+            lhs = x[r, block]
+            more = mm(lhs, wg[block, c], NN), mm(lhs, wu[block, c], NN)
+            gate, up = more if gate is None else (gate + more[0], up + more[1])
+        gate_part[r, c] = gate
+        up_part[r, c] = up
+        return 0
+
+    lax.fori_loop(0, wg.shape[1] // tn, step, 0)
+
+
 def pre_early_body(place, *refs):
-    act, active, slope, wg, wu, sems = refs[5:]
+    x, gate_part, up_part = refs[2:5]
+    act, active, slope, wg, wu, sems = refs[7:]
     for c in load_weights(Copies(sems), place, (3,), refs[:2], wg, wu):
         c.wait()
-    x = refs[2]
-    pre_blocks(x, 0, x.shape[0] // 4 * 3, wg, wu, act, active, slope)
+    tn, share = 256, wg.shape[0] // 4
+    r = slice(0, x.shape[0] // 4 * 3)
+    block = pl.ds(pl.multiple_of((place[0] ^ 3) * share, share), share)
+
+    def step(i, _):
+        c = pl.ds(pl.multiple_of(i * tn, tn), tn)
+        lhs = x[r, block]
+        gate = gate_part[r, c] + mm(lhs, wg[block, c], NN)
+        up = up_part[r, c] + mm(lhs, wu[block, c], NN)
+        activate(gate, up, r, c, act, active, slope)
+        return 0
+
+    lax.fori_loop(0, wg.shape[1] // tn, step, 0)
 
 
 def pre_late_body(place, *refs):
@@ -158,26 +193,26 @@
     pre_blocks(x, 3 * count, count, wg, wu, act, active, slope)
 
 
-def scale(experts, expert, raw, y, first):
-    tok, width = raw.shape[0] // 2, y.shape[1]
+def scale(experts, expert, raw, y, row):
+    tok, width = raw.shape[0], y.shape[1]
     lane = lax.broadcasted_iota(jnp.int32, (tok, LANES), 1)
     mine = jnp.logical_and(lane % experts == expert, lane < 3 * experts)
-    for i in (0, 1):
-        gate = jnp.sum(jnp.where(mine, raw[i * tok : (i + 1) * tok, width:].astype(F32), 0.0), axis=1, keepdims=True)
-        y[first + i * tok : first + (i + 1) * tok, :] = (raw[i * tok : (i + 1) * tok, :width].astype(F32) * gate).astype(
-            BF16
-        )
+    gate = jnp.sum(jnp.where(mine, raw[:, width:].astype(F32), 0.0), axis=1, keepdims=True)
+    y[row : row + tok, :] = (raw[:, :width].astype(F32) * gate).astype(BF16)
+
+
+def load_scaled(experts, expert, copies, pieces, raw, y, blocks):
+    tok = pieces[0].shape[0]
+    at = [raw.at[pl.ds(i * tok, tok)] for i in range(len(pieces))]
+    started = [copies.start(src, dst) for src, dst in zip(pieces, at)]
+    for copy, dst, block in zip(started, at, blocks):
+        copy.wait()
+        scale(experts, expert, dst, y, block * tok)
 
 
 def scale_early_body(experts, place, *refs):
-    pieces = refs[:6]
-    y, raw, sems = refs[6:]
-    tok = pieces[0].shape[0]
-    started = load_early(Copies(sems), pieces, raw)
-    for i in range(3):
-        started[2 * i].wait()
-        started[2 * i + 1].wait()
-        scale(experts, place[2], raw.at[pl.ds(2 * i * tok, 2 * tok)], y, 2 * i * tok)
+    y, raw, sems = refs[4:]
+    load_scaled(experts, place[2], Copies(sems), refs[:4], raw, y, (0, 1, 3, 4))
 
 
 def down_blocks(place, act, y, first, count, wanted, put):
@@ -192,7 +227,11 @@
                 put(target, mm(turned, y[rows, cols], NN))
 
 
-def down_early_body(place, act, y, part):
+def down_early_body(experts, place, *refs):
+    pieces, act = refs[:2], refs[2]
+    part, y, raw, sems = refs[4:]
+    load_scaled(experts, place[2], Copies(sems), pieces, raw, y, (2, 5))
+
     def put(target, value):
         part[target] = value
 
@@ -207,7 +246,9 @@
         c.wait()
     count = raw.shape[0]
     first = y.shape[0] - count
-    scale(experts, place[2], raw, y, first)
+    for core in (0, 1):
+        tok = count // 2
+        scale(experts, place[2], raw.at[pl.ds(core * tok, tok)], y, first + core * tok)
 
     def put(target, value):
         dst = (send_a, send_b)[target // 2]
@@ -398,14 +439,22 @@
         width * (10 * tok + 2 * hidden),
         {10: 0, 11: 1, 12: 2},
     )
+    parts = call(
+        pre_part_body,
+        [wide, wide],
+        [(place, SMEM), (x, VMEM), (wg, VMEM), (wu, VMEM)],
+        [],
+        9 * rows * width * hidden // 4,
+        3 * rows * width + 6 * width * hidden + 6 * rows * hidden,
+    )
     *pre, wg, wu = call(
         pre_early_body,
         [flat, wide, wide, weight, weight],
-        [(place, SMEM)] + anys((wg3, wu3)) + [(x, VMEM), (wg, VMEM), (wu, VMEM)],
+        [(place, SMEM)] + anys((wg3, wu3)) + [(a, VMEM) for a in (x, *parts, wg, wu)],
         [dma(2)],
-        3 * rows * width * hidden,
-        3 * rows * width + 8 * width * hidden + 8 * rows * hidden,
-        {4: 3, 5: 4},
+        3 * rows * width * hidden // 4,
+        rows * width + 2 * width * hidden + 16 * rows * hidden,
+        {4: 1, 5: 2, 6: 3, 7: 4},
     )
     act, active, slope, x = call(
         pre_late_body,
@@ -416,22 +465,24 @@
         rows * width + 4 * width * hidden + 3 * rows * hidden,
         {7 + i: i for i in range(4)},
     )
+    y_rows = ((rows, width), BF16, VMEM)
     (y,) = call(
         functools.partial(scale_early_body, experts),
-        [((rows, width), BF16, VMEM)],
-        [(place, SMEM)] + anys(y_early),
-        [pltpu.VMEM((6 * tok, width + LANES), BF16), dma(6)],
+        [y_rows],
+        [(place, SMEM)] + anys((y_early[0], y_early[1], y_early[3], y_early[4])),
+        [pltpu.VMEM((4 * tok, width + LANES), BF16), dma(4)],
         rows * width,
-        4 * rows * width,
+        3 * rows * width,
     )
     piece = (2, half, share)
-    (part,) = call(
-        down_early_body,
-        [((4, half, share), F32, VMEM)],
-        [(place, SMEM), (act, VMEM), (y, VMEM)],
-        [],
+    part, y = call(
+        functools.partial(down_early_body, experts),
+        [((4, half, share), F32, VMEM), y_rows],
+        [(place, SMEM)] + anys((y_early[2], y_early[5])) + [(act, VMEM), (y, VMEM)],
+        [pltpu.VMEM((2 * tok, width + LANES), BF16), dma(2)],
         3 * rows * width * hidden // 4,
         2 * (rows * width + rows * hidden + width * hidden),
+        {4: 1},
     )
     send_a, send_b, y = call(
         functools.partial(down_send_body, experts),

time: 265 us -> 265 us (level)
    ppermute x12, waiting for transfers between devices: 66 us -> 53.8 us  [hop(): lax.ppermute(block, 'expert', [(2 * a + c, 2 * b + c) for a, b in moves f...]
    ppermute x10, waiting for transfers between devices: 57.3 us -> 62.2 us  [to_y(): return lax.ppermute(block, 'dp', [(i, i ^ 2) for i in range(4)])]
    ppermute x10, waiting for transfers between devices: 12.9 us -> 17.8 us  [to_x(): return lax.ppermute(block, 'dp', [(i, i ^ 1) for i in range(4)])]
    pallas_call x14 -> x15, Pallas kernels: 49.1 us -> 50.9 us  [call(): pl.pallas_call(body, input_output_aliases=aliases or {}, out_shape=[jax.S...]
    unnamed x84 -> x82, local copies, waits for them, and re-layouts: 19.7 us -> 19.3 us
  transfers between devices with their start and end apart: 43 -> 43, of which waited for: 14 -> 15; matrix products, arithmetic and copies ran while one was open for 1% -> 2% of each run, Pallas kernels for 13% -> 14%
where the time goes in v9:
time: 265 us; the launch traced here: 264 us
  waiting for transfers between devices  134 us (51%)
  starting transfers between devices  52.9 us (20%)
  Pallas kernels  50.9 us (19%)
  local copies, waits for them, and re-layouts  20.5 us (8%)
  other arithmetic  4.37 us (2%)
    ppermute x10, waiting for transfers between devices, to_y(): return lax.ppermute(block, 'dp', [(i, i ^ 2) for i in range(4)])  62.2 us
    ppermute x12, waiting for transfers between devices, hop(): lax.ppermute(block, 'expert', [(2 * a + c, 2 * b + c) for a, b in moves f...  53.8 us
    pallas_call x15, Pallas kernels, call(): pl.pallas_call(body, input_output_aliases=aliases or {}, out_shape=[jax.S...  50.9 us
    ppermute x12, starting transfers between devices, hop(): lax.ppermute(block, 'expert', [(2 * a + c, 2 * b + c) for a, b in moves f...  23.8 us
    unnamed x82, local copies, waits for them, and re-layouts  19.3 us
    ppermute x10, waiting for transfers between devices, to_x(): return lax.ppermute(block, 'dp', [(i, i ^ 1) for i in range(4)])  17.8 us
    ppermute x10, starting transfers between devices, to_y(): return lax.ppermute(block, 'dp', [(i, i ^ 2) for i in range(4)])  10.9 us
    ppermute x10, starting transfers between devices, to_x(): return lax.ppermute(block, 'dp', [(i, i ^ 1) for i in range(4)])  10.6 us
  transfers between devices with their start and end apart: 43, of which 15 were waited for; matrix products, arithmetic and copies ran while one was open for 2% of the time, Pallas kernels for 14%

profile of v9, /device:TPU:0, one launch (start us, length us, event | category | flops | bytes accessed | tf_op | source)
XLA Modules:
  0.0 263.8 jit_solution(10639030757865403267)
XLA Ops:
  0.7 4.1 %collective-permute-start.6 = (bf16[128,2048]{1,0:T(8,128)(2,1)}, bf16[128,2048]{1,0:T(8,128)(2,1)S(1)}, u32[]{:S(2)}, u32[]{:S(2)}) collective-permute-start(bf16[128,2048]{1,0:T(8,128)(2,1)} %tokens.1), channel_id=1, source_target_pairs={{0,4},{1,5},{2,6},{3,7},{4,0},{5,1},{6,2},{7,3},{8,12},{9,13},{10,... | collective-permute-start | bytes 1572872 | tf_op jit(solution)/shard_map/ppermute | solution.py:381
  4.8 1.2 slice_bitcast_fusion.8
  6.0 1.6 collective-permute-start.24
  7.5 1.5 collective-permute-start.27
  9.0 1.6 collective-permute-start.14
  10.6 6.0 %collective-permute-done.24.refs_1_ = bf16[384,512]{1,0:T(8,128)(2,1)S(1)} collective-permute-done((bf16[384,512]{1,0:T(8,128)(2,1)S(1)}, bf16[384,512]{1,0:T(8,128)(2,1)S(1)}, u32[]{:S(2)}, u32[]{:S(2)}) %collective-permute-start.24) | collective-permute-done | bytes 393248 | tf_op jit(solution)/shard_map/ppermute | solution.py:375
  17.4 1.0 copy-done.30
  19.9 4.2 %collective-permute-start.1 = (bf16[128,2176]{1,0:T(8,128)(2,1)S(1)}, bf16[128,2176]{1,0:T(8,128)(2,1)}, u32[]{:S(2)}, u32[]{:S(2)}) collective-permute-start(bf16[128,2176]{1,0:T(8,128)(2,1)S(1)} %shard_map.102.refs_0_), channel_id=1, source_target_pairs={{0,4},{1,5},{2,6},{3,7},{4,0},{5,1},{6,2},{7,3},{8,12},{9,13},{10,... | collective-permute-start | bytes 1671176 | tf_op jit(solution)/shard_map/ppermute | solution.py:381
  24.2 5.7 %collective-permute-done.6.refs_0_ = bf16[128,2048]{1,0:T(8,128)(2,1)S(1)} collective-permute-done((bf16[128,2048]{1,0:T(8,128)(2,1)}, bf16[128,2048]{1,0:T(8,128)(2,1)S(1)}, u32[]{:S(2)}, u32[]{:S(2)}) %collective-permute-start.6) | collective-permute-done | bytes 524320 | tf_op jit(solution)/shard_map/ppermute | solution.py:381
  29.9 2.2 collective-permute-done.14.refs_1_
  34.2 30.0 %collective-permute-done.1.refs_1_ = bf16[128,2176]{1,0:T(8,128)(2,1)} collective-permute-done((bf16[128,2176]{1,0:T(8,128)(2,1)S(1)}, bf16[128,2176]{1,0:T(8,128)(2,1)}, u32[]{:S(2)}, u32[]{:S(2)}) %collective-permute-start.1) | collective-permute-done | bytes 557088 | tf_op jit(solution)/shard_map/ppermute | solution.py:381
  64.3 1.8 collective-permute-start.12
  66.1 0.8 copy-done.7
  66.9 1.5 collective-permute-start.18
  69.4 0.8 copy-done.20
  70.3 14.4 %collective-permute-done.12.refs_8_ = bf16[512,768]{1,0:T(8,128)(2,1)S(1)} collective-permute-done((bf16[512,768]{1,0:T(8,128)(2,1)S(1)}, bf16[512,768]{1,0:T(8,128)(2,1)S(1)}, u32[]{:S(2)}, u32[]{:S(2)}) %collective-permute-start.12) | collective-permute-done | bytes 786464 | tf_op jit(solution)/shard_map/ppermute | solution.py:378
  84.7 1.3 collective-permute-start.7
  88.3 10.7 %collective-permute-done.19.refs_7_ = bf16[512,768]{1,0:T(8,128)(2,1)S(1)} collective-permute-done((bf16[512,768]{1,0:T(8,128)(2,1)S(1)}, bf16[512,768]{1,0:T(8,128)(2,1)S(1)}, u32[]{:S(2)}, u32[]{:S(2)}) %collective-permute-start.19) | collective-permute-done | bytes 786464 | tf_op jit(solution)/shard_map/ppermute | solution.py:378
  99.0 0.9 copy-done.1
  99.9 0.8 copy-done.26
  102.0 0.8 copy-done.28
  102.8 1.3 collective-permute-start.2
  104.1 1.4 collective-permute-start.11
  106.3 1.5 collective-permute-start.13
  107.8 0.8 copy-done.9
  108.6 1.5 collective-permute-start.3
  110.9 1.9 collective-permute-start.9
  113.0 1.2 copy-done.4
  114.2 1.1 copy-done.6
  115.3 1.0 copy-done.15
  117.5 1.0 copy-done.23
  118.6 1.0 copy-done.27
  119.6 1.0 copy-done.29
  120.7 1.0 shard_map.104
  121.7 2.4 collective-permute-start.4
  124.2 4.7 %shard_map.105 = (f32[1024,768]{1,0:T(8,128)S(1)}, f32[1024,768]{1,0:T(8,128)S(1)}) custom-call(s32[3]{0:T(128)S(1)} %pad_add_fusion.place, bf16[1024,2048]{1,0:T(8,128)(2,1)S(1)} %get-tuple-element.47.x.refs_2_.refs_9_, bf16[2048,768]{1,0:T(8,128)(2,1)S(1)} %get-tuple-element.48.wg.refs_5_, bf16[2048,768]{1,0:T(8,128)(2,1)S(1)} %get-tuple-element.49.wu.refs_6_), custom_call_target="tpu_custom_call" | custom-call | flops 3623878656 | bytes 20447232 | tf_op jit(solution)/shard_map/pallas_call | solution.py:31
  129.0 2.1 shard_map.108.refs_3_
  132.4 1.3 collective-permute-start.28
  133.7 1.5 collective-permute-start.29
  135.2 4.4 %shard_map.106 = (bf16[1024,768]{1,0:T(8,128)(2,1)S(1)}, f32[1024,768]{1,0:T(8,128)S(1)}, f32[1024,768]{1,0:T(8,128)S(1)}, bf16[2048,768]{1,0:T(8,128)(2,1)S(1)}, bf16[2048,768]{1,0:T(8,128)(2,1)S(1)}) custom-call(s32[3]{0:T(128)S(1)} %pad_add_fusion.place, ...), custom_call_target="tpu_custom_call", output_to_operand_aliasing={{1}: (4, {}), {2}: (5, {}), {3}: (6, {}), {4}: (7, {})} | custom-call | flops 1207959552 | bytes 17825792 | tf_op jit(solution)/shard_map/pallas_call | solution.py:31
  139.7 4.0 %shard_map.107 = (bf16[1024,768]{1,0:T(8,128)(2,1)S(1)}, f32[1024,768]{1,0:T(8,128)S(1)}, f32[1024,768]{1,0:T(8,128)S(1)}, bf16[1024,2048]{1,0:T(8,128)(2,1)S(1)}) custom-call(s32[3]{0:T(128)S(1)} %pad_add_fusion.place, bf16[128,2048]{1,0:T(8,128)(2,1)S(1)} %copy-done.17, ...), custom_call_target="tpu_custom_call", output_to_operand_aliasing={{0}: (7, {}), {1}: (8, {}), {2}: (9, {}), {3}: (10, {})} | custom-call | flops 1610612736 | bytes 10747904 | tf_op jit(solution)/shard_map/pallas_call | solution.py:31
  143.8 2.5 shard_map.109
  146.3 2.6 shard_map.110
  148.9 2.0 collective-permute-done.28.refs_5_
  150.9 6.3 %shard_map.111 = (bf16[1024,768]{1,0:T(8,128)(2,1)S(1)}, bf16[1024,768]{1,0:T(8,128)(2,1)S(1)}) custom-call(s32[3]{0:T(128)S(1)} %pad_add_fusion.place, bf16[1024,2048]{1,0:T(8,128)(2,1)S(1)} %get-tuple-element.60.y, f32[1024,768]{1,0:T(8,128)S(1)} %get-tuple-element.61.active, f32[1024,768]{1,0:T(8,128)S(1)} %get-tuple-element.62.slope, ...), custom_call_target="tpu_custom_call" | custom-call | flops 3221225472 | bytes 16777216 | tf_op jit(solution)/shard_map/pallas_call | solution.py:31
  157.2 8.1 %shard_map.112 = (bf16[512,2048]{1,0:T(8,128)(2,1)S(1)}, bf16[512,2048]{1,0:T(8,128)(2,1)S(1)}) custom-call(bf16[1024,768]{1,0:T(8,128)(2,1)S(1)} %get-tuple-element.63.gate_delta.gd, bf16[1024,768]{1,0:T(8,128)(2,1)S(1)} %get-tuple-element.64.up_delta.ud, bf16[2048,768]{1,0:T(8,128)(2,1)S(1)} %get-tuple-element.52.refs_4_.wg, ...), custom_call_target="tpu_custom_call" | custom-call | flops 6442450944 | bytes 13631488 | tf_op jit(solution)/shard_map/pallas_call | solution.py:31
  165.4 1.6 collective-permute-start.39
  167.5 5.3 %shard_map.114 = (bf16[2,512,768]{2,1,0:T(8,128)(2,1)S(1)}, bf16[2,512,768]{2,1,0:T(8,128)(2,1)S(1)}) custom-call(s32[3]{0:T(128)S(1)} %pad_add_fusion.place, bf16[1024,2048]{1,0:T(8,128)(2,1)S(1)} %get-tuple-element.67.x, bf16[1024,768]{1,0:T(8,128)(2,1)S(1)} %get-tuple-element.63.gate_delta.gd, bf16[1024,768]{1,0:T(8,128)(2,1)S(1)} %get-tuple-element.64.up_delta.ud), custom_call_target="tpu_custom_call" | custom-call | flops 3221225472 | bytes 10485760 | tf_op jit(solution)/shard_map/pallas_call | solution.py:31
  172.8 1.6 collective-permute-start.36
  174.9 2.4 shard_map.116
  177.3 5.3 %shard_map.113 = (bf16[512,768]{1,0:T(8,128)(2,1)S(1)}, bf16[512,768]{1,0:T(8,128)(2,1)S(1)}, bf16[512,768]{1,0:T(8,128)(2,1)S(1)}, bf16[512,768]{1,0:T(8,128)(2,1)S(1)}) custom-call(s32[3]{0:T(128)S(1)} %pad_add_fusion.place, bf16[1024,2048]{1,0:T(8,128)(2,1)S(1)} %get-tuple-element.67.x, bf16[1024,768]{1,0:T(8,128)(2,1)S(1)} %get-tuple-element.63.gate_delta.gd, ...), custom_call_target="tpu_custom_call" | custom-call | flops 3221225472 | bytes 10485760 | tf_op jit(solution)/shard_map/pallas_call | solution.py:31
  182.5 3.4 %collective-permute-done.39 = bf16[2,384,512]{2,1,0:T(8,128)(2,1)S(1)} collective-permute-done((bf16[2,384,512]{2,1,0:T(8,128)(2,1)S(1)}, bf16[2,384,512]{2,1,0:T(8,128)(2,1)S(1)}, u32[]{:S(2)}, u32[]{:S(2)}) %collective-permute-start.39) | collective-permute-done | bytes 786464 | tf_op jit(solution)/shard_map/ppermute | solution.py:375
  189.1 4.1 %collective-permute-start.33 = (bf16[128,2048]{1,0:T(8,128)(2,1)S(1)}, bf16[128,2048]{1,0:T(8,128)(2,1)S(1)}, u32[]{:S(2)}, u32[]{:S(2)}) collective-permute-start(bf16[128,2048]{1,0:T(8,128)(2,1)S(1)} %get-tuple-element.85), channel_id=1, source_target_pairs={{0,2},{1,3},{6,4},{7,5},{8,10},{9,11},{14,12},{15,13},{16,18},{17,... | collective-permute-start | bytes 1572872 | tf_op jit(solution)/shard_map/ppermute | solution.py:381
  193.2 27.9 %collective-permute-done.36 = bf16[2,512,768]{2,1,0:T(8,128)(2,1)S(1)} collective-permute-done((bf16[2,512,768]{2,1,0:T(8,128)(2,1)S(1)}, bf16[2,512,768]{2,1,0:T(8,128)(2,1)S(1)}, u32[]{:S(2)}, u32[]{:S(2)}) %collective-permute-start.36) | collective-permute-done | bytes 1572896 | tf_op jit(solution)/shard_map/ppermute | solution.py:378
  224.1 5.4 %collective-permute-done.40 = bf16[384,512]{1,0:T(8,128)(2,1)S(1)} collective-permute-done((bf16[384,512]{1,0:T(8,128)(2,1)S(1)}, bf16[384,512]{1,0:T(8,128)(2,1)S(1)}, u32[]{:S(2)}, u32[]{:S(2)}) %collective-permute-start.40) | collective-permute-done | bytes 393248 | tf_op jit(solution)/shard_map/ppermute | solution.py:378
  229.5 2.1 collective-permute-start.32
  231.6 3.1 %collective-permute-start.34 = (bf16[128,2048]{1,0:T(8,128)(2,1)S(1)}, bf16[128,2048]{1,0:T(8,128)(2,1)S(1)}, u32[]{:S(2)}, u32[]{:S(2)}) collective-permute-start(bf16[128,2048]{1,0:T(8,128)(2,1)S(1)} %add_convert_fusion.2), channel_id=1, source_target_pairs={{0,4},{1,5},{2,6},{3,7},{4,0},{5,1},{6,2},{7,3},{8,12},{9,13},{10,... | collective-permute-start | bytes 1572872 | tf_op jit(solution)/shard_map/ppermute | solution.py:381
  235.0 0.9 maximum_bitcast_fusion
  235.9 8.4 %collective-permute-done.38.up_last = bf16[512,768]{1,0:T(8,128)(2,1)S(1)} collective-permute-done((bf16[512,768]{1,0:T(8,128)(2,1)S(1)}, bf16[512,768]{1,0:T(8,128)(2,1)S(1)}, u32[]{:S(2)}, u32[]{:S(2)}) %collective-permute-start.38) | collective-permute-done | bytes 786464 | tf_op jit(solution)/shard_map/ppermute | solution.py:375
  244.3 1.2 collective-permute-done.37.gate_last
  245.5 1.3 shard_map.115
  246.8 1.1 collective-permute-done.32
  247.9 14.7 %collective-permute-done.34 = bf16[128,2048]{1,0:T(8,128)(2,1)S(1)} collective-permute-done((bf16[128,2048]{1,0:T(8,128)(2,1)S(1)}, bf16[128,2048]{1,0:T(8,128)(2,1)S(1)}, u32[]{:S(2)}, u32[]{:S(2)}) %collective-permute-start.34) | collective-permute-done | bytes 524320 | tf_op jit(solution)/shard_map/ppermute | solution.py:381
  262.6 1.1 add_convert_fusion.1
  (132 shorter events, 20.9 us)
Async XLA Ops:
  0.6 32.3 %copy-start.3 = (bf16[1,512,768]{2,1,0:T(8,128)(2,1)S(1)}, bf16[1,512,768]{2,1,0:T(8,128)(2,1)}, u32[]{:S(2)}) copy-start(bf16[1,512,768]{2,1,0:T(8,128)(2,1)} %param.11) | copy-start | bytes 2359300
  0.6 63.6 %copy-start.5 = (bf16[1,512,768]{2,1,0:T(8,128)(2,1)S(1)}, bf16[1,512,768]{2,1,0:T(8,128)(2,1)}, u32[]{:S(2)}) copy-start(bf16[1,512,768]{2,1,0:T(8,128)(2,1)} %param.12) | copy-start | bytes 2359300
  0.7 29.3 %collective-permute-start.6 = (bf16[128,2048]{1,0:T(8,128)(2,1)}, bf16[128,2048]{1,0:T(8,128)(2,1)S(1)}, u32[]{:S(2)}, u32[]{:S(2)}) collective-permute-start(bf16[128,2048]{1,0:T(8,128)(2,1)} %tokens.1), channel_id=1, source_target_pairs={{0,4},{1,5},{2,6},{3,7},{4,0},{5,1},{6,2},{7,3},{8,12},{9,13},{10,... | collective-permute-start | bytes 1572872 | tf_op jit(solution)/shard_map/ppermute | solution.py:381
  6.0 106.9 %copy-start.37 = (bf16[384,512]{1,0:T(8,128)(2,1)}, bf16[384,512]{1,0:T(8,128)(2,1)S(1)}, u32[]{:S(2)}) copy-start(bf16[384,512]{1,0:T(8,128)(2,1)S(1)} %get-tuple-element.91) | copy-start | bytes 1179652
  6.0 106.9 %copy-start.39 = (bf16[384,512]{1,0:T(8,128)(2,1)}, bf16[384,512]{1,0:T(8,128)(2,1)S(1)}, u32[]{:S(2)}) copy-start(bf16[384,512]{1,0:T(8,128)(2,1)S(1)} %get-tuple-element.90) | copy-start | bytes 1179652
  6.0 10.6 %collective-permute-start.24 = (bf16[384,512]{1,0:T(8,128)(2,1)S(1)}, bf16[384,512]{1,0:T(8,128)(2,1)S(1)}, u32[]{:S(2)}, u32[]{:S(2)}) collective-permute-start(bf16[384,512]{1,0:T(8,128)(2,1)S(1)} %get-tuple-element.91), channel_id=1, source_target_pairs={{0,8},{8,0},{16,24},{24,16},{1,9},{9,1},{17,25},{25,17},{2,10},{10... | collective-permute-start | bytes 1179656 | tf_op jit(solution)/shard_map/ppermute | solution.py:375
  7.5 12.4 %collective-permute-start.27 = (bf16[384,512]{1,0:T(8,128)(2,1)S(1)}, bf16[384,512]{1,0:T(8,128)(2,1)S(1)}, u32[]{:S(2)}, u32[]{:S(2)}) collective-permute-start(bf16[384,512]{1,0:T(8,128)(2,1)S(1)} %get-tuple-element.90), channel_id=1, source_target_pairs={{0,16},{8,24},{16,0},{24,8},{1,17},{9,25},{17,1},{25,9},{2,18},{10... | collective-permute-start | bytes 1179656 | tf_op jit(solution)/shard_map/ppermute | solution.py:378
  9.0 23.1 %collective-permute-start.14 = (bf16[128,2048]{1,0:T(8,128)(2,1)}, bf16[128,2048]{1,0:T(8,128)(2,1)S(1)}, u32[]{:S(2)}, u32[]{:S(2)}) collective-permute-start(bf16[128,2048]{1,0:T(8,128)(2,1)} %tokens.1), channel_id=1, source_target_pairs={{0,2},{1,3},{2,0},{3,1},{4,6},{5,7},{6,4},{7,5},{8,10},{9,11},{10,... | collective-permute-start | bytes 1572872 | tf_op jit(solution)/shard_map/ppermute | solution.py:381
  10.6 21.5 %collective-permute-start.15 = (bf16[128,2048]{1,0:T(8,128)(2,1)}, bf16[128,2048]{1,0:T(8,128)(2,1)S(1)}, u32[]{:S(2)}, u32[]{:S(2)}) collective-permute-start(bf16[128,2048]{1,0:T(8,128)(2,1)} %tokens.1), channel_id=1, source_target_pairs={{0,1},{1,0},{2,3},{3,2},{4,5},{5,4},{6,7},{7,6},{8,9},{9,8},{10,11... | collective-permute-start | bytes 1572872 | tf_op jit(solution)/shard_map/ppermute | solution.py:384
  16.6 16.9 %collective-permute-start.5 = (bf16[128,2048]{1,0:T(8,128)(2,1)}, bf16[128,2048]{1,0:T(8,128)(2,1)S(1)}, u32[]{:S(2)}, u32[]{:S(2)}) collective-permute-start(bf16[128,2048]{1,0:T(8,128)(2,1)} %tokens.1), channel_id=1, source_target_pairs={{2,4},{3,5},{4,2},{5,3},{10,12},{11,13},{12,10},{13,11},{18,20},{1... | collective-permute-start | bytes 1572872 | tf_op jit(solution)/shard_map/ppermute | solution.py:381
  17.4 1.0 copy-start.30
  19.9 90.2 %copy-start.33 = (bf16[384,512]{1,0:T(8,128)(2,1)}, bf16[384,512]{1,0:T(8,128)(2,1)S(1)}, u32[]{:S(2)}) copy-start(bf16[384,512]{1,0:T(8,128)(2,1)S(1)} %collective-permute-done.27.refs_4_) | copy-start | bytes 1179652
  19.9 44.3 %collective-permute-start.1 = (bf16[128,2176]{1,0:T(8,128)(2,1)S(1)}, bf16[128,2176]{1,0:T(8,128)(2,1)}, u32[]{:S(2)}, u32[]{:S(2)}) collective-permute-start(bf16[128,2176]{1,0:T(8,128)(2,1)S(1)} %shard_map.102.refs_0_), channel_id=1, source_target_pairs={{0,4},{1,5},{2,6},{3,7},{4,0},{5,1},{6,2},{7,3},{8,12},{9,13},{10,... | collective-permute-start | bytes 1671176 | tf_op jit(solution)/shard_map/ppermute | solution.py:381
  29.9 36.2 %collective-permute-start.22 = (bf16[128,2176]{1,0:T(8,128)(2,1)S(1)}, bf16[128,2176]{1,0:T(8,128)(2,1)S(1)}, u32[]{:S(2)}, u32[]{:S(2)}) collective-permute-start(bf16[128,2176]{1,0:T(8,128)(2,1)S(1)} %shard_map.102.refs_0_), channel_id=1, source_target_pairs={{0,1},{1,0},{2,3},{3,2},{4,5},{5,4},{6,7},{7,6},{8,9},{9,8},{10,11... | collective-permute-start | bytes 1671176 | tf_op jit(solution)/shard_map/ppermute | solution.py:384
  32.2 36.3 %collective-permute-start.20 = (bf16[128,2176]{1,0:T(8,128)(2,1)S(1)}, bf16[128,2176]{1,0:T(8,128)(2,1)S(1)}, u32[]{:S(2)}, u32[]{:S(2)}) collective-permute-start(bf16[128,2176]{1,0:T(8,128)(2,1)S(1)} %shard_map.102.refs_0_), channel_id=1, source_target_pairs={{0,2},{1,3},{2,0},{3,1},{4,6},{5,7},{6,4},{7,5},{8,10},{9,11},{10,... | collective-permute-start | bytes 1671176 | tf_op jit(solution)/shard_map/ppermute | solution.py:381
  33.0 36.0 %collective-permute-start.10 = (bf16[512,768]{1,0:T(8,128)(2,1)S(1)}, bf16[512,768]{1,0:T(8,128)(2,1)S(1)}, u32[]{:S(2)}, u32[]{:S(2)}) collective-permute-start(bf16[512,768]{1,0:T(8,128)(2,1)S(1)} %bitcast.55), channel_id=1, source_target_pairs={{0,8},{8,0},{16,24},{24,16},{1,9},{9,1},{17,25},{25,17},{2,10},{10... | collective-permute-start | bytes 2359304 | tf_op jit(solution)/shard_map/ppermute | solution.py:375
  33.6 35.4 %collective-permute-start = (bf16[128,2176]{1,0:T(8,128)(2,1)S(1)}, bf16[128,2176]{1,0:T(8,128)(2,1)S(1)}, u32[]{:S(2)}, u32[]{:S(2)}) collective-permute-start(bf16[128,2176]{1,0:T(8,128)(2,1)S(1)} %shard_map.102.refs_0_), channel_id=1, source_target_pairs={{2,4},{3,5},{4,2},{5,3},{10,12},{11,13},{12,10},{13,11},{18,20},{1... | collective-permute-start | bytes 1671176 | tf_op jit(solution)/shard_map/ppermute | solution.py:381
  64.3 20.4 %collective-permute-start.12 = (bf16[512,768]{1,0:T(8,128)(2,1)S(1)}, bf16[512,768]{1,0:T(8,128)(2,1)S(1)}, u32[]{:S(2)}, u32[]{:S(2)}) collective-permute-start(bf16[512,768]{1,0:T(8,128)(2,1)S(1)} %bitcast.58), channel_id=1, source_target_pairs={{0,16},{8,24},{16,0},{24,8},{1,17},{9,25},{17,1},{25,9},{2,18},{10... | collective-permute-start | bytes 2359304 | tf_op jit(solution)/shard_map/ppermute | solution.py:378
  66.9 19.9 %collective-permute-start.18 = (bf16[512,768]{1,0:T(8,128)(2,1)S(1)}, bf16[512,768]{1,0:T(8,128)(2,1)S(1)}, u32[]{:S(2)}, u32[]{:S(2)}) collective-permute-start(bf16[512,768]{1,0:T(8,128)(2,1)S(1)} %bitcast.59), channel_id=1, source_target_pairs={{0,8},{8,0},{16,24},{24,16},{1,9},{9,1},{17,25},{25,17},{2,10},{10... | collective-permute-start | bytes 2359304 | tf_op jit(solution)/shard_map/ppermute | solution.py:375
  68.4 30.6 %collective-permute-start.19 = (bf16[512,768]{1,0:T(8,128)(2,1)S(1)}, bf16[512,768]{1,0:T(8,128)(2,1)S(1)}, u32[]{:S(2)}, u32[]{:S(2)}) collective-permute-start(bf16[512,768]{1,0:T(8,128)(2,1)S(1)} %bitcast.56), channel_id=1, source_target_pairs={{0,16},{8,24},{16,0},{24,8},{1,17},{9,25},{17,1},{25,9},{2,18},{10... | collective-permute-start | bytes 2359304 | tf_op jit(solution)/shard_map/ppermute | solution.py:378
  68.9 30.9 %collective-permute-start.16 = (bf16[128,2048]{1,0:T(8,128)(2,1)S(1)}, bf16[128,2048]{1,0:T(8,128)(2,1)S(1)}, u32[]{:S(2)}, u32[]{:S(2)}) collective-permute-start(bf16[128,2048]{1,0:T(8,128)(2,1)S(1)} %collective-permute-done.6.refs_0_), channel_id=1, source_target_pairs={{0,1},{1,0},{2,3},{3,2},{4,5},{5,4},{6,7},{7,6},{8,9},{9,8},{10,11... | collective-permute-start | bytes 1572872 | tf_op jit(solution)/shard_map/ppermute | solution.py:384
  68.9 33.1 %collective-permute-start.17 = (bf16[128,2048]{1,0:T(8,128)(2,1)S(1)}, bf16[128,2048]{1,0:T(8,128)(2,1)S(1)}, u32[]{:S(2)}, u32[]{:S(2)}) collective-permute-start(bf16[128,2048]{1,0:T(8,128)(2,1)S(1)} %collective-permute-done.14.refs_1_), channel_id=1, source_target_pairs={{0,1},{1,0},{2,3},{3,2},{4,5},{5,4},{6,7},{7,6},{8,9},{9,8},{10,11... | collective-permute-start | bytes 1572872 | tf_op jit(solution)/shard_map/ppermute | solution.py:384
  84.7 19.4 %collective-permute-start.7 = (bf16[128,2048]{1,0:T(8,128)(2,1)S(1)}, bf16[128,2048]{1,0:T(8,128)(2,1)}, u32[]{:S(2)}, u32[]{:S(2)}) collective-permute-start(bf16[128,2048]{1,0:T(8,128)(2,1)S(1)} %collective-permute-done.6.refs_0_), channel_id=1, source_target_pairs={{4,6},{5,7},{2,0},{3,1},{12,14},{13,15},{10,8},{11,9},{20,22},{21,... | collective-permute-start | bytes 1572872 | tf_op jit(solution)/shard_map/ppermute | solution.py:381
  86.8 18.7 %collective-permute-start.8 = (bf16[128,2048]{1,0:T(8,128)(2,1)S(1)}, bf16[128,2048]{1,0:T(8,128)(2,1)S(1)}, u32[]{:S(2)}, u32[]{:S(2)}) collective-permute-start(bf16[128,2048]{1,0:T(8,128)(2,1)S(1)} %collective-permute-done.5.refs_0_), channel_id=1, source_target_pairs={{2,3},{3,2},{4,5},{5,4},{10,11},{11,10},{12,13},{13,12},{18,19},{1... | collective-permute-start | bytes 1572872 | tf_op jit(solution)/shard_map/ppermute | solution.py:384
  99.9 7.9 %collective-permute-start.23 = (bf16[128,2176]{1,0:T(8,128)(2,1)}, bf16[128,2176]{1,0:T(8,128)(2,1)S(1)}, u32[]{:S(2)}, u32[]{:S(2)}) collective-permute-start(bf16[128,2176]{1,0:T(8,128)(2,1)} %collective-permute-done.1.refs_1_), channel_id=1, source_target_pairs={{0,1},{1,0},{2,3},{3,2},{4,5},{5,4},{6,7},{7,6},{8,9},{9,8},{10,11... | collective-permute-start | bytes 1671176 | tf_op jit(solution)/shard_map/ppermute | solution.py:384
  100.7 9.4 %collective-permute-start.21 = (bf16[128,2176]{1,0:T(8,128)(2,1)S(1)}, bf16[128,2176]{1,0:T(8,128)(2,1)S(1)}, u32[]{:S(2)}, u32[]{:S(2)}) collective-permute-start(bf16[128,2176]{1,0:T(8,128)(2,1)S(1)} %collective-permute-done.20.refs_0_), channel_id=1, source_target_pairs={{0,1},{1,0},{2,3},{3,2},{4,5},{5,4},{6,7},{7,6},{8,9},{9,8},{10,11... | collective-permute-start | bytes 1671176 | tf_op jit(solution)/shard_map/ppermute | solution.py:384
  102.8 18.9 %collective-permute-start.2 = (bf16[128,2176]{1,0:T(8,128)(2,1)}, bf16[128,2176]{1,0:T(8,128)(2,1)}, u32[]{:S(2)}, u32[]{:S(2)}) collective-permute-start(bf16[128,2176]{1,0:T(8,128)(2,1)} %collective-permute-done.1.refs_1_), channel_id=1, source_target_pairs={{4,6},{5,7},{2,0},{3,1},{12,14},{13,15},{10,8},{11,9},{20,22},{21,... | collective-permute-start | bytes 1671176 | tf_op jit(solution)/shard_map/ppermute | solution.py:381
  104.1 28.3 %collective-permute-start.11 = (bf16[512,768]{1,0:T(8,128)(2,1)S(1)}, bf16[512,768]{1,0:T(8,128)(2,1)}, u32[]{:S(2)}, u32[]{:S(2)}) collective-permute-start(bf16[512,768]{1,0:T(8,128)(2,1)S(1)} %collective-permute-done.10.refs_5_), channel_id=1, source_target_pairs={{0,16},{8,24},{16,0},{24,8},{1,17},{9,25},{17,1},{25,9},{2,18},{10... | collective-permute-start | bytes 2359304 | tf_op jit(solution)/shard_map/ppermute | solution.py:378
  106.3 27.4 %collective-permute-start.13 = (bf16[512,768]{1,0:T(8,128)(2,1)S(1)}, bf16[512,768]{1,0:T(8,128)(2,1)}, u32[]{:S(2)}, u32[]{:S(2)}) collective-permute-start(bf16[512,768]{1,0:T(8,128)(2,1)S(1)} %collective-permute-done.12.refs_8_), channel_id=1, source_target_pairs={{0,8},{8,0},{16,24},{24,16},{1,9},{9,1},{17,25},{25,17},{2,10},{10... | collective-permute-start | bytes 2359304 | tf_op jit(solution)/shard_map/ppermute | solution.py:375
  108.6 22.4 %collective-permute-start.3 = (bf16[128,2176]{1,0:T(8,128)(2,1)S(1)}, bf16[128,2176]{1,0:T(8,128)(2,1)}, u32[]{:S(2)}, u32[]{:S(2)}) collective-permute-start(bf16[128,2176]{1,0:T(8,128)(2,1)S(1)} %collective-permute-done.refs_0_), channel_id=1, source_target_pairs={{2,3},{3,2},{4,5},{5,4},{10,11},{11,10},{12,13},{13,12},{18,19},{1... | collective-permute-start | bytes 1671176 | tf_op jit(solution)/shard_map/ppermute | solution.py:384
  110.9 20.8 %collective-permute-start.9 = (bf16[128,2048]{1,0:T(8,128)(2,1)}, bf16[128,2048]{1,0:T(8,128)(2,1)}, u32[]{:S(2)}, u32[]{:S(2)}) collective-permute-start(bf16[128,2048]{1,0:T(8,128)(2,1)} %collective-permute-done.7.refs_1_), channel_id=1, source_target_pairs={{0,1},{1,0},{6,7},{7,6},{8,9},{9,8},{14,15},{15,14},{16,17},{17,16... | collective-permute-start | bytes 1572872 | tf_op jit(solution)/shard_map/ppermute | solution.py:384
  112.9 4.2 %copy-start.2 = (bf16[512,768]{1,0:T(8,128)(2,1)S(1)}, bf16[512,768]{1,0:T(8,128)(2,1)}, u32[]{:S(2)}) copy-start(bf16[512,768]{1,0:T(8,128)(2,1)} %copy-done.1) | copy-start | bytes 2359300
  113.0 1.2 copy-start.4
  114.2 1.1 copy-start.6
  116.3 1.2 copy-start.21
  121.7 24.6 %collective-permute-start.4 = (bf16[128,2176]{1,0:T(8,128)(2,1)}, bf16[128,2176]{1,0:T(8,128)(2,1)S(1)}, u32[]{:S(2)}, u32[]{:S(2)}) collective-permute-start(bf16[128,2176]{1,0:T(8,128)(2,1)} %collective-permute-done.2.refs_1_), channel_id=1, source_target_pairs={{0,1},{1,0},{6,7},{7,6},{8,9},{9,8},{14,15},{15,14},{16,17},{17,16... | collective-permute-start | bytes 1671176 | tf_op jit(solution)/shard_map/ppermute | solution.py:384
  124.1 4.8 %copy-start.8 = (bf16[128,2176]{1,0:T(8,128)(2,1)S(1)}, bf16[128,2176]{1,0:T(8,128)(2,1)}, u32[]{:S(2)}) copy-start(bf16[128,2176]{1,0:T(8,128)(2,1)} %copy-done.7) | copy-start | bytes 1671172
  124.1 4.8 %copy-start.10 = (bf16[128,2176]{1,0:T(8,128)(2,1)S(1)}, bf16[128,2176]{1,0:T(8,128)(2,1)}, u32[]{:S(2)}) copy-start(bf16[128,2176]{1,0:T(8,128)(2,1)} %copy-done.9) | copy-start | bytes 1671172
  128.9 2.2 copy-start.40
  128.9 2.8 %copy-start.38 = (bf16[384,512]{1,0:T(8,128)(2,1)S(1)}, bf16[384,512]{1,0:T(8,128)(2,1)}, u32[]{:S(2)}) copy-start(bf16[384,512]{1,0:T(8,128)(2,1)} %copy-done.37) | copy-start | bytes 1179652
  128.9 3.5 %copy-start.32 = (bf16[384,512]{1,0:T(8,128)(2,1)S(1)}, bf16[384,512]{1,0:T(8,128)(2,1)}, u32[]{:S(2)}) copy-start(bf16[384,512]{1,0:T(8,128)(2,1)} %copy-done.31) | copy-start | bytes 1179652
  128.9 4.8 %copy-start.34 = (bf16[384,512]{1,0:T(8,128)(2,1)S(1)}, bf16[384,512]{1,0:T(8,128)(2,1)}, u32[]{:S(2)}) copy-start(bf16[384,512]{1,0:T(8,128)(2,1)} %copy-done.33) | copy-start | bytes 1179652
  131.1 17.8 %collective-permute-start.25 = (bf16[384,512]{1,0:T(8,128)(2,1)S(1)}, bf16[384,512]{1,0:T(8,128)(2,1)S(1)}, u32[]{:S(2)}, u32[]{:S(2)}) collective-permute-start(bf16[384,512]{1,0:T(8,128)(2,1)S(1)} %copy-done.40), channel_id=1, source_target_pairs={{0,8},{8,0},{16,24},{24,16},{1,9},{9,1},{17,25},{25,17},{2,10},{10... | collective-permute-start | bytes 1179656 | tf_op jit(solution)/shard_map/ppermute | solution.py:375
  131.7 17.2 %collective-permute-start.26 = (bf16[384,512]{1,0:T(8,128)(2,1)S(1)}, bf16[384,512]{1,0:T(8,128)(2,1)S(1)}, u32[]{:S(2)}, u32[]{:S(2)}) collective-permute-start(bf16[384,512]{1,0:T(8,128)(2,1)S(1)} %copy-done.38), channel_id=1, source_target_pairs={{0,16},{8,24},{16,0},{24,8},{1,17},{9,25},{17,1},{25,9},{2,18},{10... | collective-permute-start | bytes 1179656 | tf_op jit(solution)/shard_map/ppermute | solution.py:378
  132.4 18.5 %collective-permute-start.28 = (bf16[384,512]{1,0:T(8,128)(2,1)S(1)}, bf16[384,512]{1,0:T(8,128)(2,1)S(1)}, u32[]{:S(2)}, u32[]{:S(2)}) collective-permute-start(bf16[384,512]{1,0:T(8,128)(2,1)S(1)} %copy-done.32), channel_id=1, source_target_pairs={{0,16},{8,24},{16,0},{24,8},{1,17},{9,25},{17,1},{25,9},{2,18},{10... | collective-permute-start | bytes 1179656 | tf_op jit(solution)/shard_map/ppermute | solution.py:378
  133.7 17.1 %collective-permute-start.29 = (bf16[384,512]{1,0:T(8,128)(2,1)S(1)}, bf16[384,512]{1,0:T(8,128)(2,1)S(1)}, u32[]{:S(2)}, u32[]{:S(2)}) collective-permute-start(bf16[384,512]{1,0:T(8,128)(2,1)S(1)} %copy-done.34), channel_id=1, source_target_pairs={{0,8},{8,0},{16,24},{24,16},{1,9},{9,1},{17,25},{25,17},{2,10},{10... | collective-permute-start | bytes 1179656 | tf_op jit(solution)/shard_map/ppermute | solution.py:375
  135.2 4.4 %copy-start.17 = (bf16[128,2048]{1,0:T(8,128)(2,1)S(1)}, bf16[128,2048]{1,0:T(8,128)(2,1)}, u32[]{:S(2)}) copy-start(bf16[128,2048]{1,0:T(8,128)(2,1)} %copy-done.16) | copy-start | bytes 1572868
  135.2 4.4 %copy-start.25 = (bf16[128,2048]{1,0:T(8,128)(2,1)S(1)}, bf16[128,2048]{1,0:T(8,128)(2,1)}, u32[]{:S(2)}) copy-start(bf16[128,2048]{1,0:T(8,128)(2,1)} %copy-done.24) | copy-start | bytes 1572868
  139.7 4.1 %copy-start.12 = (bf16[128,2176]{1,0:T(8,128)(2,1)S(1)}, bf16[128,2176]{1,0:T(8,128)(2,1)}, u32[]{:S(2)}) copy-start(bf16[128,2176]{1,0:T(8,128)(2,1)} %copy-done.11) | copy-start | bytes 1671172
  139.7 4.1 %copy-start.14 = (bf16[128,2176]{1,0:T(8,128)(2,1)S(1)}, bf16[128,2176]{1,0:T(8,128)(2,1)}, u32[]{:S(2)}) copy-start(bf16[128,2176]{1,0:T(8,128)(2,1)} %copy-done.13) | copy-start | bytes 1671172
  146.3 4.6 %copy-start = (bf16[1,768,512]{2,1,0:T(8,128)(2,1)S(1)}, bf16[1,768,512]{2,1,0:T(8,128)(2,1)}, u32[]{:S(2)}) copy-start(bf16[1,768,512]{2,1,0:T(8,128)(2,1)} %param.13) | copy-start | bytes 2359300
  165.3 22.9 %collective-permute-start.30 = (bf16[512,2048]{1,0:T(8,128)(2,1)S(1)}, bf16[512,2048]{1,0:T(8,128)(2,1)S(1)}, u32[]{:S(2)}, u32[]{:S(2)}) collective-permute-start(bf16[512,2048]{1,0:T(8,128)(2,1)S(1)} %get-tuple-element.66), channel_id=1, source_target_pairs={{0,1},{1,0},{2,3},{3,2},{4,5},{5,4},{6,7},{7,6},{8,9},{9,8},{10,11... | collective-permute-start | bytes 6291464 | tf_op jit(solution)/shard_map/ppermute | solution.py:384
  165.4 20.5 %collective-permute-start.39 = (bf16[2,384,512]{2,1,0:T(8,128)(2,1)S(1)}, bf16[2,384,512]{2,1,0:T(8,128)(2,1)S(1)}, u32[]{:S(2)}, u32[]{:S(2)}) collective-permute-start(bf16[2,384,512]{2,1,0:T(8,128)(2,1)S(1)} %get-tuple-element.79), channel_id=1, source_target_pairs={{0,8},{8,0},{16,24},{24,16},{1,9},{9,1},{17,25},{25,17},{2,10},{10... | collective-permute-start | bytes 2359304 | tf_op jit(solution)/shard_map/ppermute | solution.py:375
  167.0 20.4 %collective-permute-start.41 = (bf16[2,384,512]{2,1,0:T(8,128)(2,1)S(1)}, bf16[2,384,512]{2,1,0:T(8,128)(2,1)S(1)}, u32[]{:S(2)}, u32[]{:S(2)}) collective-permute-start(bf16[2,384,512]{2,1,0:T(8,128)(2,1)S(1)} %get-tuple-element.82), channel_id=1, source_target_pairs={{0,16},{8,24},{16,0},{24,8},{1,17},{9,25},{17,1},{25,9},{2,18},{10... | collective-permute-start | bytes 2359304 | tf_op jit(solution)/shard_map/ppermute | solution.py:378
  172.8 48.3 %collective-permute-start.36 = (bf16[2,512,768]{2,1,0:T(8,128)(2,1)S(1)}, bf16[2,512,768]{2,1,0:T(8,128)(2,1)S(1)}, u32[]{:S(2)}, u32[]{:S(2)}) collective-permute-start(bf16[2,512,768]{2,1,0:T(8,128)(2,1)S(1)} %get-tuple-element.71), channel_id=1, source_target_pairs={{0,16},{8,24},{16,0},{24,8},{1,17},{9,25},{17,1},{25,9},{2,18},{10... | collective-permute-start | bytes 4718600 | tf_op jit(solution)/shard_map/ppermute | solution.py:378
  174.4 47.7 %collective-permute-start.35 = (bf16[2,512,768]{2,1,0:T(8,128)(2,1)S(1)}, bf16[2,512,768]{2,1,0:T(8,128)(2,1)S(1)}, u32[]{:S(2)}, u32[]{:S(2)}) collective-permute-start(bf16[2,512,768]{2,1,0:T(8,128)(2,1)S(1)} %get-tuple-element.69), channel_id=1, source_target_pairs={{0,8},{8,0},{16,24},{24,16},{1,9},{9,1},{17,25},{25,17},{2,10},{10... | collective-permute-start | bytes 4718600 | tf_op jit(solution)/shard_map/ppermute | solution.py:375
  186.0 43.5 %collective-permute-start.40 = (bf16[384,512]{1,0:T(8,128)(2,1)S(1)}, bf16[384,512]{1,0:T(8,128)(2,1)S(1)}, u32[]{:S(2)}, u32[]{:S(2)}) collective-permute-start(bf16[384,512]{1,0:T(8,128)(2,1)S(1)} %fusion.7), channel_id=1, source_target_pairs={{0,16},{8,24},{16,0},{24,8},{1,17},{9,25},{17,1},{25,9},{2,18},{10... | collective-permute-start | bytes 1179656 | tf_op jit(solution)/shard_map/ppermute | solution.py:378
  187.5 44.1 %collective-permute-start.42 = (bf16[384,512]{1,0:T(8,128)(2,1)S(1)}, bf16[384,512]{1,0:T(8,128)(2,1)S(1)}, u32[]{:S(2)}, u32[]{:S(2)}) collective-permute-start(bf16[384,512]{1,0:T(8,128)(2,1)S(1)} %fusion.4), channel_id=1, source_target_pairs={{0,8},{8,0},{16,24},{24,16},{1,9},{9,1},{17,25},{25,17},{2,10},{10... | collective-permute-start | bytes 1179656 | tf_op jit(solution)/shard_map/ppermute | solution.py:375
  189.1 34.2 %collective-permute-start.33 = (bf16[128,2048]{1,0:T(8,128)(2,1)S(1)}, bf16[128,2048]{1,0:T(8,128)(2,1)S(1)}, u32[]{:S(2)}, u32[]{:S(2)}) collective-permute-start(bf16[128,2048]{1,0:T(8,128)(2,1)S(1)} %get-tuple-element.85), channel_id=1, source_target_pairs={{0,2},{1,3},{6,4},{7,5},{8,10},{9,11},{14,12},{15,13},{16,18},{17,... | collective-permute-start | bytes 1572872 | tf_op jit(solution)/shard_map/ppermute | solution.py:381
  221.5 22.8 %collective-permute-start.38 = (bf16[512,768]{1,0:T(8,128)(2,1)S(1)}, bf16[512,768]{1,0:T(8,128)(2,1)S(1)}, u32[]{:S(2)}, u32[]{:S(2)}) collective-permute-start(bf16[512,768]{1,0:T(8,128)(2,1)S(1)} %get-tuple-element.86), channel_id=1, source_target_pairs={{0,8},{8,0},{16,24},{24,16},{1,9},{9,1},{17,25},{25,17},{2,10},{10... | collective-permute-start | bytes 2359304 | tf_op jit(solution)/shard_map/ppermute | solution.py:375
  222.5 23.0 %collective-permute-start.37 = (bf16[512,768]{1,0:T(8,128)(2,1)S(1)}, bf16[512,768]{1,0:T(8,128)(2,1)S(1)}, u32[]{:S(2)}, u32[]{:S(2)}) collective-permute-start(bf16[512,768]{1,0:T(8,128)(2,1)S(1)} %get-tuple-element.88), channel_id=1, source_target_pairs={{0,16},{8,24},{16,0},{24,8},{1,17},{9,25},{17,1},{25,9},{2,18},{10... | collective-permute-start | bytes 2359304 | tf_op jit(solution)/shard_map/ppermute | solution.py:378
  223.3 23.5 %collective-permute-start.31 = (bf16[128,2048]{1,0:T(8,128)(2,1)S(1)}, bf16[128,2048]{1,0:T(8,128)(2,1)S(1)}, u32[]{:S(2)}, u32[]{:S(2)}) collective-permute-start(bf16[128,2048]{1,0:T(8,128)(2,1)S(1)} %get-tuple-element.85), channel_id=1, source_target_pairs={{2,4},{3,5},{4,2},{5,3},{10,12},{11,13},{12,10},{13,11},{18,20},{1... | collective-permute-start | bytes 1572872 | tf_op jit(solution)/shard_map/ppermute | solution.py:381
  229.5 18.4 %collective-permute-start.32 = (bf16[128,2048]{1,0:T(8,128)(2,1)S(1)}, bf16[128,2048]{1,0:T(8,128)(2,1)S(1)}, u32[]{:S(2)}, u32[]{:S(2)}) collective-permute-start(bf16[128,2048]{1,0:T(8,128)(2,1)S(1)} %get-tuple-element.84), channel_id=1, source_target_pairs={{0,2},{1,3},{2,0},{3,1},{4,6},{5,7},{6,4},{7,5},{8,10},{9,11},{10,... | collective-permute-start | bytes 1572872 | tf_op jit(solution)/shard_map/ppermute | solution.py:381
  231.6 31.0 %collective-permute-start.34 = (bf16[128,2048]{1,0:T(8,128)(2,1)S(1)}, bf16[128,2048]{1,0:T(8,128)(2,1)S(1)}, u32[]{:S(2)}, u32[]{:S(2)}) collective-permute-start(bf16[128,2048]{1,0:T(8,128)(2,1)S(1)} %add_convert_fusion.2), channel_id=1, source_target_pairs={{0,4},{1,5},{2,6},{3,7},{4,0},{5,1},{6,2},{7,3},{8,12},{9,13},{10,... | collective-permute-start | bytes 1572872 | tf_op jit(solution)/shard_map/ppermute | solution.py:381
  (20 other events, 17.2 us)

commit v10 on v9

--- a/solution.py
+++ b/solution.py
@@ -1,5 +1,3 @@
-import functools
-
 import jax
 import jax.numpy as jnp
 from jax import lax
@@ -14,7 +12,6 @@
 VMEM = pl.BlockSpec(memory_space=pltpu.VMEM)
 SMEM = pl.BlockSpec(memory_space=pltpu.SMEM)
 LIMIT = 12 * 1024 * 1024
-LANES = 128
 NN = (((1,), (0,)), ((), ()))
 NT = (((1,), (1,)), ((), ()))
 
@@ -45,19 +42,12 @@
 INNER = ((1, 2), (2, 1))
 
 
-def prep_body(experts, routes, gates, rows, out):
-    tok, width = rows.shape
-    line = lax.broadcasted_iota(jnp.int32, (LANES, tok), 0)
-    term, named = line // experts, line % experts
-    value = jnp.zeros((LANES, tok), F32)
-    for k in range(routes.shape[0]):
-        value += jnp.where(routes[k : k + 1, :] == named, gates[k : k + 1, :], 0.0)
-    high = value.astype(BF16).astype(F32)
-    mid = (value - high).astype(BF16).astype(F32)
-    low = value - high - mid
-    value = jnp.where(term == 0, high, jnp.where(term == 1, mid, jnp.where(term == 2, low, 0.0)))
-    out[:, :width] = rows[...]
-    out[:, width:] = jnp.transpose(value).astype(BF16)
+def prep_body(place, routes, gates, *outs):
+    for k, out in enumerate(outs):
+        value = jnp.zeros(out.shape, F32)
+        for i in range(routes.shape[0]):
+            value += jnp.where(routes[i : i + 1, :] == (place[2] ^ k), gates[i : i + 1, :], 0.0)
+        out[...] = value
 
 
 class Copies:
@@ -193,26 +183,24 @@
     pre_blocks(x, 3 * count, count, wg, wu, act, active, slope)
 
 
-def scale(experts, expert, raw, y, row):
-    tok, width = raw.shape[0], y.shape[1]
-    lane = lax.broadcasted_iota(jnp.int32, (tok, LANES), 1)
-    mine = jnp.logical_and(lane % experts == expert, lane < 3 * experts)
-    gate = jnp.sum(jnp.where(mine, raw[:, width:].astype(F32), 0.0), axis=1, keepdims=True)
-    y[row : row + tok, :] = (raw[:, :width].astype(F32) * gate).astype(BF16)
-
-
-def load_scaled(experts, expert, copies, pieces, raw, y, blocks):
+def scale(gate, raw, y, row):
+    tok = raw.shape[0]
+    column = jnp.transpose(jnp.broadcast_to(gate[...], (tok, tok)))[:, :1]
+    y[row : row + tok, :] = (raw[...].astype(F32) * column).astype(BF16)
+
+
+def load_scaled(copies, pieces, gates, raw, y, blocks):
     tok = pieces[0].shape[0]
     at = [raw.at[pl.ds(i * tok, tok)] for i in range(len(pieces))]
     started = [copies.start(src, dst) for src, dst in zip(pieces, at)]
-    for copy, dst, block in zip(started, at, blocks):
+    for copy, gate, dst, block in zip(started, gates, at, blocks):
         copy.wait()
-        scale(experts, expert, dst, y, block * tok)
-
-
-def scale_early_body(experts, place, *refs):
-    y, raw, sems = refs[4:]
-    load_scaled(experts, place[2], Copies(sems), refs[:4], raw, y, (0, 1, 3, 4))
+        scale(gate, dst, y, block * tok)
+
+
+def scale_early_body(*refs):
+    y, raw, sems = refs[8:]
+    load_scaled(Copies(sems), refs[:4], refs[4:8], raw, y, (0, 1, 3, 4))
 
 
 def down_blocks(place, act, y, first, count, wanted, put):
@@ -227,10 +215,10 @@
                 put(target, mm(turned, y[rows, cols], NN))
 
 
-def down_early_body(experts, place, *refs):
-    pieces, act = refs[:2], refs[2]
-    part, y, raw, sems = refs[4:]
-    load_scaled(experts, place[2], Copies(sems), pieces, raw, y, (2, 5))
+def down_early_body(place, *refs):
+    pieces, gates, act = refs[:2], refs[2:4], refs[4]
+    part, y, raw, sems = refs[6:]
+    load_scaled(Copies(sems), pieces, gates, raw, y, (2, 5))
 
     def put(target, value):
         part[target] = value
@@ -239,16 +227,16 @@
     down_blocks(place, act, y, 0, early, ((0, 1, 0), (0, 3, 1), (1, 2, 2), (1, 3, 3)), put)
 
 
-def down_send_body(experts, place, *refs):
-    pieces, act, part = refs[:4], refs[4], refs[5]
-    send_a, send_b, y, raw, sems = refs[7:]
+def down_send_body(place, *refs):
+    pieces, gates, act, part = refs[:4], refs[4:6], refs[6], refs[7]
+    send_a, send_b, y, raw, sems = refs[9:]
     for c in load_late(Copies(sems), place[1], pieces, raw):
         c.wait()
     count = raw.shape[0]
     first = y.shape[0] - count
     for core in (0, 1):
         tok = count // 2
-        scale(experts, place[2], raw.at[pl.ds(core * tok, tok)], y, first + core * tok)
+        scale(gates[core], raw.at[pl.ds(core * tok, tok)], y, first + core * tok)
 
     def put(target, value):
         dst = (send_a, send_b)[target // 2]
@@ -393,15 +381,21 @@
         return early, late
 
     x_early, x_late = line(tokens)
-    (y_own,) = call(
-        functools.partial(prep_body, experts),
-        [((tok, width + LANES), BF16, VMEM)],
-        [(routes.T, VMEM), (gate_values.T, VMEM), (out_grad, VMEM)],
+    gates = list(call(
+        prep_body,
+        [((1, tok), F32, VMEM)] * experts,
+        [(place, SMEM), (routes.T, VMEM), (gate_values.T, VMEM)],
         [],
         1000,
-        4 * tok * width,
-    )
-    y_early, y_late = line(y_own)
+        1000,
+    ))
+    for k in range(1, experts):
+        gates[k] = lax.ppermute(gates[k], "expert", [(e, e ^ k) for e in range(experts)])
+
+    def gates_of(*distances):
+        return [(gates[k], VMEM) for k in distances]
+
+    y_early, y_late = line(out_grad)
 
     wg0, wu0, wd0 = w_gate[0], w_up[0], w_down[0]
     wg1, wu2 = to_x(wg0), to_y(wu0)
@@ -456,6 +450,24 @@
         rows * width + 2 * width * hidden + 16 * rows * hidden,
         {4: 1, 5: 2, 6: 3, 7: 4},
     )
+    y_rows = ((rows, width), BF16, VMEM)
+    (y,) = call(
+        scale_early_body,
+        [y_rows],
+        anys((y_early[0], y_early[1], y_early[3], y_early[4])) + gates_of(0, 4, 1, 5),
+        [pltpu.VMEM((4 * tok, width), BF16), dma(4)],
+        rows * width,
+        3 * rows * width,
+    )
+    part, y = call(
+        down_early_body,
+        [((4, half, share), F32, VMEM), y_rows],
+        [(place, SMEM)] + anys((y_early[2], y_early[5])) + gates_of(2, 3) + [(pre[0], VMEM), (y, VMEM)],
+        [pltpu.VMEM((2 * tok, width), BF16), dma(2)],
+        3 * rows * width * hidden // 4,
+        2 * (rows * width + rows * hidden + width * hidden),
+        {6: 1},
+    )
     act, active, slope, x = call(
         pre_late_body,
         [flat, wide, wide, x_out],
@@ -465,33 +477,15 @@
         rows * width + 4 * width * hidden + 3 * rows * hidden,
         {7 + i: i for i in range(4)},
     )
-    y_rows = ((rows, width), BF16, VMEM)
-    (y,) = call(
-        functools.partial(scale_early_body, experts),
-        [y_rows],
-        [(place, SMEM)] + anys((y_early[0], y_early[1], y_early[3], y_early[4])),
-        [pltpu.VMEM((4 * tok, width + LANES), BF16), dma(4)],
-        rows * width,
-        3 * rows * width,
-    )
     piece = (2, half, share)
-    part, y = call(
-        functools.partial(down_early_body, experts),
-        [((4, half, share), F32, VMEM), y_rows],
-        [(place, SMEM)] + anys((y_early[2], y_early[5])) + [(act, VMEM), (y, VMEM)],
-        [pltpu.VMEM((2 * tok, width + LANES), BF16), dma(2)],
-        3 * rows * width * hidden // 4,
-        2 * (rows * width + rows * hidden + width * hidden),
-        {4: 1},
-    )
     send_a, send_b, y = call(
-        functools.partial(down_send_body, experts),
+        down_send_body,
         [(piece, BF16, VMEM)] * 2 + [((rows, width), BF16, VMEM)],
-        [(place, SMEM)] + anys(y_late) + [(act, VMEM), (part, VMEM), (y, VMEM)],
-        [pltpu.VMEM((2 * tok, width + LANES), BF16), dma(2)],
+        [(place, SMEM)] + anys(y_late) + gates_of(6, 7) + [(act, VMEM), (part, VMEM), (y, VMEM)],
+        [pltpu.VMEM((2 * tok, width), BF16), dma(2)],
         rows * width * hidden // 4,
         2 * (rows * width + rows * hidden // 4 + width * hidden),
-        {7: 2},
+        {9: 2},
     )
     got_a, got_b = to_x(send_a), to_y(send_b)
     gate_delta, up_delta = call(

time: 265 us -> 274 us (1.034)
  waiting for transfers between devices: 134 us -> 158 us
  local copies, waits for them, and re-layouts: 20.5 us -> 4.54 us
  starting transfers between devices: 52.9 us -> 59.6 us
  Pallas kernels: 50.9 us -> 47 us
    ppermute x0 -> x7, waiting for transfers between devices: none -> 27.8 us  [dense(): lax.ppermute(gates[k], 'expert', [(e, e ^ k) for e in range(experts)])]
    unnamed x82 -> x14, local copies, waits for them, and re-layouts: 19.3 us -> 2.43 us
    ppermute x12, waiting for transfers between devices: 53.8 us -> 43.9 us  [hop(): lax.ppermute(block, 'expert', [(2 * a + c, 2 * b + c) for a, b in moves f...]
    ppermute x0 -> x7, starting transfers between devices: none -> 8.86 us  [dense(): lax.ppermute(gates[k], 'expert', [(e, e ^ k) for e in range(experts)])]
    ppermute x10, waiting for transfers between devices: 62.2 us -> 70.9 us  [to_y(): return lax.ppermute(block, 'dp', [(i, i ^ 2) for i in range(4)])]
    ppermute x12, starting transfers between devices: 23.8 us -> 18.7 us  [hop(): lax.ppermute(block, 'expert', [(2 * a + c, 2 * b + c) for a, b in moves f...]
    pallas_call x15, Pallas kernels: 50.9 us -> 47 us  [call(): pl.pallas_call(body, input_output_aliases=aliases or {}, out_shape=[jax.S...]
    ppermute x10, waiting for transfers between devices: 17.8 us -> 14.8 us  [to_x(): return lax.ppermute(block, 'dp', [(i, i ^ 1) for i in range(4)])]
  transfers between devices with their start and end apart: 43 -> 50, of which waited for: 15 -> 20; matrix products, arithmetic and copies ran while one was open for 2% -> 2% of each run, Pallas kernels for 14% -> 12%
where the time goes in v10:
time: 274 us
  waiting for transfers between devices  158 us (58%)
  starting transfers between devices  59.6 us (22%)
  Pallas kernels  47 us (17%)
  local copies, waits for them, and re-layouts  4.54 us (2%)
  other arithmetic  4.37 us (2%)
    ppermute x10, waiting for transfers between devices, to_y(): return lax.ppermute(block, 'dp', [(i, i ^ 2) for i in range(4)])  70.9 us
    pallas_call x15, Pallas kernels, call(): pl.pallas_call(body, input_output_aliases=aliases or {}, out_shape=[jax.S...  47 us
    ppermute x12, waiting for transfers between devices, hop(): lax.ppermute(block, 'expert', [(2 * a + c, 2 * b + c) for a, b in moves f...  43.9 us
    ppermute x7, waiting for transfers between devices, dense(): lax.ppermute(gates[k], 'expert', [(e, e ^ k) for e in range(experts)])  27.8 us
    ppermute x12, starting transfers between devices, hop(): lax.ppermute(block, 'expert', [(2 * a + c, 2 * b + c) for a, b in moves f...  18.7 us
    ppermute x10, waiting for transfers between devices, to_x(): return lax.ppermute(block, 'dp', [(i, i ^ 1) for i in range(4)])  14.8 us
    ppermute x10, starting transfers between devices, to_y(): return lax.ppermute(block, 'dp', [(i, i ^ 2) for i in range(4)])  12.6 us
    ppermute x10, starting transfers between devices, to_x(): return lax.ppermute(block, 'dp', [(i, i ^ 1) for i in range(4)])  12.5 us
  transfers between devices with their start and end apart: 50, of which 20 were waited for; matrix products, arithmetic and copies ran while one was open for 2% of the time, Pallas kernels for 12%

profile of v10, /device:TPU:0, one launch (start us, length us, event | category | flops | bytes accessed | tf_op | source)
XLA Modules:
  0.0 274.1 jit_solution(4805409384722741658)
XLA Ops:
  0.7 4.1 %collective-permute-start.8 = (bf16[128,2048]{1,0:T(8,128)(2,1)}, bf16[128,2048]{1,0:T(8,128)(2,1)S(1)}, u32[]{:S(2)}, u32[]{:S(2)}) collective-permute-start(bf16[128,2048]{1,0:T(8,128)(2,1)} %tokens.1), channel_id=1, source_target_pairs={{0,4},{1,5},{2,6},{3,7},{4,0},{5,1},{6,2},{7,3},{8,12},{9,13},{10,... | collective-permute-start | bytes 1572872 | tf_op jit(solution)/shard_map/ppermute | solution.py:369
  4.8 2.0 slice_bitcast_fusion.8
  6.8 1.5 collective-permute-start.31
  8.3 1.5 collective-permute-start.34
  9.8 1.6 collective-permute-start.16
  13.9 14.5 %collective-permute-done.28.refs_5_ = f32[1,128]{1,0:T(1,128)S(1)} collective-permute-done((f32[1,128]{1,0:T(1,128)S(1)}, f32[1,128]{1,0:T(1,128)S(1)}, u32[]{:S(2)}, u32[]{:S(2)}) %collective-permute-start.28) | collective-permute-done | bytes 544 | tf_op jit(solution)/shard_map/ppermute | solution.py:393
  28.4 1.2 collective-permute-done.29.refs_6_
  29.5 2.3 collective-permute-start.30
  31.8 1.6 collective-permute-done.30.refs_7_
  33.4 1.5 collective-permute-start.24
  34.9 2.1 collective-permute-done.24.refs_2_
  37.1 2.9 %collective-permute-done.25.refs_3_ = f32[1,128]{1,0:T(1,128)S(1)} collective-permute-done((f32[1,128]{1,0:T(1,128)S(1)}, f32[1,128]{1,0:T(1,128)S(1)}, u32[]{:S(2)}, u32[]{:S(2)}) %collective-permute-start.25) | collective-permute-done | bytes 544 | tf_op jit(solution)/shard_map/ppermute | solution.py:393
  40.0 3.5 %collective-permute-start.5 = (f32[1,128]{1,0:T(1,128)S(1)}, f32[1,128]{1,0:T(1,128)S(1)}, u32[]{:S(2)}, u32[]{:S(2)}) collective-permute-start(f32[1,128]{1,0:T(1,128)S(1)} %get-tuple-element.52), channel_id=1, source_target_pairs={{0,6},{1,7},{2,4},{3,5},{4,2},{5,3},{6,0},{7,1},{8,14},{9,15},{10,... | collective-permute-start | bytes 1544 | tf_op jit(solution)/shard_map/ppermute | solution.py:393
  43.5 1.8 collective-permute-done.5.refs_4_
  45.3 1.0 collective-permute-start.6
  46.4 3.8 %collective-permute-done.6.refs_5_ = f32[1,128]{1,0:T(1,128)S(1)} collective-permute-done((f32[1,128]{1,0:T(1,128)S(1)}, f32[1,128]{1,0:T(1,128)S(1)}, u32[]{:S(2)}, u32[]{:S(2)}) %collective-permute-start.6) | collective-permute-done | bytes 544 | tf_op jit(solution)/shard_map/ppermute | solution.py:393
  50.7 3.8 %collective-permute-start.22 = (bf16[128,2048]{1,0:T(8,128)(2,1)}, bf16[128,2048]{1,0:T(8,128)(2,1)S(1)}, u32[]{:S(2)}, u32[]{:S(2)}) collective-permute-start(bf16[128,2048]{1,0:T(8,128)(2,1)} %refs_0_.1), channel_id=1, source_target_pairs={{0,2},{1,3},{2,0},{3,1},{4,6},{5,7},{6,4},{7,5},{8,10},{9,11},{10,... | collective-permute-start | bytes 1572872 | tf_op jit(solution)/shard_map/ppermute | solution.py:369
  55.2 1.6 collective-permute-start.12
  56.7 20.7 %collective-permute-done.1.refs_1_ = bf16[128,2048]{1,0:T(8,128)(2,1)S(1)} collective-permute-done((bf16[128,2048]{1,0:T(8,128)(2,1)}, bf16[128,2048]{1,0:T(8,128)(2,1)S(1)}, u32[]{:S(2)}, u32[]{:S(2)}) %collective-permute-start.1) | collective-permute-done | bytes 524320 | tf_op jit(solution)/shard_map/ppermute | solution.py:369
  78.1 1.6 collective-permute-start.14
  79.7 1.5 collective-permute-start.20
  82.2 16.6 %collective-permute-done.14.refs_8_ = bf16[512,768]{1,0:T(8,128)(2,1)S(1)} collective-permute-done((bf16[512,768]{1,0:T(8,128)(2,1)}, bf16[512,768]{1,0:T(8,128)(2,1)S(1)}, u32[]{:S(2)}, u32[]{:S(2)}) %collective-permute-start.14) | collective-permute-done | bytes 786464 | tf_op jit(solution)/shard_map/ppermute | solution.py:366
  99.3 14.3 %collective-permute-done.21.refs_7_ = bf16[512,768]{1,0:T(8,128)(2,1)S(1)} collective-permute-done((bf16[512,768]{1,0:T(8,128)(2,1)}, bf16[512,768]{1,0:T(8,128)(2,1)S(1)}, u32[]{:S(2)}, u32[]{:S(2)}) %collective-permute-start.21) | collective-permute-done | bytes 786464 | tf_op jit(solution)/shard_map/ppermute | solution.py:366
  113.7 1.3 collective-permute-start.9
  115.7 1.3 collective-permute-start.2
  117.0 1.7 collective-permute-start.13
  118.7 1.5 collective-permute-start.15
  120.2 10.2 %collective-permute-done.9.refs_1_ = bf16[128,2048]{1,0:T(8,128)(2,1)S(1)} collective-permute-done((bf16[128,2048]{1,0:T(8,128)(2,1)S(1)}, bf16[128,2048]{1,0:T(8,128)(2,1)S(1)}, u32[]{:S(2)}, u32[]{:S(2)}) %collective-permute-start.9) | collective-permute-done | bytes 524320 | tf_op jit(solution)/shard_map/ppermute | solution.py:369
  131.1 1.9 collective-permute-start.11
  133.0 1.0 copy-done.3
  134.8 1.0 shard_map.104
  135.8 2.9 %collective-permute-done.2.refs_1_ = bf16[128,2048]{1,0:T(8,128)(2,1)S(1)} collective-permute-done((bf16[128,2048]{1,0:T(8,128)(2,1)S(1)}, bf16[128,2048]{1,0:T(8,128)(2,1)S(1)}, u32[]{:S(2)}, u32[]{:S(2)}) %collective-permute-start.2) | collective-permute-done | bytes 524320 | tf_op jit(solution)/shard_map/ppermute | solution.py:369
  138.7 1.9 collective-permute-start.4
  140.7 4.7 %shard_map.105 = (f32[1024,768]{1,0:T(8,128)S(1)}, f32[1024,768]{1,0:T(8,128)S(1)}) custom-call(s32[3]{0:T(128)S(1)} %pad_add_fusion.place, bf16[1024,2048]{1,0:T(8,128)(2,1)S(1)} %get-tuple-element.57.x.refs_2_.refs_9_, bf16[2048,768]{1,0:T(8,128)(2,1)S(1)} %get-tuple-element.58.wg.refs_5_, bf16[2048,768]{1,0:T(8,128)(2,1)S(1)} %get-tuple-element.59.wu.refs_6_), custom_call_target="tpu_custom_call" | custom-call | flops 3623878656 | bytes 20447232 | tf_op jit(solution)/shard_map/pallas_call | solution.py:28
  145.4 1.0 shard_map.108.refs_5_
  146.4 1.8 collective-permute-start.32
  148.2 1.5 collective-permute-start.33
  150.6 3.2 %shard_map.106 = (bf16[1024,768]{1,0:T(8,128)(2,1)S(1)}, f32[1024,768]{1,0:T(8,128)S(1)}, f32[1024,768]{1,0:T(8,128)S(1)}, bf16[2048,768]{1,0:T(8,128)(2,1)S(1)}, bf16[2048,768]{1,0:T(8,128)(2,1)S(1)}) custom-call(s32[3]{0:T(128)S(1)} %pad_add_fusion.place, ...), custom_call_target="tpu_custom_call", output_to_operand_aliasing={{1}: (4, {}), {2}: (5, {}), {3}: (6, {}), {4}: (7, {})} | custom-call | flops 1207959552 | bytes 17825792 | tf_op jit(solution)/shard_map/pallas_call | solution.py:28
  153.7 2.5 shard_map.109
  156.2 2.9 %shard_map.107 = (bf16[1024,768]{1,0:T(8,128)(2,1)S(1)}, f32[1024,768]{1,0:T(8,128)S(1)}, f32[1024,768]{1,0:T(8,128)S(1)}, bf16[1024,2048]{1,0:T(8,128)(2,1)S(1)}) custom-call(s32[3]{0:T(128)S(1)} %pad_add_fusion.place, ...), custom_call_target="tpu_custom_call", output_to_operand_aliasing={{0}: (7, {}), {1}: (8, {}), {2}: (9, {}), {3}: (10, {})} | custom-call | flops 1610612736 | bytes 10747904 | tf_op jit(solution)/shard_map/pallas_call | solution.py:28
  159.2 1.8 shard_map.110
  161.1 7.0 %collective-permute-done.35.refs_5_ = bf16[384,512]{1,0:T(8,128)(2,1)S(1)} collective-permute-done((bf16[384,512]{1,0:T(8,128)(2,1)S(1)}, bf16[384,512]{1,0:T(8,128)(2,1)S(1)}, u32[]{:S(2)}, u32[]{:S(2)}) %collective-permute-start.35) | collective-permute-done | bytes 393248 | tf_op jit(solution)/shard_map/ppermute | solution.py:366
  168.1 6.3 %shard_map.111 = (bf16[1024,768]{1,0:T(8,128)(2,1)S(1)}, bf16[1024,768]{1,0:T(8,128)(2,1)S(1)}) custom-call(s32[3]{0:T(128)S(1)} %pad_add_fusion.place, bf16[1024,2048]{1,0:T(8,128)(2,1)S(1)} %get-tuple-element.76.y, f32[1024,768]{1,0:T(8,128)S(1)} %get-tuple-element.77.active, f32[1024,768]{1,0:T(8,128)S(1)} %get-tuple-element.78.slope, ...), custom_call_target="tpu_custom_call" | custom-call | flops 3221225472 | bytes 16777216 | tf_op jit(solution)/shard_map/pallas_call | solution.py:28
  174.4 8.1 %shard_map.112 = (bf16[512,2048]{1,0:T(8,128)(2,1)S(1)}, bf16[512,2048]{1,0:T(8,128)(2,1)S(1)}) custom-call(bf16[1024,768]{1,0:T(8,128)(2,1)S(1)} %get-tuple-element.79.gate_delta.gd, bf16[1024,768]{1,0:T(8,128)(2,1)S(1)} %get-tuple-element.80.up_delta.ud, bf16[2048,768]{1,0:T(8,128)(2,1)S(1)} %get-tuple-element.62.refs_4_.wg, ...), custom_call_target="tpu_custom_call" | custom-call | flops 6442450944 | bytes 13631488 | tf_op jit(solution)/shard_map/pallas_call | solution.py:28
  183.0 1.7 collective-permute-start.48
  184.7 5.2 %shard_map.114 = (bf16[2,512,768]{2,1,0:T(8,128)(2,1)S(1)}, bf16[2,512,768]{2,1,0:T(8,128)(2,1)S(1)}) custom-call(s32[3]{0:T(128)S(1)} %pad_add_fusion.place, bf16[1024,2048]{1,0:T(8,128)(2,1)S(1)} %get-tuple-element.83.x, bf16[1024,768]{1,0:T(8,128)(2,1)S(1)} %get-tuple-element.79.gate_delta.gd, bf16[1024,768]{1,0:T(8,128)(2,1)S(1)} %get-tuple-element.80.up_delta.ud), custom_call_target="tpu_custom_call" | custom-call | flops 3221225472 | bytes 10485760 | tf_op jit(solution)/shard_map/pallas_call | solution.py:28
  190.3 1.7 collective-permute-start.42
  192.0 2.4 shard_map.116
  194.4 5.2 %shard_map.113 = (bf16[512,768]{1,0:T(8,128)(2,1)S(1)}, bf16[512,768]{1,0:T(8,128)(2,1)S(1)}, bf16[512,768]{1,0:T(8,128)(2,1)S(1)}, bf16[512,768]{1,0:T(8,128)(2,1)S(1)}) custom-call(s32[3]{0:T(128)S(1)} %pad_add_fusion.place, bf16[1024,2048]{1,0:T(8,128)(2,1)S(1)} %get-tuple-element.83.x, bf16[1024,768]{1,0:T(8,128)(2,1)S(1)} %get-tuple-element.79.gate_delta.gd, ...), custom_call_target="tpu_custom_call" | custom-call | flops 3221225472 | bytes 10485760 | tf_op jit(solution)/shard_map/pallas_call | solution.py:28
  199.6 3.4 %collective-permute-done.46 = bf16[2,384,512]{2,1,0:T(8,128)(2,1)S(1)} collective-permute-done((bf16[2,384,512]{2,1,0:T(8,128)(2,1)S(1)}, bf16[2,384,512]{2,1,0:T(8,128)(2,1)S(1)}, u32[]{:S(2)}, u32[]{:S(2)}) %collective-permute-start.46) | collective-permute-done | bytes 786464 | tf_op jit(solution)/shard_map/ppermute | solution.py:363
  203.2 1.6 collective-permute-start.47
  205.4 0.8 add_convert_fusion
  206.3 1.3 collective-permute-start.40
  207.6 29.5 %collective-permute-done.43 = bf16[2,512,768]{2,1,0:T(8,128)(2,1)S(1)} collective-permute-done((bf16[2,512,768]{2,1,0:T(8,128)(2,1)S(1)}, bf16[2,512,768]{2,1,0:T(8,128)(2,1)S(1)}, u32[]{:S(2)}, u32[]{:S(2)}) %collective-permute-start.43) | collective-permute-done | bytes 1572896 | tf_op jit(solution)/shard_map/ppermute | solution.py:366
  237.5 1.7 collective-permute-start.45
  239.7 1.6 collective-permute-start.44
  242.1 3.4 %collective-permute-done.47 = bf16[384,512]{1,0:T(8,128)(2,1)S(1)} collective-permute-done((bf16[384,512]{1,0:T(8,128)(2,1)S(1)}, bf16[384,512]{1,0:T(8,128)(2,1)S(1)}, u32[]{:S(2)}, u32[]{:S(2)}) %collective-permute-start.47) | collective-permute-done | bytes 393248 | tf_op jit(solution)/shard_map/ppermute | solution.py:366
  245.6 3.3 %collective-permute-start.41 = (bf16[128,2048]{1,0:T(8,128)(2,1)S(1)}, bf16[128,2048]{1,0:T(8,128)(2,1)S(1)}, u32[]{:S(2)}, u32[]{:S(2)}) collective-permute-start(bf16[128,2048]{1,0:T(8,128)(2,1)S(1)} %add_convert_fusion.2), channel_id=1, source_target_pairs={{0,4},{1,5},{2,6},{3,7},{4,0},{5,1},{6,2},{7,3},{8,12},{9,13},{10,... | collective-permute-start | bytes 1572872 | tf_op jit(solution)/shard_map/ppermute | solution.py:369
  249.2 0.9 maximum_bitcast_fusion
  250.1 11.4 %collective-permute-done.45.up_last = bf16[512,768]{1,0:T(8,128)(2,1)S(1)} collective-permute-done((bf16[512,768]{1,0:T(8,128)(2,1)S(1)}, bf16[512,768]{1,0:T(8,128)(2,1)S(1)}, u32[]{:S(2)}, u32[]{:S(2)}) %collective-permute-start.45) | collective-permute-done | bytes 786464 | tf_op jit(solution)/shard_map/ppermute | solution.py:363
  261.6 1.3 shard_map.115
  262.9 3.5 %collective-permute-done.39 = bf16[128,2048]{1,0:T(8,128)(2,1)S(1)} collective-permute-done((bf16[128,2048]{1,0:T(8,128)(2,1)S(1)}, bf16[128,2048]{1,0:T(8,128)(2,1)S(1)}, u32[]{:S(2)}, u32[]{:S(2)}) %collective-permute-start.39) | collective-permute-done | bytes 524320 | tf_op jit(solution)/shard_map/ppermute | solution.py:369
  266.3 6.7 %collective-permute-done.41 = bf16[128,2048]{1,0:T(8,128)(2,1)S(1)} collective-permute-done((bf16[128,2048]{1,0:T(8,128)(2,1)S(1)}, bf16[128,2048]{1,0:T(8,128)(2,1)S(1)}, u32[]{:S(2)}, u32[]{:S(2)}) %collective-permute-start.41) | collective-permute-done | bytes 524320 | tf_op jit(solution)/shard_map/ppermute | solution.py:369
  273.0 1.1 add_convert_fusion.1
  (78 shorter events, 12.8 us)
Async XLA Ops:
  0.6 132.4 %copy-start.1 = (bf16[1,512,768]{2,1,0:T(8,128)(2,1)S(1)}, bf16[1,512,768]{2,1,0:T(8,128)(2,1)}, u32[]{:S(2)}) copy-start(bf16[1,512,768]{2,1,0:T(8,128)(2,1)} %param.11) | copy-start | bytes 2359300
  0.6 132.4 %copy-start.2 = (bf16[1,512,768]{2,1,0:T(8,128)(2,1)S(1)}, bf16[1,512,768]{2,1,0:T(8,128)(2,1)}, u32[]{:S(2)}) copy-start(bf16[1,512,768]{2,1,0:T(8,128)(2,1)} %param.12) | copy-start | bytes 2359300
  0.7 50.1 %collective-permute-start.8 = (bf16[128,2048]{1,0:T(8,128)(2,1)}, bf16[128,2048]{1,0:T(8,128)(2,1)S(1)}, u32[]{:S(2)}, u32[]{:S(2)}) collective-permute-start(bf16[128,2048]{1,0:T(8,128)(2,1)} %tokens.1), channel_id=1, source_target_pairs={{0,4},{1,5},{2,6},{3,7},{4,0},{5,1},{6,2},{7,3},{8,12},{9,13},{10,... | collective-permute-start | bytes 1572872 | tf_op jit(solution)/shard_map/ppermute | solution.py:369
  6.8 43.4 %collective-permute-start.31 = (bf16[384,512]{1,0:T(8,128)(2,1)}, bf16[384,512]{1,0:T(8,128)(2,1)S(1)}, u32[]{:S(2)}, u32[]{:S(2)}) collective-permute-start(bf16[384,512]{1,0:T(8,128)(2,1)} %get-tuple-element.107), channel_id=1, source_target_pairs={{0,8},{8,0},{16,24},{24,16},{1,9},{9,1},{17,25},{25,17},{2,10},{10... | collective-permute-start | bytes 1179656 | tf_op jit(solution)/shard_map/ppermute | solution.py:363
  8.3 41.9 %collective-permute-start.34 = (bf16[384,512]{1,0:T(8,128)(2,1)}, bf16[384,512]{1,0:T(8,128)(2,1)S(1)}, u32[]{:S(2)}, u32[]{:S(2)}) collective-permute-start(bf16[384,512]{1,0:T(8,128)(2,1)} %get-tuple-element.106), channel_id=1, source_target_pairs={{0,16},{8,24},{16,0},{24,8},{1,17},{9,25},{17,1},{25,9},{2,18},{10... | collective-permute-start | bytes 1179656 | tf_op jit(solution)/shard_map/ppermute | solution.py:366
  9.8 44.6 %collective-permute-start.16 = (bf16[128,2048]{1,0:T(8,128)(2,1)}, bf16[128,2048]{1,0:T(8,128)(2,1)S(1)}, u32[]{:S(2)}, u32[]{:S(2)}) collective-permute-start(bf16[128,2048]{1,0:T(8,128)(2,1)} %tokens.1), channel_id=1, source_target_pairs={{0,2},{1,3},{2,0},{3,1},{4,6},{5,7},{6,4},{7,5},{8,10},{9,11},{10,... | collective-permute-start | bytes 1572872 | tf_op jit(solution)/shard_map/ppermute | solution.py:369
  11.5 0.7 copy-start.5
  12.2 0.7 copy-start.6
  13.4 14.9 %collective-permute-start.28 = (f32[1,128]{1,0:T(1,128)S(1)}, f32[1,128]{1,0:T(1,128)S(1)}, u32[]{:S(2)}, u32[]{:S(2)}) collective-permute-start(f32[1,128]{1,0:T(1,128)S(1)} %get-tuple-element.71), channel_id=1, source_target_pairs={{0,4},{1,5},{2,6},{3,7},{4,0},{5,1},{6,2},{7,3},{8,12},{9,13},{10,... | collective-permute-start | bytes 1544 | tf_op jit(solution)/shard_map/ppermute | solution.py:393
  28.4 1.2 collective-permute-start.29
  29.5 3.9 %collective-permute-start.30 = (f32[1,128]{1,0:T(1,128)S(1)}, f32[1,128]{1,0:T(1,128)S(1)}, u32[]{:S(2)}, u32[]{:S(2)}) collective-permute-start(f32[1,128]{1,0:T(1,128)S(1)} %get-tuple-element.73), channel_id=1, source_target_pairs={{0,5},{1,4},{2,7},{3,6},{4,1},{5,0},{6,3},{7,2},{8,13},{9,12},{10,... | collective-permute-start | bytes 1544 | tf_op jit(solution)/shard_map/ppermute | solution.py:393
  33.4 3.6 %collective-permute-start.24 = (f32[1,128]{1,0:T(1,128)S(1)}, f32[1,128]{1,0:T(1,128)S(1)}, u32[]{:S(2)}, u32[]{:S(2)}) collective-permute-start(f32[1,128]{1,0:T(1,128)S(1)} %get-tuple-element.68), channel_id=1, source_target_pairs={{0,2},{1,3},{2,0},{3,1},{4,6},{5,7},{6,4},{7,5},{8,10},{9,11},{10,... | collective-permute-start | bytes 1544 | tf_op jit(solution)/shard_map/ppermute | solution.py:393
  37.0 3.0 %collective-permute-start.25 = (f32[1,128]{1,0:T(1,128)S(1)}, f32[1,128]{1,0:T(1,128)S(1)}, u32[]{:S(2)}, u32[]{:S(2)}) collective-permute-start(f32[1,128]{1,0:T(1,128)S(1)} %get-tuple-element.69), channel_id=1, source_target_pairs={{0,3},{1,2},{2,1},{3,0},{4,7},{5,6},{6,5},{7,4},{8,11},{9,10},{10,... | collective-permute-start | bytes 1544 | tf_op jit(solution)/shard_map/ppermute | solution.py:393
  40.0 5.4 %collective-permute-start.5 = (f32[1,128]{1,0:T(1,128)S(1)}, f32[1,128]{1,0:T(1,128)S(1)}, u32[]{:S(2)}, u32[]{:S(2)}) collective-permute-start(f32[1,128]{1,0:T(1,128)S(1)} %get-tuple-element.52), channel_id=1, source_target_pairs={{0,6},{1,7},{2,4},{3,5},{4,2},{5,3},{6,0},{7,1},{8,14},{9,15},{10,... | collective-permute-start | bytes 1544 | tf_op jit(solution)/shard_map/ppermute | solution.py:393
  45.3 4.8 %collective-permute-start.6 = (f32[1,128]{1,0:T(1,128)S(1)}, f32[1,128]{1,0:T(1,128)S(1)}, u32[]{:S(2)}, u32[]{:S(2)}) collective-permute-start(f32[1,128]{1,0:T(1,128)S(1)} %get-tuple-element.53), channel_id=1, source_target_pairs={{0,7},{1,6},{2,5},{3,4},{4,3},{5,2},{6,1},{7,0},{8,15},{9,14},{10,... | collective-permute-start | bytes 1544 | tf_op jit(solution)/shard_map/ppermute | solution.py:393
  50.1 5.0 %collective-permute-start.17 = (bf16[128,2048]{1,0:T(8,128)(2,1)}, bf16[128,2048]{1,0:T(8,128)(2,1)S(1)}, u32[]{:S(2)}, u32[]{:S(2)}) collective-permute-start(bf16[128,2048]{1,0:T(8,128)(2,1)} %tokens.1), channel_id=1, source_target_pairs={{0,1},{1,0},{2,3},{3,2},{4,5},{5,4},{6,7},{7,6},{8,9},{9,8},{10,11... | collective-permute-start | bytes 1572872 | tf_op jit(solution)/shard_map/ppermute | solution.py:372
  50.2 27.2 %collective-permute-start.1 = (bf16[128,2048]{1,0:T(8,128)(2,1)}, bf16[128,2048]{1,0:T(8,128)(2,1)S(1)}, u32[]{:S(2)}, u32[]{:S(2)}) collective-permute-start(bf16[128,2048]{1,0:T(8,128)(2,1)} %refs_0_.1), channel_id=1, source_target_pairs={{0,4},{1,5},{2,6},{3,7},{4,0},{5,1},{6,2},{7,3},{8,12},{9,13},{10,... | collective-permute-start | bytes 1572872 | tf_op jit(solution)/shard_map/ppermute | solution.py:369
  50.3 27.9 %collective-permute-start.26 = (bf16[128,2048]{1,0:T(8,128)(2,1)}, bf16[128,2048]{1,0:T(8,128)(2,1)S(1)}, u32[]{:S(2)}, u32[]{:S(2)}) collective-permute-start(bf16[128,2048]{1,0:T(8,128)(2,1)} %refs_0_.1), channel_id=1, source_target_pairs={{0,1},{1,0},{2,3},{3,2},{4,5},{5,4},{6,7},{7,6},{8,9},{9,8},{10,11... | collective-permute-start | bytes 1572872 | tf_op jit(solution)/shard_map/ppermute | solution.py:372
  50.7 29.0 %collective-permute-start.22 = (bf16[128,2048]{1,0:T(8,128)(2,1)}, bf16[128,2048]{1,0:T(8,128)(2,1)S(1)}, u32[]{:S(2)}, u32[]{:S(2)}) collective-permute-start(bf16[128,2048]{1,0:T(8,128)(2,1)} %refs_0_.1), channel_id=1, source_target_pairs={{0,2},{1,3},{2,0},{3,1},{4,6},{5,7},{6,4},{7,5},{8,10},{9,11},{10,... | collective-permute-start | bytes 1572872 | tf_op jit(solution)/shard_map/ppermute | solution.py:369
  54.5 26.7 %collective-permute-start.7 = (bf16[128,2048]{1,0:T(8,128)(2,1)}, bf16[128,2048]{1,0:T(8,128)(2,1)S(1)}, u32[]{:S(2)}, u32[]{:S(2)}) collective-permute-start(bf16[128,2048]{1,0:T(8,128)(2,1)} %tokens.1), channel_id=1, source_target_pairs={{2,4},{3,5},{4,2},{5,3},{10,12},{11,13},{12,10},{13,11},{18,20},{1... | collective-permute-start | bytes 1572872 | tf_op jit(solution)/shard_map/ppermute | solution.py:369
  55.2 26.6 %collective-permute-start.12 = (bf16[512,768]{1,0:T(8,128)(2,1)}, bf16[512,768]{1,0:T(8,128)(2,1)S(1)}, u32[]{:S(2)}, u32[]{:S(2)}) collective-permute-start(bf16[512,768]{1,0:T(8,128)(2,1)} %bitcast.55), channel_id=1, source_target_pairs={{0,8},{8,0},{16,24},{24,16},{1,9},{9,1},{17,25},{25,17},{2,10},{10... | collective-permute-start | bytes 2359304 | tf_op jit(solution)/shard_map/ppermute | solution.py:363
  77.4 4.3 %collective-permute-start = (bf16[128,2048]{1,0:T(8,128)(2,1)}, bf16[128,2048]{1,0:T(8,128)(2,1)S(1)}, u32[]{:S(2)}, u32[]{:S(2)}) collective-permute-start(bf16[128,2048]{1,0:T(8,128)(2,1)} %refs_0_.1), channel_id=1, source_target_pairs={{2,4},{3,5},{4,2},{5,3},{10,12},{11,13},{12,10},{13,11},{18,20},{1... | collective-permute-start | bytes 1572872 | tf_op jit(solution)/shard_map/ppermute | solution.py:369
  78.1 20.7 %collective-permute-start.14 = (bf16[512,768]{1,0:T(8,128)(2,1)}, bf16[512,768]{1,0:T(8,128)(2,1)S(1)}, u32[]{:S(2)}, u32[]{:S(2)}) collective-permute-start(bf16[512,768]{1,0:T(8,128)(2,1)} %bitcast.58), channel_id=1, source_target_pairs={{0,16},{8,24},{16,0},{24,8},{1,17},{9,25},{17,1},{25,9},{2,18},{10... | collective-permute-start | bytes 2359304 | tf_op jit(solution)/shard_map/ppermute | solution.py:366
  79.7 19.1 %collective-permute-start.20 = (bf16[512,768]{1,0:T(8,128)(2,1)}, bf16[512,768]{1,0:T(8,128)(2,1)S(1)}, u32[]{:S(2)}, u32[]{:S(2)}) collective-permute-start(bf16[512,768]{1,0:T(8,128)(2,1)} %bitcast.59), channel_id=1, source_target_pairs={{0,8},{8,0},{16,24},{24,16},{1,9},{9,1},{17,25},{25,17},{2,10},{10... | collective-permute-start | bytes 2359304 | tf_op jit(solution)/shard_map/ppermute | solution.py:363
  81.2 32.5 %collective-permute-start.21 = (bf16[512,768]{1,0:T(8,128)(2,1)}, bf16[512,768]{1,0:T(8,128)(2,1)S(1)}, u32[]{:S(2)}, u32[]{:S(2)}) collective-permute-start(bf16[512,768]{1,0:T(8,128)(2,1)} %bitcast.56), channel_id=1, source_target_pairs={{0,16},{8,24},{16,0},{24,8},{1,17},{9,25},{17,1},{25,9},{2,18},{10... | collective-permute-start | bytes 2359304 | tf_op jit(solution)/shard_map/ppermute | solution.py:366
  81.7 33.2 %collective-permute-start.18 = (bf16[128,2048]{1,0:T(8,128)(2,1)S(1)}, bf16[128,2048]{1,0:T(8,128)(2,1)S(1)}, u32[]{:S(2)}, u32[]{:S(2)}) collective-permute-start(bf16[128,2048]{1,0:T(8,128)(2,1)S(1)} %collective-permute-done.8.refs_0_), channel_id=1, source_target_pairs={{0,1},{1,0},{2,3},{3,2},{4,5},{5,4},{6,7},{7,6},{8,9},{9,8},{10,11... | collective-permute-start | bytes 1572872 | tf_op jit(solution)/shard_map/ppermute | solution.py:372
  81.7 33.9 %collective-permute-start.19 = (bf16[128,2048]{1,0:T(8,128)(2,1)S(1)}, bf16[128,2048]{1,0:T(8,128)(2,1)S(1)}, u32[]{:S(2)}, u32[]{:S(2)}) collective-permute-start(bf16[128,2048]{1,0:T(8,128)(2,1)S(1)} %collective-permute-done.16.refs_1_), channel_id=1, source_target_pairs={{0,1},{1,0},{2,3},{3,2},{4,5},{5,4},{6,7},{7,6},{8,9},{9,8},{10,11... | collective-permute-start | bytes 1572872 | tf_op jit(solution)/shard_map/ppermute | solution.py:372
  98.8 18.2 %collective-permute-start.27 = (bf16[128,2048]{1,0:T(8,128)(2,1)S(1)}, bf16[128,2048]{1,0:T(8,128)(2,1)S(1)}, u32[]{:S(2)}, u32[]{:S(2)}) collective-permute-start(bf16[128,2048]{1,0:T(8,128)(2,1)S(1)} %collective-permute-done.1.refs_1_), channel_id=1, source_target_pairs={{0,1},{1,0},{2,3},{3,2},{4,5},{5,4},{6,7},{7,6},{8,9},{9,8},{10,11... | collective-permute-start | bytes 1572872 | tf_op jit(solution)/shard_map/ppermute | solution.py:372
  98.8 19.9 %collective-permute-start.23 = (bf16[128,2048]{1,0:T(8,128)(2,1)S(1)}, bf16[128,2048]{1,0:T(8,128)(2,1)S(1)}, u32[]{:S(2)}, u32[]{:S(2)}) collective-permute-start(bf16[128,2048]{1,0:T(8,128)(2,1)S(1)} %collective-permute-done.22.refs_0_), channel_id=1, source_target_pairs={{0,1},{1,0},{2,3},{3,2},{4,5},{5,4},{6,7},{7,6},{8,9},{9,8},{10,11... | collective-permute-start | bytes 1572872 | tf_op jit(solution)/shard_map/ppermute | solution.py:372
  113.7 16.7 %collective-permute-start.9 = (bf16[128,2048]{1,0:T(8,128)(2,1)S(1)}, bf16[128,2048]{1,0:T(8,128)(2,1)S(1)}, u32[]{:S(2)}, u32[]{:S(2)}) collective-permute-start(bf16[128,2048]{1,0:T(8,128)(2,1)S(1)} %collective-permute-done.8.refs_0_), channel_id=1, source_target_pairs={{4,6},{5,7},{2,0},{3,1},{12,14},{13,15},{10,8},{11,9},{20,22},{21,... | collective-permute-start | bytes 1572872 | tf_op jit(solution)/shard_map/ppermute | solution.py:369
  115.0 16.1 %collective-permute-start.10 = (bf16[128,2048]{1,0:T(8,128)(2,1)S(1)}, bf16[128,2048]{1,0:T(8,128)(2,1)S(1)}, u32[]{:S(2)}, u32[]{:S(2)}) collective-permute-start(bf16[128,2048]{1,0:T(8,128)(2,1)S(1)} %collective-permute-done.7.refs_0_), channel_id=1, source_target_pairs={{2,3},{3,2},{4,5},{5,4},{10,11},{11,10},{12,13},{13,12},{18,19},{1... | collective-permute-start | bytes 1572872 | tf_op jit(solution)/shard_map/ppermute | solution.py:372
  115.7 23.0 %collective-permute-start.2 = (bf16[128,2048]{1,0:T(8,128)(2,1)S(1)}, bf16[128,2048]{1,0:T(8,128)(2,1)S(1)}, u32[]{:S(2)}, u32[]{:S(2)}) collective-permute-start(bf16[128,2048]{1,0:T(8,128)(2,1)S(1)} %collective-permute-done.1.refs_1_), channel_id=1, source_target_pairs={{4,6},{5,7},{2,0},{3,1},{12,14},{13,15},{10,8},{11,9},{20,22},{21,... | collective-permute-start | bytes 1572872 | tf_op jit(solution)/shard_map/ppermute | solution.py:369
  117.0 32.7 %collective-permute-start.13 = (bf16[512,768]{1,0:T(8,128)(2,1)S(1)}, bf16[512,768]{1,0:T(8,128)(2,1)S(1)}, u32[]{:S(2)}, u32[]{:S(2)}) collective-permute-start(bf16[512,768]{1,0:T(8,128)(2,1)S(1)} %collective-permute-done.12.refs_5_), channel_id=1, source_target_pairs={{0,16},{8,24},{16,0},{24,8},{1,17},{9,25},{17,1},{25,9},{2,18},{10... | collective-permute-start | bytes 2359304 | tf_op jit(solution)/shard_map/ppermute | solution.py:366
  118.7 31.5 %collective-permute-start.15 = (bf16[512,768]{1,0:T(8,128)(2,1)S(1)}, bf16[512,768]{1,0:T(8,128)(2,1)S(1)}, u32[]{:S(2)}, u32[]{:S(2)}) collective-permute-start(bf16[512,768]{1,0:T(8,128)(2,1)S(1)} %collective-permute-done.14.refs_8_), channel_id=1, source_target_pairs={{0,8},{8,0},{16,24},{24,16},{1,9},{9,1},{17,25},{25,17},{2,10},{10... | collective-permute-start | bytes 2359304 | tf_op jit(solution)/shard_map/ppermute | solution.py:363
  130.4 16.1 %collective-permute-start.3 = (bf16[128,2048]{1,0:T(8,128)(2,1)S(1)}, bf16[128,2048]{1,0:T(8,128)(2,1)S(1)}, u32[]{:S(2)}, u32[]{:S(2)}) collective-permute-start(bf16[128,2048]{1,0:T(8,128)(2,1)S(1)} %collective-permute-done.refs_0_), channel_id=1, source_target_pairs={{2,3},{3,2},{4,5},{5,4},{10,11},{11,10},{12,13},{13,12},{18,19},{1... | collective-permute-start | bytes 1572872 | tf_op jit(solution)/shard_map/ppermute | solution.py:372
  131.1 17.1 %collective-permute-start.11 = (bf16[128,2048]{1,0:T(8,128)(2,1)S(1)}, bf16[128,2048]{1,0:T(8,128)(2,1)S(1)}, u32[]{:S(2)}, u32[]{:S(2)}) collective-permute-start(bf16[128,2048]{1,0:T(8,128)(2,1)S(1)} %collective-permute-done.9.refs_1_), channel_id=1, source_target_pairs={{0,1},{1,0},{6,7},{7,6},{8,9},{9,8},{14,15},{15,14},{16,17},{17,16... | collective-permute-start | bytes 1572872 | tf_op jit(solution)/shard_map/ppermute | solution.py:372
  133.0 1.0 copy-start.3
  138.7 20.4 %collective-permute-start.4 = (bf16[128,2048]{1,0:T(8,128)(2,1)S(1)}, bf16[128,2048]{1,0:T(8,128)(2,1)S(1)}, u32[]{:S(2)}, u32[]{:S(2)}) collective-permute-start(bf16[128,2048]{1,0:T(8,128)(2,1)S(1)} %collective-permute-done.2.refs_1_), channel_id=1, source_target_pairs={{0,1},{1,0},{6,7},{7,6},{8,9},{9,8},{14,15},{15,14},{16,17},{17,16... | collective-permute-start | bytes 1572872 | tf_op jit(solution)/shard_map/ppermute | solution.py:372
  140.7 4.7 %copy-start.4 = (bf16[128,2048]{1,0:T(8,128)(2,1)S(1)}, bf16[128,2048]{1,0:T(8,128)(2,1)}, u32[]{:S(2)}) copy-start(bf16[128,2048]{1,0:T(8,128)(2,1)} %refs_0_.1) | copy-start | bytes 1572868
  146.4 14.6 %collective-permute-start.32 = (bf16[384,512]{1,0:T(8,128)(2,1)}, bf16[384,512]{1,0:T(8,128)(2,1)S(1)}, u32[]{:S(2)}, u32[]{:S(2)}) collective-permute-start(bf16[384,512]{1,0:T(8,128)(2,1)} %get-tuple-element.106), channel_id=1, source_target_pairs={{0,8},{8,0},{16,24},{24,16},{1,9},{9,1},{17,25},{25,17},{2,10},{10... | collective-permute-start | bytes 1179656 | tf_op jit(solution)/shard_map/ppermute | solution.py:363
  148.2 12.9 %collective-permute-start.33 = (bf16[384,512]{1,0:T(8,128)(2,1)}, bf16[384,512]{1,0:T(8,128)(2,1)S(1)}, u32[]{:S(2)}, u32[]{:S(2)}) collective-permute-start(bf16[384,512]{1,0:T(8,128)(2,1)} %get-tuple-element.107), channel_id=1, source_target_pairs={{0,16},{8,24},{16,0},{24,8},{1,17},{9,25},{17,1},{25,9},{2,18},{10... | collective-permute-start | bytes 1179656 | tf_op jit(solution)/shard_map/ppermute | solution.py:366
  149.7 18.3 %collective-permute-start.35 = (bf16[384,512]{1,0:T(8,128)(2,1)S(1)}, bf16[384,512]{1,0:T(8,128)(2,1)S(1)}, u32[]{:S(2)}, u32[]{:S(2)}) collective-permute-start(bf16[384,512]{1,0:T(8,128)(2,1)S(1)} %collective-permute-done.31.refs_1_), channel_id=1, source_target_pairs={{0,16},{8,24},{16,0},{24,8},{1,17},{9,25},{17,1},{25,9},{2,18},{10... | collective-permute-start | bytes 1179656 | tf_op jit(solution)/shard_map/ppermute | solution.py:366
  150.2 17.8 %collective-permute-start.36 = (bf16[384,512]{1,0:T(8,128)(2,1)S(1)}, bf16[384,512]{1,0:T(8,128)(2,1)S(1)}, u32[]{:S(2)}, u32[]{:S(2)}) collective-permute-start(bf16[384,512]{1,0:T(8,128)(2,1)S(1)} %collective-permute-done.34.refs_4_), channel_id=1, source_target_pairs={{0,8},{8,0},{16,24},{24,16},{1,9},{9,1},{17,25},{25,17},{2,10},{10... | collective-permute-start | bytes 1179656 | tf_op jit(solution)/shard_map/ppermute | solution.py:363
  159.2 8.9 %copy-start = (bf16[1,768,512]{2,1,0:T(8,128)(2,1)S(1)}, bf16[1,768,512]{2,1,0:T(8,128)(2,1)}, u32[]{:S(2)}) copy-start(bf16[1,768,512]{2,1,0:T(8,128)(2,1)} %param.13) | copy-start | bytes 2359300
  182.5 22.9 %collective-permute-start.37 = (bf16[512,2048]{1,0:T(8,128)(2,1)S(1)}, bf16[512,2048]{1,0:T(8,128)(2,1)S(1)}, u32[]{:S(2)}, u32[]{:S(2)}) collective-permute-start(bf16[512,2048]{1,0:T(8,128)(2,1)S(1)} %get-tuple-element.82), channel_id=1, source_target_pairs={{0,1},{1,0},{2,3},{3,2},{4,5},{5,4},{6,7},{7,6},{8,9},{9,8},{10,11... | collective-permute-start | bytes 6291464 | tf_op jit(solution)/shard_map/ppermute | solution.py:372
  182.6 20.5 %collective-permute-start.46 = (bf16[2,384,512]{2,1,0:T(8,128)(2,1)S(1)}, bf16[2,384,512]{2,1,0:T(8,128)(2,1)S(1)}, u32[]{:S(2)}, u32[]{:S(2)}) collective-permute-start(bf16[2,384,512]{2,1,0:T(8,128)(2,1)S(1)} %get-tuple-element.95), channel_id=1, source_target_pairs={{0,8},{8,0},{16,24},{24,16},{1,9},{9,1},{17,25},{25,17},{2,10},{10... | collective-permute-start | bytes 2359304 | tf_op jit(solution)/shard_map/ppermute | solution.py:363
  183.0 21.8 %collective-permute-start.48 = (bf16[2,384,512]{2,1,0:T(8,128)(2,1)S(1)}, bf16[2,384,512]{2,1,0:T(8,128)(2,1)S(1)}, u32[]{:S(2)}, u32[]{:S(2)}) collective-permute-start(bf16[2,384,512]{2,1,0:T(8,128)(2,1)S(1)} %get-tuple-element.98), channel_id=1, source_target_pairs={{0,16},{8,24},{16,0},{24,8},{1,17},{9,25},{17,1},{25,9},{2,18},{10... | collective-permute-start | bytes 2359304 | tf_op jit(solution)/shard_map/ppermute | solution.py:366
  189.9 47.2 %collective-permute-start.43 = (bf16[2,512,768]{2,1,0:T(8,128)(2,1)S(1)}, bf16[2,512,768]{2,1,0:T(8,128)(2,1)S(1)}, u32[]{:S(2)}, u32[]{:S(2)}) collective-permute-start(bf16[2,512,768]{2,1,0:T(8,128)(2,1)S(1)} %get-tuple-element.87), channel_id=1, source_target_pairs={{0,16},{8,24},{16,0},{24,8},{1,17},{9,25},{17,1},{25,9},{2,18},{10... | collective-permute-start | bytes 4718600 | tf_op jit(solution)/shard_map/ppermute | solution.py:366
  190.3 48.9 %collective-permute-start.42 = (bf16[2,512,768]{2,1,0:T(8,128)(2,1)S(1)}, bf16[2,512,768]{2,1,0:T(8,128)(2,1)S(1)}, u32[]{:S(2)}, u32[]{:S(2)}) collective-permute-start(bf16[2,512,768]{2,1,0:T(8,128)(2,1)S(1)} %get-tuple-element.85), channel_id=1, source_target_pairs={{0,8},{8,0},{16,24},{24,16},{1,9},{9,1},{17,25},{25,17},{2,10},{10... | collective-permute-start | bytes 4718600 | tf_op jit(solution)/shard_map/ppermute | solution.py:363
  203.2 42.4 %collective-permute-start.47 = (bf16[384,512]{1,0:T(8,128)(2,1)S(1)}, bf16[384,512]{1,0:T(8,128)(2,1)S(1)}, u32[]{:S(2)}, u32[]{:S(2)}) collective-permute-start(bf16[384,512]{1,0:T(8,128)(2,1)S(1)} %fusion.7), channel_id=1, source_target_pairs={{0,16},{8,24},{16,0},{24,8},{1,17},{9,25},{17,1},{25,9},{2,18},{10... | collective-permute-start | bytes 1179656 | tf_op jit(solution)/shard_map/ppermute | solution.py:366
  204.9 40.7 %collective-permute-start.49 = (bf16[384,512]{1,0:T(8,128)(2,1)S(1)}, bf16[384,512]{1,0:T(8,128)(2,1)S(1)}, u32[]{:S(2)}, u32[]{:S(2)}) collective-permute-start(bf16[384,512]{1,0:T(8,128)(2,1)S(1)} %fusion.4), channel_id=1, source_target_pairs={{0,8},{8,0},{16,24},{24,16},{1,9},{9,1},{17,25},{25,17},{2,10},{10... | collective-permute-start | bytes 1179656 | tf_op jit(solution)/shard_map/ppermute | solution.py:363
  206.3 35.0 %collective-permute-start.40 = (bf16[128,2048]{1,0:T(8,128)(2,1)S(1)}, bf16[128,2048]{1,0:T(8,128)(2,1)S(1)}, u32[]{:S(2)}, u32[]{:S(2)}) collective-permute-start(bf16[128,2048]{1,0:T(8,128)(2,1)S(1)} %get-tuple-element.101), channel_id=1, source_target_pairs={{0,2},{1,3},{6,4},{7,5},{8,10},{9,11},{14,12},{15,13},{16,18},{17,... | collective-permute-start | bytes 1572872 | tf_op jit(solution)/shard_map/ppermute | solution.py:369
  237.5 24.0 %collective-permute-start.45 = (bf16[512,768]{1,0:T(8,128)(2,1)S(1)}, bf16[512,768]{1,0:T(8,128)(2,1)S(1)}, u32[]{:S(2)}, u32[]{:S(2)}) collective-permute-start(bf16[512,768]{1,0:T(8,128)(2,1)S(1)} %get-tuple-element.102), channel_id=1, source_target_pairs={{0,8},{8,0},{16,24},{24,16},{1,9},{9,1},{17,25},{25,17},{2,10},{10... | collective-permute-start | bytes 2359304 | tf_op jit(solution)/shard_map/ppermute | solution.py:363
  239.7 21.9 %collective-permute-start.44 = (bf16[512,768]{1,0:T(8,128)(2,1)S(1)}, bf16[512,768]{1,0:T(8,128)(2,1)S(1)}, u32[]{:S(2)}, u32[]{:S(2)}) collective-permute-start(bf16[512,768]{1,0:T(8,128)(2,1)S(1)} %get-tuple-element.104), channel_id=1, source_target_pairs={{0,16},{8,24},{16,0},{24,8},{1,17},{9,25},{17,1},{25,9},{2,18},{10... | collective-permute-start | bytes 2359304 | tf_op jit(solution)/shard_map/ppermute | solution.py:366
  241.3 21.6 %collective-permute-start.38 = (bf16[128,2048]{1,0:T(8,128)(2,1)S(1)}, bf16[128,2048]{1,0:T(8,128)(2,1)S(1)}, u32[]{:S(2)}, u32[]{:S(2)}) collective-permute-start(bf16[128,2048]{1,0:T(8,128)(2,1)S(1)} %get-tuple-element.101), channel_id=1, source_target_pairs={{2,4},{3,5},{4,2},{5,3},{10,12},{11,13},{12,10},{13,11},{18,20},{1... | collective-permute-start | bytes 1572872 | tf_op jit(solution)/shard_map/ppermute | solution.py:369
  245.5 20.8 %collective-permute-start.39 = (bf16[128,2048]{1,0:T(8,128)(2,1)S(1)}, bf16[128,2048]{1,0:T(8,128)(2,1)S(1)}, u32[]{:S(2)}, u32[]{:S(2)}) collective-permute-start(bf16[128,2048]{1,0:T(8,128)(2,1)S(1)} %get-tuple-element.100), channel_id=1, source_target_pairs={{0,2},{1,3},{2,0},{3,1},{4,6},{5,7},{6,4},{7,5},{8,10},{9,11},{10,... | collective-permute-start | bytes 1572872 | tf_op jit(solution)/shard_map/ppermute | solution.py:369
  245.6 27.4 %collective-permute-start.41 = (bf16[128,2048]{1,0:T(8,128)(2,1)S(1)}, bf16[128,2048]{1,0:T(8,128)(2,1)S(1)}, u32[]{:S(2)}, u32[]{:S(2)}) collective-permute-start(bf16[128,2048]{1,0:T(8,128)(2,1)S(1)} %add_convert_fusion.2), channel_id=1, source_target_pairs={{0,4},{1,5},{2,6},{3,7},{4,0},{5,1},{6,2},{7,3},{8,12},{9,13},{10,... | collective-permute-start | bytes 1572872 | tf_op jit(solution)/shard_map/ppermute | solution.py:369

commit v11 on v10

--- a/solution.py
+++ b/solution.py
@@ -254,10 +254,10 @@
 
 def last_body(gate_sum, gate_last, up_sum, up_last, gate_out, up_out, gate, up, sems):
     copies = Copies(sems)
-    part = gate.shape[1] // 2
+    part = gate.shape[1] // 8
     started = []
     for total, last, held, out in ((gate_sum, gate_last, gate, gate_out), (up_sum, up_last, up, up_out)):
-        for i in (0, 1):
+        for i in range(8):
             r = slice(i * part, (i + 1) * part)
             held[0, r, :] = (total[r, :].astype(F32) + last[r, :].astype(F32)).astype(BF16)
             at = pl.ds(i * part, part)
@@ -541,7 +541,7 @@
         last_body,
         [(result, BF16, ANY)] * 2,
         [(a, VMEM) for a in (gate_sum, gate_last, up_sum, up_last)],
-        [pltpu.VMEM(result, BF16)] * 2 + [dma(4)],
+        [pltpu.VMEM(result, BF16)] * 2 + [dma(16)],
         share * hidden,
         12 * share * hidden,
     )

time: 274 us -> 274 us (level)
  no operation moved by 1% of the time
where the time goes in v11:
time: 274 us
  waiting for transfers between devices  158 us (58%)
  starting transfers between devices  59.6 us (22%)
  Pallas kernels  47 us (17%)
  local copies, waits for them, and re-layouts  4.54 us (2%)
  other arithmetic  4.37 us (2%)
    ppermute x10, waiting for transfers between devices, to_y(): return lax.ppermute(block, 'dp', [(i, i ^ 2) for i in range(4)])  70.9 us
    pallas_call x15, Pallas kernels, call(): pl.pallas_call(body, input_output_aliases=aliases or {}, out_shape=[jax.S...  47 us
    ppermute x12, waiting for transfers between devices, hop(): lax.ppermute(block, 'expert', [(2 * a + c, 2 * b + c) for a, b in moves f...  43.9 us
    ppermute x7, waiting for transfers between devices, dense(): lax.ppermute(gates[k], 'expert', [(e, e ^ k) for e in range(experts)])  27.8 us
    ppermute x12, starting transfers between devices, hop(): lax.ppermute(block, 'expert', [(2 * a + c, 2 * b + c) for a, b in moves f...  18.7 us
    ppermute x10, waiting for transfers between devices, to_x(): return lax.ppermute(block, 'dp', [(i, i ^ 1) for i in range(4)])  14.8 us
    ppermute x10, starting transfers between devices, to_y(): return lax.ppermute(block, 'dp', [(i, i ^ 2) for i in range(4)])  12.6 us
    ppermute x10, starting transfers between devices, to_x(): return lax.ppermute(block, 'dp', [(i, i ^ 1) for i in range(4)])  12.5 us
  transfers between devices with their start and end apart: 50, of which 20 were waited for; matrix products, arithmetic and copies ran while one was open for 2% of the time, Pallas kernels for 12%

profile of v11, /device:TPU:0, one launch (start us, length us, event | category | flops | bytes accessed | tf_op | source)
XLA Modules:
  0.0 274.1 jit_solution(9284219964540295183)
XLA Ops:
  0.7 4.1 %collective-permute-start.8 = (bf16[128,2048]{1,0:T(8,128)(2,1)}, bf16[128,2048]{1,0:T(8,128)(2,1)S(1)}, u32[]{:S(2)}, u32[]{:S(2)}) collective-permute-start(bf16[128,2048]{1,0:T(8,128)(2,1)} %tokens.1), channel_id=1, source_target_pairs={{0,4},{1,5},{2,6},{3,7},{4,0},{5,1},{6,2},{7,3},{8,12},{9,13},{10,... | collective-permute-start | bytes 1572872 | tf_op jit(solution)/shard_map/ppermute | solution.py:369
  4.8 2.0 slice_bitcast_fusion.8
  6.8 1.5 collective-permute-start.31
  8.3 1.5 collective-permute-start.34
  9.8 1.6 collective-permute-start.16
  13.9 14.5 %collective-permute-done.28.refs_5_ = f32[1,128]{1,0:T(1,128)S(1)} collective-permute-done((f32[1,128]{1,0:T(1,128)S(1)}, f32[1,128]{1,0:T(1,128)S(1)}, u32[]{:S(2)}, u32[]{:S(2)}) %collective-permute-start.28) | collective-permute-done | bytes 544 | tf_op jit(solution)/shard_map/ppermute | solution.py:393
  28.4 1.2 collective-permute-done.29.refs_6_
  29.5 2.3 collective-permute-start.30
  31.8 1.6 collective-permute-done.30.refs_7_
  33.4 1.5 collective-permute-start.24
  34.9 2.1 collective-permute-done.24.refs_2_
  37.1 2.9 %collective-permute-done.25.refs_3_ = f32[1,128]{1,0:T(1,128)S(1)} collective-permute-done((f32[1,128]{1,0:T(1,128)S(1)}, f32[1,128]{1,0:T(1,128)S(1)}, u32[]{:S(2)}, u32[]{:S(2)}) %collective-permute-start.25) | collective-permute-done | bytes 544 | tf_op jit(solution)/shard_map/ppermute | solution.py:393
  40.0 3.5 %collective-permute-start.5 = (f32[1,128]{1,0:T(1,128)S(1)}, f32[1,128]{1,0:T(1,128)S(1)}, u32[]{:S(2)}, u32[]{:S(2)}) collective-permute-start(f32[1,128]{1,0:T(1,128)S(1)} %get-tuple-element.52), channel_id=1, source_target_pairs={{0,6},{1,7},{2,4},{3,5},{4,2},{5,3},{6,0},{7,1},{8,14},{9,15},{10,... | collective-permute-start | bytes 1544 | tf_op jit(solution)/shard_map/ppermute | solution.py:393
  43.5 1.8 collective-permute-done.5.refs_4_
  45.3 1.0 collective-permute-start.6
  46.4 3.8 %collective-permute-done.6.refs_5_ = f32[1,128]{1,0:T(1,128)S(1)} collective-permute-done((f32[1,128]{1,0:T(1,128)S(1)}, f32[1,128]{1,0:T(1,128)S(1)}, u32[]{:S(2)}, u32[]{:S(2)}) %collective-permute-start.6) | collective-permute-done | bytes 544 | tf_op jit(solution)/shard_map/ppermute | solution.py:393
  50.7 3.8 %collective-permute-start.22 = (bf16[128,2048]{1,0:T(8,128)(2,1)}, bf16[128,2048]{1,0:T(8,128)(2,1)S(1)}, u32[]{:S(2)}, u32[]{:S(2)}) collective-permute-start(bf16[128,2048]{1,0:T(8,128)(2,1)} %refs_0_.1), channel_id=1, source_target_pairs={{0,2},{1,3},{2,0},{3,1},{4,6},{5,7},{6,4},{7,5},{8,10},{9,11},{10,... | collective-permute-start | bytes 1572872 | tf_op jit(solution)/shard_map/ppermute | solution.py:369
  55.2 1.6 collective-permute-start.12
  56.7 20.7 %collective-permute-done.1.refs_1_ = bf16[128,2048]{1,0:T(8,128)(2,1)S(1)} collective-permute-done((bf16[128,2048]{1,0:T(8,128)(2,1)}, bf16[128,2048]{1,0:T(8,128)(2,1)S(1)}, u32[]{:S(2)}, u32[]{:S(2)}) %collective-permute-start.1) | collective-permute-done | bytes 524320 | tf_op jit(solution)/shard_map/ppermute | solution.py:369
  78.1 1.6 collective-permute-start.14
  79.7 1.5 collective-permute-start.20
  82.2 16.6 %collective-permute-done.14.refs_8_ = bf16[512,768]{1,0:T(8,128)(2,1)S(1)} collective-permute-done((bf16[512,768]{1,0:T(8,128)(2,1)}, bf16[512,768]{1,0:T(8,128)(2,1)S(1)}, u32[]{:S(2)}, u32[]{:S(2)}) %collective-permute-start.14) | collective-permute-done | bytes 786464 | tf_op jit(solution)/shard_map/ppermute | solution.py:366
  99.3 14.3 %collective-permute-done.21.refs_7_ = bf16[512,768]{1,0:T(8,128)(2,1)S(1)} collective-permute-done((bf16[512,768]{1,0:T(8,128)(2,1)}, bf16[512,768]{1,0:T(8,128)(2,1)S(1)}, u32[]{:S(2)}, u32[]{:S(2)}) %collective-permute-start.21) | collective-permute-done | bytes 786464 | tf_op jit(solution)/shard_map/ppermute | solution.py:366
  113.7 1.3 collective-permute-start.9
  115.7 1.3 collective-permute-start.2
  117.0 1.7 collective-permute-start.13
  118.7 1.5 collective-permute-start.15
  120.2 10.2 %collective-permute-done.9.refs_1_ = bf16[128,2048]{1,0:T(8,128)(2,1)S(1)} collective-permute-done((bf16[128,2048]{1,0:T(8,128)(2,1)S(1)}, bf16[128,2048]{1,0:T(8,128)(2,1)S(1)}, u32[]{:S(2)}, u32[]{:S(2)}) %collective-permute-start.9) | collective-permute-done | bytes 524320 | tf_op jit(solution)/shard_map/ppermute | solution.py:369
  131.1 1.9 collective-permute-start.11
  133.0 1.0 copy-done.3
  134.8 1.0 shard_map.104
  135.8 2.9 %collective-permute-done.2.refs_1_ = bf16[128,2048]{1,0:T(8,128)(2,1)S(1)} collective-permute-done((bf16[128,2048]{1,0:T(8,128)(2,1)S(1)}, bf16[128,2048]{1,0:T(8,128)(2,1)S(1)}, u32[]{:S(2)}, u32[]{:S(2)}) %collective-permute-start.2) | collective-permute-done | bytes 524320 | tf_op jit(solution)/shard_map/ppermute | solution.py:369
  138.7 1.9 collective-permute-start.4
  140.7 4.7 %shard_map.105 = (f32[1024,768]{1,0:T(8,128)S(1)}, f32[1024,768]{1,0:T(8,128)S(1)}) custom-call(s32[3]{0:T(128)S(1)} %pad_add_fusion.place, bf16[1024,2048]{1,0:T(8,128)(2,1)S(1)} %get-tuple-element.57.x.refs_2_.refs_9_, bf16[2048,768]{1,0:T(8,128)(2,1)S(1)} %get-tuple-element.58.wg.refs_5_, bf16[2048,768]{1,0:T(8,128)(2,1)S(1)} %get-tuple-element.59.wu.refs_6_), custom_call_target="tpu_custom_call" | custom-call | flops 3623878656 | bytes 20447232 | tf_op jit(solution)/shard_map/pallas_call | solution.py:28
  145.4 1.0 shard_map.108.refs_5_
  146.4 1.8 collective-permute-start.32
  148.2 1.5 collective-permute-start.33
  150.6 3.2 %shard_map.106 = (bf16[1024,768]{1,0:T(8,128)(2,1)S(1)}, f32[1024,768]{1,0:T(8,128)S(1)}, f32[1024,768]{1,0:T(8,128)S(1)}, bf16[2048,768]{1,0:T(8,128)(2,1)S(1)}, bf16[2048,768]{1,0:T(8,128)(2,1)S(1)}) custom-call(s32[3]{0:T(128)S(1)} %pad_add_fusion.place, ...), custom_call_target="tpu_custom_call", output_to_operand_aliasing={{1}: (4, {}), {2}: (5, {}), {3}: (6, {}), {4}: (7, {})} | custom-call | flops 1207959552 | bytes 17825792 | tf_op jit(solution)/shard_map/pallas_call | solution.py:28
  153.7 2.5 shard_map.109
  156.2 2.9 %shard_map.107 = (bf16[1024,768]{1,0:T(8,128)(2,1)S(1)}, f32[1024,768]{1,0:T(8,128)S(1)}, f32[1024,768]{1,0:T(8,128)S(1)}, bf16[1024,2048]{1,0:T(8,128)(2,1)S(1)}) custom-call(s32[3]{0:T(128)S(1)} %pad_add_fusion.place, ...), custom_call_target="tpu_custom_call", output_to_operand_aliasing={{0}: (7, {}), {1}: (8, {}), {2}: (9, {}), {3}: (10, {})} | custom-call | flops 1610612736 | bytes 10747904 | tf_op jit(solution)/shard_map/pallas_call | solution.py:28
  159.2 1.8 shard_map.110
  161.1 7.0 %collective-permute-done.35.refs_5_ = bf16[384,512]{1,0:T(8,128)(2,1)S(1)} collective-permute-done((bf16[384,512]{1,0:T(8,128)(2,1)S(1)}, bf16[384,512]{1,0:T(8,128)(2,1)S(1)}, u32[]{:S(2)}, u32[]{:S(2)}) %collective-permute-start.35) | collective-permute-done | bytes 393248 | tf_op jit(solution)/shard_map/ppermute | solution.py:366
  168.1 6.3 %shard_map.111 = (bf16[1024,768]{1,0:T(8,128)(2,1)S(1)}, bf16[1024,768]{1,0:T(8,128)(2,1)S(1)}) custom-call(s32[3]{0:T(128)S(1)} %pad_add_fusion.place, bf16[1024,2048]{1,0:T(8,128)(2,1)S(1)} %get-tuple-element.76.y, f32[1024,768]{1,0:T(8,128)S(1)} %get-tuple-element.77.active, f32[1024,768]{1,0:T(8,128)S(1)} %get-tuple-element.78.slope, ...), custom_call_target="tpu_custom_call" | custom-call | flops 3221225472 | bytes 16777216 | tf_op jit(solution)/shard_map/pallas_call | solution.py:28
  174.4 8.1 %shard_map.112 = (bf16[512,2048]{1,0:T(8,128)(2,1)S(1)}, bf16[512,2048]{1,0:T(8,128)(2,1)S(1)}) custom-call(bf16[1024,768]{1,0:T(8,128)(2,1)S(1)} %get-tuple-element.79.gate_delta.gd, bf16[1024,768]{1,0:T(8,128)(2,1)S(1)} %get-tuple-element.80.up_delta.ud, bf16[2048,768]{1,0:T(8,128)(2,1)S(1)} %get-tuple-element.62.refs_4_.wg, ...), custom_call_target="tpu_custom_call" | custom-call | flops 6442450944 | bytes 13631488 | tf_op jit(solution)/shard_map/pallas_call | solution.py:28
  183.0 1.7 collective-permute-start.48
  184.7 5.2 %shard_map.114 = (bf16[2,512,768]{2,1,0:T(8,128)(2,1)S(1)}, bf16[2,512,768]{2,1,0:T(8,128)(2,1)S(1)}) custom-call(s32[3]{0:T(128)S(1)} %pad_add_fusion.place, bf16[1024,2048]{1,0:T(8,128)(2,1)S(1)} %get-tuple-element.83.x, bf16[1024,768]{1,0:T(8,128)(2,1)S(1)} %get-tuple-element.79.gate_delta.gd, bf16[1024,768]{1,0:T(8,128)(2,1)S(1)} %get-tuple-element.80.up_delta.ud), custom_call_target="tpu_custom_call" | custom-call | flops 3221225472 | bytes 10485760 | tf_op jit(solution)/shard_map/pallas_call | solution.py:28
  190.3 1.7 collective-permute-start.42
  192.0 2.4 shard_map.116
  194.4 5.2 %shard_map.113 = (bf16[512,768]{1,0:T(8,128)(2,1)S(1)}, bf16[512,768]{1,0:T(8,128)(2,1)S(1)}, bf16[512,768]{1,0:T(8,128)(2,1)S(1)}, bf16[512,768]{1,0:T(8,128)(2,1)S(1)}) custom-call(s32[3]{0:T(128)S(1)} %pad_add_fusion.place, bf16[1024,2048]{1,0:T(8,128)(2,1)S(1)} %get-tuple-element.83.x, bf16[1024,768]{1,0:T(8,128)(2,1)S(1)} %get-tuple-element.79.gate_delta.gd, ...), custom_call_target="tpu_custom_call" | custom-call | flops 3221225472 | bytes 10485760 | tf_op jit(solution)/shard_map/pallas_call | solution.py:28
  199.6 3.4 %collective-permute-done.46 = bf16[2,384,512]{2,1,0:T(8,128)(2,1)S(1)} collective-permute-done((bf16[2,384,512]{2,1,0:T(8,128)(2,1)S(1)}, bf16[2,384,512]{2,1,0:T(8,128)(2,1)S(1)}, u32[]{:S(2)}, u32[]{:S(2)}) %collective-permute-start.46) | collective-permute-done | bytes 786464 | tf_op jit(solution)/shard_map/ppermute | solution.py:363
  203.2 1.6 collective-permute-start.47
  205.4 0.8 add_convert_fusion
  206.3 1.3 collective-permute-start.40
  207.6 29.5 %collective-permute-done.43 = bf16[2,512,768]{2,1,0:T(8,128)(2,1)S(1)} collective-permute-done((bf16[2,512,768]{2,1,0:T(8,128)(2,1)S(1)}, bf16[2,512,768]{2,1,0:T(8,128)(2,1)S(1)}, u32[]{:S(2)}, u32[]{:S(2)}) %collective-permute-start.43) | collective-permute-done | bytes 1572896 | tf_op jit(solution)/shard_map/ppermute | solution.py:366
  237.5 1.7 collective-permute-start.45
  239.7 1.6 collective-permute-start.44
  242.1 3.4 %collective-permute-done.47 = bf16[384,512]{1,0:T(8,128)(2,1)S(1)} collective-permute-done((bf16[384,512]{1,0:T(8,128)(2,1)S(1)}, bf16[384,512]{1,0:T(8,128)(2,1)S(1)}, u32[]{:S(2)}, u32[]{:S(2)}) %collective-permute-start.47) | collective-permute-done | bytes 393248 | tf_op jit(solution)/shard_map/ppermute | solution.py:366
  245.6 3.3 %collective-permute-start.41 = (bf16[128,2048]{1,0:T(8,128)(2,1)S(1)}, bf16[128,2048]{1,0:T(8,128)(2,1)S(1)}, u32[]{:S(2)}, u32[]{:S(2)}) collective-permute-start(bf16[128,2048]{1,0:T(8,128)(2,1)S(1)} %add_convert_fusion.2), channel_id=1, source_target_pairs={{0,4},{1,5},{2,6},{3,7},{4,0},{5,1},{6,2},{7,3},{8,12},{9,13},{10,... | collective-permute-start | bytes 1572872 | tf_op jit(solution)/shard_map/ppermute | solution.py:369
  249.2 0.9 maximum_bitcast_fusion
  250.1 11.4 %collective-permute-done.45.up_last = bf16[512,768]{1,0:T(8,128)(2,1)S(1)} collective-permute-done((bf16[512,768]{1,0:T(8,128)(2,1)S(1)}, bf16[512,768]{1,0:T(8,128)(2,1)S(1)}, u32[]{:S(2)}, u32[]{:S(2)}) %collective-permute-start.45) | collective-permute-done | bytes 786464 | tf_op jit(solution)/shard_map/ppermute | solution.py:363
  261.6 1.3 shard_map.115
  262.9 3.4 %collective-permute-done.39 = bf16[128,2048]{1,0:T(8,128)(2,1)S(1)} collective-permute-done((bf16[128,2048]{1,0:T(8,128)(2,1)S(1)}, bf16[128,2048]{1,0:T(8,128)(2,1)S(1)}, u32[]{:S(2)}, u32[]{:S(2)}) %collective-permute-start.39) | collective-permute-done | bytes 524320 | tf_op jit(solution)/shard_map/ppermute | solution.py:369
  266.3 6.7 %collective-permute-done.41 = bf16[128,2048]{1,0:T(8,128)(2,1)S(1)} collective-permute-done((bf16[128,2048]{1,0:T(8,128)(2,1)S(1)}, bf16[128,2048]{1,0:T(8,128)(2,1)S(1)}, u32[]{:S(2)}, u32[]{:S(2)}) %collective-permute-start.41) | collective-permute-done | bytes 524320 | tf_op jit(solution)/shard_map/ppermute | solution.py:369
  273.0 1.1 add_convert_fusion.1
  (78 shorter events, 12.8 us)
Async XLA Ops:
  0.6 132.4 %copy-start.1 = (bf16[1,512,768]{2,1,0:T(8,128)(2,1)S(1)}, bf16[1,512,768]{2,1,0:T(8,128)(2,1)}, u32[]{:S(2)}) copy-start(bf16[1,512,768]{2,1,0:T(8,128)(2,1)} %param.11) | copy-start | bytes 2359300
  0.6 132.4 %copy-start.2 = (bf16[1,512,768]{2,1,0:T(8,128)(2,1)S(1)}, bf16[1,512,768]{2,1,0:T(8,128)(2,1)}, u32[]{:S(2)}) copy-start(bf16[1,512,768]{2,1,0:T(8,128)(2,1)} %param.12) | copy-start | bytes 2359300
  0.7 50.1 %collective-permute-start.8 = (bf16[128,2048]{1,0:T(8,128)(2,1)}, bf16[128,2048]{1,0:T(8,128)(2,1)S(1)}, u32[]{:S(2)}, u32[]{:S(2)}) collective-permute-start(bf16[128,2048]{1,0:T(8,128)(2,1)} %tokens.1), channel_id=1, source_target_pairs={{0,4},{1,5},{2,6},{3,7},{4,0},{5,1},{6,2},{7,3},{8,12},{9,13},{10,... | collective-permute-start | bytes 1572872 | tf_op jit(solution)/shard_map/ppermute | solution.py:369
  6.8 43.4 %collective-permute-start.31 = (bf16[384,512]{1,0:T(8,128)(2,1)}, bf16[384,512]{1,0:T(8,128)(2,1)S(1)}, u32[]{:S(2)}, u32[]{:S(2)}) collective-permute-start(bf16[384,512]{1,0:T(8,128)(2,1)} %get-tuple-element.107), channel_id=1, source_target_pairs={{0,8},{8,0},{16,24},{24,16},{1,9},{9,1},{17,25},{25,17},{2,10},{10... | collective-permute-start | bytes 1179656 | tf_op jit(solution)/shard_map/ppermute | solution.py:363
  8.3 41.9 %collective-permute-start.34 = (bf16[384,512]{1,0:T(8,128)(2,1)}, bf16[384,512]{1,0:T(8,128)(2,1)S(1)}, u32[]{:S(2)}, u32[]{:S(2)}) collective-permute-start(bf16[384,512]{1,0:T(8,128)(2,1)} %get-tuple-element.106), channel_id=1, source_target_pairs={{0,16},{8,24},{16,0},{24,8},{1,17},{9,25},{17,1},{25,9},{2,18},{10... | collective-permute-start | bytes 1179656 | tf_op jit(solution)/shard_map/ppermute | solution.py:366
  9.8 44.6 %collective-permute-start.16 = (bf16[128,2048]{1,0:T(8,128)(2,1)}, bf16[128,2048]{1,0:T(8,128)(2,1)S(1)}, u32[]{:S(2)}, u32[]{:S(2)}) collective-permute-start(bf16[128,2048]{1,0:T(8,128)(2,1)} %tokens.1), channel_id=1, source_target_pairs={{0,2},{1,3},{2,0},{3,1},{4,6},{5,7},{6,4},{7,5},{8,10},{9,11},{10,... | collective-permute-start | bytes 1572872 | tf_op jit(solution)/shard_map/ppermute | solution.py:369
  11.5 0.7 copy-start.5
  12.2 0.7 copy-start.6
  13.4 14.9 %collective-permute-start.28 = (f32[1,128]{1,0:T(1,128)S(1)}, f32[1,128]{1,0:T(1,128)S(1)}, u32[]{:S(2)}, u32[]{:S(2)}) collective-permute-start(f32[1,128]{1,0:T(1,128)S(1)} %get-tuple-element.71), channel_id=1, source_target_pairs={{0,4},{1,5},{2,6},{3,7},{4,0},{5,1},{6,2},{7,3},{8,12},{9,13},{10,... | collective-permute-start | bytes 1544 | tf_op jit(solution)/shard_map/ppermute | solution.py:393
  28.4 1.2 collective-permute-start.29
  29.5 3.9 %collective-permute-start.30 = (f32[1,128]{1,0:T(1,128)S(1)}, f32[1,128]{1,0:T(1,128)S(1)}, u32[]{:S(2)}, u32[]{:S(2)}) collective-permute-start(f32[1,128]{1,0:T(1,128)S(1)} %get-tuple-element.73), channel_id=1, source_target_pairs={{0,5},{1,4},{2,7},{3,6},{4,1},{5,0},{6,3},{7,2},{8,13},{9,12},{10,... | collective-permute-start | bytes 1544 | tf_op jit(solution)/shard_map/ppermute | solution.py:393
  33.4 3.6 %collective-permute-start.24 = (f32[1,128]{1,0:T(1,128)S(1)}, f32[1,128]{1,0:T(1,128)S(1)}, u32[]{:S(2)}, u32[]{:S(2)}) collective-permute-start(f32[1,128]{1,0:T(1,128)S(1)} %get-tuple-element.68), channel_id=1, source_target_pairs={{0,2},{1,3},{2,0},{3,1},{4,6},{5,7},{6,4},{7,5},{8,10},{9,11},{10,... | collective-permute-start | bytes 1544 | tf_op jit(solution)/shard_map/ppermute | solution.py:393
  37.0 3.0 %collective-permute-start.25 = (f32[1,128]{1,0:T(1,128)S(1)}, f32[1,128]{1,0:T(1,128)S(1)}, u32[]{:S(2)}, u32[]{:S(2)}) collective-permute-start(f32[1,128]{1,0:T(1,128)S(1)} %get-tuple-element.69), channel_id=1, source_target_pairs={{0,3},{1,2},{2,1},{3,0},{4,7},{5,6},{6,5},{7,4},{8,11},{9,10},{10,... | collective-permute-start | bytes 1544 | tf_op jit(solution)/shard_map/ppermute | solution.py:393
  40.0 5.4 %collective-permute-start.5 = (f32[1,128]{1,0:T(1,128)S(1)}, f32[1,128]{1,0:T(1,128)S(1)}, u32[]{:S(2)}, u32[]{:S(2)}) collective-permute-start(f32[1,128]{1,0:T(1,128)S(1)} %get-tuple-element.52), channel_id=1, source_target_pairs={{0,6},{1,7},{2,4},{3,5},{4,2},{5,3},{6,0},{7,1},{8,14},{9,15},{10,... | collective-permute-start | bytes 1544 | tf_op jit(solution)/shard_map/ppermute | solution.py:393
  45.3 4.8 %collective-permute-start.6 = (f32[1,128]{1,0:T(1,128)S(1)}, f32[1,128]{1,0:T(1,128)S(1)}, u32[]{:S(2)}, u32[]{:S(2)}) collective-permute-start(f32[1,128]{1,0:T(1,128)S(1)} %get-tuple-element.53), channel_id=1, source_target_pairs={{0,7},{1,6},{2,5},{3,4},{4,3},{5,2},{6,1},{7,0},{8,15},{9,14},{10,... | collective-permute-start | bytes 1544 | tf_op jit(solution)/shard_map/ppermute | solution.py:393
  50.1 5.0 %collective-permute-start.17 = (bf16[128,2048]{1,0:T(8,128)(2,1)}, bf16[128,2048]{1,0:T(8,128)(2,1)S(1)}, u32[]{:S(2)}, u32[]{:S(2)}) collective-permute-start(bf16[128,2048]{1,0:T(8,128)(2,1)} %tokens.1), channel_id=1, source_target_pairs={{0,1},{1,0},{2,3},{3,2},{4,5},{5,4},{6,7},{7,6},{8,9},{9,8},{10,11... | collective-permute-start | bytes 1572872 | tf_op jit(solution)/shard_map/ppermute | solution.py:372
  50.2 27.2 %collective-permute-start.1 = (bf16[128,2048]{1,0:T(8,128)(2,1)}, bf16[128,2048]{1,0:T(8,128)(2,1)S(1)}, u32[]{:S(2)}, u32[]{:S(2)}) collective-permute-start(bf16[128,2048]{1,0:T(8,128)(2,1)} %refs_0_.1), channel_id=1, source_target_pairs={{0,4},{1,5},{2,6},{3,7},{4,0},{5,1},{6,2},{7,3},{8,12},{9,13},{10,... | collective-permute-start | bytes 1572872 | tf_op jit(solution)/shard_map/ppermute | solution.py:369
  50.3 27.9 %collective-permute-start.26 = (bf16[128,2048]{1,0:T(8,128)(2,1)}, bf16[128,2048]{1,0:T(8,128)(2,1)S(1)}, u32[]{:S(2)}, u32[]{:S(2)}) collective-permute-start(bf16[128,2048]{1,0:T(8,128)(2,1)} %refs_0_.1), channel_id=1, source_target_pairs={{0,1},{1,0},{2,3},{3,2},{4,5},{5,4},{6,7},{7,6},{8,9},{9,8},{10,11... | collective-permute-start | bytes 1572872 | tf_op jit(solution)/shard_map/ppermute | solution.py:372
  50.7 29.0 %collective-permute-start.22 = (bf16[128,2048]{1,0:T(8,128)(2,1)}, bf16[128,2048]{1,0:T(8,128)(2,1)S(1)}, u32[]{:S(2)}, u32[]{:S(2)}) collective-permute-start(bf16[128,2048]{1,0:T(8,128)(2,1)} %refs_0_.1), channel_id=1, source_target_pairs={{0,2},{1,3},{2,0},{3,1},{4,6},{5,7},{6,4},{7,5},{8,10},{9,11},{10,... | collective-permute-start | bytes 1572872 | tf_op jit(solution)/shard_map/ppermute | solution.py:369
  54.5 26.7 %collective-permute-start.7 = (bf16[128,2048]{1,0:T(8,128)(2,1)}, bf16[128,2048]{1,0:T(8,128)(2,1)S(1)}, u32[]{:S(2)}, u32[]{:S(2)}) collective-permute-start(bf16[128,2048]{1,0:T(8,128)(2,1)} %tokens.1), channel_id=1, source_target_pairs={{2,4},{3,5},{4,2},{5,3},{10,12},{11,13},{12,10},{13,11},{18,20},{1... | collective-permute-start | bytes 1572872 | tf_op jit(solution)/shard_map/ppermute | solution.py:369
  55.2 26.6 %collective-permute-start.12 = (bf16[512,768]{1,0:T(8,128)(2,1)}, bf16[512,768]{1,0:T(8,128)(2,1)S(1)}, u32[]{:S(2)}, u32[]{:S(2)}) collective-permute-start(bf16[512,768]{1,0:T(8,128)(2,1)} %bitcast.55), channel_id=1, source_target_pairs={{0,8},{8,0},{16,24},{24,16},{1,9},{9,1},{17,25},{25,17},{2,10},{10... | collective-permute-start | bytes 2359304 | tf_op jit(solution)/shard_map/ppermute | solution.py:363
  77.4 4.3 %collective-permute-start = (bf16[128,2048]{1,0:T(8,128)(2,1)}, bf16[128,2048]{1,0:T(8,128)(2,1)S(1)}, u32[]{:S(2)}, u32[]{:S(2)}) collective-permute-start(bf16[128,2048]{1,0:T(8,128)(2,1)} %refs_0_.1), channel_id=1, source_target_pairs={{2,4},{3,5},{4,2},{5,3},{10,12},{11,13},{12,10},{13,11},{18,20},{1... | collective-permute-start | bytes 1572872 | tf_op jit(solution)/shard_map/ppermute | solution.py:369
  78.1 20.7 %collective-permute-start.14 = (bf16[512,768]{1,0:T(8,128)(2,1)}, bf16[512,768]{1,0:T(8,128)(2,1)S(1)}, u32[]{:S(2)}, u32[]{:S(2)}) collective-permute-start(bf16[512,768]{1,0:T(8,128)(2,1)} %bitcast.58), channel_id=1, source_target_pairs={{0,16},{8,24},{16,0},{24,8},{1,17},{9,25},{17,1},{25,9},{2,18},{10... | collective-permute-start | bytes 2359304 | tf_op jit(solution)/shard_map/ppermute | solution.py:366
  79.7 19.1 %collective-permute-start.20 = (bf16[512,768]{1,0:T(8,128)(2,1)}, bf16[512,768]{1,0:T(8,128)(2,1)S(1)}, u32[]{:S(2)}, u32[]{:S(2)}) collective-permute-start(bf16[512,768]{1,0:T(8,128)(2,1)} %bitcast.59), channel_id=1, source_target_pairs={{0,8},{8,0},{16,24},{24,16},{1,9},{9,1},{17,25},{25,17},{2,10},{10... | collective-permute-start | bytes 2359304 | tf_op jit(solution)/shard_map/ppermute | solution.py:363
  81.2 32.5 %collective-permute-start.21 = (bf16[512,768]{1,0:T(8,128)(2,1)}, bf16[512,768]{1,0:T(8,128)(2,1)S(1)}, u32[]{:S(2)}, u32[]{:S(2)}) collective-permute-start(bf16[512,768]{1,0:T(8,128)(2,1)} %bitcast.56), channel_id=1, source_target_pairs={{0,16},{8,24},{16,0},{24,8},{1,17},{9,25},{17,1},{25,9},{2,18},{10... | collective-permute-start | bytes 2359304 | tf_op jit(solution)/shard_map/ppermute | solution.py:366
  81.7 33.2 %collective-permute-start.18 = (bf16[128,2048]{1,0:T(8,128)(2,1)S(1)}, bf16[128,2048]{1,0:T(8,128)(2,1)S(1)}, u32[]{:S(2)}, u32[]{:S(2)}) collective-permute-start(bf16[128,2048]{1,0:T(8,128)(2,1)S(1)} %collective-permute-done.8.refs_0_), channel_id=1, source_target_pairs={{0,1},{1,0},{2,3},{3,2},{4,5},{5,4},{6,7},{7,6},{8,9},{9,8},{10,11... | collective-permute-start | bytes 1572872 | tf_op jit(solution)/shard_map/ppermute | solution.py:372
  81.7 33.9 %collective-permute-start.19 = (bf16[128,2048]{1,0:T(8,128)(2,1)S(1)}, bf16[128,2048]{1,0:T(8,128)(2,1)S(1)}, u32[]{:S(2)}, u32[]{:S(2)}) collective-permute-start(bf16[128,2048]{1,0:T(8,128)(2,1)S(1)} %collective-permute-done.16.refs_1_), channel_id=1, source_target_pairs={{0,1},{1,0},{2,3},{3,2},{4,5},{5,4},{6,7},{7,6},{8,9},{9,8},{10,11... | collective-permute-start | bytes 1572872 | tf_op jit(solution)/shard_map/ppermute | solution.py:372
  98.8 18.2 %collective-permute-start.27 = (bf16[128,2048]{1,0:T(8,128)(2,1)S(1)}, bf16[128,2048]{1,0:T(8,128)(2,1)S(1)}, u32[]{:S(2)}, u32[]{:S(2)}) collective-permute-start(bf16[128,2048]{1,0:T(8,128)(2,1)S(1)} %collective-permute-done.1.refs_1_), channel_id=1, source_target_pairs={{0,1},{1,0},{2,3},{3,2},{4,5},{5,4},{6,7},{7,6},{8,9},{9,8},{10,11... | collective-permute-start | bytes 1572872 | tf_op jit(solution)/shard_map/ppermute | solution.py:372
  98.8 19.9 %collective-permute-start.23 = (bf16[128,2048]{1,0:T(8,128)(2,1)S(1)}, bf16[128,2048]{1,0:T(8,128)(2,1)S(1)}, u32[]{:S(2)}, u32[]{:S(2)}) collective-permute-start(bf16[128,2048]{1,0:T(8,128)(2,1)S(1)} %collective-permute-done.22.refs_0_), channel_id=1, source_target_pairs={{0,1},{1,0},{2,3},{3,2},{4,5},{5,4},{6,7},{7,6},{8,9},{9,8},{10,11... | collective-permute-start | bytes 1572872 | tf_op jit(solution)/shard_map/ppermute | solution.py:372
  113.7 16.7 %collective-permute-start.9 = (bf16[128,2048]{1,0:T(8,128)(2,1)S(1)}, bf16[128,2048]{1,0:T(8,128)(2,1)S(1)}, u32[]{:S(2)}, u32[]{:S(2)}) collective-permute-start(bf16[128,2048]{1,0:T(8,128)(2,1)S(1)} %collective-permute-done.8.refs_0_), channel_id=1, source_target_pairs={{4,6},{5,7},{2,0},{3,1},{12,14},{13,15},{10,8},{11,9},{20,22},{21,... | collective-permute-start | bytes 1572872 | tf_op jit(solution)/shard_map/ppermute | solution.py:369
  115.0 16.1 %collective-permute-start.10 = (bf16[128,2048]{1,0:T(8,128)(2,1)S(1)}, bf16[128,2048]{1,0:T(8,128)(2,1)S(1)}, u32[]{:S(2)}, u32[]{:S(2)}) collective-permute-start(bf16[128,2048]{1,0:T(8,128)(2,1)S(1)} %collective-permute-done.7.refs_0_), channel_id=1, source_target_pairs={{2,3},{3,2},{4,5},{5,4},{10,11},{11,10},{12,13},{13,12},{18,19},{1... | collective-permute-start | bytes 1572872 | tf_op jit(solution)/shard_map/ppermute | solution.py:372
  115.7 23.0 %collective-permute-start.2 = (bf16[128,2048]{1,0:T(8,128)(2,1)S(1)}, bf16[128,2048]{1,0:T(8,128)(2,1)S(1)}, u32[]{:S(2)}, u32[]{:S(2)}) collective-permute-start(bf16[128,2048]{1,0:T(8,128)(2,1)S(1)} %collective-permute-done.1.refs_1_), channel_id=1, source_target_pairs={{4,6},{5,7},{2,0},{3,1},{12,14},{13,15},{10,8},{11,9},{20,22},{21,... | collective-permute-start | bytes 1572872 | tf_op jit(solution)/shard_map/ppermute | solution.py:369
  117.0 32.7 %collective-permute-start.13 = (bf16[512,768]{1,0:T(8,128)(2,1)S(1)}, bf16[512,768]{1,0:T(8,128)(2,1)S(1)}, u32[]{:S(2)}, u32[]{:S(2)}) collective-permute-start(bf16[512,768]{1,0:T(8,128)(2,1)S(1)} %collective-permute-done.12.refs_5_), channel_id=1, source_target_pairs={{0,16},{8,24},{16,0},{24,8},{1,17},{9,25},{17,1},{25,9},{2,18},{10... | collective-permute-start | bytes 2359304 | tf_op jit(solution)/shard_map/ppermute | solution.py:366
  118.7 31.5 %collective-permute-start.15 = (bf16[512,768]{1,0:T(8,128)(2,1)S(1)}, bf16[512,768]{1,0:T(8,128)(2,1)S(1)}, u32[]{:S(2)}, u32[]{:S(2)}) collective-permute-start(bf16[512,768]{1,0:T(8,128)(2,1)S(1)} %collective-permute-done.14.refs_8_), channel_id=1, source_target_pairs={{0,8},{8,0},{16,24},{24,16},{1,9},{9,1},{17,25},{25,17},{2,10},{10... | collective-permute-start | bytes 2359304 | tf_op jit(solution)/shard_map/ppermute | solution.py:363
  130.4 16.1 %collective-permute-start.3 = (bf16[128,2048]{1,0:T(8,128)(2,1)S(1)}, bf16[128,2048]{1,0:T(8,128)(2,1)S(1)}, u32[]{:S(2)}, u32[]{:S(2)}) collective-permute-start(bf16[128,2048]{1,0:T(8,128)(2,1)S(1)} %collective-permute-done.refs_0_), channel_id=1, source_target_pairs={{2,3},{3,2},{4,5},{5,4},{10,11},{11,10},{12,13},{13,12},{18,19},{1... | collective-permute-start | bytes 1572872 | tf_op jit(solution)/shard_map/ppermute | solution.py:372
  131.1 17.1 %collective-permute-start.11 = (bf16[128,2048]{1,0:T(8,128)(2,1)S(1)}, bf16[128,2048]{1,0:T(8,128)(2,1)S(1)}, u32[]{:S(2)}, u32[]{:S(2)}) collective-permute-start(bf16[128,2048]{1,0:T(8,128)(2,1)S(1)} %collective-permute-done.9.refs_1_), channel_id=1, source_target_pairs={{0,1},{1,0},{6,7},{7,6},{8,9},{9,8},{14,15},{15,14},{16,17},{17,16... | collective-permute-start | bytes 1572872 | tf_op jit(solution)/shard_map/ppermute | solution.py:372
  133.0 1.0 copy-start.3
  138.7 20.4 %collective-permute-start.4 = (bf16[128,2048]{1,0:T(8,128)(2,1)S(1)}, bf16[128,2048]{1,0:T(8,128)(2,1)S(1)}, u32[]{:S(2)}, u32[]{:S(2)}) collective-permute-start(bf16[128,2048]{1,0:T(8,128)(2,1)S(1)} %collective-permute-done.2.refs_1_), channel_id=1, source_target_pairs={{0,1},{1,0},{6,7},{7,6},{8,9},{9,8},{14,15},{15,14},{16,17},{17,16... | collective-permute-start | bytes 1572872 | tf_op jit(solution)/shard_map/ppermute | solution.py:372
  140.7 4.7 %copy-start.4 = (bf16[128,2048]{1,0:T(8,128)(2,1)S(1)}, bf16[128,2048]{1,0:T(8,128)(2,1)}, u32[]{:S(2)}) copy-start(bf16[128,2048]{1,0:T(8,128)(2,1)} %refs_0_.1) | copy-start | bytes 1572868
  146.4 14.6 %collective-permute-start.32 = (bf16[384,512]{1,0:T(8,128)(2,1)}, bf16[384,512]{1,0:T(8,128)(2,1)S(1)}, u32[]{:S(2)}, u32[]{:S(2)}) collective-permute-start(bf16[384,512]{1,0:T(8,128)(2,1)} %get-tuple-element.106), channel_id=1, source_target_pairs={{0,8},{8,0},{16,24},{24,16},{1,9},{9,1},{17,25},{25,17},{2,10},{10... | collective-permute-start | bytes 1179656 | tf_op jit(solution)/shard_map/ppermute | solution.py:363
  148.2 12.9 %collective-permute-start.33 = (bf16[384,512]{1,0:T(8,128)(2,1)}, bf16[384,512]{1,0:T(8,128)(2,1)S(1)}, u32[]{:S(2)}, u32[]{:S(2)}) collective-permute-start(bf16[384,512]{1,0:T(8,128)(2,1)} %get-tuple-element.107), channel_id=1, source_target_pairs={{0,16},{8,24},{16,0},{24,8},{1,17},{9,25},{17,1},{25,9},{2,18},{10... | collective-permute-start | bytes 1179656 | tf_op jit(solution)/shard_map/ppermute | solution.py:366
  149.7 18.3 %collective-permute-start.35 = (bf16[384,512]{1,0:T(8,128)(2,1)S(1)}, bf16[384,512]{1,0:T(8,128)(2,1)S(1)}, u32[]{:S(2)}, u32[]{:S(2)}) collective-permute-start(bf16[384,512]{1,0:T(8,128)(2,1)S(1)} %collective-permute-done.31.refs_1_), channel_id=1, source_target_pairs={{0,16},{8,24},{16,0},{24,8},{1,17},{9,25},{17,1},{25,9},{2,18},{10... | collective-permute-start | bytes 1179656 | tf_op jit(solution)/shard_map/ppermute | solution.py:366
  150.2 17.8 %collective-permute-start.36 = (bf16[384,512]{1,0:T(8,128)(2,1)S(1)}, bf16[384,512]{1,0:T(8,128)(2,1)S(1)}, u32[]{:S(2)}, u32[]{:S(2)}) collective-permute-start(bf16[384,512]{1,0:T(8,128)(2,1)S(1)} %collective-permute-done.34.refs_4_), channel_id=1, source_target_pairs={{0,8},{8,0},{16,24},{24,16},{1,9},{9,1},{17,25},{25,17},{2,10},{10... | collective-permute-start | bytes 1179656 | tf_op jit(solution)/shard_map/ppermute | solution.py:363
  159.2 8.9 %copy-start = (bf16[1,768,512]{2,1,0:T(8,128)(2,1)S(1)}, bf16[1,768,512]{2,1,0:T(8,128)(2,1)}, u32[]{:S(2)}) copy-start(bf16[1,768,512]{2,1,0:T(8,128)(2,1)} %param.13) | copy-start | bytes 2359300
  182.5 22.9 %collective-permute-start.37 = (bf16[512,2048]{1,0:T(8,128)(2,1)S(1)}, bf16[512,2048]{1,0:T(8,128)(2,1)S(1)}, u32[]{:S(2)}, u32[]{:S(2)}) collective-permute-start(bf16[512,2048]{1,0:T(8,128)(2,1)S(1)} %get-tuple-element.82), channel_id=1, source_target_pairs={{0,1},{1,0},{2,3},{3,2},{4,5},{5,4},{6,7},{7,6},{8,9},{9,8},{10,11... | collective-permute-start | bytes 6291464 | tf_op jit(solution)/shard_map/ppermute | solution.py:372
  182.6 20.5 %collective-permute-start.46 = (bf16[2,384,512]{2,1,0:T(8,128)(2,1)S(1)}, bf16[2,384,512]{2,1,0:T(8,128)(2,1)S(1)}, u32[]{:S(2)}, u32[]{:S(2)}) collective-permute-start(bf16[2,384,512]{2,1,0:T(8,128)(2,1)S(1)} %get-tuple-element.95), channel_id=1, source_target_pairs={{0,8},{8,0},{16,24},{24,16},{1,9},{9,1},{17,25},{25,17},{2,10},{10... | collective-permute-start | bytes 2359304 | tf_op jit(solution)/shard_map/ppermute | solution.py:363
  183.0 21.8 %collective-permute-start.48 = (bf16[2,384,512]{2,1,0:T(8,128)(2,1)S(1)}, bf16[2,384,512]{2,1,0:T(8,128)(2,1)S(1)}, u32[]{:S(2)}, u32[]{:S(2)}) collective-permute-start(bf16[2,384,512]{2,1,0:T(8,128)(2,1)S(1)} %get-tuple-element.98), channel_id=1, source_target_pairs={{0,16},{8,24},{16,0},{24,8},{1,17},{9,25},{17,1},{25,9},{2,18},{10... | collective-permute-start | bytes 2359304 | tf_op jit(solution)/shard_map/ppermute | solution.py:366
  189.9 47.2 %collective-permute-start.43 = (bf16[2,512,768]{2,1,0:T(8,128)(2,1)S(1)}, bf16[2,512,768]{2,1,0:T(8,128)(2,1)S(1)}, u32[]{:S(2)}, u32[]{:S(2)}) collective-permute-start(bf16[2,512,768]{2,1,0:T(8,128)(2,1)S(1)} %get-tuple-element.87), channel_id=1, source_target_pairs={{0,16},{8,24},{16,0},{24,8},{1,17},{9,25},{17,1},{25,9},{2,18},{10... | collective-permute-start | bytes 4718600 | tf_op jit(solution)/shard_map/ppermute | solution.py:366
  190.3 48.9 %collective-permute-start.42 = (bf16[2,512,768]{2,1,0:T(8,128)(2,1)S(1)}, bf16[2,512,768]{2,1,0:T(8,128)(2,1)S(1)}, u32[]{:S(2)}, u32[]{:S(2)}) collective-permute-start(bf16[2,512,768]{2,1,0:T(8,128)(2,1)S(1)} %get-tuple-element.85), channel_id=1, source_target_pairs={{0,8},{8,0},{16,24},{24,16},{1,9},{9,1},{17,25},{25,17},{2,10},{10... | collective-permute-start | bytes 4718600 | tf_op jit(solution)/shard_map/ppermute | solution.py:363
  203.2 42.4 %collective-permute-start.47 = (bf16[384,512]{1,0:T(8,128)(2,1)S(1)}, bf16[384,512]{1,0:T(8,128)(2,1)S(1)}, u32[]{:S(2)}, u32[]{:S(2)}) collective-permute-start(bf16[384,512]{1,0:T(8,128)(2,1)S(1)} %fusion.7), channel_id=1, source_target_pairs={{0,16},{8,24},{16,0},{24,8},{1,17},{9,25},{17,1},{25,9},{2,18},{10... | collective-permute-start | bytes 1179656 | tf_op jit(solution)/shard_map/ppermute | solution.py:366
  204.9 40.7 %collective-permute-start.49 = (bf16[384,512]{1,0:T(8,128)(2,1)S(1)}, bf16[384,512]{1,0:T(8,128)(2,1)S(1)}, u32[]{:S(2)}, u32[]{:S(2)}) collective-permute-start(bf16[384,512]{1,0:T(8,128)(2,1)S(1)} %fusion.4), channel_id=1, source_target_pairs={{0,8},{8,0},{16,24},{24,16},{1,9},{9,1},{17,25},{25,17},{2,10},{10... | collective-permute-start | bytes 1179656 | tf_op jit(solution)/shard_map/ppermute | solution.py:363
  206.3 35.0 %collective-permute-start.40 = (bf16[128,2048]{1,0:T(8,128)(2,1)S(1)}, bf16[128,2048]{1,0:T(8,128)(2,1)S(1)}, u32[]{:S(2)}, u32[]{:S(2)}) collective-permute-start(bf16[128,2048]{1,0:T(8,128)(2,1)S(1)} %get-tuple-element.101), channel_id=1, source_target_pairs={{0,2},{1,3},{6,4},{7,5},{8,10},{9,11},{14,12},{15,13},{16,18},{17,... | collective-permute-start | bytes 1572872 | tf_op jit(solution)/shard_map/ppermute | solution.py:369
  237.5 24.0 %collective-permute-start.45 = (bf16[512,768]{1,0:T(8,128)(2,1)S(1)}, bf16[512,768]{1,0:T(8,128)(2,1)S(1)}, u32[]{:S(2)}, u32[]{:S(2)}) collective-permute-start(bf16[512,768]{1,0:T(8,128)(2,1)S(1)} %get-tuple-element.102), channel_id=1, source_target_pairs={{0,8},{8,0},{16,24},{24,16},{1,9},{9,1},{17,25},{25,17},{2,10},{10... | collective-permute-start | bytes 2359304 | tf_op jit(solution)/shard_map/ppermute | solution.py:363
  239.7 21.9 %collective-permute-start.44 = (bf16[512,768]{1,0:T(8,128)(2,1)S(1)}, bf16[512,768]{1,0:T(8,128)(2,1)S(1)}, u32[]{:S(2)}, u32[]{:S(2)}) collective-permute-start(bf16[512,768]{1,0:T(8,128)(2,1)S(1)} %get-tuple-element.104), channel_id=1, source_target_pairs={{0,16},{8,24},{16,0},{24,8},{1,17},{9,25},{17,1},{25,9},{2,18},{10... | collective-permute-start | bytes 2359304 | tf_op jit(solution)/shard_map/ppermute | solution.py:366
  241.3 21.6 %collective-permute-start.38 = (bf16[128,2048]{1,0:T(8,128)(2,1)S(1)}, bf16[128,2048]{1,0:T(8,128)(2,1)S(1)}, u32[]{:S(2)}, u32[]{:S(2)}) collective-permute-start(bf16[128,2048]{1,0:T(8,128)(2,1)S(1)} %get-tuple-element.101), channel_id=1, source_target_pairs={{2,4},{3,5},{4,2},{5,3},{10,12},{11,13},{12,10},{13,11},{18,20},{1... | collective-permute-start | bytes 1572872 | tf_op jit(solution)/shard_map/ppermute | solution.py:369
  245.5 20.8 %collective-permute-start.39 = (bf16[128,2048]{1,0:T(8,128)(2,1)S(1)}, bf16[128,2048]{1,0:T(8,128)(2,1)S(1)}, u32[]{:S(2)}, u32[]{:S(2)}) collective-permute-start(bf16[128,2048]{1,0:T(8,128)(2,1)S(1)} %get-tuple-element.100), channel_id=1, source_target_pairs={{0,2},{1,3},{2,0},{3,1},{4,6},{5,7},{6,4},{7,5},{8,10},{9,11},{10,... | collective-permute-start | bytes 1572872 | tf_op jit(solution)/shard_map/ppermute | solution.py:369
  245.6 27.4 %collective-permute-start.41 = (bf16[128,2048]{1,0:T(8,128)(2,1)S(1)}, bf16[128,2048]{1,0:T(8,128)(2,1)S(1)}, u32[]{:S(2)}, u32[]{:S(2)}) collective-permute-start(bf16[128,2048]{1,0:T(8,128)(2,1)S(1)} %add_convert_fusion.2), channel_id=1, source_target_pairs={{0,4},{1,5},{2,6},{3,7},{4,0},{5,1},{6,2},{7,3},{8,12},{9,13},{10,... | collective-permute-start | bytes 1572872 | tf_op jit(solution)/shard_map/ppermute | solution.py:369
